TPU v7x, 32 devices: a whole 2x2x4 slice. The times are simulated.
32 devices in a mesh: section: 2 (over y), dp: 4 (over x, core), tensor: 4 (over z).
Axes of the slice: x: 2, y: 2, z: 4, core: 2. Of those that a mesh axis runs over, the one named last changes fastest.
Arguments:
- acts_in: bfloat16 [4, 1024, 4, 1024], P(None, 'tensor', 'dp'), may hold values from -6 to 6
- cotangent: bfloat16 [4, 1024, 4, 1024], P(None, 'tensor', 'dp'), may hold values from -6 to 6
- norm_gains: float32 [2, 2, 1024], P('section', None, ('dp', 'tensor')), may hold values from 0.5 to 1.5
- vec_bias: float32 [2, 4, 1024], P('section', None, ('dp', 'tensor')), may hold values from -1.8 to 1.8
- w_qkv: bfloat16 [2, 1024, 3072], P('section', 'dp', 'tensor'), may hold values from -0.25 to 0.25
- b_qkv: bfloat16 [2, 16, 192], P('section', 'tensor', 'dp'), may hold values from -1.796875 to 1.796875
- w_out: bfloat16 [2, 1024, 1024], P('section', 'tensor', 'dp'), may hold values from -0.75 to 0.75
- w_up: bfloat16 [2, 1024, 4096], P('section', 'dp', 'tensor'), may hold values from -0.1875 to 0.1875
- b_up: bfloat16 [2, 32, 128], P('section', 'tensor', 'dp'), may hold values from -1.796875 to 1.796875
- w_down: bfloat16 [2, 4096, 1024], P('section', 'tensor', 'dp'), may hold values from -0.09375 to 0.09375
Outputs:
- acts_out: bfloat16 [2, 4, 1024, 4, 1024], P('section', None, 'tensor', 'dp')
- grad_in: bfloat16 [2, 4, 1024, 4, 1024], P('section', None, 'tensor', 'dp')
- grad_norm_gains: float32 [2, 2, 1024], P('section', None, ('dp', 'tensor'))
- grad_vec_bias: float32 [2, 4, 1024], P('section', None, ('dp', 'tensor'))
- grad_w_qkv: float32 [2, 1024, 3072], P('section', 'dp', 'tensor')
- grad_b_qkv: float32 [2, 16, 192], P('section', 'tensor', 'dp')
- grad_w_out: float32 [2, 1024, 1024], P('section', 'tensor', 'dp')
- grad_w_up: float32 [2, 1024, 4096], P('section', 'dp', 'tensor')
- grad_b_up: float32 [2, 32, 128], P('section', 'tensor', 'dp')
- grad_w_down: float32 [2, 4096, 1024], P('section', 'tensor', 'dp')
All inputs are finite; a program needn't handle non-finite values.
Results may differ from a plain program's by a relative error of at most 0.025.
Values may be sent and summed in bfloat16 or wider, within the bound.
No kernel may reach another device: no remote copies, remote signals or barrier semaphores. Data moves between devices by JAX's collectives and lax.ppermute only.
A program may use at most 384 MiB of HBM per device.

v0:
```python
from functools import partial
import math

import jax
import jax.numpy as jnp
from jax import lax
from jax.sharding import PartitionSpec as P

ROT = 16
QBLOCK = 512
MICRO = 4


NORM_EPS = 1e-05
ROPE_BASE = 10000.0
MASK_FILL = -1e30


def from_behind(value, axis, by):
    length = lax.axis_size(axis)
    pairs = [(i, i + by) for i in range(length) if 0 <= i + by < length]
    return lax.ppermute(value, axis, pairs)


def layer_norm(values, norm_gain, norm_shift):
    average = jnp.mean(values, axis=-1, keepdims=True)
    centred = values - average
    variance = jnp.mean(centred * centred, axis=-1, keepdims=True)
    return centred * lax.rsqrt(variance + NORM_EPS) * norm_gain + norm_shift


def both_norms(values, gain_attn, shift_attn, gain_mlp, shift_mlp):
    return (layer_norm(values, gain_attn, shift_attn), layer_norm(values, gain_mlp, shift_mlp))


def rotary_tables(length):
    half_rot = ROT // 2
    frequency = jnp.exp(
        jnp.arange(half_rot, dtype=jnp.float32) * (-2.0 * math.log(ROPE_BASE) / ROT)
    )
    angles = jnp.arange(length, dtype=jnp.float32)[:, None] * frequency[None, :]
    return (jnp.cos(angles), jnp.sin(angles))


def rotate(values, cosine, sine_tab):
    half_rot = ROT // 2
    low_half = values[..., :half_rot]
    high_half = values[..., half_rot:ROT]
    return jnp.concatenate(
        [
            low_half * cosine - high_half * sine_tab,
            high_half * cosine + low_half * sine_tab,
            values[..., ROT:],
        ],
        axis=-1,
    )


def rotate_back(grads_rot, cosine, sine_tab):
    half_rot = ROT // 2
    low_half = grads_rot[..., :half_rot]
    high_half = grads_rot[..., half_rot:ROT]
    return jnp.concatenate(
        [
            low_half * cosine + high_half * sine_tab,
            high_half * cosine - low_half * sine_tab,
            grads_rot[..., ROT:],
        ],
        axis=-1,
    )


def causal_scores(queries, key_rows, first_row, score_scale):
    block_rows = queries.shape[0]
    last_row = key_rows.shape[0]
    scores = (
        jnp.einsum("qshd,kshd->shqk", queries, key_rows, preferred_element_type=jnp.float32)
        * score_scale
    )
    row_pos = first_row + jnp.arange(block_rows, dtype=jnp.int32)
    col_pos = jnp.arange(last_row, dtype=jnp.int32)
    allowed = col_pos[None, :] <= row_pos[:, None]
    return (scores, allowed)


def attend(queries, key_rows, val_rows):
    length = queries.shape[0]
    block_rows = min(QBLOCK, length)
    score_scale = queries.shape[-1] ** (-0.5)
    outputs = []
    totals = []
    for block_index in range(length // block_rows):
        first_row = block_index * block_rows
        last_row = first_row + block_rows
        scores, allowed = causal_scores(
            queries[first_row:last_row], key_rows[:last_row], first_row, score_scale
        )
        scores = jnp.where(allowed, scores, MASK_FILL)
        highest = jnp.max(scores, axis=-1, keepdims=True)
        exponent = jnp.exp(scores - highest)
        denominator = jnp.sum(exponent, axis=-1, keepdims=True)
        probability = (exponent / denominator).astype(jnp.bfloat16)
        block_out = jnp.einsum(
            "shqk,kshd->qshd", probability, val_rows[:last_row], preferred_element_type=jnp.float32
        )
        outputs.append(block_out.astype(jnp.bfloat16))
        totals.append((highest + jnp.log(denominator))[..., 0])
    context = jnp.concatenate(outputs, axis=0)
    return (context.reshape(length, context.shape[1], -1), jnp.concatenate(totals, axis=-1))


def attend_back(queries, key_rows, val_rows, d_context, log_total):
    length = queries.shape[0]
    block_rows = min(QBLOCK, length)
    score_scale = queries.shape[-1] ** (-0.5)
    grad_query_list = []
    grad_keys = jnp.zeros(queries.shape, jnp.float32)
    grad_vals = jnp.zeros(queries.shape, jnp.float32)
    for block_index in range(length // block_rows):
        first_row = block_index * block_rows
        last_row = first_row + block_rows
        query_block = queries[first_row:last_row]
        scores, allowed = causal_scores(query_block, key_rows[:last_row], first_row, score_scale)
        probability = jnp.where(
            allowed, jnp.exp(scores - log_total[:, :, first_row:last_row, None]), 0.0
        )
        d_block = d_context[first_row:last_row]
        d_prob = jnp.einsum(
            "qshd,kshd->shqk", d_block, val_rows[:last_row], preferred_element_type=jnp.float32
        )
        delta = jnp.sum(probability * d_prob, axis=-1, keepdims=True)
        d_scores = (probability * (d_prob - delta)).astype(jnp.bfloat16)
        grad_query_list.append(
            jnp.einsum(
                "shqk,kshd->qshd", d_scores, key_rows[:last_row], preferred_element_type=jnp.float32
            )
            * score_scale
        )
        grad_keys = grad_keys.at[:last_row].add(
            jnp.einsum("shqk,qshd->kshd", d_scores, query_block, preferred_element_type=jnp.float32)
            * score_scale
        )
        grad_vals = grad_vals.at[:last_row].add(
            jnp.einsum(
                "shqk,qshd->kshd",
                probability.astype(jnp.bfloat16),
                d_block,
                preferred_element_type=jnp.float32,
            )
        )
    return (jnp.concatenate(grad_query_list, axis=0), grad_keys, grad_vals)


def local(acts_in, cotangent, norm_gains, vec_bias, w_qkv, b_qkv, w_out, w_up, b_up, w_down):
    section_index = lax.axis_index("section")
    own_start = lax.axis_index("tensor") * acts_in.shape[1]
    local_len = acts_in.shape[1]
    seq_count = acts_in.shape[2]
    model_width = acts_in.shape[3]
    length = local_len * lax.axis_size("tensor")
    all_rows = length * seq_count
    gain_full, bias_full = (
        lax.all_gather(norm_gains[0], ("dp", "tensor"), axis=1, tiled=True),
        lax.all_gather(vec_bias[0], ("dp", "tensor"), axis=1, tiled=True),
    )
    mat_qkv, bias_qkv, mat_out, mat_up, bias_up, mat_down = (
        lax.all_gather(w_qkv[0], "dp", axis=0, tiled=True),
        lax.all_gather(b_qkv[0], "dp", axis=1, tiled=True),
        lax.all_gather(w_out[0], "dp", axis=1, tiled=True),
        lax.all_gather(w_up[0], "dp", axis=0, tiled=True),
        lax.all_gather(b_up[0], "dp", axis=1, tiled=True),
        lax.all_gather(w_down[0], "dp", axis=1, tiled=True),
    )
    head_count = bias_qkv.shape[0]
    head_dim = bias_qkv.shape[1] // 3
    qkv_shift = bias_qkv.reshape(-1).astype(jnp.float32)
    up_shift = bias_up.reshape(-1).astype(jnp.float32)
    cosine, sine_tab = rotary_tables(length)
    cosine = cosine[:, None, None, :]
    sine_tab = sine_tab[:, None, None, :]
    received = jnp.zeros_like(acts_in[0])
    stash_list = []
    out_list = []
    for moment in range(MICRO + 1):
        own_rows = acts_in[min(moment, MICRO - 1)]
        inputs = jnp.where(section_index == 0, own_rows, received)
        forward_gathered = lax.all_gather(inputs, "tensor", axis=0, tiled=True)
        full_attn, full_mlp = both_norms(
            forward_gathered.astype(jnp.float32),
            gain_full[0],
            bias_full[0],
            gain_full[1],
            bias_full[1],
        )
        forward_normed_attn = full_attn.astype(jnp.bfloat16)
        forward_normed_mlp = full_mlp.astype(jnp.bfloat16)
        forward_flat_attn = forward_normed_attn.reshape(all_rows, model_width)
        forward_flat_mlp = forward_normed_mlp.reshape(all_rows, model_width)
        projected = (
            jnp.dot(forward_flat_attn, mat_qkv, preferred_element_type=jnp.float32) + qkv_shift
        )
        projected = projected.reshape(length, seq_count, head_count, 3, head_dim)
        forward_queries = rotate(projected[:, :, :, 0], cosine, sine_tab).astype(jnp.bfloat16)
        forward_key_rows = rotate(projected[:, :, :, 1], cosine, sine_tab).astype(jnp.bfloat16)
        forward_val_rows = projected[:, :, :, 2].astype(jnp.bfloat16)
        forward_context, forward_log_total = attend(
            forward_queries, forward_key_rows, forward_val_rows
        )
        forward_up_proj = (
            jnp.dot(forward_flat_mlp, mat_up, preferred_element_type=jnp.float32) + up_shift
        )
        forward_activated = jax.nn.gelu(forward_up_proj, approximate=False).astype(jnp.bfloat16)
        active_rows = forward_activated.reshape(length, seq_count, -1)
        context_part = forward_context.reshape(lax.axis_size("tensor") * local_len * seq_count, -1)
        active_part = active_rows.reshape(lax.axis_size("tensor") * local_len * seq_count, -1)
        summed = jnp.dot(context_part, mat_out, preferred_element_type=jnp.float32) + jnp.dot(
            active_part, mat_down, preferred_element_type=jnp.float32
        )
        mixed_sum = lax.psum_scatter(
            summed.reshape(lax.axis_size("tensor") * local_len, seq_count, model_width),
            "tensor",
            scatter_dimension=0,
            tiled=True,
        )
        result = inputs.astype(jnp.float32) + mixed_sum + bias_full[2] + bias_full[3]
        forward_stashed = (
            forward_gathered,
            forward_normed_attn,
            forward_normed_mlp,
            forward_queries,
            forward_key_rows,
            forward_val_rows,
            forward_context,
            forward_log_total,
            forward_up_proj,
            forward_activated,
        )
        result, stashed = (result.astype(jnp.bfloat16), forward_stashed)
        stash_list.append(stashed)
        out_list.append(result)
        if moment < MICRO:
            received = from_behind(result, "section", 1)
    stash_all = jax.tree.map(lambda *parts: jnp.stack(parts), *stash_list)
    acts_local = lax.dynamic_slice_in_dim(jnp.stack(out_list), section_index, MICRO, 0)
    back_received = jnp.zeros_like(cotangent[0])
    grad_list = []
    weight_sums = None
    vector_sums = None
    for moment in range(MICRO + 1):
        micro_index = moment - 1 + section_index
        is_valid = (micro_index >= 0) & (micro_index < MICRO)
        source_clock = jnp.clip(micro_index + section_index, 0, MICRO)
        stashed = jax.tree.map(
            lambda part: lax.dynamic_index_in_dim(part, source_clock, 0, keepdims=False), stash_all
        )
        upstream = jnp.where(section_index == 1, cotangent[min(moment, MICRO - 1)], back_received)
        (
            gathered,
            normed_attn,
            normed_mlp,
            queries,
            key_rows,
            val_rows,
            context,
            log_total,
            up_proj,
            activated,
        ) = stashed
        backward_inputs = lax.dynamic_slice_in_dim(gathered, own_start, local_len, 0)
        upstream_rows = lax.all_gather(upstream, "tensor", axis=0, tiled=True)
        flat_grad = upstream_rows.reshape(all_rows, model_width)
        d_context = jnp.dot(flat_grad, mat_out.T, preferred_element_type=jnp.float32).astype(
            jnp.bfloat16
        )
        d_context = d_context.reshape(length, seq_count, head_count, head_dim)
        d_active = jnp.dot(flat_grad, mat_down.T, preferred_element_type=jnp.float32)
        _, gelu_pullback = jax.vjp(partial(jax.nn.gelu, approximate=False), up_proj)
        d_up = gelu_pullback(d_active)[0].astype(jnp.bfloat16)
        grad_query, grad_key, grad_val = attend_back(
            queries, key_rows, val_rows, d_context, log_total
        )
        d_qkv = jnp.stack(
            [
                rotate_back(grad_query, cosine, sine_tab),
                rotate_back(grad_key, cosine, sine_tab),
                grad_val,
            ],
            axis=3,
        ).astype(jnp.bfloat16)
        d_qkv_flat = d_qkv.reshape(all_rows, -1)
        d_qkv_rows = d_qkv.reshape(length, seq_count, -1)
        d_up_rows = d_up.reshape(length, seq_count, -1)
        flat_attn = normed_attn.reshape(all_rows, model_width)
        flat_mlp = normed_mlp.reshape(all_rows, model_width)
        weight_terms = (
            jnp.einsum("tc,te->ce", flat_attn, d_qkv_flat, preferred_element_type=jnp.float32),
            jnp.sum(d_qkv_flat.astype(jnp.float32), axis=0).reshape(bias_qkv.shape),
            jnp.einsum(
                "tc,te->ce",
                context.reshape(all_rows, -1),
                flat_grad,
                preferred_element_type=jnp.float32,
            ),
            jnp.einsum("tc,te->ce", flat_mlp, d_up, preferred_element_type=jnp.float32),
            jnp.sum(d_up.astype(jnp.float32), axis=0).reshape(bias_up.shape),
            jnp.einsum("tc,te->ce", activated, flat_grad, preferred_element_type=jnp.float32),
        )
        attn_part = d_qkv_rows.reshape(lax.axis_size("tensor") * local_len * seq_count, -1)
        mlp_part = d_up_rows.reshape(lax.axis_size("tensor") * local_len * seq_count, -1)
        joined = jnp.concatenate(
            [
                jnp.dot(attn_part, mat_qkv.T, preferred_element_type=jnp.float32),
                jnp.dot(mlp_part, mat_up.T, preferred_element_type=jnp.float32),
            ],
            axis=-1,
        )
        d_normed = lax.psum_scatter(
            joined.reshape(lax.axis_size("tensor") * local_len, seq_count, 2 * model_width).astype(
                jnp.bfloat16
            ),
            "tensor",
            scatter_dimension=0,
            tiled=True,
        ).astype(jnp.float32)
        _, norm_pullback = jax.vjp(
            both_norms,
            backward_inputs.astype(jnp.float32),
            gain_full[0],
            bias_full[0],
            gain_full[1],
            bias_full[1],
        )
        d_local, d_gain_attn, d_shift_attn, d_gain_mlp, d_shift_mlp = norm_pullback(
            (d_normed[..., :model_width], d_normed[..., model_width:])
        )
        upstream_float = upstream.astype(jnp.float32)
        d_inputs = (upstream_float + d_local).astype(jnp.bfloat16)
        out_shift = jnp.sum(upstream_float, axis=(0, 1))
        vector_terms = (
            jnp.stack([d_gain_attn, d_gain_mlp]),
            jnp.stack([d_shift_attn, d_shift_mlp, out_shift, out_shift]),
        )
        d_inputs, weight_terms, vector_terms = (d_inputs, weight_terms, vector_terms)
        grad_list.append(d_inputs)
        if moment < MICRO:
            back_received = from_behind(d_inputs, "section", -1)
        weight_terms = tuple((jnp.where(is_valid, term, 0.0) for term in weight_terms))
        vector_terms = tuple((jnp.where(is_valid, term, 0.0) for term in vector_terms))
        if moment == 0:
            weight_sums = tuple(weight_terms)
            vector_sums = vector_terms
        else:
            weight_sums = tuple((a + b for a, b in zip(weight_sums, weight_terms)))
            vector_sums = tuple((a + b for a, b in zip(vector_sums, vector_terms)))
    sum_qkv, sum_bqkv, sum_out, sum_up, sum_bup, sum_down = weight_sums
    share_qkv, share_bqkv, share_out, share_up, share_bup, share_down = (
        lax.psum_scatter(
            sum_qkv.astype(jnp.bfloat16), "dp", scatter_dimension=0, tiled=True
        ).astype(jnp.float32),
        lax.psum_scatter(
            sum_bqkv.astype(jnp.bfloat16), "dp", scatter_dimension=1, tiled=True
        ).astype(jnp.float32),
        lax.psum_scatter(
            sum_out.astype(jnp.bfloat16), "dp", scatter_dimension=1, tiled=True
        ).astype(jnp.float32),
        lax.psum_scatter(sum_up.astype(jnp.bfloat16), "dp", scatter_dimension=0, tiled=True).astype(
            jnp.float32
        ),
        lax.psum_scatter(
            sum_bup.astype(jnp.bfloat16), "dp", scatter_dimension=1, tiled=True
        ).astype(jnp.float32),
        lax.psum_scatter(
            sum_down.astype(jnp.bfloat16), "dp", scatter_dimension=1, tiled=True
        ).astype(jnp.float32),
    )
    grad_local = lax.dynamic_slice_in_dim(jnp.stack(grad_list), 1 - section_index, MICRO, 0)
    gain_share, bias_share = (
        lax.psum_scatter(vector_sums[0], ("dp", "tensor"), scatter_dimension=1, tiled=True),
        lax.psum_scatter(vector_sums[1], ("dp", "tensor"), scatter_dimension=1, tiled=True),
    )
    return (
        acts_local[None],
        grad_local[None],
        gain_share[None],
        bias_share[None],
        share_qkv[None],
        share_bqkv[None],
        share_out[None],
        share_up[None],
        share_bup[None],
        share_down[None],
    )


def solution(mesh):
    placed = (
        P(None, "tensor", "dp", None),
        P(None, "tensor", "dp", None),
        P("section", None, ("dp", "tensor")),
        P("section", None, ("dp", "tensor")),
        P("section", "dp", "tensor"),
        P("section", "tensor", "dp"),
        P("section", "tensor", "dp"),
        P("section", "dp", "tensor"),
        P("section", "tensor", "dp"),
        P("section", "tensor", "dp"),
    )
    return jax.shard_map(
        local,
        mesh=mesh,
        in_specs=placed,
        out_specs=(
            P("section", None, "tensor", "dp", None),
            P("section", None, "tensor", "dp", None),
            P("section", None, ("dp", "tensor")),
            P("section", None, ("dp", "tensor")),
            P("section", "dp", "tensor"),
            P("section", "tensor", "dp"),
            P("section", "tensor", "dp"),
            P("section", "dp", "tensor"),
            P("section", "tensor", "dp"),
            P("section", "tensor", "dp"),
        ),
        check_vma=False,
    )
```

profile of v0, /device:TPU:0, one launch (start us, length us, event | category | flops | bytes accessed | tf_op | source)
XLA Modules:
  0.0 2166.3 jit_solution(13644089878775212534)
XLA Ops:
  12.2 47.0 %all-gather.2 = f32[1,4,1024]{1,0,2:T(1,128)S(1)} all-gather(f32[1,4,64]{1,0,2:T(1,128)S(1)} %copy.228), channel_id=4, replica_groups=mesh['section'=2,'dp'=4,'tensor'=4] {'dp','tensor'}, dimensions={2}, use_global_device_ids=true | all-gather | bytes 17408 | tf_op jit(solution)/shard_map/all_gather | solution.py:164
  59.2 21.7 %slice_reduce_fusion.11 = (f32[1024]{0:T(1024)S(1)}, f32[1024]{0:T(1024)S(1)}, f32[1024]{0:T(1024)S(1)}, f32[1024]{0:T(1024)S(1)}) fusion(f32[1,4,1024]{1,0,2:T(1,128)S(1)} %all-gather.2), kind=kLoop, calls=%fused_computation.917 | loop fusion | bytes 32768 | tf_op jit(solution)/shard_map/slice | solution.py:225
  81.0 5.8 all-gather.7
  87.0 35.0 %all-gather.1 = f32[1,2,1024]{1,0,2:T(1,128)S(1)} all-gather(f32[1,2,64]{1,0,2:T(1,128)S(1)} %copy.227), channel_id=3, replica_groups=mesh['section'=2,'dp'=4,'tensor'=4] {'dp','tensor'}, dimensions={2}, use_global_device_ids=true | all-gather | bytes 8704 | tf_op jit(solution)/shard_map/all_gather | solution.py:163
  122.0 7.2 slice_reduce_fusion.15
  129.7 5.8 all-gather.4
  136.5 7.3 all-gather.5
  155.8 14.3 fusion.5
  177.2 14.8 bitcast_dynamic-update-slice_fusion.9
  192.0 4.6 fusion.360
  199.5 76.0 %reduce-scatter.27.cloned.1.call-done = f32[256,1,1024]{2,0,1:T(8,128)} async-done(((f32[1024,1,1024]{2,0,1:T(8,128)}), f32[256,1,1024]{2,0,1:T(8,128)}) %reduce-scatter.27.cloned.1.call-update) | async-done | bytes 1048592 | tf_op jit(solution)/shard_map/reduce_scatter | solution.py:219
  281.2 11.2 collective-permute-done
  293.3 47.6 %all-gather.24.cloned.1.call-done = bf16[1024,1,1024]{2,0,1:T(8,128)(2,1)} async-done(((bf16[256,1,1024]{2,0,1:T(8,128)(2,1)}), bf16[1024,1,1024]{2,0,1:T(8,128)(2,1)}) %all-gather.24.cloned.1.call-update) | async-done | bytes 2097168 | tf_op jit(solution)/shard_map/all_gather | solution.py:187
  361.4 13.1 bitcast_dynamic-update-slice_fusion.8
  379.7 75.6 %reduce-scatter.29.cloned.1.call-done = f32[256,1,1024]{2,0,1:T(8,128)} async-done(((f32[1024,1,1024]{2,0,1:T(8,128)}), f32[256,1,1024]{2,0,1:T(8,128)}) %reduce-scatter.29.cloned.1.call-update) | async-done | bytes 1048592 | tf_op jit(solution)/shard_map/reduce_scatter | solution.py:219
  461.0 11.2 collective-permute-done.1
  474.5 47.2 %all-gather.26.cloned.1.call-done = bf16[1024,1,1024]{2,0,1:T(8,128)(2,1)} async-done(((bf16[256,1,1024]{2,0,1:T(8,128)(2,1)}), bf16[1024,1,1024]{2,0,1:T(8,128)(2,1)}) %all-gather.26.cloned.1.call-update) | async-done | bytes 2097168 | tf_op jit(solution)/shard_map/all_gather | solution.py:187
  542.3 13.1 bitcast_dynamic-update-slice_fusion.7
  560.6 75.6 %reduce-scatter.31.cloned.1.call-done = f32[256,1,1024]{2,0,1:T(8,128)} async-done(((f32[1024,1,1024]{2,0,1:T(8,128)}), f32[256,1,1024]{2,0,1:T(8,128)}) %reduce-scatter.31.cloned.1.call-update) | async-done | bytes 1048592 | tf_op jit(solution)/shard_map/reduce_scatter | solution.py:219
  641.9 11.2 collective-permute-done.2
  657.8 44.8 %all-gather.28.cloned.1.call-done = bf16[1024,1,1024]{2,0,1:T(8,128)(2,1)} async-done(((bf16[256,1,1024]{2,0,1:T(8,128)(2,1)}), bf16[1024,1,1024]{2,0,1:T(8,128)(2,1)}) %all-gather.28.cloned.1.call-update) | async-done | bytes 2097168 | tf_op jit(solution)/shard_map/all_gather | solution.py:187
  723.3 13.1 bitcast_dynamic-update-slice_fusion.6
  759.7 67.0 %reduce-scatter.33.cloned.1.call-done = f32[256,1,1024]{2,0,1:T(8,128)} async-done(((f32[1024,1,1024]{2,0,1:T(8,128)}), f32[256,1,1024]{2,0,1:T(8,128)}) %reduce-scatter.33.cloned.1.call-update) | async-done | bytes 1048592 | tf_op jit(solution)/shard_map/reduce_scatter | solution.py:219
  834.5 4.8 bitcast_dynamic-update-slice_fusion.3
  853.4 5.2 bitcast_dynamic-update-slice_fusion.2
  865.0 28.1 %all-gather.30.cloned.1.call-done = bf16[1024,1,1024]{2,0,1:T(8,128)(2,1)} async-done(((bf16[256,1,1024]{2,0,1:T(8,128)(2,1)}), bf16[1024,1,1024]{2,0,1:T(8,128)(2,1)}) %all-gather.30.cloned.1.call-update) | async-done | bytes 2097168 | tf_op jit(solution)/shard_map/all_gather | solution.py:187
  938.7 13.0 bitcast_dynamic-update-slice_fusion.5
  955.4 13.8 convert_reduce_fusion.9
  998.2 53.5 %reduce-scatter.37.cloned.1.call-done = bf16[256,1,2048]{2,0,1:T(8,128)(2,1)} async-done(((bf16[1024,1,2048]{2,0,1:T(8,128)(2,1)}), bf16[256,1,2048]{2,0,1:T(8,128)(2,1)}) %reduce-scatter.37.cloned.1.call-update) | async-done | bytes 1048592 | tf_op jit(solution)/shard_map/reduce_scatter | solution.py:317
  1062.2 14.3 collective-permute-done.4
  1083.3 5.6 fusion.780
  1089.0 35.8 %all-gather.32.cloned.1.call-done = bf16[1024,1,1024]{2,0,1:T(8,128)(2,1)} async-done(((bf16[256,1,1024]{2,0,1:T(8,128)(2,1)}), bf16[1024,1,1024]{2,0,1:T(8,128)(2,1)}) %all-gather.32.cloned.1.call-update) | async-done | bytes 2097168 | tf_op jit(solution)/shard_map/all_gather | solution.py:270
  1149.6 14.2 convert_reduce_fusion.8
  1170.6 75.5 %reduce-scatter.39.cloned.1.call-done = bf16[256,1,2048]{2,0,1:T(8,128)(2,1)} async-done(((bf16[1024,1,2048]{2,0,1:T(8,128)(2,1)}), bf16[256,1,2048]{2,0,1:T(8,128)(2,1)}) %reduce-scatter.39.cloned.1.call-update) | async-done | bytes 1048592 | tf_op jit(solution)/shard_map/reduce_scatter | solution.py:317
  1256.8 14.3 collective-permute-done.5
  1278.0 5.6 fusion.775
  1283.6 35.9 %all-gather.34.cloned.1.call-done = bf16[1024,1,1024]{2,0,1:T(8,128)(2,1)} async-done(((bf16[256,1,1024]{2,0,1:T(8,128)(2,1)}), bf16[1024,1,1024]{2,0,1:T(8,128)(2,1)}) %all-gather.34.cloned.1.call-update) | async-done | bytes 2097168 | tf_op jit(solution)/shard_map/all_gather | solution.py:270
  1345.1 14.2 convert_reduce_fusion.7
  1366.7 75.0 %reduce-scatter.41.cloned.1.call-done = bf16[256,1,2048]{2,0,1:T(8,128)(2,1)} async-done(((bf16[1024,1,2048]{2,0,1:T(8,128)(2,1)}), bf16[256,1,2048]{2,0,1:T(8,128)(2,1)}) %reduce-scatter.41.cloned.1.call-update) | async-done | bytes 1048592 | tf_op jit(solution)/shard_map/reduce_scatter | solution.py:317
  1452.3 14.3 collective-permute-done.6
  1473.3 5.6 fusion.770
  1478.9 36.0 %all-gather.36.cloned.1.call-done = bf16[1024,1,1024]{2,0,1:T(8,128)(2,1)} async-done(((bf16[256,1,1024]{2,0,1:T(8,128)(2,1)}), bf16[1024,1,1024]{2,0,1:T(8,128)(2,1)}) %all-gather.36.cloned.1.call-update) | async-done | bytes 2097168 | tf_op jit(solution)/shard_map/all_gather | solution.py:270
  1540.8 13.6 convert_reduce_fusion.6
  1561.9 75.0 %reduce-scatter.43.cloned.1.call-done = bf16[256,1,2048]{2,0,1:T(8,128)(2,1)} async-done(((bf16[1024,1,2048]{2,0,1:T(8,128)(2,1)}), bf16[256,1,2048]{2,0,1:T(8,128)(2,1)}) %reduce-scatter.43.cloned.1.call-update) | async-done | bytes 1048592 | tf_op jit(solution)/shard_map/reduce_scatter | solution.py:317
  1655.2 7.1 collective-permute-done.7
  1668.9 5.0 fusion.628
  1674.1 5.7 fusion.765
  1694.5 5.3 fusion.294
  1699.8 5.3 fusion.292
  1707.8 5.3 fusion.290
  1726.5 4.7 multiply_reduce_fusion
  1742.6 15.1 convert_reduce_fusion.5
  1770.0 5.4 add_convert_fusion.2
  1790.9 7.6 add_convert_fusion.1
  1807.4 4.4 fusion.270
  1811.8 4.4 fusion.268
  1816.3 8.3 add_convert_fusion
  1840.8 17.5 reduce-scatter.49.cloned.1.call-done
  1859.9 29.0 %reduce-scatter.47.cloned.1.call-done = bf16[256,768]{1,0:T(8,128)(2,1)} async-done(((bf16[1024,768]{1,0:T(8,128)(2,1)}), bf16[256,768]{1,0:T(8,128)(2,1)}) %reduce-scatter.47.cloned.1.call-update) | async-done | bytes 393232 | tf_op jit(solution)/shard_map/reduce_scatter | solution.py:357
  1890.8 32.1 %reduce-scatter.51.cloned.1.call-done = bf16[256,1024]{1,0:T(8,128)(2,1)} async-done(((bf16[1024,1024]{1,0:T(8,128)(2,1)}), bf16[256,1024]{1,0:T(8,128)(2,1)}) %reduce-scatter.51.cloned.1.call-update) | async-done | bytes 524304 | tf_op jit(solution)/shard_map/reduce_scatter | solution.py:366
  1925.0 31.9 %reduce-scatter.53.cloned.1.call-done = bf16[1024,256]{1,0:T(8,128)(2,1)} async-done(((bf16[1024,1024]{1,0:T(8,128)(2,1)}), bf16[1024,256]{1,0:T(8,128)(2,1)}) %reduce-scatter.53.cloned.1.call-update) | async-done | bytes 524304 | tf_op jit(solution)/shard_map/reduce_scatter | solution.py:372
  1959.1 77.0 %reduce-scatter.45.cloned.1.call-done = bf16[256,1,2048]{2,0,1:T(8,128)(2,1)} async-done(((bf16[1024,1,2048]{2,0,1:T(8,128)(2,1)}), bf16[256,1,2048]{2,0,1:T(8,128)(2,1)}) %reduce-scatter.45.cloned.1.call-update) | async-done | bytes 1048592 | tf_op jit(solution)/shard_map/reduce_scatter | solution.py:317
  2049.7 49.4 %reduce-scatter.55.cloned.1.call-done = f32[64,2]{1,0:T(8,128)} async-done(((f32[1024,2]{1,0:T(8,128)}), f32[64,2]{1,0:T(8,128)}) %reduce-scatter.55.cloned.1.call-update) | async-done | bytes 528
  2100.5 57.4 %reduce-scatter.57.cloned.1.call-done = f32[64,4]{1,0:T(8,128)} async-done(((f32[1024,4]{1,0:T(8,128)}), f32[64,4]{1,0:T(8,128)}) %reduce-scatter.57.cloned.1.call-update) | async-done | bytes 1040
  (967 shorter events, 546.0 us)
Async XLA Ops:
  7.2 122.4 %copy-start.206 = (bf16[1,4,48]{2,1,0:T(4,128)(2,1)S(1)}, bf16[1,4,48]{2,1,0:T(4,128)(2,1)}, u32[]{:S(2)}) copy-start(bf16[1,4,48]{2,1,0:T(4,128)(2,1)} %param.75) | copy-start | bytes 1156
  7.2 136.6 %all-gather.40.cloned.1.call-start = ((), (), s32[]{:S(2)}) async-start(), calls=%async_computation.40 | async-start | bytes 2621440 | tf_op jit(solution)/shard_map/all_gather | solution.py:187
  7.3 129.3 %copy-start.117 = (bf16[1,256,256]{2,1,0:T(8,128)(2,1)S(1)}, bf16[1,256,256]{2,1,0:T(8,128)(2,1)}, u32[]{:S(2)}) copy-start(bf16[1,256,256]{2,1,0:T(8,128)(2,1)} %param.76) | copy-start | bytes 393220
  9.2 139.1 %all-gather.42.cloned.1.call-start = ((), (), s32[]{:S(2)}) async-start(), calls=%async_computation.41 | async-start | bytes 1966080 | tf_op jit(solution)/shard_map/all_gather | solution.py:167
  10.0 167.2 %all-gather.44.cloned.1.call-start = ((), (), s32[]{:S(2)}) async-start(), calls=%async_computation.42 | async-start | bytes 2621440 | tf_op jit(solution)/shard_map/all_gather | solution.py:170
  10.7 181.3 %all-gather.46.cloned.1.call-start = ((), (), s32[]{:S(2)}) async-start(), calls=%async_computation.43 | async-start | bytes 2621440 | tf_op jit(solution)/shard_map/all_gather | solution.py:172
  11.3 264.3 %reduce-scatter.27.cloned.1.call-start = ((), (), s32[]{:S(2)}) async-start(), calls=%async_computation.18 | async-start | bytes 5242880 | tf_op jit(solution)/shard_map/reduce_scatter | solution.py:219
  80.9 555.2 %copy-start.111 = (f32[1024]{0:T(1024)}, f32[1024]{0:T(1024)S(1)}, u32[]{:S(2)}) copy-start(f32[1024]{0:T(1024)S(1)} %get-tuple-element.395) | copy-start | bytes 12292
  80.9 555.2 %copy-start.113 = (f32[1024]{0:T(1024)}, f32[1024]{0:T(1024)S(1)}, u32[]{:S(2)}) copy-start(f32[1024]{0:T(1024)S(1)} %get-tuple-element.398) | copy-start | bytes 12292
  86.9 636.2 %copy-start.115 = (f32[1024]{0:T(1024)}, f32[1024]{0:T(1024)S(1)}, u32[]{:S(2)}) copy-start(f32[1024]{0:T(1024)S(1)} %bitcast_convert_fusion.5) | copy-start | bytes 12292
  129.2 1514.2 %copy-start.61 = (f32[1024]{0:T(1024)}, f32[1024]{0:T(1024)S(1)}, u32[]{:S(2)}) copy-start(f32[1024]{0:T(1024)S(1)} %get-tuple-element.399) | copy-start | bytes 12292
  129.2 1514.2 %copy-start.63 = (f32[1024]{0:T(1024)}, f32[1024]{0:T(1024)S(1)}, u32[]{:S(2)}) copy-start(f32[1024]{0:T(1024)S(1)} %get-tuple-element.400) | copy-start | bytes 12292
  143.8 595.0 %copy-start.4 = (bf16[1,256,1024]{2,1,0:T(8,128)(2,1)}, bf16[1,256,1024]{2,1,0:T(8,128)(2,1)S(1)}, u32[]{:S(2)}) copy-start(bf16[1,256,1024]{2,1,0:T(8,128)(2,1)S(1)} %all-gather.5) | copy-start | bytes 1572868
  199.5 141.4 %all-gather.24.cloned.1.call-start = ((), (), s32[]{:S(2)}) async-start(), calls=%async_computation.19 | async-start | bytes 2621440 | tf_op jit(solution)/shard_map/all_gather | solution.py:187
  277.8 14.6 collective-permute-start
  293.2 162.1 %reduce-scatter.29.cloned.1.call-start = ((), (), s32[]{:S(2)}) async-start(), calls=%async_computation.20 | async-start | bytes 5242880 | tf_op jit(solution)/shard_map/reduce_scatter | solution.py:219
  379.7 142.0 %all-gather.26.cloned.1.call-start = ((), (), s32[]{:S(2)}) async-start(), calls=%async_computation.21 | async-start | bytes 2621440 | tf_op jit(solution)/shard_map/all_gather | solution.py:187
  457.6 14.6 collective-permute-start.1
  474.1 162.1 %reduce-scatter.31.cloned.1.call-start = ((), (), s32[]{:S(2)}) async-start(), calls=%async_computation.22 | async-start | bytes 5242880 | tf_op jit(solution)/shard_map/reduce_scatter | solution.py:219
  560.5 142.1 %all-gather.28.cloned.1.call-start = ((), (), s32[]{:S(2)}) async-start(), calls=%async_computation.23 | async-start | bytes 2621440 | tf_op jit(solution)/shard_map/all_gather | solution.py:187
  638.4 14.6 collective-permute-start.2
  654.9 94.0 %all-gather.48.cloned.1.call-start = ((), (), s32[]{:S(2)}) async-start(), calls=%async_computation.44 | async-start | bytes 2621440 | tf_op jit(solution)/shard_map/all_gather | solution.py:270
  657.5 169.1 %reduce-scatter.33.cloned.1.call-start = ((), (), s32[]{:S(2)}) async-start(), calls=%async_computation.24 | async-start | bytes 5242880 | tf_op jit(solution)/shard_map/reduce_scatter | solution.py:219
  741.6 151.6 %all-gather.30.cloned.1.call-start = ((), (), s32[]{:S(2)}) async-start(), calls=%async_computation.25 | async-start | bytes 2621440 | tf_op jit(solution)/shard_map/all_gather | solution.py:187
  829.0 14.6 collective-permute-start.3
  845.6 206.1 %reduce-scatter.37.cloned.1.call-start = ((), (), s32[]{:S(2)}) async-start(), calls=%async_computation.27 | async-start | bytes 5242880 | tf_op jit(solution)/shard_map/reduce_scatter | solution.py:317
  976.0 148.8 %all-gather.32.cloned.1.call-start = ((), (), s32[]{:S(2)}) async-start(), calls=%async_computation.28 | async-start | bytes 2621440 | tf_op jit(solution)/shard_map/all_gather | solution.py:270
  1060.9 15.6 collective-permute-start.4
  1079.1 167.1 %reduce-scatter.39.cloned.1.call-start = ((), (), s32[]{:S(2)}) async-start(), calls=%async_computation.29 | async-start | bytes 5242880 | tf_op jit(solution)/shard_map/reduce_scatter | solution.py:317
  1170.6 148.9 %all-gather.34.cloned.1.call-start = ((), (), s32[]{:S(2)}) async-start(), calls=%async_computation.30 | async-start | bytes 2621440 | tf_op jit(solution)/shard_map/all_gather | solution.py:270
  1255.4 15.7 collective-permute-start.5
  1273.8 167.9 %reduce-scatter.41.cloned.1.call-start = ((), (), s32[]{:S(2)}) async-start(), calls=%async_computation.31 | async-start | bytes 5242880 | tf_op jit(solution)/shard_map/reduce_scatter | solution.py:317
  1366.1 148.9 %all-gather.36.cloned.1.call-start = ((), (), s32[]{:S(2)}) async-start(), calls=%async_computation.32 | async-start | bytes 2621440 | tf_op jit(solution)/shard_map/all_gather | solution.py:270
  1450.9 15.7 collective-permute-start.6
  1469.2 167.6 %reduce-scatter.43.cloned.1.call-start = ((), (), s32[]{:S(2)}) async-start(), calls=%async_computation.33 | async-start | bytes 5242880 | tf_op jit(solution)/shard_map/reduce_scatter | solution.py:317
  1561.2 154.7 %all-gather.38.cloned.1.call-start = ((), (), s32[]{:S(2)}) async-start(), calls=%async_computation.34 | async-start | bytes 2621440 | tf_op jit(solution)/shard_map/all_gather | solution.py:270
  1646.3 16.1 collective-permute-start.7
  1665.1 168.7 %reduce-scatter.35.cloned.1.call-start = ((), (), s32[]{:S(2)}) async-start(), calls=%async_computation.26 | async-start | bytes 5242880 | tf_op jit(solution)/shard_map/reduce_scatter | solution.py:219
  1684.9 153.1 %reduce-scatter.59.cloned.1.call-start = ((), (), s32[]{:S(2)}) async-start(), calls=%async_computation.47 | async-start | bytes 61440
  1742.3 97.0 %reduce-scatter.61.cloned.1.call-start = ((), (), s32[]{:S(2)}) async-start(), calls=%async_computation.48 | async-start | bytes 40960
  1758.4 99.9 %reduce-scatter.49.cloned.1.call-start = ((), (), s32[]{:S(2)}) async-start(), calls=%async_computation.37 | async-start | bytes 655360 | tf_op jit(solution)/shard_map/reduce_scatter | solution.py:363
  1764.6 124.3 %reduce-scatter.47.cloned.1.call-start = ((), (), s32[]{:S(2)}) async-start(), calls=%async_computation.36 | async-start | bytes 1966080 | tf_op jit(solution)/shard_map/reduce_scatter | solution.py:357
  1775.4 147.5 %reduce-scatter.51.cloned.1.call-start = ((), (), s32[]{:S(2)}) async-start(), calls=%async_computation.38 | async-start | bytes 2621440 | tf_op jit(solution)/shard_map/reduce_scatter | solution.py:366
  1798.5 158.4 %reduce-scatter.53.cloned.1.call-start = ((), (), s32[]{:S(2)}) async-start(), calls=%async_computation.39 | async-start | bytes 2621440 | tf_op jit(solution)/shard_map/reduce_scatter | solution.py:372
  1824.6 211.5 %reduce-scatter.45.cloned.1.call-start = ((), (), s32[]{:S(2)}) async-start(), calls=%async_computation.35 | async-start | bytes 5242880 | tf_op jit(solution)/shard_map/reduce_scatter | solution.py:317
  1833.2 265.9 %reduce-scatter.55.cloned.1.call-start = ((), (), s32[]{:S(2)}) async-start(), calls=%async_computation.45 | async-start | bytes 557056
  1838.0 199.6 %copy-start.62 = (f32[1024]{0:T(1024)S(1)}, f32[1024]{0:T(1024)}, u32[]{:S(2)}) copy-start(f32[1024]{0:T(1024)} %copy-done.61) | copy-start | bytes 12292
  1838.0 199.6 %copy-start.64 = (f32[1024]{0:T(1024)S(1)}, f32[1024]{0:T(1024)}, u32[]{:S(2)}) copy-start(f32[1024]{0:T(1024)} %copy-done.63) | copy-start | bytes 12292
  1959.0 82.5 %copy-start.191 = (f32[1024]{0:T(1024)S(1)}, f32[1024]{0:T(1024)}, u32[]{:S(2)}) copy-start(f32[1024]{0:T(1024)} %get-tuple-element.338) | copy-start | bytes 12292
  1959.0 82.5 %copy-start.192 = (f32[1024]{0:T(1024)S(1)}, f32[1024]{0:T(1024)}, u32[]{:S(2)}) copy-start(f32[1024]{0:T(1024)} %get-tuple-element.339) | copy-start | bytes 12292
  1959.0 83.7 %copy-start.177 = (f32[1024]{0:T(1024)S(1)}, f32[1024]{0:T(1024)}, u32[]{:S(2)}) copy-start(f32[1024]{0:T(1024)} %get-tuple-element.429) | copy-start | bytes 12292
  1959.0 83.7 %copy-start.178 = (f32[1024]{0:T(1024)S(1)}, f32[1024]{0:T(1024)}, u32[]{:S(2)}) copy-start(f32[1024]{0:T(1024)} %get-tuple-element.390) | copy-start | bytes 12292
  1959.0 83.7 %copy-start.179 = (f32[1024]{0:T(1024)S(1)}, f32[1024]{0:T(1024)}, u32[]{:S(2)}) copy-start(f32[1024]{0:T(1024)} %get-tuple-element.391) | copy-start | bytes 12292
  1959.0 83.7 %copy-start.180 = (f32[1024]{0:T(1024)S(1)}, f32[1024]{0:T(1024)}, u32[]{:S(2)}) copy-start(f32[1024]{0:T(1024)} %get-tuple-element.427) | copy-start | bytes 12292
  1959.1 83.7 %copy-start.183 = (f32[1024]{0:T(1024)S(1)}, f32[1024]{0:T(1024)}, u32[]{:S(2)}) copy-start(f32[1024]{0:T(1024)} %get-tuple-element.385) | copy-start | bytes 12292
  1959.1 83.7 %copy-start.184 = (f32[1024]{0:T(1024)S(1)}, f32[1024]{0:T(1024)}, u32[]{:S(2)}) copy-start(f32[1024]{0:T(1024)} %get-tuple-element.386) | copy-start | bytes 12292
  1959.1 83.7 %copy-start.185 = (f32[1024]{0:T(1024)S(1)}, f32[1024]{0:T(1024)}, u32[]{:S(2)}) copy-start(f32[1024]{0:T(1024)} %get-tuple-element.425) | copy-start | bytes 12292
  1959.1 83.7 %copy-start.188 = (f32[1024]{0:T(1024)S(1)}, f32[1024]{0:T(1024)}, u32[]{:S(2)}) copy-start(f32[1024]{0:T(1024)} %get-tuple-element.380) | copy-start | bytes 12292
  1959.1 83.7 %copy-start.189 = (f32[1024]{0:T(1024)S(1)}, f32[1024]{0:T(1024)}, u32[]{:S(2)}) copy-start(f32[1024]{0:T(1024)} %get-tuple-element.381) | copy-start | bytes 12292
  1959.1 83.7 %copy-start.190 = (f32[1024]{0:T(1024)S(1)}, f32[1024]{0:T(1024)}, u32[]{:S(2)}) copy-start(f32[1024]{0:T(1024)} %get-tuple-element.423) | copy-start | bytes 12292
  1959.1 83.7 %copy-start.193 = (f32[1024]{0:T(1024)S(1)}, f32[1024]{0:T(1024)}, u32[]{:S(2)}) copy-start(f32[1024]{0:T(1024)} %get-tuple-element.375) | copy-start | bytes 12292
  1959.1 83.7 %copy-start.194 = (f32[1024]{0:T(1024)S(1)}, f32[1024]{0:T(1024)}, u32[]{:S(2)}) copy-start(f32[1024]{0:T(1024)} %get-tuple-element.376) | copy-start | bytes 12292
  1959.1 83.7 %copy-start.197 = (f32[1024]{0:T(1024)S(1)}, f32[1024]{0:T(1024)}, u32[]{:S(2)}) copy-start(f32[1024]{0:T(1024)} %get-tuple-element.421) | copy-start | bytes 12292
  2042.7 115.3 %reduce-scatter.57.cloned.1.call-start = ((), (), s32[]{:S(2)}) async-start(), calls=%async_computation.46 | async-start | bytes 557056
  (230 other events, 2203.0 us)
Sparse Core Ops, SparseCore 0:
  10.2 56.9 all-gather.39
  68.7 19.4 all-gather.41
  89.8 23.6 all-gather.43
  114.9 23.3 all-gather.45
  199.6 75.9 reduce-scatter.26
  293.3 47.4 all-gather.23
  379.8 75.4 reduce-scatter.28
  474.2 47.4 all-gather.25
  560.6 75.4 reduce-scatter.30
  655.0 47.4 all-gather.27
  704.2 44.6 all-gather.47
  751.2 75.4 reduce-scatter.32
  845.7 47.4 all-gather.29
  976.1 75.4 reduce-scatter.36
  1079.2 45.5 all-gather.31
  1170.7 75.4 reduce-scatter.38
  1273.9 45.5 all-gather.33
  1366.2 75.4 reduce-scatter.40
  1469.4 45.5 all-gather.35
  1561.3 75.4 reduce-scatter.42
  1665.3 45.5 all-gather.37
  1713.1 75.4 reduce-scatter.34
  1791.8 19.8 reduce-scatter.58
  1814.0 19.3 reduce-scatter.60
  1836.6 21.6 reduce-scatter.48
  1860.7 28.1 reduce-scatter.46
  1891.4 31.4 reduce-scatter.50
  1925.4 31.4 reduce-scatter.52
  1959.3 76.7 reduce-scatter.44
  2042.8 56.2 reduce-scatter.54
  2103.1 54.7 reduce-scatter.56
where the time goes:
time: 2180 us; the launch traced here: 2170 us
  waiting for transfers between devices  1230 us (56%)
  matrix products  471 us (22%)
  other arithmetic  220 us (10%)
  blocking collectives  101 us (5%)
  local copies, waits for them, and re-layouts  98.1 us (4%)
  starting transfers between devices  23.5 us (1%)
    reduce_scatter x5, waiting for transfers between devices, local(): lax.psum_scatter(joined.reshape(lax.axis_size('tensor') * local_len, seq_...  356 us
    reduce_scatter x5, waiting for transfers between devices, local(): lax.psum_scatter(summed.reshape(lax.axis_size('tensor') * local_len, seq_...  294 us
    all_gather x5, waiting for transfers between devices, local(): forward_gathered = lax.all_gather(inputs, 'tensor', axis=0, tiled=True)  168 us
    unnamed x35, waiting for transfers between devices  109 us
    all_gather x5, waiting for transfers between devices, local(): upstream_rows = lax.all_gather(upstream, 'tensor', axis=0, tiled=True)  109 us
    ppermute x8, waiting for transfers between devices, from_behind(): return lax.ppermute(value, axis, pairs)  87.8 us
    dot_general x5, matrix products, local(): jnp.dot(flat_grad, mat_down.T, preferred_element_type=jnp.float32)  70.9 us
    dot_general x5, matrix products, local(): jnp.dot(forward_flat_mlp, mat_up, preferred_element_type=jnp.float32)  67.1 us
  transfers between devices with their start and end apart: 39, of which 31 were waited for; matrix products, arithmetic and copies ran while one was open for 18% of the time, Pallas kernels for 0%

commit v1 on v0

--- a/solution.py
+++ b/solution.py
@@ -4,6 +4,8 @@
 import jax
 import jax.numpy as jnp
 from jax import lax
+from jax.experimental import pallas as pl
+from jax.experimental.pallas import tpu as pltpu
 from jax.sharding import PartitionSpec as P
 
 ROT = 16
@@ -392,6 +394,691 @@
     )
 
 
+FAR_ORDER = (0, 2, 3, 1)
+VMEM_LIMIT = 60 * 1024 * 1024
+ROW_BLOCK = 256
+CHUNKS = 2
+
+
+def ring(value, axis, by):
+    length = lax.axis_size(axis)
+    return lax.ppermute(value, axis, [(i, (i + by) % length) for i in range(length)])
+
+
+def swap(value, axis, bit):
+    length = lax.axis_size(axis)
+    return lax.ppermute(value, axis, [(i, i ^ bit) for i in range(length)])
+
+
+def pick(value, index, axis=0):
+    return lax.dynamic_index_in_dim(value, index, axis, keepdims=False)
+
+
+def place(value, block, index):
+    return lax.dynamic_update_index_in_dim(value, block, index, 0)
+
+
+def relative(values, own):
+    parts = values.reshape(values.shape[:-1] + (4, values.shape[-1] // 4))
+    axis = parts.ndim - 2
+    picked = [pick(parts, jnp.bitwise_xor(own, k), axis) for k in range(4)]
+    return jnp.concatenate(picked, axis=-1)
+
+
+def exchange(blocks, own):
+    rows = blocks.shape[1]
+    half = rows // 2
+    far = pick(blocks, (own + 2) % 4)
+    ahead = jnp.concatenate([pick(blocks, (own + 1) % 4), far[:half]], axis=0)
+    behind = jnp.concatenate([pick(blocks, (own + 3) % 4), far[half:]], axis=0)
+    from_left = ring(ahead, "tensor", 1)
+    from_right = ring(behind, "tensor", -1)
+    first = ring(from_left[rows:], "tensor", 1)
+    second = ring(from_right[rows:], "tensor", -1)
+    result = jnp.zeros_like(blocks)
+    result = place(result, pick(blocks, own), own)
+    result = place(result, from_left[:rows], (own + 3) % 4)
+    result = place(result, from_right[:rows], (own + 1) % 4)
+    return place(result, jnp.concatenate([first, second], axis=0), (own + 2) % 4)
+
+
+def gather_across_first(shard):
+    pair = jnp.stack([shard, swap(shard, "dp", 2)])
+    left = ring(pair, "tensor", 1)
+    right = ring(pair, "tensor", -1)
+    far = jnp.stack([ring(left[0], "tensor", 1), ring(right[1], "tensor", -1)])
+    mine = jnp.stack([pair, left, right, far])
+    return jnp.stack([mine, swap(mine, "dp", 1)], axis=2)
+
+
+def gather_along_first(shard):
+    half = shard.shape[0] // 2
+    left = ring(shard, "tensor", 1)
+    right = ring(shard, "tensor", -1)
+    own_far = swap(shard, "dp", 2)
+    far = jnp.concatenate(
+        [ring(left[:half], "tensor", 1), ring(right[half:], "tensor", -1)], axis=0
+    )
+    mine = jnp.stack(
+        [
+            jnp.stack([shard, own_far]),
+            jnp.stack([left, swap(left, "dp", 2)]),
+            jnp.stack([right, swap(right, "dp", 2)]),
+            jnp.stack([far, swap(far, "dp", 2)]),
+        ]
+    )
+    return jnp.stack([mine, swap(mine, "dp", 1)], axis=2)
+
+
+def add_wide(left, right):
+    return (left.astype(jnp.float32) + right.astype(jnp.float32)).astype(jnp.bfloat16)
+
+
+def reduce_ring(blocks):
+    own, left, right, far = blocks
+    half = own.shape[0] // 2
+    to_right = ring(far[:half], "tensor", 1)
+    to_left = ring(far[half:], "tensor", -1)
+    right = jnp.concatenate([add_wide(right[:half], to_right), right[half:]], axis=0)
+    left = jnp.concatenate([left[:half], add_wide(left[half:], to_left)], axis=0)
+    got_left = ring(right, "tensor", 1)
+    got_right = ring(left, "tensor", -1)
+    total = own.astype(jnp.float32) + got_left.astype(jnp.float32) + got_right.astype(jnp.float32)
+    return total.astype(jnp.bfloat16)
+
+
+def reduce_core(grads):
+    return add_wide(grads[:, 0], swap(grads[:, 1], "dp", 1))
+
+
+def reduce_across_last(grads):
+    shared = reduce_core(grads)
+    own = reduce_ring([shared[:, :, k] for k in range(4)])
+    return add_wide(own[0], swap(own[1], "dp", 2))
+
+
+def reduce_along_last(grads):
+    shared = reduce_core(grads)
+    own = add_wide(shared[0], swap(shared[1], "dp", 2))
+    return reduce_ring([own[:, k] for k in range(4)])
+
+
+def normalised(x):
+    average = jnp.mean(x, axis=-1, keepdims=True)
+    centred = x - average
+    variance = jnp.mean(centred * centred, axis=-1, keepdims=True)
+    inverse = lax.rsqrt(variance + NORM_EPS)
+    return centred * inverse, inverse
+
+
+def nt_dot(left, right):
+    return lax.dot_general(
+        left, right, (((1,), (1,)), ((), ())), preferred_element_type=jnp.float32
+    )
+
+
+def tn_dot(left, right):
+    return lax.dot_general(
+        left, right, (((0,), (0,)), ((), ())), preferred_element_type=jnp.float32
+    )
+
+
+def nn_dot(left, right):
+    return jnp.dot(left, right, preferred_element_type=jnp.float32)
+
+
+def turn(values, cosine, low_sine, high_sine):
+    lanes = values.shape[-1]
+    return (
+        values * cosine
+        + pltpu.roll(values, ROT // 2, 1) * low_sine
+        + pltpu.roll(values, lanes - ROT // 2, 1) * high_sine
+    )
+
+
+def call(body, name, grid, ins, outs, scratch=(), limit=VMEM_LIMIT):
+    return pl.pallas_call(
+        body,
+        name=name,
+        grid=grid,
+        in_specs=[pl.BlockSpec(block, index) for _, block, index in ins],
+        out_specs=[pl.BlockSpec(block, index) for _, _, block, index in outs],
+        out_shape=[jax.ShapeDtypeStruct(shape, kind) for shape, kind, _, _ in outs],
+        scratch_shapes=list(scratch),
+        compiler_params=pltpu.CompilerParams(
+            vmem_limit_bytes=limit, dimension_semantics=("arbitrary",) * len(grid)
+        ),
+    )(*[array for array, _, _ in ins])
+
+
+def whole(array):
+    return (array, array.shape, lambda *_: (0,) * array.ndim)
+
+
+def rows_of(array, first=0, block=ROW_BLOCK):
+    base = first // block
+    return (array, (block, array.shape[1]), lambda i: (i + base, 0))
+
+
+def qkv_body(x, vecs, shift, cos, low, high, w, ln_a, ln_m, qkv):
+    hat, _ = normalised(x[...].astype(jnp.float32))
+    attn = (hat * vecs[0:1, :] + vecs[1:2, :]).astype(jnp.bfloat16)
+    ln_a[...] = attn
+    ln_m[...] = (hat * vecs[2:3, :] + vecs[3:4, :]).astype(jnp.bfloat16)
+    out = nn_dot(attn, w[...]) + shift[...]
+    for block in range(qkv.shape[1] // 384):
+        for part in range(3):
+            at = block * 384 + part * 128
+            piece = out[:, at : at + 128]
+            if part < 2:
+                piece = turn(piece, cos[...], low[...], high[...])
+            qkv[:, at : at + 128] = piece.astype(jnp.bfloat16)
+
+
+def run_qkv(x, vecs, shift, tables, w, first):
+    rows, width = x.shape
+    cols = w.shape[1]
+    bf = jnp.bfloat16
+    own = lambda i: (i, 0)
+    return call(
+        qkv_body,
+        "norm_qkv",
+        (rows // ROW_BLOCK,),
+        [rows_of(x), whole(vecs), whole(shift)]
+        + [rows_of(t, first) for t in tables]
+        + [whole(w)],
+        [
+            ((rows, width), bf, (ROW_BLOCK, width), own),
+            ((rows, width), bf, (ROW_BLOCK, width), own),
+            ((rows, cols), bf, (ROW_BLOCK, cols), own),
+        ],
+    )
+
+
+def attend_body(q, k, v, ctx, lse):
+    length = q.shape[0]
+    step = ROW_BLOCK
+    for head in range(2):
+        lanes = slice(head * 64, head * 64 + 64)
+        keys = k[:, lanes]
+        vals = v[:, lanes]
+        for at in range(0, length, step):
+            end = at + step
+            queries = q[at:end, lanes] * jnp.bfloat16(0.125)
+            scores = nt_dot(queries, keys[:end])
+            row = lax.broadcasted_iota(jnp.int32, (step, step), 0)
+            col = lax.broadcasted_iota(jnp.int32, (step, step), 1)
+            last = jnp.where(col <= row, scores[:, at:], MASK_FILL)
+            scores = last if at == 0 else jnp.concatenate([scores[:, :at], last], axis=1)
+            top = jnp.max(scores, axis=1, keepdims=True)
+            power = jnp.exp(scores - top)
+            total = jnp.sum(power, axis=1, keepdims=True)
+            probs = (power * (1.0 / total)).astype(jnp.bfloat16)
+            ctx[at:end, lanes] = nn_dot(probs, vals[:end]).astype(jnp.bfloat16)
+            level = jnp.broadcast_to(top + jnp.log(total), (step, 128))
+            lse[0, head : head + 1, at:end] = level.T[0:1]
+
+
+def run_attend(qkv):
+    length, cols = qkv.shape
+    groups = cols // 384
+    return call(
+        attend_body,
+        "attend",
+        (groups,),
+        [
+            (qkv, (length, 128), lambda i: (0, 3 * i)),
+            (qkv, (length, 128), lambda i: (0, 3 * i + 1)),
+            (qkv, (length, 128), lambda i: (0, 3 * i + 2)),
+        ],
+        [
+            ((length, groups * 128), jnp.bfloat16, (length, 128), lambda i: (0, i)),
+            ((groups, 8, length), jnp.float32, (1, 8, length), lambda i: (i, 0, 0)),
+        ],
+    )
+
+
+ERF_TOP = (
+    0.00022905065861350646,
+    0.0034082910107109506,
+    0.050955695062380861,
+    0.18520832239976145,
+    1.128379143519084,
+)
+ERF_BOTTOM = (
+    -1.1791602954361697e-7,
+    0.000023547966471313185,
+    0.0010179625278914885,
+    0.014070470171167667,
+    0.11098505178285362,
+    0.49746925110067538,
+    1.0,
+)
+
+
+def erf(x):
+    x = jnp.clip(x, -3.7439211627767994, 3.7439211627767994)
+    square = x * x
+    top = jnp.full_like(x, ERF_TOP[0])
+    for term in ERF_TOP[1:]:
+        top = top * square + term
+    bottom = jnp.full_like(x, ERF_BOTTOM[0])
+    for term in ERF_BOTTOM[1:]:
+        bottom = bottom * square + term
+    return x * top / bottom
+
+
+def mlp_body(ctx, ln_m, shift, w_out, w_up, w_down, act, slope, part):
+    up = nn_dot(ln_m[...], w_up[...]) + shift[...]
+    half_erf = 0.5 * erf(up * (2.0**-0.5)) + 0.5
+    bell = jnp.exp(up * up * -0.5) * ((2.0 * math.pi) ** -0.5)
+    active = (up * half_erf).astype(jnp.bfloat16)
+    act[...] = active
+    slope[...] = (half_erf + up * bell).astype(jnp.bfloat16)
+    part[...] = (nt_dot(ctx[...], w_out[...]) + nt_dot(active, w_down[...])).astype(jnp.bfloat16)
+
+
+def run_mlp(ctx, ln_m, shift, w_out, w_up, w_down, first, rows):
+    width = ln_m.shape[1]
+    cols = w_up.shape[1]
+    bf = jnp.bfloat16
+    own = lambda i: (i, 0)
+    return call(
+        mlp_body,
+        "mlp_out",
+        (rows // ROW_BLOCK,),
+        [
+            rows_of(ctx, first),
+            rows_of(ln_m, first),
+            whole(shift),
+            whole(w_out),
+            whole(w_up),
+            whole(w_down),
+        ],
+        [
+            ((rows, cols), bf, (ROW_BLOCK, cols), own),
+            ((rows, cols), bf, (ROW_BLOCK, cols), own),
+            ((rows, width), bf, (ROW_BLOCK, width), own),
+        ],
+    )
+
+
+def mlp_back_body(g, slope, w_out, w_down, d_up, d_ctx, sum_up, sum_g):
+    grad = g[...]
+    du = (nn_dot(grad, w_down[...]) * slope[...].astype(jnp.float32)).astype(jnp.bfloat16)
+    d_up[...] = du
+    d_ctx[...] = nn_dot(grad, w_out[...]).astype(jnp.bfloat16)
+
+    @pl.when(pl.program_id(0) == 0)
+    def _():
+        sum_up[...] = jnp.zeros_like(sum_up)
+        sum_g[...] = jnp.zeros_like(sum_g)
+
+    sum_up[...] += jnp.sum(du.astype(jnp.float32), axis=0, keepdims=True)
+    sum_g[...] += jnp.sum(grad.astype(jnp.float32), axis=0, keepdims=True)
+
+
+def run_mlp_back(g, slope, w_out, w_down):
+    rows, width = g.shape
+    cols, heads = w_down.shape[1], w_out.shape[1]
+    bf = jnp.bfloat16
+    own = lambda i: (i, 0)
+    fixed = lambda i: (0, 0)
+    return call(
+        mlp_back_body,
+        "mlp_back",
+        (rows // ROW_BLOCK,),
+        [rows_of(g), rows_of(slope), whole(w_out), whole(w_down)],
+        [
+            ((rows, cols), bf, (ROW_BLOCK, cols), own),
+            ((rows, heads), bf, (ROW_BLOCK, heads), own),
+            ((1, cols), jnp.float32, (1, cols), fixed),
+            ((1, width), jnp.float32, (1, width), fixed),
+        ],
+    )
+
+
+def attend_back_body(q, k, v, d_ctx, lse, cos, low, high, d_qkv, sums, dk_sum, dv_sum, dq_all):
+    length = q.shape[0]
+    step = ROW_BLOCK
+    for head in range(2):
+        lanes = slice(head * 64, head * 64 + 64)
+        keys = k[:, lanes]
+        vals = v[:, lanes]
+        dk_sum[:, lanes] = jnp.zeros((length, 64), jnp.float32)
+        dv_sum[:, lanes] = jnp.zeros((length, 64), jnp.float32)
+        for at in range(0, length, step):
+            end = at + step
+            queries = q[at:end, lanes] * jnp.bfloat16(0.125)
+            grads = d_ctx[at:end, lanes]
+            scores = nt_dot(keys[:end], queries)
+            power = jnp.exp(scores - lse[0, head : head + 1, at:end])
+            key = lax.broadcasted_iota(jnp.int32, (step, step), 0)
+            row = lax.broadcasted_iota(jnp.int32, (step, step), 1)
+            last = jnp.where(key <= row, power[at:], 0.0)
+            probs = last if at == 0 else jnp.concatenate([power[:at], last], axis=0)
+            d_probs = nt_dot(vals[:end], grads)
+            delta = jnp.sum(probs * d_probs, axis=0, keepdims=True)
+            d_scores = (probs * (d_probs - delta)).astype(jnp.bfloat16)
+            dv_sum[:end, lanes] += nn_dot(probs.astype(jnp.bfloat16), grads)
+            dk_sum[:end, lanes] += nn_dot(d_scores, queries)
+            dq_all[at:end, lanes] = tn_dot(d_scores, keys[:end]) * 0.125
+    dq = turn(dq_all[...], cos[...], -low[...], -high[...]).astype(jnp.bfloat16)
+    dk = turn(dk_sum[...], cos[...], -low[...], -high[...]).astype(jnp.bfloat16)
+    dv = dv_sum[...].astype(jnp.bfloat16)
+    for part, piece in enumerate((dq, dk, dv)):
+        at = part * 128
+        d_qkv[:, at : at + 128] = piece
+        sums[:, at : at + 128] = jnp.sum(piece.astype(jnp.float32), axis=0, keepdims=True)
+
+
+def run_attend_back(qkv, d_ctx, lse, tables):
+    length, cols = qkv.shape
+    groups = cols // 384
+    wide = pltpu.VMEM((length, 128), jnp.float32)
+    return call(
+        attend_back_body,
+        "attend_back",
+        (groups,),
+        [
+            (qkv, (length, 128), lambda i: (0, 3 * i)),
+            (qkv, (length, 128), lambda i: (0, 3 * i + 1)),
+            (qkv, (length, 128), lambda i: (0, 3 * i + 2)),
+            (d_ctx, (length, 128), lambda i: (0, i)),
+            (lse, (1, 8, length), lambda i: (i, 0, 0)),
+        ]
+        + [whole(t) for t in tables],
+        [
+            ((length, cols), jnp.bfloat16, (length, 384), lambda i: (0, i)),
+            ((1, cols), jnp.float32, (1, 384), lambda i: (0, i)),
+        ],
+        [wide, wide, wide],
+    )
+
+
+def norm_back_body(x, d_qkv, d_up, vecs, w_qkv, w_up, part, sums):
+    hat, inverse = normalised(x[...].astype(jnp.float32))
+    d_attn = nt_dot(d_qkv[...], w_qkv[...])
+    d_mlp = nt_dot(d_up[...], w_up[...])
+
+    @pl.when(pl.program_id(0) == 0)
+    def _():
+        sums[...] = jnp.zeros_like(sums)
+
+    for row, term in enumerate((d_attn * hat, d_mlp * hat, d_attn, d_mlp)):
+        sums[row : row + 1, :] += jnp.sum(term, axis=0, keepdims=True)
+    d_hat = d_attn * vecs[0:1, :] + d_mlp * vecs[2:3, :]
+    along = jnp.mean(d_hat * hat, axis=-1, keepdims=True)
+    level = jnp.mean(d_hat, axis=-1, keepdims=True)
+    part[...] = (inverse * (d_hat - level - hat * along)).astype(jnp.bfloat16)
+
+
+def run_norm_back(x, d_qkv, d_up, vecs, w_qkv, w_up, first, rows):
+    width = x.shape[1]
+    return call(
+        norm_back_body,
+        "norm_back",
+        (rows // ROW_BLOCK,),
+        [
+            rows_of(x, first),
+            rows_of(d_qkv, first),
+            rows_of(d_up, first),
+            whole(vecs),
+            whole(w_qkv),
+            whole(w_up),
+        ],
+        [
+            ((rows, width), jnp.bfloat16, (ROW_BLOCK, width), lambda i: (i, 0)),
+            ((8, width), jnp.float32, (8, width), lambda i: (0, 0)),
+        ],
+    )
+
+
+def turn_tables(length):
+    cosine, sine_tab = rotary_tables(length)
+    zero = jnp.zeros_like(sine_tab)
+    rest = jnp.zeros((length, 64 - ROT), jnp.float32)
+    cos = jnp.concatenate([cosine, cosine, rest + 1.0], axis=1)
+    low = jnp.concatenate([zero, sine_tab, rest], axis=1)
+    high = jnp.concatenate([-sine_tab, zero, rest], axis=1)
+    return tuple(jnp.concatenate([t, t], axis=1) for t in (cos, low, high))
+
+
+def by_sequence(
+    acts_in, cotangent, norm_gains, vec_bias, w_qkv, b_qkv, w_out, w_up, b_up, w_down
+):
+    section = lax.axis_index("section")
+    across = lax.axis_index("dp")
+    along = lax.axis_index("tensor")
+    first_section = section == 0
+    width = acts_in.shape[3]
+    rows = w_qkv.shape[1]
+    positions = acts_in.shape[1]
+    length = 4 * positions
+    heads = b_qkv.shape[1]
+    bf = jnp.bfloat16
+
+    qkv_halves = (
+        w_qkv[0].reshape(rows, 2, 2, 3, 64).transpose(1, 0, 3, 2, 4).reshape(2, rows, -1)
+    )
+    out_halves = w_out[0].T.reshape(rows, 2, -1).transpose(1, 0, 2)
+    up_halves = w_up[0].reshape(rows, 2, -1).transpose(1, 0, 2)
+    down_halves = w_down[0].T.reshape(rows, 2, -1).transpose(1, 0, 2)
+    n_qkv, n_out, n_up = qkv_halves.shape[2], out_halves.shape[2], up_halves.shape[2]
+
+    def both_layers(halves):
+        keep = pick(halves, section)
+        got = swap(pick(halves, 1 - section), "section", 1)
+        return jnp.where(first_section, keep, got), jnp.where(first_section, got, keep)
+
+    small = jnp.concatenate(
+        [
+            norm_gains[0].reshape(-1),
+            vec_bias[0].reshape(-1),
+            b_qkv[0].reshape(-1).astype(jnp.float32),
+            b_up[0].reshape(-1).astype(jnp.float32),
+        ]
+    )
+    other = swap(small, "section", 1)
+    small = jnp.where(first_section, jnp.stack([small, other]), jnp.stack([other, small]))
+    small = jnp.stack([small, swap(small, "dp", 1)])
+    small = jnp.concatenate([small, swap(small, "dp", 2)])
+    small = jnp.stack(
+        [small, ring(small, "tensor", 1), ring(small, "tensor", -1), ring(small, "tensor", 2)]
+    )
+
+    narrow = jnp.stack([jnp.concatenate([qkv_halves[h], out_halves[h]], axis=1) for h in (0, 1)])
+    broad = jnp.stack([jnp.concatenate([up_halves[h], down_halves[h]], axis=1) for h in (0, 1)])
+    narrow_shards = both_layers(narrow)
+    acts = exchange(acts_in[:, :, 0, :], along).reshape(length, width)
+    acts = relative(acts, across)
+    broad_shards = both_layers(broad)
+
+    def join(pieces, start, size):
+        part = pieces[..., start : start + size]
+        return part.transpose(1, 2, 3, 0, 4).reshape(width, -1)
+
+    mats = []
+    for layer in (0, 1):
+        pieces = gather_across_first(narrow_shards[layer])
+        mat_qkv, mat_out = join(pieces, 0, n_qkv), join(pieces, n_qkv, n_out)
+        pieces = gather_along_first(broad_shards[layer])
+        mats.append((mat_qkv, mat_out, join(pieces, 0, n_up), join(pieces, n_up, n_up)))
+        if layer == 0:
+            grads_in = exchange(cotangent[:, :, 0, :], along).reshape(length, width)
+            grads_in = relative(grads_in, across)
+
+    share = norm_gains.shape[2]
+    vec_part = small[..., : 6 * share].reshape(4, 4, 2, 6, share)
+    offsets = jnp.array(FAR_ORDER, jnp.int32)
+    order = jnp.stack([pick(offsets, (k - along) % 4) for k in range(4)])
+    vec_part = jnp.stack([pick(vec_part, order[k]) for k in range(4)])
+    vecs_full = vec_part.transpose(2, 3, 1, 0, 4).reshape(2, 6, width)
+    at = 6 * share
+    share_q = b_qkv.shape[2]
+    dp_order = [jnp.bitwise_xor(across, k) for k in range(4)]
+    qkv_bias = small[..., at : at + heads * share_q].reshape(4, 4, 2, heads, share_q)
+    qkv_bias = jnp.stack([pick(qkv_bias, i, 1) for i in dp_order], axis=1)
+    qkv_bias = qkv_bias.transpose(2, 0, 3, 1, 4).reshape(2, 4, 2, heads // 2, 3, 64)
+    qkv_bias = pick(qkv_bias, section, 2).transpose(0, 1, 3, 2, 4).reshape(2, 1, -1)
+    at += heads * share_q
+    bias_rows, share_u = b_up.shape[1], b_up.shape[2]
+    up_bias = small[..., at : at + bias_rows * share_u].reshape(4, 4, 2, bias_rows, share_u)
+    up_bias = jnp.stack([pick(up_bias, i, 1) for i in dp_order], axis=1)
+    up_bias = up_bias.transpose(2, 0, 3, 1, 4).reshape(2, 4, 2, bias_rows // 2, 4 * share_u)
+    up_bias = pick(up_bias, section, 2).reshape(2, 1, -1)
+    zero_rows = jnp.zeros((4, width), jnp.float32)
+
+    tables = turn_tables(length)
+    chunk = length // CHUNKS
+    starts = [i * chunk for i in range(CHUNKS)]
+
+    inputs = [acts[a : a + chunk] for a in starts]
+    kept = []
+    for layer in (0, 1):
+        mat_qkv, mat_out, mat_up, mat_down = mats[layer]
+        full = vecs_full[layer]
+        vecs = jnp.concatenate(
+            [full[0:1], full[2:3], full[1:2], full[3:4], zero_rows], axis=0
+        )
+        pieces = [
+            run_qkv(inputs[i], vecs, qkv_bias[layer], tables, mat_qkv, starts[i])
+            for i in range(CHUNKS)
+        ]
+        ln_a, ln_m, qkv = (jnp.concatenate(p, axis=0) for p in zip(*pieces))
+        ctx, lse = run_attend(qkv)
+        acts_list, slopes, outs = [], [], []
+        for i in range(CHUNKS):
+            act, slope, part = run_mlp(
+                ctx, ln_m, up_bias[layer], mat_out, mat_up, mat_down, starts[i], chunk
+            )
+            got = swap(part, "section", 1)
+            total = part.astype(jnp.float32) + got.astype(jnp.float32)
+            total = inputs[i].astype(jnp.float32) + total + (full[4] + full[5])
+            outs.append(total.astype(bf))
+            acts_list.append(act)
+            slopes.append(slope)
+        kept.append(
+            (inputs, vecs, ln_a, ln_m, qkv, ctx, lse, jnp.concatenate(acts_list), slopes, outs)
+        )
+        inputs = outs
+
+    upstream = [grads_in[a : a + chunk] for a in starts]
+    reduced = [None, None]
+    vectors = [None, None]
+    layer_grads = [None, None]
+    for layer in (1, 0):
+        mat_qkv, mat_out, mat_up, mat_down = mats[layer]
+        x_list, vecs, ln_a, ln_m, qkv, ctx, lse, act, slopes, _ = kept[layer]
+        pieces = [
+            run_mlp_back(upstream[i], slopes[i], mat_out, mat_down) for i in range(CHUNKS)
+        ]
+        d_up, d_ctx = (jnp.concatenate(p, axis=0) for p in list(zip(*pieces))[:2])
+        sum_up = sum(p[2] for p in pieces)
+        sum_g = sum(p[3] for p in pieces)
+        g_full = jnp.concatenate(upstream, axis=0)
+        d_qkv, sum_qkv = run_attend_back(qkv, d_ctx, lse, tables)
+        x_full = jnp.concatenate(x_list, axis=0)
+        downs, norm_sums = [], 0.0
+        for i in range(CHUNKS):
+            part, sums = run_norm_back(
+                x_full, d_qkv, d_up, vecs, mat_qkv, mat_up, starts[i], chunk
+            )
+            got = swap(part, "section", 1)
+            total = part.astype(jnp.float32) + got.astype(jnp.float32)
+            downs.append((upstream[i].astype(jnp.float32) + total).astype(bf))
+            norm_sums = norm_sums + sums[:4]
+
+        def split(left, right):
+            grad = tn_dot(left, right).astype(bf)
+            return grad.reshape(2, 2, rows, 4, -1)
+
+        broad_grad = jnp.concatenate([split(ln_m, d_up), split(g_full, act)], axis=-1)
+        narrow_grad = jnp.concatenate([split(ln_a, d_qkv), split(g_full, ctx)], axis=-1)
+        reduced[layer] = (reduce_across_last(narrow_grad), reduce_along_last(broad_grad))
+        vectors[layer] = (norm_sums, sum_g, sum_qkv, sum_up)
+        layer_grads[layer] = jnp.concatenate(downs, axis=0)
+        upstream = downs
+
+    def deliver(values):
+        return exchange(relative(values, across).reshape(4, positions, width), along)
+
+    acts_local = deliver(
+        jnp.where(first_section, jnp.concatenate(kept[0][9]), jnp.concatenate(kept[1][9]))
+    )
+    grad_local = deliver(jnp.where(first_section, layer_grads[0], layer_grads[1]))
+
+    def whole_layer(first, second):
+        keep = jnp.where(first_section, first, second)
+        got = swap(jnp.where(first_section, second, first), "section", 1)
+        keep, got = keep.astype(jnp.float32), got.astype(jnp.float32)
+        return jnp.where(first_section, jnp.stack([keep, got], 1), jnp.stack([got, keep], 1))
+
+    narrow_out = whole_layer(reduced[0][0], reduced[1][0])
+    broad_out = whole_layer(reduced[0][1], reduced[1][1])
+    grad_qkv = narrow_out[..., :n_qkv].reshape(rows, 2, 3, 2, 64)
+    grad_qkv = grad_qkv.transpose(0, 1, 3, 2, 4).reshape(rows, -1)
+    grad_out = narrow_out[..., n_qkv:].reshape(rows, -1).T
+    grad_up = broad_out[..., :n_up].reshape(rows, -1)
+    grad_down = broad_out[..., n_up:].reshape(rows, -1).T
+
+    flat = []
+    for norm_sums, sum_g, sum_qkv, sum_up in vectors:
+        feature = relative(jnp.concatenate([norm_sums, sum_g], axis=0), across)
+        q_sum = sum_qkv.reshape(4, 3, 2, 64).transpose(0, 2, 1, 3).reshape(4, -1)
+        both = jnp.concatenate([q_sum, sum_up.reshape(4, -1)], axis=1)
+        both = jnp.stack([pick(both, order[k]) for k in range(4)])
+        flat.append(jnp.concatenate([feature.reshape(-1), both.reshape(-1)]))
+    flat = jnp.stack(flat)
+    for axis, bit in (("dp", 1), ("dp", 2), ("tensor", 1), ("tensor", 2)):
+        flat = flat + swap(flat, axis, bit)
+    keep = pick(flat, section)
+    mine = pick(flat, 1 - section)
+    got = swap(mine, "section", 1)
+    n_feature = 5 * width
+    feature_own = keep[:n_feature].reshape(5, width)
+    feature = feature_own[:4] + got[: 4 * width].reshape(4, width)
+    place_at = (across * 4 + along) * share
+    gain_share = lax.dynamic_slice_in_dim(feature[:2], place_at, share, 1)
+    shifts = jnp.concatenate([feature[2:4], feature_own[4:5], feature_own[4:5]], axis=0)
+    bias_share = lax.dynamic_slice_in_dim(shifts, place_at, share, 1)
+    low_half = jnp.where(first_section, keep, got)[n_feature:].reshape(4, -1)
+    high_half = jnp.where(first_section, got, keep)[n_feature:].reshape(4, -1)
+    halves = jnp.stack([pick(low_half, along), pick(high_half, along)])
+    n_head = (heads // 2) * 192
+    head_sums = halves[:, :n_head].reshape(heads, 192)
+    head_share = lax.dynamic_slice_in_dim(head_sums, across * share_q, share_q, 1)
+    unit_sums = halves[:, n_head:].reshape(bias_rows, 4 * share_u)
+    unit_share = lax.dynamic_slice_in_dim(unit_sums, across * share_u, share_u, 1)
+    return (
+        acts_local[None, :, :, None],
+        grad_local[None, :, :, None],
+        gain_share[None],
+        bias_share[None],
+        grad_qkv[None],
+        head_share[None],
+        grad_out[None],
+        grad_up[None],
+        unit_share[None],
+        grad_down[None],
+    )
+
+
+def fits(mesh, args):
+    acts_in, b_qkv = args[0], args[5]
+    sizes = dict(mesh.shape)
+    return (
+        sizes["section"] == 2
+        and sizes["dp"] == 4
+        and sizes["tensor"] == MICRO
+        and MICRO == 4
+        and acts_in.shape[2] == sizes["dp"]
+        and b_qkv.shape[1] == 16
+        and b_qkv.shape[2] == 192
+        and acts_in.shape[1] % (CHUNKS * ROW_BLOCK) == 0
+    )
+
+
 def solution(mesh):
     placed = (
         P(None, "tensor", "dp", None),
@@ -405,21 +1092,24 @@
         P("section", "tensor", "dp"),
         P("section", "tensor", "dp"),
     )
-    return jax.shard_map(
-        local,
-        mesh=mesh,
-        in_specs=placed,
-        out_specs=(
-            P("section", None, "tensor", "dp", None),
-            P("section", None, "tensor", "dp", None),
-            P("section", None, ("dp", "tensor")),
-            P("section", None, ("dp", "tensor")),
-            P("section", "dp", "tensor"),
-            P("section", "tensor", "dp"),
-            P("section", "tensor", "dp"),
-            P("section", "dp", "tensor"),
-            P("section", "tensor", "dp"),
-            P("section", "tensor", "dp"),
-        ),
-        check_vma=False,
-    )
+    def wrap(body):
+        return jax.shard_map(
+            body,
+            mesh=mesh,
+            in_specs=placed,
+            out_specs=(
+                P("section", None, "tensor", "dp", None),
+                P("section", None, "tensor", "dp", None),
+                P("section", None, ("dp", "tensor")),
+                P("section", None, ("dp", "tensor")),
+                P("section", "dp", "tensor"),
+                P("section", "tensor", "dp"),
+                P("section", "tensor", "dp"),
+                P("section", "dp", "tensor"),
+                P("section", "tensor", "dp"),
+                P("section", "tensor", "dp"),
+            ),
+            check_vma=False,
+        )
+
+    return lambda *args: wrap(by_sequence if fits(mesh, args) else local)(*args)

time: 2180 us -> 1160 us (0.53)
  waiting for transfers between devices: 1230 us -> 257 us
  matrix products: 471 us -> 54.4 us
  Pallas kernels: 0 us -> 259 us
  starting transfers between devices: 23.5 us -> 218 us
  local copies, waits for them, and re-layouts: 98.1 us -> 261 us
  other arithmetic: 220 us -> 92.8 us
  blocking collectives: 101 us -> 0 us
    reduce_scatter x14 -> x0, waiting for transfers between devices: 761 us -> none  [the longest x5 356 us: local(): lax.psum_scatter(joined.reshape(lax.axis_size('tensor') * local_len, seq_...]
    dot_general x130 -> x8, matrix products: 471 us -> 54.4 us  [tn_dot(): lax.dot_general(left, right, (((0,), (0,)), ((), ())), preferred_element_...]
    all_gather x13 -> x0, waiting for transfers between devices: 276 us -> none  [the longest x5 168 us: local(): forward_gathered = lax.all_gather(inputs, 'tensor', axis=0, tiled=True)]
    pallas_call x0 -> x20, Pallas kernels: none -> 259 us  [call(): pl.pallas_call(body, name=name, grid=grid, in_specs=[pl.BlockSpec(block,...]
    ppermute x8 -> x93, starting transfers between devices: 19.3 us -> 218 us  [the longest x51 186 us: ring(): lax.ppermute(value, axis, [(i, (i + by) % length) for i in range(length)])]
    ppermute x8 -> x93, waiting for transfers between devices: 87.8 us -> 257 us  [the longest x51 160 us: ring(): lax.ppermute(value, axis, [(i, (i + by) % length) for i in range(length)])]
    unnamed x35 -> x0, waiting for transfers between devices: 109 us -> none
    all_gather x5 -> x0, blocking collectives: 101 us -> none  [the longest x1 47 us: local(): lax.all_gather(vec_bias[0], ('dp', 'tensor'), axis=1, tiled=True)]
  transfers between devices with their start and end apart: 39 -> 93, of which waited for: 31 -> 51; matrix products, arithmetic and copies ran while one was open for 18% -> 30% of each run, Pallas kernels for 0% -> 12%
where the time goes in v1:
time: 1160 us; the launch traced here: 1150 us
  local copies, waits for them, and re-layouts  261 us (22%)
  Pallas kernels  259 us (22%)
  waiting for transfers between devices  257 us (22%)
  starting transfers between devices  218 us (19%)
  other arithmetic  92.8 us (8%)
  matrix products  54.4 us (5%)
  between operations  11.7 us (1%)
    pallas_call x20, Pallas kernels, call(): pl.pallas_call(body, name=name, grid=grid, in_specs=[pl.BlockSpec(block,...  259 us
    ppermute x51, starting transfers between devices, ring(): lax.ppermute(value, axis, [(i, (i + by) % length) for i in range(length)])  186 us
    ppermute x51, waiting for transfers between devices, ring(): lax.ppermute(value, axis, [(i, (i + by) % length) for i in range(length)])  160 us
    ppermute x42, waiting for transfers between devices, swap(): return lax.ppermute(value, axis, [(i, i ^ bit) for i in range(length)])  97 us
    unnamed x269, local copies, waits for them, and re-layouts  80.3 us
    dot_general x8, matrix products, tn_dot(): lax.dot_general(left, right, (((0,), (0,)), ((), ())), preferred_element_...  54.4 us
    reshape x8, local copies, waits for them, and re-layouts, split(): return grad.reshape(2, 2, rows, 4, -1)  47.8 us
    ppermute x42, starting transfers between devices, swap(): return lax.ppermute(value, axis, [(i, i ^ bit) for i in range(length)])  32.5 us
  transfers between devices with their start and end apart: 93, of which 51 were waited for; matrix products, arithmetic and copies ran while one was open for 30% of the time, Pallas kernels for 12%

profile of v1, /device:TPU:0, one launch (start us, length us, event | category | flops | bytes accessed | tf_op | source)
XLA Modules:
  0.0 1153.2 jit_solution(3251982458367117789)
XLA Ops:
  79.4 13.4 %collective-permute-start.19 = (bf16[256,1024]{1,0:T(8,128)(2,1)S(1)}, bf16[256,1024]{1,0:T(8,128)(2,1)S(1)}, u32[]{:S(2)}, u32[]{:S(2)}) collective-permute-start(bf16[256,1024]{1,0:T(8,128)(2,1)S(1)} %get-tuple-element.227), channel_id=1, source_target_pairs={{0,1},{1,2},{2,3},{3,0},{4,5},{5,6},{6,7},{7,4},{8,9},{9,10},{10,1... | collective-permute-start | bytes 1572872 | tf_op jit(solution)/shard_map/ppermute | solution.py:405
  94.7 14.2 %collective-permute-done.1 = bf16[384,1024]{1,0:T(8,128)(2,1)} collective-permute-done((bf16[384,1024]{1,0:T(8,128)(2,1)}, bf16[384,1024]{1,0:T(8,128)(2,1)}, u32[]{:S(2)}, u32[]{:S(2)}) %collective-permute-start.1) | collective-permute-done | bytes 786464 | tf_op jit(solution)/shard_map/ppermute | solution.py:405
  113.2 13.3 %collective-permute-start.12 = (bf16[2,256,512]{2,1,0:T(8,128)(2,1)S(1)}, bf16[2,256,512]{2,1,0:T(8,128)(2,1)S(1)}, u32[]{:S(2)}, u32[]{:S(2)}) collective-permute-start(bf16[2,256,512]{2,1,0:T(8,128)(2,1)S(1)} %get-tuple-element.237), channel_id=1, source_target_pairs={{0,1},{1,2},{2,3},{3,0},{4,5},{5,6},{6,7},{7,4},{8,9},{9,10},{10,1... | collective-permute-start | bytes 1572872 | tf_op jit(solution)/shard_map/ppermute | solution.py:405
  133.0 8.5 collective-permute-done.36
  152.5 10.3 collective-permute-start.38
  166.1 8.9 collective-permute-done.12
  175.8 8.2 collective-permute-done.13
  187.7 9.8 collective-permute-done.38
  214.5 5.6 collective-permute-done.23
  225.0 6.1 collective-permute-done.41
  247.8 9.6 collective-permute-done.25
  262.8 5.8 collective-permute-done.37
  270.6 9.2 collective-permute-done.39
  280.0 5.7 collective-permute-done.42
  304.8 5.2 collective-permute-start.32
  317.1 8.4 constant_dynamic-slice_fusion.30
  343.8 6.0 norm_qkv.5
  349.8 6.0 norm_qkv.4
  359.5 28.7 %attend.2 = (bf16[1024,512]{1,0:T(8,128)(2,1)}, f32[4,8,1024]{2,1,0:T(8,128)}) custom-call(bf16[1024,1536]{1,0:T(8,128)(2,1)} %copy-done, bf16[1024,1536]{1,0:T(8,128)(2,1)} %copy-done, bf16[1024,1536]{1,0:T(8,128)(2,1)} %copy-done), custom_call_target="tpu_custom_call" | custom-call | tf_op jit(solution)/shard_map/attend/pallas_call | solution.py:540
  407.7 15.6 %mlp_out.5 = (bf16[512,2048]{1,0:T(8,128)(2,1)}, bf16[512,2048]{1,0:T(8,128)(2,1)}, bf16[512,1024]{1,0:T(8,128)(2,1)}) custom-call(bf16[1024,512]{1,0:T(8,128)(2,1)} %get-tuple-element.68.ctx, bf16[1024,1024]{1,0:T(8,128)(2,1)} %copy-done.18, f32[1,2048]{1,0:T(1,128)} %bitcast.718, bf16[1024,512]{1,0:T(8,128)(2,1)} %bitcast.611, ...), custom_call_target="tpu_custom_call" | custom-call | tf_op jit(solution)/shard_map/mlp_out/pallas_call | solution.py:540
  423.3 15.0 %mlp_out.4 = (bf16[512,2048]{1,0:T(8,128)(2,1)}, bf16[512,2048]{1,0:T(8,128)(2,1)}, bf16[512,1024]{1,0:T(8,128)(2,1)}) custom-call(bf16[1024,512]{1,0:T(8,128)(2,1)} %get-tuple-element.68.ctx, bf16[1024,1024]{1,0:T(8,128)(2,1)} %copy-done.18, f32[1,2048]{1,0:T(1,128)} %bitcast.719, bf16[1024,512]{1,0:T(8,128)(2,1)} %bitcast.612, ...), custom_call_target="tpu_custom_call" | custom-call | tf_op jit(solution)/shard_map/mlp_out/pallas_call | solution.py:540
  468.6 17.8 %collective-permute-done.27 = bf16[512,1024]{1,0:T(8,128)(2,1)S(1)} collective-permute-done((bf16[512,1024]{1,0:T(8,128)(2,1)}, bf16[512,1024]{1,0:T(8,128)(2,1)S(1)}, u32[]{:S(2)}, u32[]{:S(2)}) %collective-permute-start.27) | collective-permute-done | bytes 1048608 | tf_op jit(solution)/shard_map/ppermute | solution.py:410
  489.3 6.3 norm_qkv.7
  495.6 6.0 norm_qkv.6
  507.3 19.1 %attend.3 = (bf16[1024,512]{1,0:T(8,128)(2,1)}, f32[4,8,1024]{2,1,0:T(8,128)}) custom-call(bf16[1024,1536]{1,0:T(8,128)(2,1)} %copy-done.1, bf16[1024,1536]{1,0:T(8,128)(2,1)} %copy-done.1, bf16[1024,1536]{1,0:T(8,128)(2,1)} %copy-done.1), custom_call_target="tpu_custom_call" | custom-call | tf_op jit(solution)/shard_map/attend/pallas_call | solution.py:540
  528.7 14.8 %mlp_out.6 = (bf16[512,2048]{1,0:T(8,128)(2,1)}, bf16[512,2048]{1,0:T(8,128)(2,1)}, bf16[512,1024]{1,0:T(8,128)(2,1)}) custom-call(bf16[1024,512]{1,0:T(8,128)(2,1)} %get-tuple-element.75.ctx, bf16[1024,1024]{1,0:T(8,128)(2,1)} %constant_dynamic-update-slice_fusion.8.ln_m, f32[1,2048]{1,0:T(1,128)} %bitcast.716, bf16[1024,512]{1,0:T(8,128)(2,1)} %bitcast.615, ...), custom_call_target="tpu_custom_call" | custom-call | tf_op jit(solution)/shard_map/mlp_out/pallas_call | solution.py:540
  543.6 15.8 %mlp_out.7 = (bf16[512,2048]{1,0:T(8,128)(2,1)}, bf16[512,2048]{1,0:T(8,128)(2,1)}, bf16[512,1024]{1,0:T(8,128)(2,1)}) custom-call(bf16[1024,512]{1,0:T(8,128)(2,1)} %get-tuple-element.75.ctx, bf16[1024,1024]{1,0:T(8,128)(2,1)} %constant_dynamic-update-slice_fusion.8.ln_m, f32[1,2048]{1,0:T(1,128)} %bitcast.717, bf16[1024,512]{1,0:T(8,128)(2,1)} %bitcast.616, ...), custom_call_target="tpu_custom_call" | custom-call | tf_op jit(solution)/shard_map/mlp_out/pallas_call | solution.py:540
  560.9 7.4 mlp_back.4
  571.4 7.4 mlp_back.5
  583.2 26.0 %attend_back.2 = (bf16[1024,1536]{1,0:T(8,128)(2,1)}, f32[1,1536]{1,0:T(1,128)}) custom-call(bf16[1024,1536]{1,0:T(8,128)(2,1)} %copy-done.1, bf16[1024,1536]{1,0:T(8,128)(2,1)} %copy-done.1, bf16[1024,1536]{1,0:T(8,128)(2,1)} %copy-done.1, bf16[1024,512]{1,0:T(8,128)(2,1)} %pad_maximum_fusion.16.d_ctx, f32[4,8,1024]{2,1,0:T(8,128)} %get-tuple-element.84.lse, ...), custom_call_target="tpu_custom_call" | custom-call | tf_op jit(solution)/shard_map/attend_back/pallas_call | solution.py:540
  609.2 10.8 norm_back.5
  620.0 11.0 norm_back.4
  631.0 9.5 convolution_convert_fusion.2
  645.4 9.2 fusion.20
  654.7 7.8 reshape.503
  662.5 8.2 reshape.502
  686.9 6.2 reshape.493
  704.3 5.0 add_convert_fusion.3
  709.2 7.5 mlp_back.6
  719.9 7.4 mlp_back.7
  731.6 26.0 %attend_back.3 = (bf16[1024,1536]{1,0:T(8,128)(2,1)}, f32[1,1536]{1,0:T(1,128)}) custom-call(bf16[1024,1536]{1,0:T(8,128)(2,1)} %copy-done, bf16[1024,1536]{1,0:T(8,128)(2,1)} %copy-done, bf16[1024,1536]{1,0:T(8,128)(2,1)} %copy-done, bf16[1024,512]{1,0:T(8,128)(2,1)} %pad_maximum_fusion.17.d_ctx, f32[4,8,1024]{2,1,0:T(8,128)} %get-tuple-element.94.lse, ...), custom_call_target="tpu_custom_call" | custom-call | tf_op jit(solution)/shard_map/attend_back/pallas_call | solution.py:540
  757.6 10.8 norm_back.6
  768.4 11.2 norm_back.7
  779.6 9.6 convolution_convert_fusion.3
  792.3 9.1 fusion.23
  801.4 7.9 reshape.501
  809.3 7.8 reshape.500
  817.1 5.2 copy_dynamic-update-slice_fusion.3
  824.4 7.7 convolution_convert_fusion.1
  832.1 6.4 reshape.491
  886.1 19.1 %collective-permute-done.57 = bf16[512,1024]{1,0:T(8,128)(2,1)} collective-permute-done((bf16[512,1024]{1,0:T(8,128)(2,1)}, bf16[512,1024]{1,0:T(8,128)(2,1)}, u32[]{:S(2)}, u32[]{:S(2)}) %collective-permute-start.57) | collective-permute-done | bytes 1048608 | tf_op jit(solution)/shard_map/ppermute | solution.py:410
  921.5 5.4 collective-permute-done.74
  936.2 13.3 %collective-permute-done.58 = bf16[384,1024]{1,0:T(8,128)(2,1)S(1)} collective-permute-done((bf16[384,1024]{1,0:T(8,128)(2,1)S(1)}, bf16[384,1024]{1,0:T(8,128)(2,1)S(1)}, u32[]{:S(2)}, u32[]{:S(2)}) %collective-permute-start.58) | collective-permute-done | bytes 786464 | tf_op jit(solution)/shard_map/ppermute | solution.py:405
  950.0 5.0 collective-permute-done.68
  955.0 20.0 %collective-permute-start.75 = (bf16[2,256,512]{2,1,0:T(8,128)(2,1)S(1)}, bf16[2,256,512]{2,1,0:T(8,128)(2,1)}, u32[]{:S(2)}, u32[]{:S(2)}) collective-permute-start(bf16[2,256,512]{2,1,0:T(8,128)(2,1)S(1)} %pad_maximum_fusion.30), channel_id=1, source_target_pairs={{0,1},{1,2},{2,3},{3,0},{4,5},{5,6},{6,7},{7,4},{8,9},{9,10},{10,1... | collective-permute-start | bytes 1572872 | tf_op jit(solution)/shard_map/ppermute | solution.py:405
  989.8 13.4 %collective-permute-start.71 = (bf16[2,256,512]{2,1,0:T(8,128)(2,1)S(1)}, bf16[2,256,512]{2,1,0:T(8,128)(2,1)S(1)}, u32[]{:S(2)}, u32[]{:S(2)}) collective-permute-start(bf16[2,256,512]{2,1,0:T(8,128)(2,1)S(1)} %pad_maximum_fusion.29), channel_id=1, source_target_pairs={{0,3},{1,0},{2,1},{3,2},{4,7},{5,4},{6,5},{7,6},{8,11},{9,8},{10,9... | collective-permute-start | bytes 1572872 | tf_op jit(solution)/shard_map/ppermute | solution.py:405
  1011.3 27.2 %collective-permute-start.46 = (bf16[384,1024]{1,0:T(8,128)(2,1)S(1)}, bf16[384,1024]{1,0:T(8,128)(2,1)S(1)}, u32[]{:S(2)}, u32[]{:S(2)}) collective-permute-start(bf16[384,1024]{1,0:T(8,128)(2,1)S(1)} %copy-done.75), channel_id=1, source_target_pairs={{0,1},{1,2},{2,3},{3,0},{4,5},{5,6},{6,7},{7,4},{8,9},{9,10},{10,1... | collective-permute-start | bytes 2359304 | tf_op jit(solution)/shard_map/ppermute | solution.py:405
  1045.9 12.3 %collective-permute-done.81 = bf16[256,4,1024]{2,0,1:T(8,128)(2,1)S(1)} collective-permute-done((bf16[256,4,1024]{2,0,1:T(8,128)(2,1)S(1)}, bf16[256,4,1024]{2,0,1:T(8,128)(2,1)S(1)}, u32[]{:S(2)}, u32[]{:S(2)}) %collective-permute-start.81) | collective-permute-done | bytes 2097184 | tf_op jit(solution)/shard_map/ppermute | solution.py:410
  1061.9 7.1 collective-permute-start.82
  1078.0 7.7 collective-permute-start.89
  1092.3 5.8 collective-permute-done.89
  1100.6 11.6 %collective-permute-done.91 = bf16[256,1024]{1,0:T(8,128)(2,1)S(1)} collective-permute-done((bf16[256,1024]{1,0:T(8,128)(2,1)S(1)}, bf16[256,1024]{1,0:T(8,128)(2,1)S(1)}, u32[]{:S(2)}, u32[]{:S(2)}) %collective-permute-start.91) | collective-permute-done | bytes 524320 | tf_op jit(solution)/shard_map/ppermute | solution.py:405
  1113.9 6.7 collective-permute-done.83
  1120.6 12.6 %collective-permute-start.48 = (bf16[128,1024]{1,0:T(8,128)(2,1)S(1)}, bf16[128,1024]{1,0:T(8,128)(2,1)S(1)}, u32[]{:S(2)}, u32[]{:S(2)}) collective-permute-start(bf16[128,1024]{1,0:T(8,128)(2,1)S(1)} %slice.793), channel_id=1, source_target_pairs={{0,1},{1,2},{2,3},{3,0},{4,5},{5,6},{6,7},{7,4},{8,9},{9,10},{10,1... | collective-permute-start | bytes 786440 | tf_op jit(solution)/shard_map/ppermute | solution.py:405
  (751 shorter events, 456.3 us)
Async XLA Ops:
  4.5 63.8 %collective-permute-start.17 = (bf16[256,1024]{1,0:T(8,128)(2,1)}, bf16[256,1024]{1,0:T(8,128)(2,1)}, u32[]{:S(2)}, u32[]{:S(2)}) collective-permute-start(bf16[256,1024]{1,0:T(8,128)(2,1)} %fusion.47), channel_id=1, source_target_pairs={{0,16},{16,0},{1,17},{17,1},{2,18},{18,2},{3,19},{19,3},{4,20},{20... | collective-permute-start | bytes 1572872 | tf_op jit(solution)/shard_map/ppermute | solution.py:410
  10.6 51.3 %collective-permute-start.10 = (bf16[256,512]{1,0:T(8,128)(2,1)}, bf16[256,512]{1,0:T(8,128)(2,1)}, u32[]{:S(2)}, u32[]{:S(2)}) collective-permute-start(bf16[256,512]{1,0:T(8,128)(2,1)} %bitcast.38), channel_id=1, source_target_pairs={{0,16},{16,0},{1,17},{17,1},{2,18},{18,2},{3,19},{19,3},{4,20},{20... | collective-permute-start | bytes 786440 | tf_op jit(solution)/shard_map/ppermute | solution.py:410
  57.4 51.5 %collective-permute-start.1 = (bf16[384,1024]{1,0:T(8,128)(2,1)}, bf16[384,1024]{1,0:T(8,128)(2,1)}, u32[]{:S(2)}, u32[]{:S(2)}) collective-permute-start(bf16[384,1024]{1,0:T(8,128)(2,1)} %pad_maximum_fusion.19), channel_id=1, source_target_pairs={{0,3},{1,0},{2,1},{3,2},{4,7},{5,4},{6,5},{7,6},{8,11},{9,8},{10,9... | collective-permute-start | bytes 2359304 | tf_op jit(solution)/shard_map/ppermute | solution.py:405
  60.7 52.5 %collective-permute-start.50 = (bf16[384,1024]{1,0:T(8,128)(2,1)}, bf16[384,1024]{1,0:T(8,128)(2,1)}, u32[]{:S(2)}, u32[]{:S(2)}) collective-permute-start(bf16[384,1024]{1,0:T(8,128)(2,1)} %pad_maximum_fusion.22), channel_id=1, source_target_pairs={{0,1},{1,2},{2,3},{3,0},{4,5},{5,6},{6,7},{7,4},{8,9},{9,10},{10,1... | collective-permute-start | bytes 2359304 | tf_op jit(solution)/shard_map/ppermute | solution.py:405
  68.3 62.0 %collective-permute-start.51 = (bf16[384,1024]{1,0:T(8,128)(2,1)}, bf16[384,1024]{1,0:T(8,128)(2,1)S(1)}, u32[]{:S(2)}, u32[]{:S(2)}) collective-permute-start(bf16[384,1024]{1,0:T(8,128)(2,1)} %pad_maximum_fusion.23), channel_id=1, source_target_pairs={{0,3},{1,0},{2,1},{3,2},{4,7},{5,4},{6,5},{7,6},{8,11},{9,8},{10,9... | collective-permute-start | bytes 2359304 | tf_op jit(solution)/shard_map/ppermute | solution.py:405
  78.5 62.9 %collective-permute-start.36 = (bf16[256,1024]{1,0:T(8,128)(2,1)S(1)}, bf16[256,1024]{1,0:T(8,128)(2,1)}, u32[]{:S(2)}, u32[]{:S(2)}) collective-permute-start(bf16[256,1024]{1,0:T(8,128)(2,1)S(1)} %get-tuple-element.226), channel_id=1, source_target_pairs={{0,1},{1,2},{2,3},{3,0},{4,5},{5,6},{6,7},{7,4},{8,9},{9,10},{10,1... | collective-permute-start | bytes 1572872 | tf_op jit(solution)/shard_map/ppermute | solution.py:405
  79.4 73.0 %collective-permute-start.19 = (bf16[256,1024]{1,0:T(8,128)(2,1)S(1)}, bf16[256,1024]{1,0:T(8,128)(2,1)S(1)}, u32[]{:S(2)}, u32[]{:S(2)}) collective-permute-start(bf16[256,1024]{1,0:T(8,128)(2,1)S(1)} %get-tuple-element.227), channel_id=1, source_target_pairs={{0,1},{1,2},{2,3},{3,0},{4,5},{5,6},{6,7},{7,4},{8,9},{9,10},{10,1... | collective-permute-start | bytes 1572872 | tf_op jit(solution)/shard_map/ppermute | solution.py:405
  108.8 55.0 %collective-permute-start.21 = (bf16[256,1024]{1,0:T(8,128)(2,1)S(1)}, bf16[256,1024]{1,0:T(8,128)(2,1)}, u32[]{:S(2)}, u32[]{:S(2)}) collective-permute-start(bf16[256,1024]{1,0:T(8,128)(2,1)S(1)} %get-tuple-element.227), channel_id=1, source_target_pairs={{0,3},{1,0},{2,1},{3,2},{4,7},{5,4},{6,5},{7,6},{8,11},{9,8},{10,9... | collective-permute-start | bytes 1572872 | tf_op jit(solution)/shard_map/ppermute | solution.py:405
  113.2 61.8 %collective-permute-start.12 = (bf16[2,256,512]{2,1,0:T(8,128)(2,1)S(1)}, bf16[2,256,512]{2,1,0:T(8,128)(2,1)S(1)}, u32[]{:S(2)}, u32[]{:S(2)}) collective-permute-start(bf16[2,256,512]{2,1,0:T(8,128)(2,1)S(1)} %get-tuple-element.237), channel_id=1, source_target_pairs={{0,1},{1,2},{2,3},{3,0},{4,5},{5,6},{6,7},{7,4},{8,9},{9,10},{10,1... | collective-permute-start | bytes 1572872 | tf_op jit(solution)/shard_map/ppermute | solution.py:405
  130.3 53.7 %collective-permute-start.13 = (bf16[2,256,512]{2,1,0:T(8,128)(2,1)S(1)}, bf16[2,256,512]{2,1,0:T(8,128)(2,1)S(1)}, u32[]{:S(2)}, u32[]{:S(2)}) collective-permute-start(bf16[2,256,512]{2,1,0:T(8,128)(2,1)S(1)} %get-tuple-element.237), channel_id=1, source_target_pairs={{0,3},{1,0},{2,1},{3,2},{4,7},{5,4},{6,5},{7,6},{8,11},{9,8},{10,9... | collective-permute-start | bytes 1572872 | tf_op jit(solution)/shard_map/ppermute | solution.py:405
  141.4 46.2 %collective-permute-start.35 = (bf16[256,1024]{1,0:T(8,128)(2,1)S(1)}, bf16[256,1024]{1,0:T(8,128)(2,1)S(1)}, u32[]{:S(2)}, u32[]{:S(2)}) collective-permute-start(bf16[256,1024]{1,0:T(8,128)(2,1)S(1)} %get-tuple-element.226), channel_id=1, source_target_pairs={{0,8},{4,12},{8,0},{12,4},{1,9},{5,13},{9,1},{13,5},{2,10},{6,14},... | collective-permute-start | bytes 1572872 | tf_op jit(solution)/shard_map/ppermute | solution.py:410
  152.5 45.0 %collective-permute-start.38 = (bf16[256,1024]{1,0:T(8,128)(2,1)S(1)}, bf16[256,1024]{1,0:T(8,128)(2,1)S(1)}, u32[]{:S(2)}, u32[]{:S(2)}) collective-permute-start(bf16[256,1024]{1,0:T(8,128)(2,1)S(1)} %get-tuple-element.226), channel_id=1, source_target_pairs={{0,3},{1,0},{2,1},{3,2},{4,7},{5,4},{6,5},{7,6},{8,11},{9,8},{10,9... | collective-permute-start | bytes 1572872 | tf_op jit(solution)/shard_map/ppermute | solution.py:405
  163.9 34.1 %collective-permute-start.18 = (bf16[256,1024]{1,0:T(8,128)(2,1)S(1)}, bf16[256,1024]{1,0:T(8,128)(2,1)S(1)}, u32[]{:S(2)}, u32[]{:S(2)}) collective-permute-start(bf16[256,1024]{1,0:T(8,128)(2,1)S(1)} %get-tuple-element.227), channel_id=1, source_target_pairs={{0,8},{4,12},{8,0},{12,4},{1,9},{5,13},{9,1},{13,5},{2,10},{6,14},... | collective-permute-start | bytes 1572872 | tf_op jit(solution)/shard_map/ppermute | solution.py:410
  175.0 28.1 %collective-permute-start.2 = (bf16[128,1024]{1,0:T(8,128)(2,1)S(1)}, bf16[128,1024]{1,0:T(8,128)(2,1)S(1)}, u32[]{:S(2)}, u32[]{:S(2)}) collective-permute-start(bf16[128,1024]{1,0:T(8,128)(2,1)S(1)} %slice.748), channel_id=1, source_target_pairs={{0,1},{1,2},{2,3},{3,0},{4,5},{5,6},{6,7},{7,4},{8,9},{9,10},{10,1... | collective-permute-start | bytes 786440 | tf_op jit(solution)/shard_map/ppermute | solution.py:405
  184.0 24.7 %collective-permute-start.3 = (bf16[128,1024]{1,0:T(8,128)(2,1)S(1)}, bf16[128,1024]{1,0:T(8,128)(2,1)S(1)}, u32[]{:S(2)}, u32[]{:S(2)}) collective-permute-start(bf16[128,1024]{1,0:T(8,128)(2,1)S(1)} %slice.749), channel_id=1, source_target_pairs={{0,3},{1,0},{2,1},{3,2},{4,7},{5,4},{6,5},{7,6},{8,11},{9,8},{10,9... | collective-permute-start | bytes 786440 | tf_op jit(solution)/shard_map/ppermute | solution.py:405
  187.6 34.1 %collective-permute-start.40 = (bf16[128,1024]{1,0:T(8,128)(2,1)}, bf16[128,1024]{1,0:T(8,128)(2,1)}, u32[]{:S(2)}, u32[]{:S(2)}) collective-permute-start(bf16[128,1024]{1,0:T(8,128)(2,1)} %slice.785), channel_id=1, source_target_pairs={{0,1},{1,2},{2,3},{3,0},{4,5},{5,6},{6,7},{7,4},{8,9},{9,10},{10,1... | collective-permute-start | bytes 786440 | tf_op jit(solution)/shard_map/ppermute | solution.py:405
  197.5 22.6 %collective-permute-start.23 = (bf16[128,1024]{1,0:T(8,128)(2,1)}, bf16[128,1024]{1,0:T(8,128)(2,1)}, u32[]{:S(2)}, u32[]{:S(2)}) collective-permute-start(bf16[128,1024]{1,0:T(8,128)(2,1)} %slice.770), channel_id=1, source_target_pairs={{0,1},{1,2},{2,3},{3,0},{4,5},{5,6},{6,7},{7,4},{8,9},{9,10},{10,1... | collective-permute-start | bytes 786440 | tf_op jit(solution)/shard_map/ppermute | solution.py:405
  198.0 25.4 %collective-permute-start.24 = (bf16[128,1024]{1,0:T(8,128)(2,1)}, bf16[128,1024]{1,0:T(8,128)(2,1)}, u32[]{:S(2)}, u32[]{:S(2)}) collective-permute-start(bf16[128,1024]{1,0:T(8,128)(2,1)} %slice.771), channel_id=1, source_target_pairs={{0,3},{1,0},{2,1},{3,2},{4,7},{5,4},{6,5},{7,6},{8,11},{9,8},{10,9... | collective-permute-start | bytes 786440 | tf_op jit(solution)/shard_map/ppermute | solution.py:405
  203.1 28.0 %collective-permute-start.41 = (bf16[128,1024]{1,0:T(8,128)(2,1)}, bf16[128,1024]{1,0:T(8,128)(2,1)S(1)}, u32[]{:S(2)}, u32[]{:S(2)}) collective-permute-start(bf16[128,1024]{1,0:T(8,128)(2,1)} %slice.786), channel_id=1, source_target_pairs={{0,3},{1,0},{2,1},{3,2},{4,7},{5,4},{6,5},{7,6},{8,11},{9,8},{10,9... | collective-permute-start | bytes 786440 | tf_op jit(solution)/shard_map/ppermute | solution.py:405
  208.7 28.3 %collective-permute-start.14 = (bf16[256,512]{1,0:T(8,128)(2,1)}, bf16[256,512]{1,0:T(8,128)(2,1)}, u32[]{:S(2)}, u32[]{:S(2)}) collective-permute-start(bf16[256,512]{1,0:T(8,128)(2,1)} %slice_bitcast_fusion.59), channel_id=1, source_target_pairs={{0,1},{1,2},{2,3},{3,0},{4,5},{5,6},{6,7},{7,4},{8,9},{9,10},{10,1... | collective-permute-start | bytes 786440 | tf_op jit(solution)/shard_map/ppermute | solution.py:405
  223.4 22.8 %collective-permute-start.22 = (bf16[256,1024]{1,0:T(8,128)(2,1)}, bf16[256,1024]{1,0:T(8,128)(2,1)S(1)}, u32[]{:S(2)}, u32[]{:S(2)}) collective-permute-start(bf16[256,1024]{1,0:T(8,128)(2,1)} %collective-permute-done.21), channel_id=1, source_target_pairs={{0,8},{4,12},{8,0},{12,4},{1,9},{5,13},{9,1},{13,5},{2,10},{6,14},... | collective-permute-start | bytes 1572872 | tf_op jit(solution)/shard_map/ppermute | solution.py:410
  231.1 26.3 %collective-permute-start.25 = (bf16[256,1024]{1,0:T(8,128)(2,1)S(1)}, bf16[256,1024]{1,0:T(8,128)(2,1)S(1)}, u32[]{:S(2)}, u32[]{:S(2)}) collective-permute-start(bf16[256,1024]{1,0:T(8,128)(2,1)S(1)} %constant_dynamic-update-slice_fusion.4), channel_id=1, source_target_pairs={{0,8},{4,12},{8,0},{12,4},{1,9},{5,13},{9,1},{13,5},{2,10},{6,14},... | collective-permute-start | bytes 1572872 | tf_op jit(solution)/shard_map/ppermute | solution.py:410
  237.0 56.8 %collective-permute-start.30 = (bf16[2,256,512]{2,1,0:T(8,128)(2,1)S(1)}, bf16[2,256,512]{2,1,0:T(8,128)(2,1)S(1)}, u32[]{:S(2)}, u32[]{:S(2)}) collective-permute-start(bf16[2,256,512]{2,1,0:T(8,128)(2,1)S(1)} %copy-done.78), channel_id=1, source_target_pairs={{0,1},{1,2},{2,3},{3,0},{4,5},{5,6},{6,7},{7,4},{8,9},{9,10},{10,1... | collective-permute-start | bytes 1572872 | tf_op jit(solution)/shard_map/ppermute | solution.py:405
  240.1 28.6 %collective-permute-start.37 = (bf16[256,1024]{1,0:T(8,128)(2,1)}, bf16[256,1024]{1,0:T(8,128)(2,1)S(1)}, u32[]{:S(2)}, u32[]{:S(2)}) collective-permute-start(bf16[256,1024]{1,0:T(8,128)(2,1)} %collective-permute-done.36), channel_id=1, source_target_pairs={{0,8},{4,12},{8,0},{12,4},{1,9},{5,13},{9,1},{13,5},{2,10},{6,14},... | collective-permute-start | bytes 1572872 | tf_op jit(solution)/shard_map/ppermute | solution.py:410
  241.6 38.2 %collective-permute-start.39 = (bf16[256,1024]{1,0:T(8,128)(2,1)S(1)}, bf16[256,1024]{1,0:T(8,128)(2,1)S(1)}, u32[]{:S(2)}, u32[]{:S(2)}) collective-permute-start(bf16[256,1024]{1,0:T(8,128)(2,1)S(1)} %copy-done.69), channel_id=1, source_target_pairs={{0,8},{4,12},{8,0},{12,4},{1,9},{5,13},{9,1},{13,5},{2,10},{6,14},... | collective-permute-start | bytes 1572872 | tf_op jit(solution)/shard_map/ppermute | solution.py:410
  246.1 39.5 %collective-permute-start.42 = (bf16[256,1024]{1,0:T(8,128)(2,1)S(1)}, bf16[256,1024]{1,0:T(8,128)(2,1)S(1)}, u32[]{:S(2)}, u32[]{:S(2)}) collective-permute-start(bf16[256,1024]{1,0:T(8,128)(2,1)S(1)} %constant_dynamic-update-slice_fusion.10), channel_id=1, source_target_pairs={{0,8},{4,12},{8,0},{12,4},{1,9},{5,13},{9,1},{13,5},{2,10},{6,14},... | collective-permute-start | bytes 1572872 | tf_op jit(solution)/shard_map/ppermute | solution.py:410
  261.1 130.0 %collective-permute-start.26 = (bf16[4,2,256,1024]{3,2,1,0:T(8,128)(2,1)}, bf16[4,2,256,1024]{3,2,1,0:T(8,128)(2,1)}, u32[]{:S(2)}, u32[]{:S(2)}) collective-permute-start(bf16[4,2,256,1024]{3,2,1,0:T(8,128)(2,1)} %get-tuple-element.152), channel_id=1, source_target_pairs={{0,4},{4,0},{8,12},{12,8},{1,5},{5,1},{9,13},{13,9},{2,6},{6,2},{1... | collective-permute-start | bytes 12582920 | tf_op jit(solution)/shard_map/ppermute | solution.py:410
  268.6 26.7 %collective-permute-start.31 = (bf16[2,256,512]{2,1,0:T(8,128)(2,1)S(1)}, bf16[2,256,512]{2,1,0:T(8,128)(2,1)S(1)}, u32[]{:S(2)}, u32[]{:S(2)}) collective-permute-start(bf16[2,256,512]{2,1,0:T(8,128)(2,1)S(1)} %copy-done.78), channel_id=1, source_target_pairs={{0,3},{1,0},{2,1},{3,2},{4,7},{5,4},{6,5},{7,6},{8,11},{9,8},{10,9... | collective-permute-start | bytes 1572872 | tf_op jit(solution)/shard_map/ppermute | solution.py:405
  279.9 54.6 %collective-permute-start.16 = (bf16[4,2,256,512]{3,2,1,0:T(8,128)(2,1)}, bf16[4,2,256,512]{3,2,1,0:T(8,128)(2,1)}, u32[]{:S(2)}, u32[]{:S(2)}) collective-permute-start(bf16[4,2,256,512]{3,2,1,0:T(8,128)(2,1)} %get-tuple-element.214), channel_id=1, source_target_pairs={{0,4},{4,0},{8,12},{12,8},{1,5},{5,1},{9,13},{13,9},{2,6},{6,2},{1... | collective-permute-start | bytes 6291464 | tf_op jit(solution)/shard_map/ppermute | solution.py:410
  289.4 162.0 %collective-permute-start.43 = (bf16[4,2,256,1024]{3,2,1,0:T(8,128)(2,1)}, bf16[4,2,256,1024]{3,2,1,0:T(8,128)(2,1)}, u32[]{:S(2)}, u32[]{:S(2)}) collective-permute-start(bf16[4,2,256,1024]{3,2,1,0:T(8,128)(2,1)} %get-tuple-element.150), channel_id=1, source_target_pairs={{0,4},{4,0},{8,12},{12,8},{1,5},{5,1},{9,13},{13,9},{2,6},{6,2},{1... | collective-permute-start | bytes 12582920 | tf_op jit(solution)/shard_map/ppermute | solution.py:410
  304.8 25.2 %collective-permute-start.32 = (bf16[256,512]{1,0:T(8,128)(2,1)}, bf16[256,512]{1,0:T(8,128)(2,1)S(1)}, u32[]{:S(2)}, u32[]{:S(2)}) collective-permute-start(bf16[256,512]{1,0:T(8,128)(2,1)} %slice_bitcast_fusion.53), channel_id=1, source_target_pairs={{0,1},{1,2},{2,3},{3,0},{4,5},{5,6},{6,7},{7,4},{8,9},{9,10},{10,1... | collective-permute-start | bytes 786440 | tf_op jit(solution)/shard_map/ppermute | solution.py:405
  332.8 109.2 %collective-permute-start.34 = (bf16[4,2,256,512]{3,2,1,0:T(8,128)(2,1)}, bf16[4,2,256,512]{3,2,1,0:T(8,128)(2,1)}, u32[]{:S(2)}, u32[]{:S(2)}) collective-permute-start(bf16[4,2,256,512]{3,2,1,0:T(8,128)(2,1)} %get-tuple-element.210), channel_id=1, source_target_pairs={{0,4},{4,0},{8,12},{12,8},{1,5},{5,1},{9,13},{13,9},{2,6},{6,2},{1... | collective-permute-start | bytes 6291464 | tf_op jit(solution)/shard_map/ppermute | solution.py:410
  438.3 30.3 %collective-permute-start.28 = (bf16[512,1024]{1,0:T(8,128)(2,1)S(1)}, bf16[512,1024]{1,0:T(8,128)(2,1)S(1)}, u32[]{:S(2)}, u32[]{:S(2)}) collective-permute-start(bf16[512,1024]{1,0:T(8,128)(2,1)S(1)} %copy-done.73), channel_id=1, source_target_pairs={{0,16},{16,0},{1,17},{17,1},{2,18},{18,2},{3,19},{19,3},{4,20},{20... | collective-permute-start | bytes 3145736 | tf_op jit(solution)/shard_map/ppermute | solution.py:410
  438.9 47.5 %collective-permute-start.27 = (bf16[512,1024]{1,0:T(8,128)(2,1)}, bf16[512,1024]{1,0:T(8,128)(2,1)S(1)}, u32[]{:S(2)}, u32[]{:S(2)}) collective-permute-start(bf16[512,1024]{1,0:T(8,128)(2,1)} %get-tuple-element.71), channel_id=1, source_target_pairs={{0,16},{16,0},{1,17},{17,1},{2,18},{18,2},{3,19},{19,3},{4,20},{20... | collective-permute-start | bytes 3145736 | tf_op jit(solution)/shard_map/ppermute | solution.py:410
  642.8 59.9 %collective-permute-start.55 = (bf16[512,1024]{1,0:T(8,128)(2,1)}, bf16[512,1024]{1,0:T(8,128)(2,1)}, u32[]{:S(2)}, u32[]{:S(2)}) collective-permute-start(bf16[512,1024]{1,0:T(8,128)(2,1)} %get-tuple-element.91), channel_id=1, source_target_pairs={{0,16},{16,0},{1,17},{17,1},{2,18},{18,2},{3,19},{19,3},{4,20},{20... | collective-permute-start | bytes 3145736 | tf_op jit(solution)/shard_map/ppermute | solution.py:410
  643.3 61.0 %collective-permute-start.54 = (bf16[512,1024]{1,0:T(8,128)(2,1)}, bf16[512,1024]{1,0:T(8,128)(2,1)}, u32[]{:S(2)}, u32[]{:S(2)}) collective-permute-start(bf16[512,1024]{1,0:T(8,128)(2,1)} %get-tuple-element.88), channel_id=1, source_target_pairs={{0,16},{16,0},{1,17},{17,1},{2,18},{18,2},{3,19},{19,3},{4,20},{20... | collective-permute-start | bytes 3145736 | tf_op jit(solution)/shard_map/ppermute | solution.py:410
  681.7 293.6 %collective-permute-start.86 = (bf16[2,256,4,1024]{3,1,2,0:T(8,128)(2,1)}, bf16[2,256,4,1024]{3,1,2,0:T(8,128)(2,1)}, u32[]{:S(2)}, u32[]{:S(2)}) collective-permute-start(bf16[2,256,4,1024]{3,1,2,0:T(8,128)(2,1)} %slice_bitcast_fusion), channel_id=1, source_target_pairs={{0,4},{4,0},{8,12},{12,8},{1,5},{5,1},{9,13},{13,9},{2,6},{6,2},{1... | collective-permute-start | bytes 12582920 | tf_op jit(solution)/shard_map/ppermute | solution.py:410
  699.9 212.3 %collective-permute-start.73 = (bf16[2,256,4,512]{3,1,2,0:T(8,128)(2,1)}, bf16[2,256,4,512]{3,1,2,0:T(8,128)(2,1)}, u32[]{:S(2)}, u32[]{:S(2)}) collective-permute-start(bf16[2,256,4,512]{3,1,2,0:T(8,128)(2,1)} %slice_bitcast_fusion.8), channel_id=1, source_target_pairs={{0,4},{4,0},{8,12},{12,8},{1,5},{5,1},{9,13},{13,9},{2,6},{6,2},{1... | collective-permute-start | bytes 6291464 | tf_op jit(solution)/shard_map/ppermute | solution.py:410
  700.1 153.8 %collective-permute-start.45 = (bf16[512,1024]{1,0:T(8,128)(2,1)}, bf16[512,1024]{1,0:T(8,128)(2,1)}, u32[]{:S(2)}, u32[]{:S(2)}) collective-permute-start(bf16[512,1024]{1,0:T(8,128)(2,1)} %get-tuple-element.79), channel_id=1, source_target_pairs={{0,16},{16,0},{1,17},{17,1},{2,18},{18,2},{3,19},{19,3},{4,20},{20... | collective-permute-start | bytes 3145736 | tf_op jit(solution)/shard_map/ppermute | solution.py:410
  702.7 151.7 %collective-permute-start.44 = (bf16[512,1024]{1,0:T(8,128)(2,1)}, bf16[512,1024]{1,0:T(8,128)(2,1)}, u32[]{:S(2)}, u32[]{:S(2)}) collective-permute-start(bf16[512,1024]{1,0:T(8,128)(2,1)} %get-tuple-element.78), channel_id=1, source_target_pairs={{0,16},{16,0},{1,17},{17,1},{2,18},{18,2},{3,19},{19,3},{4,20},{20... | collective-permute-start | bytes 3145736 | tf_op jit(solution)/shard_map/ppermute | solution.py:410
  792.2 66.6 %collective-permute-start.62 = (f32[2,8704]{1,0:T(2,128)S(1)}, f32[2,8704]{1,0:T(2,128)S(1)}, u32[]{:S(2)}, u32[]{:S(2)}) collective-permute-start(f32[2,8704]{1,0:T(2,128)S(1)} %pad_maximum_fusion.37), channel_id=1, source_target_pairs={{0,4},{4,0},{8,12},{12,8},{1,5},{5,1},{9,13},{13,9},{2,6},{6,2},{1... | collective-permute-start | bytes 208904 | tf_op jit(solution)/shard_map/ppermute | solution.py:410
  853.9 126.6 %collective-permute-start.80 = (bf16[2,256,4,1024]{3,1,2,0:T(8,128)(2,1)}, bf16[2,256,4,1024]{3,1,2,0:T(8,128)(2,1)}, u32[]{:S(2)}, u32[]{:S(2)}) collective-permute-start(bf16[2,256,4,1024]{3,1,2,0:T(8,128)(2,1)} %slice_bitcast_fusion.2), channel_id=1, source_target_pairs={{0,4},{4,0},{8,12},{12,8},{1,5},{5,1},{9,13},{13,9},{2,6},{6,2},{1... | collective-permute-start | bytes 12582920 | tf_op jit(solution)/shard_map/ppermute | solution.py:410
  854.4 29.5 %collective-permute-start.56 = (bf16[512,1024]{1,0:T(8,128)(2,1)}, bf16[512,1024]{1,0:T(8,128)(2,1)}, u32[]{:S(2)}, u32[]{:S(2)}) collective-permute-start(bf16[512,1024]{1,0:T(8,128)(2,1)} %get-tuple-element.98), channel_id=1, source_target_pairs={{0,16},{16,0},{1,17},{17,1},{2,18},{18,2},{3,19},{19,3},{4,20},{20... | collective-permute-start | bytes 3145736 | tf_op jit(solution)/shard_map/ppermute | solution.py:410
  880.6 24.7 %collective-permute-start.57 = (bf16[512,1024]{1,0:T(8,128)(2,1)}, bf16[512,1024]{1,0:T(8,128)(2,1)}, u32[]{:S(2)}, u32[]{:S(2)}) collective-permute-start(bf16[512,1024]{1,0:T(8,128)(2,1)} %get-tuple-element.99), channel_id=1, source_target_pairs={{0,16},{16,0},{1,17},{17,1},{2,18},{18,2},{3,19},{19,3},{4,20},{20... | collective-permute-start | bytes 3145736 | tf_op jit(solution)/shard_map/ppermute | solution.py:410
  883.9 46.9 %collective-permute-start.67 = (bf16[2,256,4,512]{3,1,2,0:T(8,128)(2,1)}, bf16[2,256,4,512]{3,1,2,0:T(8,128)(2,1)S(1)}, u32[]{:S(2)}, u32[]{:S(2)}) collective-permute-start(bf16[2,256,4,512]{3,1,2,0:T(8,128)(2,1)} %slice_bitcast_fusion.10), channel_id=1, source_target_pairs={{0,4},{4,0},{8,12},{12,8},{1,5},{5,1},{9,13},{13,9},{2,6},{6,2},{1... | collective-permute-start | bytes 6291464 | tf_op jit(solution)/shard_map/ppermute | solution.py:410
  931.5 23.5 %collective-permute-start.68 = (bf16[1,256,512]{2,1,0:T(8,128)(2,1)S(1)}, bf16[1,256,512]{2,1,0:T(8,128)(2,1)S(1)}, u32[]{:S(2)}, u32[]{:S(2)}) collective-permute-start(bf16[1,256,512]{2,1,0:T(8,128)(2,1)S(1)} %get-tuple-element.178), channel_id=1, source_target_pairs={{0,1},{1,2},{2,3},{3,0},{4,5},{5,6},{6,7},{7,4},{8,9},{9,10},{10,1... | collective-permute-start | bytes 786440 | tf_op jit(solution)/shard_map/ppermute | solution.py:405
  934.0 41.1 %collective-permute-start.70 = (bf16[1,256,512]{2,1,0:T(8,128)(2,1)S(1)}, bf16[1,256,512]{2,1,0:T(8,128)(2,1)S(1)}, u32[]{:S(2)}, u32[]{:S(2)}) collective-permute-start(bf16[1,256,512]{2,1,0:T(8,128)(2,1)S(1)} %get-tuple-element.179), channel_id=1, source_target_pairs={{0,3},{1,0},{2,1},{3,2},{4,7},{5,4},{6,5},{7,6},{8,11},{9,8},{10,9... | collective-permute-start | bytes 786440 | tf_op jit(solution)/shard_map/ppermute | solution.py:405
  949.5 37.2 %collective-permute-start.59 = (bf16[384,1024]{1,0:T(8,128)(2,1)}, bf16[384,1024]{1,0:T(8,128)(2,1)}, u32[]{:S(2)}, u32[]{:S(2)}) collective-permute-start(bf16[384,1024]{1,0:T(8,128)(2,1)} %pad_maximum_fusion.25), channel_id=1, source_target_pairs={{0,3},{1,0},{2,1},{3,2},{4,7},{5,4},{6,5},{7,6},{8,11},{9,8},{10,9... | collective-permute-start | bytes 2359304 | tf_op jit(solution)/shard_map/ppermute | solution.py:405
  955.0 34.7 %collective-permute-start.75 = (bf16[2,256,512]{2,1,0:T(8,128)(2,1)S(1)}, bf16[2,256,512]{2,1,0:T(8,128)(2,1)}, u32[]{:S(2)}, u32[]{:S(2)}) collective-permute-start(bf16[2,256,512]{2,1,0:T(8,128)(2,1)S(1)} %pad_maximum_fusion.30), channel_id=1, source_target_pairs={{0,1},{1,2},{2,3},{3,0},{4,5},{5,6},{6,7},{7,4},{8,9},{9,10},{10,1... | collective-permute-start | bytes 1572872 | tf_op jit(solution)/shard_map/ppermute | solution.py:405
  975.1 31.4 %collective-permute-start.77 = (bf16[2,256,512]{2,1,0:T(8,128)(2,1)}, bf16[2,256,512]{2,1,0:T(8,128)(2,1)}, u32[]{:S(2)}, u32[]{:S(2)}) collective-permute-start(bf16[2,256,512]{2,1,0:T(8,128)(2,1)} %pad_maximum_fusion.31), channel_id=1, source_target_pairs={{0,3},{1,0},{2,1},{3,2},{4,7},{5,4},{6,5},{7,6},{8,11},{9,8},{10,9... | collective-permute-start | bytes 1572872 | tf_op jit(solution)/shard_map/ppermute | solution.py:405
  979.9 60.3 %collective-permute-start.87 = (bf16[256,4,1024]{2,0,1:T(8,128)(2,1)S(1)}, bf16[256,4,1024]{2,0,1:T(8,128)(2,1)}, u32[]{:S(2)}, u32[]{:S(2)}) collective-permute-start(bf16[256,4,1024]{2,0,1:T(8,128)(2,1)S(1)} %slice_bitcast_fusion.4), channel_id=1, source_target_pairs={{0,8},{4,12},{8,0},{12,4},{1,9},{5,13},{9,1},{13,5},{2,10},{6,14},... | collective-permute-start | bytes 6291464 | tf_op jit(solution)/shard_map/ppermute | solution.py:410
  985.0 73.2 %collective-permute-start.81 = (bf16[256,4,1024]{2,0,1:T(8,128)(2,1)S(1)}, bf16[256,4,1024]{2,0,1:T(8,128)(2,1)S(1)}, u32[]{:S(2)}, u32[]{:S(2)}) collective-permute-start(bf16[256,4,1024]{2,0,1:T(8,128)(2,1)S(1)} %slice_bitcast_fusion.6), channel_id=1, source_target_pairs={{0,8},{4,12},{8,0},{12,4},{1,9},{5,13},{9,1},{13,5},{2,10},{6,14},... | collective-permute-start | bytes 6291464 | tf_op jit(solution)/shard_map/ppermute | solution.py:410
  986.7 24.6 %collective-permute-start.69 = (bf16[2,256,512]{2,1,0:T(8,128)(2,1)S(1)}, bf16[2,256,512]{2,1,0:T(8,128)(2,1)S(1)}, u32[]{:S(2)}, u32[]{:S(2)}) collective-permute-start(bf16[2,256,512]{2,1,0:T(8,128)(2,1)S(1)} %pad_maximum_fusion.28), channel_id=1, source_target_pairs={{0,1},{1,2},{2,3},{3,0},{4,5},{5,6},{6,7},{7,4},{8,9},{9,10},{10,1... | collective-permute-start | bytes 1572872 | tf_op jit(solution)/shard_map/ppermute | solution.py:405
  989.8 48.7 %collective-permute-start.71 = (bf16[2,256,512]{2,1,0:T(8,128)(2,1)S(1)}, bf16[2,256,512]{2,1,0:T(8,128)(2,1)S(1)}, u32[]{:S(2)}, u32[]{:S(2)}) collective-permute-start(bf16[2,256,512]{2,1,0:T(8,128)(2,1)S(1)} %pad_maximum_fusion.29), channel_id=1, source_target_pairs={{0,3},{1,0},{2,1},{3,2},{4,7},{5,4},{6,5},{7,6},{8,11},{9,8},{10,9... | collective-permute-start | bytes 1572872 | tf_op jit(solution)/shard_map/ppermute | solution.py:405
  1006.5 79.6 %collective-permute-start.47 = (bf16[384,1024]{1,0:T(8,128)(2,1)S(1)}, bf16[384,1024]{1,0:T(8,128)(2,1)S(1)}, u32[]{:S(2)}, u32[]{:S(2)}) collective-permute-start(bf16[384,1024]{1,0:T(8,128)(2,1)S(1)} %copy-done.76), channel_id=1, source_target_pairs={{0,3},{1,0},{2,1},{3,2},{4,7},{5,4},{6,5},{7,6},{8,11},{9,8},{10,9... | collective-permute-start | bytes 2359304 | tf_op jit(solution)/shard_map/ppermute | solution.py:405
  1011.3 74.8 %collective-permute-start.46 = (bf16[384,1024]{1,0:T(8,128)(2,1)S(1)}, bf16[384,1024]{1,0:T(8,128)(2,1)S(1)}, u32[]{:S(2)}, u32[]{:S(2)}) collective-permute-start(bf16[384,1024]{1,0:T(8,128)(2,1)S(1)} %copy-done.75), channel_id=1, source_target_pairs={{0,1},{1,2},{2,3},{3,0},{4,5},{5,6},{6,7},{7,4},{8,9},{9,10},{10,1... | collective-permute-start | bytes 2359304 | tf_op jit(solution)/shard_map/ppermute | solution.py:405
  1038.5 49.7 %collective-permute-start.78 = (bf16[256,512]{1,0:T(8,128)(2,1)S(1)}, bf16[256,512]{1,0:T(8,128)(2,1)S(1)}, u32[]{:S(2)}, u32[]{:S(2)}) collective-permute-start(bf16[256,512]{1,0:T(8,128)(2,1)S(1)} %slice_bitcast_fusion.36), channel_id=1, source_target_pairs={{0,8},{4,12},{8,0},{12,4},{1,9},{5,13},{9,1},{13,5},{2,10},{6,14},... | collective-permute-start | bytes 786440 | tf_op jit(solution)/shard_map/ppermute | solution.py:410
  1086.0 26.2 %collective-permute-start.91 = (bf16[256,1024]{1,0:T(8,128)(2,1)S(1)}, bf16[256,1024]{1,0:T(8,128)(2,1)S(1)}, u32[]{:S(2)}, u32[]{:S(2)}) collective-permute-start(bf16[256,1024]{1,0:T(8,128)(2,1)S(1)} %pad_maximum_fusion.35), channel_id=1, source_target_pairs={{0,3},{1,0},{2,1},{3,2},{4,7},{5,4},{6,5},{7,6},{8,11},{9,8},{10,9... | collective-permute-start | bytes 1572872 | tf_op jit(solution)/shard_map/ppermute | solution.py:405
  1086.1 34.5 %collective-permute-start.83 = (bf16[256,1024]{1,0:T(8,128)(2,1)S(1)}, bf16[256,1024]{1,0:T(8,128)(2,1)S(1)}, u32[]{:S(2)}, u32[]{:S(2)}) collective-permute-start(bf16[256,1024]{1,0:T(8,128)(2,1)S(1)} %pad_maximum_fusion.32), channel_id=1, source_target_pairs={{0,1},{1,2},{2,3},{3,0},{4,5},{5,6},{6,7},{7,4},{8,9},{9,10},{10,1... | collective-permute-start | bytes 1572872 | tf_op jit(solution)/shard_map/ppermute | solution.py:405
  1088.1 45.2 %collective-permute-start.85 = (bf16[256,1024]{1,0:T(8,128)(2,1)S(1)}, bf16[256,1024]{1,0:T(8,128)(2,1)S(1)}, u32[]{:S(2)}, u32[]{:S(2)}) collective-permute-start(bf16[256,1024]{1,0:T(8,128)(2,1)S(1)} %pad_maximum_fusion.33), channel_id=1, source_target_pairs={{0,3},{1,0},{2,1},{3,2},{4,7},{5,4},{6,5},{7,6},{8,11},{9,8},{10,9... | collective-permute-start | bytes 1572872 | tf_op jit(solution)/shard_map/ppermute | solution.py:405
  1092.1 42.7 %collective-permute-start.61 = (bf16[128,1024]{1,0:T(8,128)(2,1)S(1)}, bf16[128,1024]{1,0:T(8,128)(2,1)S(1)}, u32[]{:S(2)}, u32[]{:S(2)}) collective-permute-start(bf16[128,1024]{1,0:T(8,128)(2,1)S(1)} %slice.804), channel_id=1, source_target_pairs={{0,3},{1,0},{2,1},{3,2},{4,7},{5,4},{6,5},{7,6},{8,11},{9,8},{10,9... | collective-permute-start | bytes 786440 | tf_op jit(solution)/shard_map/ppermute | solution.py:405
  1098.1 40.8 %collective-permute-start.60 = (bf16[128,1024]{1,0:T(8,128)(2,1)S(1)}, bf16[128,1024]{1,0:T(8,128)(2,1)S(1)}, u32[]{:S(2)}, u32[]{:S(2)}) collective-permute-start(bf16[128,1024]{1,0:T(8,128)(2,1)S(1)} %slice.803), channel_id=1, source_target_pairs={{0,1},{1,2},{2,3},{3,0},{4,5},{5,6},{6,7},{7,4},{8,9},{9,10},{10,1... | collective-permute-start | bytes 786440 | tf_op jit(solution)/shard_map/ppermute | solution.py:405
  1112.2 28.6 %collective-permute-start.49 = (bf16[128,1024]{1,0:T(8,128)(2,1)S(1)}, bf16[128,1024]{1,0:T(8,128)(2,1)S(1)}, u32[]{:S(2)}, u32[]{:S(2)}) collective-permute-start(bf16[128,1024]{1,0:T(8,128)(2,1)S(1)} %slice.794), channel_id=1, source_target_pairs={{0,3},{1,0},{2,1},{3,2},{4,7},{5,4},{6,5},{7,6},{8,11},{9,8},{10,9... | collective-permute-start | bytes 786440 | tf_op jit(solution)/shard_map/ppermute | solution.py:405
  1120.6 23.9 %collective-permute-start.48 = (bf16[128,1024]{1,0:T(8,128)(2,1)S(1)}, bf16[128,1024]{1,0:T(8,128)(2,1)S(1)}, u32[]{:S(2)}, u32[]{:S(2)}) collective-permute-start(bf16[128,1024]{1,0:T(8,128)(2,1)S(1)} %slice.793), channel_id=1, source_target_pairs={{0,1},{1,2},{2,3},{3,0},{4,5},{5,6},{6,7},{7,4},{8,9},{9,10},{10,1... | collective-permute-start | bytes 786440 | tf_op jit(solution)/shard_map/ppermute | solution.py:405
  (143 other events, 1314.4 us)

commit v2 on v1

--- a/solution.py
+++ b/solution.py
@@ -419,10 +419,16 @@
 
 
 def relative(values, own):
-    parts = values.reshape(values.shape[:-1] + (4, values.shape[-1] // 4))
-    axis = parts.ndim - 2
-    picked = [pick(parts, jnp.bitwise_xor(own, k), axis) for k in range(4)]
+    size = values.shape[-1] // 4
+    picked = [
+        lax.dynamic_slice_in_dim(values, jnp.bitwise_xor(own, k) * size, size, values.ndim - 1)
+        for k in range(4)
+    ]
     return jnp.concatenate(picked, axis=-1)
+
+
+def after(values, *earlier):
+    return lax.optimization_barrier((values, earlier))[0]
 
 
 def exchange(blocks, own):
@@ -442,32 +448,27 @@
     return place(result, jnp.concatenate([first, second], axis=0), (own + 2) % 4)
 
 
+def with_other_core(pieces):
+    return tuple(pieces) + tuple(swap(piece, "dp", 1) for piece in pieces)
+
+
 def gather_across_first(shard):
     pair = jnp.stack([shard, swap(shard, "dp", 2)])
     left = ring(pair, "tensor", 1)
     right = ring(pair, "tensor", -1)
     far = jnp.stack([ring(left[0], "tensor", 1), ring(right[1], "tensor", -1)])
-    mine = jnp.stack([pair, left, right, far])
-    return jnp.stack([mine, swap(mine, "dp", 1)], axis=2)
+    return with_other_core((pair, left, right, far))
 
 
 def gather_along_first(shard):
     half = shard.shape[0] // 2
     left = ring(shard, "tensor", 1)
     right = ring(shard, "tensor", -1)
-    own_far = swap(shard, "dp", 2)
     far = jnp.concatenate(
         [ring(left[:half], "tensor", 1), ring(right[half:], "tensor", -1)], axis=0
     )
-    mine = jnp.stack(
-        [
-            jnp.stack([shard, own_far]),
-            jnp.stack([left, swap(left, "dp", 2)]),
-            jnp.stack([right, swap(right, "dp", 2)]),
-            jnp.stack([far, swap(far, "dp", 2)]),
-        ]
-    )
-    return jnp.stack([mine, swap(mine, "dp", 1)], axis=2)
+    pieces = [jnp.stack([part, swap(part, "dp", 2)]) for part in (shard, left, right, far)]
+    return with_other_core(pieces)
 
 
 def add_wide(left, right):
@@ -487,20 +488,14 @@
     return total.astype(jnp.bfloat16)
 
 
-def reduce_core(grads):
-    return add_wide(grads[:, 0], swap(grads[:, 1], "dp", 1))
-
-
-def reduce_across_last(grads):
-    shared = reduce_core(grads)
-    own = reduce_ring([shared[:, :, k] for k in range(4)])
+def reduce_across_last(shared):
+    own = reduce_ring([shared[k] for k in range(4)])
     return add_wide(own[0], swap(own[1], "dp", 2))
 
 
-def reduce_along_last(grads):
-    shared = reduce_core(grads)
-    own = add_wide(shared[0], swap(shared[1], "dp", 2))
-    return reduce_ring([own[:, k] for k in range(4)])
+def reduce_along_last(shared):
+    own = add_wide(shared[:, 0], swap(shared[:, 1], "dp", 2))
+    return reduce_ring([own[k] for k in range(4)])
 
 
 def normalised(x):
@@ -536,23 +531,50 @@
     )
 
 
-def call(body, name, grid, ins, outs, scratch=(), limit=VMEM_LIMIT):
+def call(body, name, grid, ins, outs, scratch=(), filled=()):
+    count = len(ins)
+
+    def run(*refs):
+        body(*refs[:count], *refs[count + len(filled) :])
+
     return pl.pallas_call(
-        body,
+        run,
         name=name,
         grid=grid,
-        in_specs=[pl.BlockSpec(block, index) for _, block, index in ins],
+        in_specs=[pl.BlockSpec(block, index) for _, block, index in ins]
+        + [pl.BlockSpec(memory_space=pl.ANY)] * len(filled),
         out_specs=[pl.BlockSpec(block, index) for _, _, block, index in outs],
         out_shape=[jax.ShapeDtypeStruct(shape, kind) for shape, kind, _, _ in outs],
         scratch_shapes=list(scratch),
+        input_output_aliases={count + i: i for i in range(len(filled))},
         compiler_params=pltpu.CompilerParams(
-            vmem_limit_bytes=limit, dimension_semantics=("arbitrary",) * len(grid)
+            vmem_limit_bytes=VMEM_LIMIT, dimension_semantics=("arbitrary",) * len(grid)
         ),
-    )(*[array for array, _, _ in ins])
+    )(*[array for array, _, _ in ins], *filled)
 
 
 def whole(array):
     return (array, array.shape, lambda *_: (0,) * array.ndim)
+
+
+def matrix(pieces, size, block):
+    shape = (2, pieces[0].shape[1], size)
+    return [(piece, shape, lambda *_: (0, 0, block)) for piece in pieces]
+
+
+def room(pieces, size):
+    return pltpu.VMEM((4 * pieces[0].shape[1], 4 * size), jnp.bfloat16)
+
+
+def assemble(refs, target):
+    _, rows, size = refs[0].shape
+    for core in range(2):
+        for offset in range(4):
+            for side in range(2):
+                at = (2 * side + core) * rows
+                target[at : at + rows, offset * size : (offset + 1) * size] = refs[
+                    core * 4 + offset
+                ][side]
 
 
 def rows_of(array, first=0, block=ROW_BLOCK):
@@ -560,7 +582,13 @@
     return (array, (block, array.shape[1]), lambda i: (i + base, 0))
 
 
-def qkv_body(x, vecs, shift, cos, low, high, w, ln_a, ln_m, qkv):
+def qkv_body(x, vecs, shift, cos, low, high, *rest):
+    ln_a, ln_m, qkv, w = rest[8:]
+
+    @pl.when(pl.program_id(0) == 0)
+    def _():
+        assemble(rest[:8], w)
+
     hat, _ = normalised(x[...].astype(jnp.float32))
     attn = (hat * vecs[0:1, :] + vecs[1:2, :]).astype(jnp.bfloat16)
     ln_a[...] = attn
@@ -575,23 +603,28 @@
             qkv[:, at : at + 128] = piece.astype(jnp.bfloat16)
 
 
-def run_qkv(x, vecs, shift, tables, w, first):
-    rows, width = x.shape
-    cols = w.shape[1]
+def run_qkv(source, vecs, shift, tables, pieces, at, rows, filled):
+    x, first = source
+    width = x.shape[1]
+    length = tables[0].shape[0]
+    cols = shift.shape[1]
     bf = jnp.bfloat16
-    own = lambda i: (i, 0)
+    base = at // ROW_BLOCK
+    own = lambda i: (i + base, 0)
     return call(
         qkv_body,
         "norm_qkv",
         (rows // ROW_BLOCK,),
-        [rows_of(x), whole(vecs), whole(shift)]
-        + [rows_of(t, first) for t in tables]
-        + [whole(w)],
+        [rows_of(x, first), whole(vecs), whole(shift)]
+        + [rows_of(t, at) for t in tables]
+        + matrix(pieces, cols // 4, 0),
         [
-            ((rows, width), bf, (ROW_BLOCK, width), own),
-            ((rows, width), bf, (ROW_BLOCK, width), own),
-            ((rows, cols), bf, (ROW_BLOCK, cols), own),
+            ((length, width), bf, (ROW_BLOCK, width), own),
+            ((length, width), bf, (ROW_BLOCK, width), own),
+            ((length, cols), bf, (ROW_BLOCK, cols), own),
         ],
+        [room(pieces, cols // 4)],
+        filled,
     )
 
 
@@ -668,7 +701,15 @@
     return x * top / bottom
 
 
-def mlp_body(ctx, ln_m, shift, w_out, w_up, w_down, act, slope, part):
+def mlp_body(ctx, ln_m, shift, *rest):
+    act, slope, part, w_out, w_up, w_down = rest[24:]
+
+    @pl.when(pl.program_id(0) == 0)
+    def _():
+        assemble(rest[:8], w_out)
+        assemble(rest[8:16], w_up)
+        assemble(rest[16:24], w_down)
+
     up = nn_dot(ln_m[...], w_up[...]) + shift[...]
     half_erf = 0.5 * erf(up * (2.0**-0.5)) + 0.5
     bell = jnp.exp(up * up * -0.5) * ((2.0 * math.pi) ** -0.5)
@@ -678,63 +719,71 @@
     part[...] = (nt_dot(ctx[...], w_out[...]) + nt_dot(active, w_down[...])).astype(jnp.bfloat16)
 
 
-def run_mlp(ctx, ln_m, shift, w_out, w_up, w_down, first, rows):
-    width = ln_m.shape[1]
-    cols = w_up.shape[1]
+def run_mlp(ctx, ln_m, shift, narrow, broad, at, rows, filled):
+    length, width = ln_m.shape
+    cols, heads = shift.shape[1], ctx.shape[1]
     bf = jnp.bfloat16
-    own = lambda i: (i, 0)
+    base = at // ROW_BLOCK
+    own = lambda i: (i + base, 0)
     return call(
         mlp_body,
         "mlp_out",
         (rows // ROW_BLOCK,),
+        [rows_of(ctx, at), rows_of(ln_m, at), whole(shift)]
+        + matrix(narrow, heads // 4, 3)
+        + matrix(broad, cols // 4, 0)
+        + matrix(broad, cols // 4, 1),
         [
-            rows_of(ctx, first),
-            rows_of(ln_m, first),
-            whole(shift),
-            whole(w_out),
-            whole(w_up),
-            whole(w_down),
+            ((length, cols), bf, (ROW_BLOCK, cols), own),
+            ((length, cols), bf, (ROW_BLOCK, cols), own),
+            ((rows, width), bf, (ROW_BLOCK, width), lambda i: (i, 0)),
         ],
-        [
-            ((rows, cols), bf, (ROW_BLOCK, cols), own),
-            ((rows, cols), bf, (ROW_BLOCK, cols), own),
-            ((rows, width), bf, (ROW_BLOCK, width), own),
-        ],
-    )
-
-
-def mlp_back_body(g, slope, w_out, w_down, d_up, d_ctx, sum_up, sum_g):
+        [room(narrow, heads // 4), room(broad, cols // 4), room(broad, cols // 4)],
+        filled,
+    )
+
+
+def mlp_back_body(g, slope, *rest):
+    d_up, d_ctx, sum_up, sum_g, w_out, w_down = rest[16:]
+
+    @pl.when(pl.program_id(0) == 0)
+    def _():
+        assemble(rest[:8], w_out)
+        assemble(rest[8:16], w_down)
+        sum_up[...] = jnp.zeros_like(sum_up)
+        sum_g[...] = jnp.zeros_like(sum_g)
+
     grad = g[...]
     du = (nn_dot(grad, w_down[...]) * slope[...].astype(jnp.float32)).astype(jnp.bfloat16)
     d_up[...] = du
     d_ctx[...] = nn_dot(grad, w_out[...]).astype(jnp.bfloat16)
-
-    @pl.when(pl.program_id(0) == 0)
-    def _():
-        sum_up[...] = jnp.zeros_like(sum_up)
-        sum_g[...] = jnp.zeros_like(sum_g)
-
     sum_up[...] += jnp.sum(du.astype(jnp.float32), axis=0, keepdims=True)
     sum_g[...] += jnp.sum(grad.astype(jnp.float32), axis=0, keepdims=True)
 
 
-def run_mlp_back(g, slope, w_out, w_down):
-    rows, width = g.shape
-    cols, heads = w_down.shape[1], w_out.shape[1]
+def run_mlp_back(source, slope, narrow, broad, at, rows, heads, filled):
+    g, first = source
+    width = g.shape[1]
+    length, cols = slope.shape
     bf = jnp.bfloat16
-    own = lambda i: (i, 0)
+    base = at // ROW_BLOCK
+    own = lambda i: (i + base, 0)
     fixed = lambda i: (0, 0)
     return call(
         mlp_back_body,
         "mlp_back",
         (rows // ROW_BLOCK,),
-        [rows_of(g), rows_of(slope), whole(w_out), whole(w_down)],
+        [rows_of(g, first), rows_of(slope, at)]
+        + matrix(narrow, heads // 4, 3)
+        + matrix(broad, cols // 4, 1),
         [
-            ((rows, cols), bf, (ROW_BLOCK, cols), own),
-            ((rows, heads), bf, (ROW_BLOCK, heads), own),
+            ((length, cols), bf, (ROW_BLOCK, cols), own),
+            ((length, heads), bf, (ROW_BLOCK, heads), own),
             ((1, cols), jnp.float32, (1, cols), fixed),
             ((1, width), jnp.float32, (1, width), fixed),
         ],
+        [room(narrow, heads // 4), room(broad, cols // 4)],
+        filled,
     )
 
 
@@ -796,15 +845,18 @@
     )
 
 
-def norm_back_body(x, d_qkv, d_up, vecs, w_qkv, w_up, part, sums):
+def norm_back_body(x, d_qkv, d_up, vecs, *rest):
+    part, sums, w_qkv, w_up = rest[16:]
+
+    @pl.when(pl.program_id(0) == 0)
+    def _():
+        assemble(rest[:8], w_qkv)
+        assemble(rest[8:16], w_up)
+        sums[...] = jnp.zeros_like(sums)
+
     hat, inverse = normalised(x[...].astype(jnp.float32))
     d_attn = nt_dot(d_qkv[...], w_qkv[...])
     d_mlp = nt_dot(d_up[...], w_up[...])
-
-    @pl.when(pl.program_id(0) == 0)
-    def _():
-        sums[...] = jnp.zeros_like(sums)
-
     for row, term in enumerate((d_attn * hat, d_mlp * hat, d_attn, d_mlp)):
         sums[row : row + 1, :] += jnp.sum(term, axis=0, keepdims=True)
     d_hat = d_attn * vecs[0:1, :] + d_mlp * vecs[2:3, :]
@@ -813,24 +865,64 @@
     part[...] = (inverse * (d_hat - level - hat * along)).astype(jnp.bfloat16)
 
 
-def run_norm_back(x, d_qkv, d_up, vecs, w_qkv, w_up, first, rows):
+def run_norm_back(source, d_qkv, d_up, vecs, narrow, broad, at, rows):
+    x, first = source
     width = x.shape[1]
+    n_qkv, n_up = d_qkv.shape[1] // 4, d_up.shape[1] // 4
     return call(
         norm_back_body,
         "norm_back",
         (rows // ROW_BLOCK,),
-        [
-            rows_of(x, first),
-            rows_of(d_qkv, first),
-            rows_of(d_up, first),
-            whole(vecs),
-            whole(w_qkv),
-            whole(w_up),
-        ],
+        [rows_of(x, first), rows_of(d_qkv, at), rows_of(d_up, at), whole(vecs)]
+        + matrix(narrow, n_qkv, 0)
+        + matrix(broad, n_up, 0),
         [
             ((rows, width), jnp.bfloat16, (ROW_BLOCK, width), lambda i: (i, 0)),
             ((8, width), jnp.float32, (8, width), lambda i: (0, 0)),
         ],
+        [room(narrow, n_qkv), room(broad, n_up)],
+    )
+
+
+def weight_grad_body(cuts, *refs):
+    a_refs, b_refs, rest = refs[: sum(cuts)], refs[sum(cuts) :], refs[sum(cuts) + 2 :]
+    keep, send, turned_one, turned_two = rest
+    groups = (a_refs[: cuts[0]], a_refs[cuts[0] :])
+
+    @pl.when(pl.program_id(0) == 0)
+    def _():
+        for group, turned in zip(groups, (turned_one, turned_two)):
+            at = 0
+            for ref in group:
+                turned[:, at : at + ref.shape[0]] = ref[...].T
+                at += ref.shape[0]
+
+    at = 0
+    rows = keep.shape[2]
+    for turned, right in zip((turned_one, turned_two), b_refs[:2]):
+        size = right.shape[1]
+        grad = nn_dot(turned[...], right[...]).astype(jnp.bfloat16)
+        for side in range(2):
+            first = 2 * side * rows
+            keep[0, side, :, at : at + size] = grad[first : first + rows]
+            send[0, side, :, at : at + size] = grad[first + rows : first + 2 * rows]
+        at += size
+
+
+def run_weight_grad(lefts, rights):
+    length, width = rights[0].shape[0], lefts[0][0].shape[1]
+    sizes = [right.shape[1] // 4 for right in rights]
+    shape = (4, 2, width // 4, sum(sizes))
+    out = (shape, jnp.bfloat16, (1,) + shape[1:], lambda i: (i, 0, 0, 0))
+    turned = pltpu.VMEM((width, length), jnp.bfloat16)
+    return call(
+        partial(weight_grad_body, tuple(len(group) for group in lefts)),
+        "weight_grad",
+        (4,),
+        [whole(left) for group in lefts for left in group]
+        + [(r, (length, n), lambda i: (0, i)) for r, n in zip(rights, sizes)],
+        [out, out],
+        [turned, turned],
     )
 
 
@@ -894,19 +986,9 @@
     acts = relative(acts, across)
     broad_shards = both_layers(broad)
 
-    def join(pieces, start, size):
-        part = pieces[..., start : start + size]
-        return part.transpose(1, 2, 3, 0, 4).reshape(width, -1)
-
-    mats = []
-    for layer in (0, 1):
-        pieces = gather_across_first(narrow_shards[layer])
-        mat_qkv, mat_out = join(pieces, 0, n_qkv), join(pieces, n_qkv, n_out)
-        pieces = gather_along_first(broad_shards[layer])
-        mats.append((mat_qkv, mat_out, join(pieces, 0, n_up), join(pieces, n_up, n_up)))
-        if layer == 0:
-            grads_in = exchange(cotangent[:, :, 0, :], along).reshape(length, width)
-            grads_in = relative(grads_in, across)
+    mats = [(gather_across_first(narrow_shards[0]), gather_along_first(broad_shards[0]))]
+    later = after((narrow_shards[1], broad_shards[1]), mats[0][1][:4])
+    mats.append((gather_across_first(later[0]), gather_along_first(later[1])))
 
     share = norm_gains.shape[2]
     vec_part = small[..., : 6 * share].reshape(4, 4, 2, 6, share)
@@ -933,79 +1015,93 @@
     chunk = length // CHUNKS
     starts = [i * chunk for i in range(CHUNKS)]
 
+    sources = [(acts, a) for a in starts]
     inputs = [acts[a : a + chunk] for a in starts]
     kept = []
+    grads_in = None
     for layer in (0, 1):
-        mat_qkv, mat_out, mat_up, mat_down = mats[layer]
+        narrow, broad = mats[layer]
         full = vecs_full[layer]
         vecs = jnp.concatenate(
             [full[0:1], full[2:3], full[1:2], full[3:4], zero_rows], axis=0
         )
-        pieces = [
-            run_qkv(inputs[i], vecs, qkv_bias[layer], tables, mat_qkv, starts[i])
-            for i in range(CHUNKS)
-        ]
-        ln_a, ln_m, qkv = (jnp.concatenate(p, axis=0) for p in zip(*pieces))
+        first = ()
+        for i in range(CHUNKS):
+            first = run_qkv(
+                sources[i], vecs, qkv_bias[layer], tables, narrow, starts[i], chunk, first
+            )
+        ln_a, ln_m, qkv = first
+        if layer == 1:
+            qkv = after(qkv, grads_in)
         ctx, lse = run_attend(qkv)
-        acts_list, slopes, outs = [], [], []
+        if layer == 0:
+            given = after(cotangent[:, :, 0, :], ctx, mats[1][1][:4])
+            grads_in = exchange(given, along).reshape(length, width)
+            grads_in = relative(grads_in, across)
+        outs, first = [], ()
         for i in range(CHUNKS):
-            act, slope, part = run_mlp(
-                ctx, ln_m, up_bias[layer], mat_out, mat_up, mat_down, starts[i], chunk
+            *first, part = run_mlp(
+                ctx, ln_m, up_bias[layer], narrow, broad, starts[i], chunk, first
             )
             got = swap(part, "section", 1)
             total = part.astype(jnp.float32) + got.astype(jnp.float32)
             total = inputs[i].astype(jnp.float32) + total + (full[4] + full[5])
             outs.append(total.astype(bf))
-            acts_list.append(act)
-            slopes.append(slope)
-        kept.append(
-            (inputs, vecs, ln_a, ln_m, qkv, ctx, lse, jnp.concatenate(acts_list), slopes, outs)
-        )
+        kept.append((sources, vecs, ln_a, ln_m, qkv, ctx, lse, *first, outs))
         inputs = outs
-
+        sources = [(out, 0) for out in outs]
+
+    def deliver(values):
+        return exchange(relative(values, across).reshape(4, positions, width), along)
+
+    acts_local = deliver(
+        jnp.where(first_section, jnp.concatenate(kept[0][9]), jnp.concatenate(kept[1][9]))
+    )
+
+    sources = [(grads_in, a) for a in starts]
     upstream = [grads_in[a : a + chunk] for a in starts]
+    whole_up = [grads_in]
     reduced = [None, None]
     vectors = [None, None]
     layer_grads = [None, None]
     for layer in (1, 0):
-        mat_qkv, mat_out, mat_up, mat_down = mats[layer]
-        x_list, vecs, ln_a, ln_m, qkv, ctx, lse, act, slopes, _ = kept[layer]
-        pieces = [
-            run_mlp_back(upstream[i], slopes[i], mat_out, mat_down) for i in range(CHUNKS)
-        ]
-        d_up, d_ctx = (jnp.concatenate(p, axis=0) for p in list(zip(*pieces))[:2])
-        sum_up = sum(p[2] for p in pieces)
-        sum_g = sum(p[3] for p in pieces)
-        g_full = jnp.concatenate(upstream, axis=0)
+        narrow, broad = mats[layer]
+        x_list, vecs, ln_a, ln_m, qkv, ctx, lse, act, slope, _ = kept[layer]
+        first, sum_up, sum_g = (), 0.0, 0.0
+        if layer == 0:
+            sources = [(after(down, acts_local), at) for down, at in sources]
+        for i in range(CHUNKS):
+            *first, up_term, g_term = run_mlp_back(
+                sources[i], slope, narrow, broad, starts[i], chunk, ctx.shape[1], first
+            )
+            sum_up, sum_g = sum_up + up_term, sum_g + g_term
+        d_up, d_ctx = first
+        if layer == 0:
+            keep, send = run_weight_grad([[ln_m], whole_up], [d_up, act])
+            broad_sum = add_wide(keep, swap(send, "dp", 1))
+            d_ctx = after(d_ctx, keep)
         d_qkv, sum_qkv = run_attend_back(qkv, d_ctx, lse, tables)
-        x_full = jnp.concatenate(x_list, axis=0)
         downs, norm_sums = [], 0.0
         for i in range(CHUNKS):
             part, sums = run_norm_back(
-                x_full, d_qkv, d_up, vecs, mat_qkv, mat_up, starts[i], chunk
+                x_list[i], d_qkv, d_up, vecs, narrow, broad, starts[i], chunk
             )
             got = swap(part, "section", 1)
             total = part.astype(jnp.float32) + got.astype(jnp.float32)
             downs.append((upstream[i].astype(jnp.float32) + total).astype(bf))
             norm_sums = norm_sums + sums[:4]
-
-        def split(left, right):
-            grad = tn_dot(left, right).astype(bf)
-            return grad.reshape(2, 2, rows, 4, -1)
-
-        broad_grad = jnp.concatenate([split(ln_m, d_up), split(g_full, act)], axis=-1)
-        narrow_grad = jnp.concatenate([split(ln_a, d_qkv), split(g_full, ctx)], axis=-1)
-        reduced[layer] = (reduce_across_last(narrow_grad), reduce_along_last(broad_grad))
+        if layer == 1:
+            keep, send = run_weight_grad([[ln_m], whole_up], [d_up, act])
+            broad_sum = add_wide(keep, swap(send, "dp", 1))
+        keep, send = run_weight_grad([[ln_a], whole_up], [d_qkv, ctx])
+        narrow_sum = add_wide(keep, swap(send, "dp", 1))
+        reduced[layer] = (reduce_across_last(narrow_sum), reduce_along_last(broad_sum))
         vectors[layer] = (norm_sums, sum_g, sum_qkv, sum_up)
         layer_grads[layer] = jnp.concatenate(downs, axis=0)
         upstream = downs
-
-    def deliver(values):
-        return exchange(relative(values, across).reshape(4, positions, width), along)
-
-    acts_local = deliver(
-        jnp.where(first_section, jnp.concatenate(kept[0][9]), jnp.concatenate(kept[1][9]))
-    )
+        whole_up = downs
+        sources = [(down, 0) for down in downs]
+
     grad_local = deliver(jnp.where(first_section, layer_grads[0], layer_grads[1]))
 
     def whole_layer(first, second):

time: 1160 us -> 939 us (0.81)
  local copies, waits for them, and re-layouts: 261 us -> 74.3 us
  starting transfers between devices: 218 us -> 127 us
  waiting for transfers between devices: 257 us -> 335 us
  matrix products: 54.4 us -> 0 us
  Pallas kernels: 259 us -> 307 us
  other arithmetic: 92.8 us -> 73.4 us
    ppermute x51, starting transfers between devices: 186 us -> 88.2 us  [ring(): lax.ppermute(value, axis, [(i, (i + by) % length) for i in range(length)])]
    unnamed x269 -> x125, local copies, waits for them, and re-layouts: 80.3 us -> 9.89 us
    ppermute x42 -> x54, waiting for transfers between devices: 97 us -> 152 us  [swap(): return lax.ppermute(value, axis, [(i, i ^ bit) for i in range(length)])]
    dot_general x8 -> x0, matrix products: 54.4 us -> none  [tn_dot(): lax.dot_general(left, right, (((0,), (0,)), ((), ())), preferred_element_...]
    reshape x10 -> x0, local copies, waits for them, and re-layouts: 47.8 us -> none  [the longest x8 47.8 us: split(): return grad.reshape(2, 2, rows, 4, -1)]
    pallas_call x20 -> x24, Pallas kernels: 259 us -> 307 us  [call(): pl.pallas_call(run, name=name, grid=grid, in_specs=[pl.BlockSpec(block, i...]
    ppermute x51, waiting for transfers between devices: 160 us -> 183 us  [ring(): lax.ppermute(value, axis, [(i, (i + by) % length) for i in range(length)])]
    transpose x8 -> x0, local copies, waits for them, and re-layouts: 19.4 us -> none  [join(): return part.transpose(1, 2, 3, 0, 4).reshape(width, -1)]
  transfers between devices with their start and end apart: 93 -> 105, of which waited for: 51 -> 43; matrix products, arithmetic and copies ran while one was open for 30% -> 14% of each run, Pallas kernels for 12% -> 30%
where the time goes in v2:
time: 939 us; the launch traced here: 928 us
  waiting for transfers between devices  335 us (36%)
  Pallas kernels  307 us (33%)
  starting transfers between devices  127 us (14%)
  local copies, waits for them, and re-layouts  74.3 us (8%)
  other arithmetic  73.4 us (8%)
  between operations  11 us (1%)
    pallas_call x24, Pallas kernels, call(): pl.pallas_call(run, name=name, grid=grid, in_specs=[pl.BlockSpec(block, i...  307 us
    ppermute x51, waiting for transfers between devices, ring(): lax.ppermute(value, axis, [(i, (i + by) % length) for i in range(length)])  183 us
    ppermute x54, waiting for transfers between devices, swap(): return lax.ppermute(value, axis, [(i, i ^ bit) for i in range(length)])  152 us
    ppermute x51, starting transfers between devices, ring(): lax.ppermute(value, axis, [(i, (i + by) % length) for i in range(length)])  88.2 us
    ppermute x54, starting transfers between devices, swap(): return lax.ppermute(value, axis, [(i, i ^ bit) for i in range(length)])  39.1 us
  transfers between devices with their start and end apart: 105, of which 43 were waited for; matrix products, arithmetic and copies ran while one was open for 14% of the time, Pallas kernels for 30%

profile of v2, /device:TPU:0, one launch (start us, length us, event | category | flops | bytes accessed | tf_op | source)
XLA Modules:
  0.0 927.5 jit_solution(9591308972891972997)
XLA Ops:
  17.6 7.8 collective-permute-done.4
  65.4 36.9 %collective-permute-done.22 = bf16[256,1024]{1,0:T(8,128)(2,1)S(1)} collective-permute-done((bf16[256,1024]{1,0:T(8,128)(2,1)S(1)}, bf16[256,1024]{1,0:T(8,128)(2,1)S(1)}, u32[]{:S(2)}, u32[]{:S(2)}) %collective-permute-start.22) | collective-permute-done | bytes 524320 | tf_op jit(solution)/shard_map/ppermute | solution.py:405
  103.3 7.5 collective-permute-start.26
  118.0 6.9 collective-permute-done.12.refs_7_.refs_4_.refs_3_.refs_5_
  124.9 5.6 collective-permute-done.26
  131.8 12.1 %collective-permute-done.27 = bf16[128,1024]{1,0:T(8,128)(2,1)S(1)} collective-permute-done((bf16[128,1024]{1,0:T(8,128)(2,1)S(1)}, bf16[128,1024]{1,0:T(8,128)(2,1)S(1)}, u32[]{:S(2)}, u32[]{:S(2)}) %collective-permute-start.27) | collective-permute-done | bytes 262176 | tf_op jit(solution)/shard_map/ppermute | solution.py:405
  153.2 5.6 collective-permute-done.25
  160.8 7.0 collective-permute-done.28
  178.2 8.5 collective-permute-done.15
  191.0 4.7 collective-permute-done.35
  206.1 6.4 norm_qkv.4
  212.5 6.5 norm_qkv.5
  219.0 19.1 %attend.2 = (bf16[1024,512]{1,0:T(8,128)(2,1)}, f32[4,8,1024]{2,1,0:T(8,128)}) custom-call(bf16[1024,1536]{1,0:T(8,128)(2,1)} %get-tuple-element.84.refs_0_.refs_1_.refs_2_, bf16[1024,1536]{1,0:T(8,128)(2,1)} %get-tuple-element.84.refs_0_.refs_1_.refs_2_, bf16[1024,1536]{1,0:T(8,128)(2,1)} %get-tuple-element.84.refs_0_.refs_1_.refs_2_), custom_call_target="tpu_custom_call" | custom-call | tf_op jit(solution)/shard_map/attend/pallas_call | solution.py:540
  245.3 7.6 collective-permute-done.48
  252.9 11.2 %collective-permute-done.46 = bf16[256,1024]{1,0:T(8,128)(2,1)S(1)} collective-permute-done((bf16[256,1024]{1,0:T(8,128)(2,1)S(1)}, bf16[256,1024]{1,0:T(8,128)(2,1)S(1)}, u32[]{:S(2)}, u32[]{:S(2)}) %collective-permute-start.46) | collective-permute-done | bytes 524320 | tf_op jit(solution)/shard_map/ppermute | solution.py:410
  264.4 8.0 collective-permute-done.51
  277.5 6.8 collective-permute-done.37.refs_8_.refs_5_.refs_4_.refs_6_
  284.3 3.8 collective-permute-start.53
  291.4 15.7 %mlp_out.4 = (bf16[1024,2048]{1,0:T(8,128)(2,1)}, bf16[1024,2048]{1,0:T(8,128)(2,1)}, bf16[512,1024]{1,0:T(8,128)(2,1)}) custom-call(bf16[1024,512]{1,0:T(8,128)(2,1)} %get-tuple-element.85.refs_0_.refs_4_, bf16[1024,1024]{1,0:T(8,128)(2,1)} %get-tuple-element.86.refs_1_.refs_0_, f32[1,2048]{1,0:T(1,128)} %bitcast.428, bf16[2,256,512]{2,1,0:T(8,128)(2,1)} %copy-done.4, ...), custom_call_target="tpu_custom_call" | custom-call | tf_op jit(solution)/shard_map/mlp_out/pallas_call | solution.py:540
  307.1 15.8 %mlp_out.5 = (bf16[1024,2048]{1,0:T(8,128)(2,1)}, bf16[1024,2048]{1,0:T(8,128)(2,1)}, bf16[512,1024]{1,0:T(8,128)(2,1)}) custom-call(bf16[1024,512]{1,0:T(8,128)(2,1)} %get-tuple-element.85.refs_0_.refs_4_, bf16[1024,1024]{1,0:T(8,128)(2,1)} %get-tuple-element.86.refs_1_.refs_0_, ...), custom_call_target="tpu_custom_call", output_to_operand_aliasing={{0}: (27, {}), {1}: (28, {})} | custom-call | tf_op jit(solution)/shard_map/mlp_out/pallas_call | solution.py:540
  334.1 14.7 %collective-permute-done.52 = bf16[384,1024]{1,0:T(8,128)(2,1)} collective-permute-done((bf16[384,1024]{1,0:T(8,128)(2,1)}, bf16[384,1024]{1,0:T(8,128)(2,1)}, u32[]{:S(2)}, u32[]{:S(2)}) %collective-permute-start.52) | collective-permute-done | bytes 786464 | tf_op jit(solution)/shard_map/ppermute | solution.py:405
  349.4 22.2 %collective-permute-done.33 = bf16[512,1024]{1,0:T(8,128)(2,1)} collective-permute-done((bf16[512,1024]{1,0:T(8,128)(2,1)}, bf16[512,1024]{1,0:T(8,128)(2,1)}, u32[]{:S(2)}, u32[]{:S(2)}) %collective-permute-start.33) | collective-permute-done | bytes 1048608 | tf_op jit(solution)/shard_map/ppermute | solution.py:410
  371.9 5.7 add_convert_fusion.11
  382.8 6.4 norm_qkv.6
  389.2 6.3 norm_qkv.7
  401.6 19.1 %attend.3 = (bf16[1024,512]{1,0:T(8,128)(2,1)}, f32[4,8,1024]{2,1,0:T(8,128)}) custom-call(bf16[1024,1536]{1,0:T(8,128)(2,1)} %get-tuple-element.98.refs_0_.refs_1_.refs_2_, bf16[1024,1536]{1,0:T(8,128)(2,1)} %get-tuple-element.98.refs_0_.refs_1_.refs_2_, bf16[1024,1536]{1,0:T(8,128)(2,1)} %get-tuple-element.98.refs_0_.refs_1_.refs_2_), custom_call_target="tpu_custom_call" | custom-call | tf_op jit(solution)/shard_map/attend/pallas_call | solution.py:540
  420.7 15.9 %mlp_out.6 = (bf16[1024,2048]{1,0:T(8,128)(2,1)}, bf16[1024,2048]{1,0:T(8,128)(2,1)}, bf16[512,1024]{1,0:T(8,128)(2,1)}) custom-call(bf16[1024,512]{1,0:T(8,128)(2,1)} %get-tuple-element.99.refs_0_.refs_3_, bf16[1024,1024]{1,0:T(8,128)(2,1)} %get-tuple-element.100.refs_1_.refs_0_, f32[1,2048]{1,0:T(1,128)} %bitcast.426, bf16[2,256,512]{2,1,0:T(8,128)(2,1)} %copy-done.6, ...), custom_call_target="tpu_custom_call" | custom-call | tf_op jit(solution)/shard_map/mlp_out/pallas_call | solution.py:540
  436.6 15.8 %mlp_out.7 = (bf16[1024,2048]{1,0:T(8,128)(2,1)}, bf16[1024,2048]{1,0:T(8,128)(2,1)}, bf16[512,1024]{1,0:T(8,128)(2,1)}) custom-call(bf16[1024,512]{1,0:T(8,128)(2,1)} %get-tuple-element.99.refs_0_.refs_3_, bf16[1024,1024]{1,0:T(8,128)(2,1)} %get-tuple-element.100.refs_1_.refs_0_, ...), custom_call_target="tpu_custom_call", output_to_operand_aliasing={{0}: (27, {}), {1}: (28, {})} | custom-call | tf_op jit(solution)/shard_map/mlp_out/pallas_call | solution.py:540
  454.6 8.0 mlp_back.4
  462.6 7.6 mlp_back.5
  470.2 25.8 %attend_back.2 = (bf16[1024,1536]{1,0:T(8,128)(2,1)}, f32[1,1536]{1,0:T(1,128)}) custom-call(bf16[1024,1536]{1,0:T(8,128)(2,1)} %get-tuple-element.98.refs_0_.refs_1_.refs_2_, bf16[1024,1536]{1,0:T(8,128)(2,1)} %get-tuple-element.98.refs_0_.refs_1_.refs_2_, bf16[1024,1536]{1,0:T(8,128)(2,1)} %get-tuple-element.98.refs_0_.refs_1_.refs_2_, ...), custom_call_target="tpu_custom_call" | custom-call | tf_op jit(solution)/shard_map/attend_back/pallas_call | solution.py:540
  496.0 10.8 %norm_back.5 = (bf16[512,1024]{1,0:T(8,128)(2,1)}, f32[8,1024]{1,0:T(8,128)}) custom-call(bf16[512,1024]{1,0:T(8,128)(2,1)} %get-tuple-element.177.refs_0_, bf16[1024,1536]{1,0:T(8,128)(2,1)} %get-tuple-element.110.refs_1_.refs_2_, bf16[1024,2048]{1,0:T(8,128)(2,1)} %get-tuple-element.111.refs_2_, f32[8,1024]{1,0:T(8,128)} %concatenate.187.refs_1_.refs_3_, ...), custom_call_target="tpu_custom_call" | custom-call | tf_op jit(solution)/shard_map/norm_back/pallas_call | solution.py:540
  508.6 10.6 %norm_back.4 = (bf16[512,1024]{1,0:T(8,128)(2,1)}, f32[8,1024]{1,0:T(8,128)}) custom-call(bf16[512,1024]{1,0:T(8,128)(2,1)} %get-tuple-element.176.refs_0_, bf16[1024,1536]{1,0:T(8,128)(2,1)} %get-tuple-element.110.refs_1_.refs_2_, bf16[1024,2048]{1,0:T(8,128)(2,1)} %get-tuple-element.111.refs_2_, f32[8,1024]{1,0:T(8,128)} %concatenate.187.refs_1_.refs_3_, ...), custom_call_target="tpu_custom_call" | custom-call | tf_op jit(solution)/shard_map/norm_back/pallas_call | solution.py:540
  532.5 15.0 %weight_grad.7 = (bf16[4,2,256,1024]{3,2,1,0:T(8,128)(2,1)}, bf16[4,2,256,1024]{3,2,1,0:T(8,128)(2,1)}) custom-call(bf16[1024,1024]{1,0:T(8,128)(2,1)} %get-tuple-element.100.refs_1_.refs_0_, bf16[1024,1024]{1,0:T(8,128)(2,1)} %pad_maximum_fusion.1.refs_0_.refs_1_, bf16[1024,2048]{1,0:T(8,128)(2,1)} %get-tuple-element.111.refs_2_, ...), custom_call_target="tpu_custom_call" | custom-call | tf_op jit(solution)/shard_map/weight_grad/pallas_call | solution.py:540
  547.6 12.1 %weight_grad.6 = (bf16[4,2,256,512]{3,2,1,0:T(8,128)(2,1)}, bf16[4,2,256,512]{3,2,1,0:T(8,128)(2,1)}) custom-call(bf16[1024,1024]{1,0:T(8,128)(2,1)} %get-tuple-element.145.refs_0_, bf16[1024,1024]{1,0:T(8,128)(2,1)} %pad_maximum_fusion.1.refs_0_.refs_1_, bf16[1024,1536]{1,0:T(8,128)(2,1)} %get-tuple-element.110.refs_1_.refs_2_, ...), custom_call_target="tpu_custom_call" | custom-call | tf_op jit(solution)/shard_map/weight_grad/pallas_call | solution.py:540
  560.3 4.7 add_convert_fusion.7
  565.9 3.9 collective-permute-start.65
  576.5 5.4 collective-permute-done.64
  582.7 8.0 mlp_back.6
  590.7 7.6 mlp_back.7
  598.3 14.8 %weight_grad.4 = (bf16[4,2,256,1024]{3,2,1,0:T(8,128)(2,1)}, bf16[4,2,256,1024]{3,2,1,0:T(8,128)(2,1)}) custom-call(bf16[1024,1024]{1,0:T(8,128)(2,1)} %get-tuple-element.86.refs_1_.refs_0_, bf16[512,1024]{1,0:T(8,128)(2,1)} %get-tuple-element.116.refs_0_.refs_1_, bf16[512,1024]{1,0:T(8,128)(2,1)} %get-tuple-element.114.refs_0_.refs_2_, ...), custom_call_target="tpu_custom_call" | custom-call | tf_op jit(solution)/shard_map/weight_grad/pallas_call | solution.py:540
  613.2 25.8 %attend_back.3 = (bf16[1024,1536]{1,0:T(8,128)(2,1)}, f32[1,1536]{1,0:T(1,128)}) custom-call(bf16[1024,1536]{1,0:T(8,128)(2,1)} %get-tuple-element.84.refs_0_.refs_1_.refs_2_, bf16[1024,1536]{1,0:T(8,128)(2,1)} %get-tuple-element.84.refs_0_.refs_1_.refs_2_, bf16[1024,1536]{1,0:T(8,128)(2,1)} %get-tuple-element.84.refs_0_.refs_1_.refs_2_, ...), custom_call_target="tpu_custom_call" | custom-call | tf_op jit(solution)/shard_map/attend_back/pallas_call | solution.py:540
  639.0 10.8 %norm_back.6 = (bf16[512,1024]{1,0:T(8,128)(2,1)}, f32[8,1024]{1,0:T(8,128)}) custom-call(bf16[1024,1024]{1,0:T(8,128)(2,1)} %pad_maximum_fusion.refs_0_, bf16[1024,1536]{1,0:T(8,128)(2,1)} %get-tuple-element.125.refs_1_.refs_3_, bf16[1024,2048]{1,0:T(8,128)(2,1)} %get-tuple-element.120.refs_3_.refs_2_, f32[8,1024]{1,0:T(8,128)} %concatenate.177.refs_1_.refs_3_, ...), custom_call_target="tpu_custom_call" | custom-call | tf_op jit(solution)/shard_map/norm_back/pallas_call | solution.py:540
  649.8 10.6 %norm_back.7 = (bf16[512,1024]{1,0:T(8,128)(2,1)}, f32[8,1024]{1,0:T(8,128)}) custom-call(bf16[1024,1024]{1,0:T(8,128)(2,1)} %pad_maximum_fusion.refs_0_, bf16[1024,1536]{1,0:T(8,128)(2,1)} %get-tuple-element.125.refs_1_.refs_3_, bf16[1024,2048]{1,0:T(8,128)(2,1)} %get-tuple-element.120.refs_3_.refs_2_, f32[8,1024]{1,0:T(8,128)} %concatenate.177.refs_1_.refs_3_, ...), custom_call_target="tpu_custom_call" | custom-call | tf_op jit(solution)/shard_map/norm_back/pallas_call | solution.py:540
  671.5 4.6 copy.99
  676.1 12.1 %weight_grad.5 = (bf16[4,2,256,512]{3,2,1,0:T(8,128)(2,1)}, bf16[4,2,256,512]{3,2,1,0:T(8,128)(2,1)}) custom-call(bf16[1024,1024]{1,0:T(8,128)(2,1)} %get-tuple-element.142.refs_0_, bf16[512,1024]{1,0:T(8,128)(2,1)} %get-tuple-element.116.refs_0_.refs_1_, bf16[512,1024]{1,0:T(8,128)(2,1)} %get-tuple-element.114.refs_0_.refs_2_, ...), custom_call_target="tpu_custom_call" | custom-call | tf_op jit(solution)/shard_map/weight_grad/pallas_call | solution.py:540
  692.6 3.9 collective-permute-done.77
  698.4 16.5 %collective-permute-done.78 = f32[8704]{0:T(1024)} collective-permute-done((f32[8704]{0:T(1024)S(1)}, f32[8704]{0:T(1024)}, u32[]{:S(2)}, u32[]{:S(2)}) %collective-permute-start.78) | collective-permute-done | bytes 34848 | tf_op jit(solution)/shard_map/ppermute | solution.py:410
  721.8 7.1 collective-permute-done.89
  734.1 9.6 %collective-permute-done.69 = bf16[512,1024]{1,0:T(8,128)(2,1)S(1)} collective-permute-done((bf16[512,1024]{1,0:T(8,128)(2,1)}, bf16[512,1024]{1,0:T(8,128)(2,1)S(1)}, u32[]{:S(2)}, u32[]{:S(2)}) %collective-permute-start.69) | collective-permute-done | bytes 1048608 | tf_op jit(solution)/shard_map/ppermute | solution.py:410
  748.0 4.3 add_convert_fusion
  759.4 4.3 add_convert_fusion.1
  773.3 12.5 %collective-permute-done.81 = bf16[2,256,512]{2,1,0:T(8,128)(2,1)S(1)} collective-permute-done((bf16[2,256,512]{2,1,0:T(8,128)(2,1)S(1)}, bf16[2,256,512]{2,1,0:T(8,128)(2,1)S(1)}, u32[]{:S(2)}, u32[]{:S(2)}) %collective-permute-start.81) | collective-permute-done | bytes 524320 | tf_op jit(solution)/shard_map/ppermute | solution.py:405
  785.8 9.3 %collective-permute-done.83 = bf16[2,256,512]{2,1,0:T(8,128)(2,1)S(1)} collective-permute-done((bf16[2,256,512]{2,1,0:T(8,128)(2,1)S(1)}, bf16[2,256,512]{2,1,0:T(8,128)(2,1)S(1)}, u32[]{:S(2)}, u32[]{:S(2)}) %collective-permute-start.83) | collective-permute-done | bytes 524320 | tf_op jit(solution)/shard_map/ppermute | solution.py:405
  795.9 5.2 collective-permute-done.99
  803.4 40.2 %collective-permute-done.93 = bf16[4,256,1024]{2,1,0:T(8,128)(2,1)S(1)} collective-permute-done((bf16[4,256,1024]{2,1,0:T(8,128)(2,1)S(1)}, bf16[4,256,1024]{2,1,0:T(8,128)(2,1)S(1)}, u32[]{:S(2)}, u32[]{:S(2)}) %collective-permute-start.93) | collective-permute-done | bytes 2097184 | tf_op jit(solution)/shard_map/ppermute | solution.py:410
  846.9 7.4 collective-permute-done.102
  867.4 3.8 collective-permute-start.97
  873.6 6.3 collective-permute-done.101
  880.0 6.3 collective-permute-start.72
  886.2 4.7 collective-permute-done.103
  892.4 9.9 %collective-permute-done.95 = bf16[256,1024]{1,0:T(8,128)(2,1)S(1)} collective-permute-done((bf16[256,1024]{1,0:T(8,128)(2,1)S(1)}, bf16[256,1024]{1,0:T(8,128)(2,1)S(1)}, u32[]{:S(2)}, u32[]{:S(2)}) %collective-permute-start.95) | collective-permute-done | bytes 524320 | tf_op jit(solution)/shard_map/ppermute | solution.py:405
  902.4 7.2 collective-permute-done.97
  911.6 3.9 collective-permute-done.73
  (567 shorter events, 246.3 us)
Async XLA Ops:
  4.5 54.0 %collective-permute-start.20 = (bf16[256,1024]{1,0:T(8,128)(2,1)}, bf16[256,1024]{1,0:T(8,128)(2,1)}, u32[]{:S(2)}, u32[]{:S(2)}) collective-permute-start(bf16[256,1024]{1,0:T(8,128)(2,1)} %fusion.11), channel_id=1, source_target_pairs={{0,16},{16,0},{1,17},{17,1},{2,18},{18,2},{3,19},{19,3},{4,20},{20... | collective-permute-start | bytes 1572872 | tf_op jit(solution)/shard_map/ppermute | solution.py:410
  8.9 47.5 %collective-permute-start.10 = (bf16[256,512]{1,0:T(8,128)(2,1)}, bf16[256,512]{1,0:T(8,128)(2,1)}, u32[]{:S(2)}, u32[]{:S(2)}) collective-permute-start(bf16[256,512]{1,0:T(8,128)(2,1)} %bitcast.39), channel_id=1, source_target_pairs={{0,16},{16,0},{1,17},{17,1},{2,18},{18,2},{3,19},{19,3},{4,20},{20... | collective-permute-start | bytes 786440 | tf_op jit(solution)/shard_map/ppermute | solution.py:410
  51.6 51.7 %collective-permute-start = (bf16[384,1024]{1,0:T(8,128)(2,1)}, bf16[384,1024]{1,0:T(8,128)(2,1)}, u32[]{:S(2)}, u32[]{:S(2)}) collective-permute-start(bf16[384,1024]{1,0:T(8,128)(2,1)} %pad_maximum_fusion.12), channel_id=1, source_target_pairs={{0,1},{1,2},{2,3},{3,0},{4,5},{5,6},{6,7},{7,4},{8,9},{9,10},{10,1... | collective-permute-start | bytes 2359304 | tf_op jit(solution)/shard_map/ppermute | solution.py:405
  52.1 61.6 %collective-permute-start.1 = (bf16[384,1024]{1,0:T(8,128)(2,1)}, bf16[384,1024]{1,0:T(8,128)(2,1)}, u32[]{:S(2)}, u32[]{:S(2)}) collective-permute-start(bf16[384,1024]{1,0:T(8,128)(2,1)} %pad_maximum_fusion.13), channel_id=1, source_target_pairs={{0,3},{1,0},{2,1},{3,2},{4,7},{5,4},{6,5},{7,6},{8,11},{9,8},{10,9... | collective-permute-start | bytes 2359304 | tf_op jit(solution)/shard_map/ppermute | solution.py:405
  59.7 42.5 %collective-permute-start.22 = (bf16[256,1024]{1,0:T(8,128)(2,1)S(1)}, bf16[256,1024]{1,0:T(8,128)(2,1)S(1)}, u32[]{:S(2)}, u32[]{:S(2)}) collective-permute-start(bf16[256,1024]{1,0:T(8,128)(2,1)S(1)} %get-tuple-element.243), channel_id=1, source_target_pairs={{0,1},{1,2},{2,3},{3,0},{4,5},{5,6},{6,7},{7,4},{8,9},{9,10},{10,1... | collective-permute-start | bytes 1572872 | tf_op jit(solution)/shard_map/ppermute | solution.py:405
  59.8 58.1 %collective-permute-start.24 = (bf16[256,1024]{1,0:T(8,128)(2,1)S(1)}, bf16[256,1024]{1,0:T(8,128)(2,1)S(1)}, u32[]{:S(2)}, u32[]{:S(2)}) collective-permute-start(bf16[256,1024]{1,0:T(8,128)(2,1)S(1)} %get-tuple-element.243), channel_id=1, source_target_pairs={{0,3},{1,0},{2,1},{3,2},{4,7},{5,4},{6,5},{7,6},{8,11},{9,8},{10,9... | collective-permute-start | bytes 1572872 | tf_op jit(solution)/shard_map/ppermute | solution.py:405
  64.5 60.3 %collective-permute-start.12 = (bf16[2,256,512]{2,1,0:T(8,128)(2,1)S(1)}, bf16[2,256,512]{2,1,0:T(8,128)(2,1)S(1)}, u32[]{:S(2)}, u32[]{:S(2)}) collective-permute-start(bf16[2,256,512]{2,1,0:T(8,128)(2,1)S(1)} %pad_maximum_fusion.20.refs_6_.refs_3_.refs_2_.refs_4_), channel_id=1, source_target_pairs={{0,1},{1,2},{2,3},{3,0},{4,5},{5,6},{6,7},{7,4},{8,9},{9,10},{10,1... | collective-permute-start | bytes 1572872 | tf_op jit(solution)/shard_map/ppermute | solution.py:405
  102.2 42.2 %collective-permute-start.21 = (bf16[256,1024]{1,0:T(8,128)(2,1)S(1)}, bf16[256,1024]{1,0:T(8,128)(2,1)}, u32[]{:S(2)}, u32[]{:S(2)}) collective-permute-start(bf16[256,1024]{1,0:T(8,128)(2,1)S(1)} %get-tuple-element.243), channel_id=1, source_target_pairs={{0,8},{4,12},{8,0},{12,4},{1,9},{5,13},{9,1},{13,5},{2,10},{6,14},... | collective-permute-start | bytes 1572872 | tf_op jit(solution)/shard_map/ppermute | solution.py:410
  103.3 27.2 %collective-permute-start.26 = (bf16[128,1024]{1,0:T(8,128)(2,1)}, bf16[128,1024]{1,0:T(8,128)(2,1)}, u32[]{:S(2)}, u32[]{:S(2)}) collective-permute-start(bf16[128,1024]{1,0:T(8,128)(2,1)} %slice.701), channel_id=1, source_target_pairs={{0,1},{1,2},{2,3},{3,0},{4,5},{5,6},{6,7},{7,4},{8,9},{9,10},{10,1... | collective-permute-start | bytes 786440 | tf_op jit(solution)/shard_map/ppermute | solution.py:405
  113.7 34.4 %collective-permute-start.13 = (bf16[2,256,512]{2,1,0:T(8,128)(2,1)S(1)}, bf16[2,256,512]{2,1,0:T(8,128)(2,1)S(1)}, u32[]{:S(2)}, u32[]{:S(2)}) collective-permute-start(bf16[2,256,512]{2,1,0:T(8,128)(2,1)S(1)} %pad_maximum_fusion.20.refs_6_.refs_3_.refs_2_.refs_4_), channel_id=1, source_target_pairs={{0,3},{1,0},{2,1},{3,2},{4,7},{5,4},{6,5},{7,6},{8,11},{9,8},{10,9... | collective-permute-start | bytes 1572872 | tf_op jit(solution)/shard_map/ppermute | solution.py:405
  117.9 68.9 %collective-permute-start.16 = (bf16[2,256,512]{2,1,0:T(8,128)(2,1)S(1)}, bf16[2,256,512]{2,1,0:T(8,128)(2,1)S(1)}, u32[]{:S(2)}, u32[]{:S(2)}) collective-permute-start(bf16[2,256,512]{2,1,0:T(8,128)(2,1)S(1)} %pad_maximum_fusion.20.refs_6_.refs_3_.refs_2_.refs_4_), channel_id=1, source_target_pairs={{0,4},{4,0},{8,12},{12,8},{1,5},{5,1},{9,13},{13,9},{2,6},{6,2},{1... | collective-permute-start | bytes 1572872 | tf_op jit(solution)/shard_map/ppermute | solution.py:410
  144.5 23.4 %collective-permute-start.28 = (bf16[256,1024]{1,0:T(8,128)(2,1)S(1)}, bf16[256,1024]{1,0:T(8,128)(2,1)S(1)}, u32[]{:S(2)}, u32[]{:S(2)}) collective-permute-start(bf16[256,1024]{1,0:T(8,128)(2,1)S(1)} %constant_dynamic-update-slice_fusion), channel_id=1, source_target_pairs={{0,8},{4,12},{8,0},{12,4},{1,9},{5,13},{9,1},{13,5},{2,10},{6,14},... | collective-permute-start | bytes 1572872 | tf_op jit(solution)/shard_map/ppermute | solution.py:410
  148.1 22.5 %collective-permute-start.2 = (bf16[128,1024]{1,0:T(8,128)(2,1)S(1)}, bf16[128,1024]{1,0:T(8,128)(2,1)S(1)}, u32[]{:S(2)}, u32[]{:S(2)}) collective-permute-start(bf16[128,1024]{1,0:T(8,128)(2,1)S(1)} %slice.682), channel_id=1, source_target_pairs={{0,1},{1,2},{2,3},{3,0},{4,5},{5,6},{6,7},{7,4},{8,9},{9,10},{10,1... | collective-permute-start | bytes 786440 | tf_op jit(solution)/shard_map/ppermute | solution.py:405
  149.2 23.7 %collective-permute-start.3 = (bf16[128,1024]{1,0:T(8,128)(2,1)S(1)}, bf16[128,1024]{1,0:T(8,128)(2,1)S(1)}, u32[]{:S(2)}, u32[]{:S(2)}) collective-permute-start(bf16[128,1024]{1,0:T(8,128)(2,1)S(1)} %slice.683), channel_id=1, source_target_pairs={{0,3},{1,0},{2,1},{3,2},{4,7},{5,4},{6,5},{7,6},{8,11},{9,8},{10,9... | collective-permute-start | bytes 786440 | tf_op jit(solution)/shard_map/ppermute | solution.py:405
  172.8 23.9 %collective-permute-start.47 = (bf16[256,1024]{1,0:T(8,128)(2,1)S(1)}, bf16[256,1024]{1,0:T(8,128)(2,1)S(1)}, u32[]{:S(2)}, u32[]{:S(2)}) collective-permute-start(bf16[256,1024]{1,0:T(8,128)(2,1)S(1)} %get-tuple-element.96), channel_id=1, source_target_pairs={{0,3},{1,0},{2,1},{3,2},{4,7},{5,4},{6,5},{7,6},{8,11},{9,8},{10,9... | collective-permute-start | bytes 1572872 | tf_op jit(solution)/shard_map/ppermute | solution.py:405
  195.7 44.5 %collective-permute-start.44 = (bf16[256,1024]{1,0:T(8,128)(2,1)S(1)}, bf16[256,1024]{1,0:T(8,128)(2,1)}, u32[]{:S(2)}, u32[]{:S(2)}) collective-permute-start(bf16[256,1024]{1,0:T(8,128)(2,1)S(1)} %get-tuple-element.96), channel_id=1, source_target_pairs={{0,8},{4,12},{8,0},{12,4},{1,9},{5,13},{9,1},{13,5},{2,10},{6,14},... | collective-permute-start | bytes 1572872 | tf_op jit(solution)/shard_map/ppermute | solution.py:410
  196.8 43.0 %collective-permute-start.49 = (bf16[128,1024]{1,0:T(8,128)(2,1)S(1)}, bf16[128,1024]{1,0:T(8,128)(2,1)S(1)}, u32[]{:S(2)}, u32[]{:S(2)}) collective-permute-start(bf16[128,1024]{1,0:T(8,128)(2,1)S(1)} %slice.713), channel_id=1, source_target_pairs={{0,1},{1,2},{2,3},{3,0},{4,5},{5,6},{6,7},{7,4},{8,9},{9,10},{10,1... | collective-permute-start | bytes 786440 | tf_op jit(solution)/shard_map/ppermute | solution.py:405
  199.0 44.2 %collective-permute-start.36 = (bf16[2,256,512]{2,1,0:T(8,128)(2,1)S(1)}, bf16[2,256,512]{2,1,0:T(8,128)(2,1)}, u32[]{:S(2)}, u32[]{:S(2)}) collective-permute-start(bf16[2,256,512]{2,1,0:T(8,128)(2,1)S(1)} %pad_maximum_fusion.22.refs_6_.refs_3_.refs_2_.refs_4_), channel_id=1, source_target_pairs={{0,1},{1,2},{2,3},{3,0},{4,5},{5,6},{6,7},{7,4},{8,9},{9,10},{10,1... | collective-permute-start | bytes 1572872 | tf_op jit(solution)/shard_map/ppermute | solution.py:405
  200.1 40.0 %collective-permute-start.50 = (bf16[128,1024]{1,0:T(8,128)(2,1)S(1)}, bf16[128,1024]{1,0:T(8,128)(2,1)S(1)}, u32[]{:S(2)}, u32[]{:S(2)}) collective-permute-start(bf16[128,1024]{1,0:T(8,128)(2,1)S(1)} %slice.714), channel_id=1, source_target_pairs={{0,3},{1,0},{2,1},{3,2},{4,7},{5,4},{6,5},{7,6},{8,11},{9,8},{10,9... | collective-permute-start | bytes 786440 | tf_op jit(solution)/shard_map/ppermute | solution.py:405
  239.8 24.3 %collective-permute-start.46 = (bf16[256,1024]{1,0:T(8,128)(2,1)S(1)}, bf16[256,1024]{1,0:T(8,128)(2,1)S(1)}, u32[]{:S(2)}, u32[]{:S(2)}) collective-permute-start(bf16[256,1024]{1,0:T(8,128)(2,1)S(1)} %collective-permute-done.45), channel_id=1, source_target_pairs={{0,8},{4,12},{8,0},{12,4},{1,9},{5,13},{9,1},{13,5},{2,10},{6,14},... | collective-permute-start | bytes 1572872 | tf_op jit(solution)/shard_map/ppermute | solution.py:410
  240.1 36.4 %collective-permute-start.29 = (bf16[2,256,1024]{2,1,0:T(8,128)(2,1)}, bf16[2,256,1024]{2,1,0:T(8,128)(2,1)}, u32[]{:S(2)}, u32[]{:S(2)}) collective-permute-start(bf16[2,256,1024]{2,1,0:T(8,128)(2,1)} %pad_maximum_fusion.4.refs_11_.refs_19_.refs_10_.refs_12_), channel_id=1, source_target_pairs={{0,4},{4,0},{8,12},{12,8},{1,5},{5,1},{9,13},{13,9},{2,6},{6,2},{1... | collective-permute-start | bytes 3145736 | tf_op jit(solution)/shard_map/ppermute | solution.py:410
  240.2 32.2 %collective-permute-start.51 = (bf16[256,1024]{1,0:T(8,128)(2,1)S(1)}, bf16[256,1024]{1,0:T(8,128)(2,1)S(1)}, u32[]{:S(2)}, u32[]{:S(2)}) collective-permute-start(bf16[256,1024]{1,0:T(8,128)(2,1)S(1)} %constant_dynamic-update-slice_fusion.2), channel_id=1, source_target_pairs={{0,8},{4,12},{8,0},{12,4},{1,9},{5,13},{9,1},{13,5},{2,10},{6,14},... | collective-permute-start | bytes 1572872 | tf_op jit(solution)/shard_map/ppermute | solution.py:410
  243.3 41.0 %collective-permute-start.30 = (bf16[2,256,1024]{2,1,0:T(8,128)(2,1)}, bf16[2,256,1024]{2,1,0:T(8,128)(2,1)}, u32[]{:S(2)}, u32[]{:S(2)}) collective-permute-start(bf16[2,256,1024]{2,1,0:T(8,128)(2,1)} %pad_maximum_fusion.5.refs_12_.refs_20_.refs_11_.refs_13_), channel_id=1, source_target_pairs={{0,4},{4,0},{8,12},{12,8},{1,5},{5,1},{9,13},{13,9},{2,6},{6,2},{1... | collective-permute-start | bytes 3145736 | tf_op jit(solution)/shard_map/ppermute | solution.py:410
  252.9 37.5 %collective-permute-start.31 = (bf16[2,256,1024]{2,1,0:T(8,128)(2,1)}, bf16[2,256,1024]{2,1,0:T(8,128)(2,1)}, u32[]{:S(2)}, u32[]{:S(2)}) collective-permute-start(bf16[2,256,1024]{2,1,0:T(8,128)(2,1)} %pad_maximum_fusion.6.refs_13_.refs_21_.refs_12_.refs_14_), channel_id=1, source_target_pairs={{0,4},{4,0},{8,12},{12,8},{1,5},{5,1},{9,13},{13,9},{2,6},{6,2},{1... | collective-permute-start | bytes 3145736 | tf_op jit(solution)/shard_map/ppermute | solution.py:410
  264.1 27.3 %collective-permute-start.32 = (bf16[2,256,1024]{2,1,0:T(8,128)(2,1)}, bf16[2,256,1024]{2,1,0:T(8,128)(2,1)}, u32[]{:S(2)}, u32[]{:S(2)}) collective-permute-start(bf16[2,256,1024]{2,1,0:T(8,128)(2,1)} %pad_maximum_fusion.7.refs_14_.refs_22_.refs_13_.refs_15_), channel_id=1, source_target_pairs={{0,4},{4,0},{8,12},{12,8},{1,5},{5,1},{9,13},{13,9},{2,6},{6,2},{1... | collective-permute-start | bytes 3145736 | tf_op jit(solution)/shard_map/ppermute | solution.py:410
  276.5 46.5 %collective-permute-start.40 = (bf16[2,256,512]{2,1,0:T(8,128)(2,1)S(1)}, bf16[2,256,512]{2,1,0:T(8,128)(2,1)}, u32[]{:S(2)}, u32[]{:S(2)}) collective-permute-start(bf16[2,256,512]{2,1,0:T(8,128)(2,1)S(1)} %copy-done.7), channel_id=1, source_target_pairs={{0,4},{4,0},{8,12},{12,8},{1,5},{5,1},{9,13},{13,9},{2,6},{6,2},{1... | collective-permute-start | bytes 1572872 | tf_op jit(solution)/shard_map/ppermute | solution.py:410
  284.3 40.7 %collective-permute-start.38 = (bf16[256,512]{1,0:T(8,128)(2,1)}, bf16[256,512]{1,0:T(8,128)(2,1)}, u32[]{:S(2)}, u32[]{:S(2)}) collective-permute-start(bf16[256,512]{1,0:T(8,128)(2,1)} %slice_bitcast_fusion.45), channel_id=1, source_target_pairs={{0,1},{1,2},{2,3},{3,0},{4,5},{5,6},{6,7},{7,4},{8,9},{9,10},{10,1... | collective-permute-start | bytes 786440 | tf_op jit(solution)/shard_map/ppermute | solution.py:405
  284.3 46.0 %collective-permute-start.53 = (bf16[384,1024]{1,0:T(8,128)(2,1)}, bf16[384,1024]{1,0:T(8,128)(2,1)}, u32[]{:S(2)}, u32[]{:S(2)}) collective-permute-start(bf16[384,1024]{1,0:T(8,128)(2,1)} %pad_maximum_fusion.15), channel_id=1, source_target_pairs={{0,3},{1,0},{2,1},{3,2},{4,7},{5,4},{6,5},{7,6},{8,11},{9,8},{10,9... | collective-permute-start | bytes 2359304 | tf_op jit(solution)/shard_map/ppermute | solution.py:405
  290.4 36.7 %collective-permute-start.39 = (bf16[256,512]{1,0:T(8,128)(2,1)}, bf16[256,512]{1,0:T(8,128)(2,1)}, u32[]{:S(2)}, u32[]{:S(2)}) collective-permute-start(bf16[256,512]{1,0:T(8,128)(2,1)} %slice_bitcast_fusion.44), channel_id=1, source_target_pairs={{0,3},{1,0},{2,1},{3,2},{4,7},{5,4},{6,5},{7,6},{8,11},{9,8},{10,9... | collective-permute-start | bytes 786440 | tf_op jit(solution)/shard_map/ppermute | solution.py:405
  291.4 38.8 %collective-permute-start.41 = (bf16[2,256,512]{2,1,0:T(8,128)(2,1)}, bf16[2,256,512]{2,1,0:T(8,128)(2,1)}, u32[]{:S(2)}, u32[]{:S(2)}) collective-permute-start(bf16[2,256,512]{2,1,0:T(8,128)(2,1)} %collective-permute-done.36.refs_7_.refs_4_.refs_3_.refs_5_), channel_id=1, source_target_pairs={{0,4},{4,0},{8,12},{12,8},{1,5},{5,1},{9,13},{13,9},{2,6},{6,2},{1... | collective-permute-start | bytes 1572872 | tf_op jit(solution)/shard_map/ppermute | solution.py:410
  323.0 26.4 %collective-permute-start.34 = (bf16[512,1024]{1,0:T(8,128)(2,1)}, bf16[512,1024]{1,0:T(8,128)(2,1)}, u32[]{:S(2)}, u32[]{:S(2)}) collective-permute-start(bf16[512,1024]{1,0:T(8,128)(2,1)} %get-tuple-element.90), channel_id=1, source_target_pairs={{0,16},{16,0},{1,17},{17,1},{2,18},{18,2},{3,19},{19,3},{4,20},{20... | collective-permute-start | bytes 3145736 | tf_op jit(solution)/shard_map/ppermute | solution.py:410
  325.0 46.6 %collective-permute-start.33 = (bf16[512,1024]{1,0:T(8,128)(2,1)}, bf16[512,1024]{1,0:T(8,128)(2,1)}, u32[]{:S(2)}, u32[]{:S(2)}) collective-permute-start(bf16[512,1024]{1,0:T(8,128)(2,1)} %get-tuple-element.87), channel_id=1, source_target_pairs={{0,16},{16,0},{1,17},{17,1},{2,18},{18,2},{3,19},{19,3},{4,20},{20... | collective-permute-start | bytes 3145736 | tf_op jit(solution)/shard_map/ppermute | solution.py:410
  333.6 87.1 %collective-permute-start.56 = (bf16[2,256,1024]{2,1,0:T(8,128)(2,1)S(1)}, bf16[2,256,1024]{2,1,0:T(8,128)(2,1)}, u32[]{:S(2)}, u32[]{:S(2)}) collective-permute-start(bf16[2,256,1024]{2,1,0:T(8,128)(2,1)S(1)} %pad_maximum_fusion.8.refs_11_.refs_19_.refs_10_.refs_12_), channel_id=1, source_target_pairs={{0,4},{4,0},{8,12},{12,8},{1,5},{5,1},{9,13},{13,9},{2,6},{6,2},{1... | collective-permute-start | bytes 3145736 | tf_op jit(solution)/shard_map/ppermute | solution.py:410
  333.7 86.9 %collective-permute-start.58 = (bf16[2,256,1024]{2,1,0:T(8,128)(2,1)S(1)}, bf16[2,256,1024]{2,1,0:T(8,128)(2,1)}, u32[]{:S(2)}, u32[]{:S(2)}) collective-permute-start(bf16[2,256,1024]{2,1,0:T(8,128)(2,1)S(1)} %pad_maximum_fusion.10.refs_13_.refs_21_.refs_12_.refs_14_), channel_id=1, source_target_pairs={{0,4},{4,0},{8,12},{12,8},{1,5},{5,1},{9,13},{13,9},{2,6},{6,2},{1... | collective-permute-start | bytes 3145736 | tf_op jit(solution)/shard_map/ppermute | solution.py:410
  348.9 71.8 %collective-permute-start.57 = (bf16[2,256,1024]{2,1,0:T(8,128)(2,1)S(1)}, bf16[2,256,1024]{2,1,0:T(8,128)(2,1)}, u32[]{:S(2)}, u32[]{:S(2)}) collective-permute-start(bf16[2,256,1024]{2,1,0:T(8,128)(2,1)S(1)} %pad_maximum_fusion.9.refs_12_.refs_20_.refs_11_.refs_13_), channel_id=1, source_target_pairs={{0,4},{4,0},{8,12},{12,8},{1,5},{5,1},{9,13},{13,9},{2,6},{6,2},{1... | collective-permute-start | bytes 3145736 | tf_op jit(solution)/shard_map/ppermute | solution.py:410
  349.4 71.3 %collective-permute-start.59 = (bf16[2,256,1024]{2,1,0:T(8,128)(2,1)}, bf16[2,256,1024]{2,1,0:T(8,128)(2,1)}, u32[]{:S(2)}, u32[]{:S(2)}) collective-permute-start(bf16[2,256,1024]{2,1,0:T(8,128)(2,1)} %pad_maximum_fusion.11.refs_14_.refs_22_.refs_13_.refs_15_), channel_id=1, source_target_pairs={{0,4},{4,0},{8,12},{12,8},{1,5},{5,1},{9,13},{13,9},{2,6},{6,2},{1... | collective-permute-start | bytes 3145736 | tf_op jit(solution)/shard_map/ppermute | solution.py:410
  452.5 68.5 %collective-permute-start.61 = (bf16[512,1024]{1,0:T(8,128)(2,1)}, bf16[512,1024]{1,0:T(8,128)(2,1)}, u32[]{:S(2)}, u32[]{:S(2)}) collective-permute-start(bf16[512,1024]{1,0:T(8,128)(2,1)} %get-tuple-element.104), channel_id=1, source_target_pairs={{0,16},{16,0},{1,17},{17,1},{2,18},{18,2},{3,19},{19,3},{4,20},{20... | collective-permute-start | bytes 3145736 | tf_op jit(solution)/shard_map/ppermute | solution.py:410
  454.2 66.8 %collective-permute-start.60 = (bf16[512,1024]{1,0:T(8,128)(2,1)S(1)}, bf16[512,1024]{1,0:T(8,128)(2,1)}, u32[]{:S(2)}, u32[]{:S(2)}) collective-permute-start(bf16[512,1024]{1,0:T(8,128)(2,1)S(1)} %copy-done.32), channel_id=1, source_target_pairs={{0,16},{16,0},{1,17},{17,1},{2,18},{18,2},{3,19},{19,3},{4,20},{20... | collective-permute-start | bytes 3145736 | tf_op jit(solution)/shard_map/ppermute | solution.py:410
  506.9 52.9 %collective-permute-start.67 = (bf16[512,1024]{1,0:T(8,128)(2,1)}, bf16[512,1024]{1,0:T(8,128)(2,1)}, u32[]{:S(2)}, u32[]{:S(2)}) collective-permute-start(bf16[512,1024]{1,0:T(8,128)(2,1)} %get-tuple-element.113), channel_id=1, source_target_pairs={{0,16},{16,0},{1,17},{17,1},{2,18},{18,2},{3,19},{19,3},{4,20},{20... | collective-permute-start | bytes 3145736 | tf_op jit(solution)/shard_map/ppermute | solution.py:410
  519.2 41.0 %collective-permute-start.66 = (bf16[512,1024]{1,0:T(8,128)(2,1)}, bf16[512,1024]{1,0:T(8,128)(2,1)}, u32[]{:S(2)}, u32[]{:S(2)}) collective-permute-start(bf16[512,1024]{1,0:T(8,128)(2,1)} %get-tuple-element.112), channel_id=1, source_target_pairs={{0,16},{16,0},{1,17},{17,1},{2,18},{18,2},{3,19},{19,3},{4,20},{20... | collective-permute-start | bytes 3145736 | tf_op jit(solution)/shard_map/ppermute | solution.py:410
  529.6 35.4 %collective-permute-start.63 = (bf16[384,1024]{1,0:T(8,128)(2,1)}, bf16[384,1024]{1,0:T(8,128)(2,1)}, u32[]{:S(2)}, u32[]{:S(2)}) collective-permute-start(bf16[384,1024]{1,0:T(8,128)(2,1)} %pad_maximum_fusion.17), channel_id=1, source_target_pairs={{0,3},{1,0},{2,1},{3,2},{4,7},{5,4},{6,5},{7,6},{8,11},{9,8},{10,9... | collective-permute-start | bytes 2359304 | tf_op jit(solution)/shard_map/ppermute | solution.py:405
  532.3 37.4 %collective-permute-start.62 = (bf16[384,1024]{1,0:T(8,128)(2,1)S(1)}, bf16[384,1024]{1,0:T(8,128)(2,1)}, u32[]{:S(2)}, u32[]{:S(2)}) collective-permute-start(bf16[384,1024]{1,0:T(8,128)(2,1)S(1)} %pad_maximum_fusion.16), channel_id=1, source_target_pairs={{0,1},{1,2},{2,3},{3,0},{4,5},{5,6},{6,7},{7,4},{8,9},{9,10},{10,1... | collective-permute-start | bytes 2359304 | tf_op jit(solution)/shard_map/ppermute | solution.py:405
  547.6 198.5 %collective-permute-start.98 = (bf16[4,2,256,1024]{3,2,1,0:T(8,128)(2,1)}, bf16[4,2,256,1024]{3,2,1,0:T(8,128)(2,1)}, u32[]{:S(2)}, u32[]{:S(2)}) collective-permute-start(bf16[4,2,256,1024]{3,2,1,0:T(8,128)(2,1)} %get-tuple-element.151), channel_id=1, source_target_pairs={{0,4},{4,0},{8,12},{12,8},{1,5},{5,1},{9,13},{13,9},{2,6},{6,2},{1... | collective-permute-start | bytes 12582920 | tf_op jit(solution)/shard_map/ppermute | solution.py:410
  559.7 102.2 %collective-permute-start.85 = (bf16[4,2,256,512]{3,2,1,0:T(8,128)(2,1)}, bf16[4,2,256,512]{3,2,1,0:T(8,128)(2,1)}, u32[]{:S(2)}, u32[]{:S(2)}) collective-permute-start(bf16[4,2,256,512]{3,2,1,0:T(8,128)(2,1)} %get-tuple-element.147), channel_id=1, source_target_pairs={{0,4},{4,0},{8,12},{12,8},{1,5},{5,1},{9,13},{13,9},{2,6},{6,2},{1... | collective-permute-start | bytes 6291464 | tf_op jit(solution)/shard_map/ppermute | solution.py:410
  667.3 22.4 %collective-permute-start.86 = (bf16[1,256,512]{2,1,0:T(8,128)(2,1)}, bf16[1,256,512]{2,1,0:T(8,128)(2,1)S(1)}, u32[]{:S(2)}, u32[]{:S(2)}) collective-permute-start(bf16[1,256,512]{2,1,0:T(8,128)(2,1)} %get-tuple-element.194), channel_id=1, source_target_pairs={{0,1},{1,2},{2,3},{3,0},{4,5},{5,6},{6,7},{7,4},{8,9},{9,10},{10,1... | collective-permute-start | bytes 786440 | tf_op jit(solution)/shard_map/ppermute | solution.py:405
  669.1 22.3 %collective-permute-start.88 = (bf16[1,256,512]{2,1,0:T(8,128)(2,1)}, bf16[1,256,512]{2,1,0:T(8,128)(2,1)S(1)}, u32[]{:S(2)}, u32[]{:S(2)}) collective-permute-start(bf16[1,256,512]{2,1,0:T(8,128)(2,1)} %get-tuple-element.195), channel_id=1, source_target_pairs={{0,3},{1,0},{2,1},{3,2},{4,7},{5,4},{6,5},{7,6},{8,11},{9,8},{10,9... | collective-permute-start | bytes 786440 | tf_op jit(solution)/shard_map/ppermute | solution.py:405
  676.1 83.4 %collective-permute-start.92 = (bf16[4,2,256,1024]{3,2,0,1:T(8,128)(2,1)}, bf16[4,2,256,1024]{3,2,0,1:T(8,128)(2,1)}, u32[]{:S(2)}, u32[]{:S(2)}) collective-permute-start(bf16[4,2,256,1024]{3,2,0,1:T(8,128)(2,1)} %copy.99), channel_id=1, source_target_pairs={{0,4},{4,0},{8,12},{12,8},{1,5},{5,1},{9,13},{13,9},{2,6},{6,2},{1... | collective-permute-start | bytes 12582920 | tf_op jit(solution)/shard_map/ppermute | solution.py:410
  688.1 42.3 %collective-permute-start.68 = (bf16[512,1024]{1,0:T(8,128)(2,1)}, bf16[512,1024]{1,0:T(8,128)(2,1)}, u32[]{:S(2)}, u32[]{:S(2)}) collective-permute-start(bf16[512,1024]{1,0:T(8,128)(2,1)} %get-tuple-element.126), channel_id=1, source_target_pairs={{0,16},{16,0},{1,17},{17,1},{2,18},{18,2},{3,19},{19,3},{4,20},{20... | collective-permute-start | bytes 3145736 | tf_op jit(solution)/shard_map/ppermute | solution.py:410
  692.4 26.7 %collective-permute-start.87 = (bf16[2,256,512]{2,1,0:T(8,128)(2,1)}, bf16[2,256,512]{2,1,0:T(8,128)(2,1)}, u32[]{:S(2)}, u32[]{:S(2)}) collective-permute-start(bf16[2,256,512]{2,1,0:T(8,128)(2,1)} %pad_maximum_fusion.26), channel_id=1, source_target_pairs={{0,1},{1,2},{2,3},{3,0},{4,5},{5,6},{6,7},{7,4},{8,9},{9,10},{10,1... | collective-permute-start | bytes 1572872 | tf_op jit(solution)/shard_map/ppermute | solution.py:405
  719.0 24.7 %collective-permute-start.69 = (bf16[512,1024]{1,0:T(8,128)(2,1)}, bf16[512,1024]{1,0:T(8,128)(2,1)S(1)}, u32[]{:S(2)}, u32[]{:S(2)}) collective-permute-start(bf16[512,1024]{1,0:T(8,128)(2,1)} %get-tuple-element.127), channel_id=1, source_target_pairs={{0,16},{16,0},{1,17},{17,1},{2,18},{18,2},{3,19},{19,3},{4,20},{20... | collective-permute-start | bytes 3145736 | tf_op jit(solution)/shard_map/ppermute | solution.py:410
  729.0 25.0 %collective-permute-start.79 = (bf16[4,2,256,512]{3,2,1,0:T(8,128)(2,1)}, bf16[4,2,256,512]{3,2,1,0:T(8,128)(2,1)S(1)}, u32[]{:S(2)}, u32[]{:S(2)}) collective-permute-start(bf16[4,2,256,512]{3,2,1,0:T(8,128)(2,1)} %get-tuple-element.144), channel_id=1, source_target_pairs={{0,4},{4,0},{8,12},{12,8},{1,5},{5,1},{9,13},{13,9},{2,6},{6,2},{1... | collective-permute-start | bytes 6291464 | tf_op jit(solution)/shard_map/ppermute | solution.py:410
  730.5 133.2 %collective-permute-start.90 = (bf16[256,512]{1,0:T(8,128)(2,1)S(1)}, bf16[256,512]{1,0:T(8,128)(2,1)}, u32[]{:S(2)}, u32[]{:S(2)}) collective-permute-start(bf16[256,512]{1,0:T(8,128)(2,1)S(1)} %slice_bitcast_fusion.28), channel_id=1, source_target_pairs={{0,8},{4,12},{8,0},{12,4},{1,9},{5,13},{9,1},{13,5},{2,10},{6,14},... | collective-permute-start | bytes 786440 | tf_op jit(solution)/shard_map/ppermute | solution.py:410
  752.5 48.6 %collective-permute-start.99 = (bf16[4,256,1024]{2,1,0:T(8,128)(2,1)S(1)}, bf16[4,256,1024]{2,1,0:T(8,128)(2,1)S(1)}, u32[]{:S(2)}, u32[]{:S(2)}) collective-permute-start(bf16[4,256,1024]{2,1,0:T(8,128)(2,1)S(1)} %slice_bitcast_fusion), channel_id=1, source_target_pairs={{0,8},{4,12},{8,0},{12,4},{1,9},{5,13},{9,1},{13,5},{2,10},{6,14},... | collective-permute-start | bytes 6291464 | tf_op jit(solution)/shard_map/ppermute | solution.py:410
  763.9 79.6 %collective-permute-start.93 = (bf16[4,256,1024]{2,1,0:T(8,128)(2,1)S(1)}, bf16[4,256,1024]{2,1,0:T(8,128)(2,1)S(1)}, u32[]{:S(2)}, u32[]{:S(2)}) collective-permute-start(bf16[4,256,1024]{2,1,0:T(8,128)(2,1)S(1)} %slice_bitcast_fusion.2), channel_id=1, source_target_pairs={{0,8},{4,12},{8,0},{12,4},{1,9},{5,13},{9,1},{13,5},{2,10},{6,14},... | collective-permute-start | bytes 6291464 | tf_op jit(solution)/shard_map/ppermute | solution.py:410
  770.7 24.5 %collective-permute-start.83 = (bf16[2,256,512]{2,1,0:T(8,128)(2,1)S(1)}, bf16[2,256,512]{2,1,0:T(8,128)(2,1)S(1)}, u32[]{:S(2)}, u32[]{:S(2)}) collective-permute-start(bf16[2,256,512]{2,1,0:T(8,128)(2,1)S(1)} %pad_maximum_fusion.25), channel_id=1, source_target_pairs={{0,3},{1,0},{2,1},{3,2},{4,7},{5,4},{6,5},{7,6},{8,11},{9,8},{10,9... | collective-permute-start | bytes 1572872 | tf_op jit(solution)/shard_map/ppermute | solution.py:405
  785.8 81.6 %collective-permute-start.71 = (bf16[384,1024]{1,0:T(8,128)(2,1)S(1)}, bf16[384,1024]{1,0:T(8,128)(2,1)S(1)}, u32[]{:S(2)}, u32[]{:S(2)}) collective-permute-start(bf16[384,1024]{1,0:T(8,128)(2,1)S(1)} %pad_maximum_fusion.19), channel_id=1, source_target_pairs={{0,3},{1,0},{2,1},{3,2},{4,7},{5,4},{6,5},{7,6},{8,11},{9,8},{10,9... | collective-permute-start | bytes 2359304 | tf_op jit(solution)/shard_map/ppermute | solution.py:405
  795.2 72.2 %collective-permute-start.70 = (bf16[384,1024]{1,0:T(8,128)(2,1)S(1)}, bf16[384,1024]{1,0:T(8,128)(2,1)S(1)}, u32[]{:S(2)}, u32[]{:S(2)}) collective-permute-start(bf16[384,1024]{1,0:T(8,128)(2,1)S(1)} %pad_maximum_fusion.18), channel_id=1, source_target_pairs={{0,1},{1,2},{2,3},{3,0},{4,5},{5,6},{6,7},{7,4},{8,9},{9,10},{10,1... | collective-permute-start | bytes 2359304 | tf_op jit(solution)/shard_map/ppermute | solution.py:405
  802.2 44.6 %collective-permute-start.100 = (bf16[128,1024]{1,0:T(8,128)(2,1)S(1)}, bf16[128,1024]{1,0:T(8,128)(2,1)S(1)}, u32[]{:S(2)}, u32[]{:S(2)}) collective-permute-start(bf16[128,1024]{1,0:T(8,128)(2,1)S(1)} %get-tuple-element.182), channel_id=1, source_target_pairs={{0,1},{1,2},{2,3},{3,0},{4,5},{5,6},{6,7},{7,4},{8,9},{9,10},{10,1... | collective-permute-start | bytes 786440 | tf_op jit(solution)/shard_map/ppermute | solution.py:405
  863.7 27.3 %collective-permute-start.103 = (bf16[256,1024]{1,0:T(8,128)(2,1)S(1)}, bf16[256,1024]{1,0:T(8,128)(2,1)S(1)}, u32[]{:S(2)}, u32[]{:S(2)}) collective-permute-start(bf16[256,1024]{1,0:T(8,128)(2,1)S(1)} %pad_maximum_fusion.31), channel_id=1, source_target_pairs={{0,3},{1,0},{2,1},{3,2},{4,7},{5,4},{6,5},{7,6},{8,11},{9,8},{10,9... | collective-permute-start | bytes 1572872 | tf_op jit(solution)/shard_map/ppermute | solution.py:405
  867.4 35.0 %collective-permute-start.95 = (bf16[256,1024]{1,0:T(8,128)(2,1)S(1)}, bf16[256,1024]{1,0:T(8,128)(2,1)S(1)}, u32[]{:S(2)}, u32[]{:S(2)}) collective-permute-start(bf16[256,1024]{1,0:T(8,128)(2,1)S(1)} %pad_maximum_fusion.28), channel_id=1, source_target_pairs={{0,1},{1,2},{2,3},{3,0},{4,5},{5,6},{6,7},{7,4},{8,9},{9,10},{10,1... | collective-permute-start | bytes 1572872 | tf_op jit(solution)/shard_map/ppermute | solution.py:405
  867.4 42.1 %collective-permute-start.97 = (bf16[256,1024]{1,0:T(8,128)(2,1)S(1)}, bf16[256,1024]{1,0:T(8,128)(2,1)S(1)}, u32[]{:S(2)}, u32[]{:S(2)}) collective-permute-start(bf16[256,1024]{1,0:T(8,128)(2,1)S(1)} %pad_maximum_fusion.29), channel_id=1, source_target_pairs={{0,3},{1,0},{2,1},{3,2},{4,7},{5,4},{6,5},{7,6},{8,11},{9,8},{10,9... | collective-permute-start | bytes 1572872 | tf_op jit(solution)/shard_map/ppermute | solution.py:405
  871.7 43.9 %collective-permute-start.73 = (bf16[128,1024]{1,0:T(8,128)(2,1)S(1)}, bf16[128,1024]{1,0:T(8,128)(2,1)S(1)}, u32[]{:S(2)}, u32[]{:S(2)}) collective-permute-start(bf16[128,1024]{1,0:T(8,128)(2,1)S(1)} %slice.730), channel_id=1, source_target_pairs={{0,3},{1,0},{2,1},{3,2},{4,7},{5,4},{6,5},{7,6},{8,11},{9,8},{10,9... | collective-permute-start | bytes 786440 | tf_op jit(solution)/shard_map/ppermute | solution.py:405
  880.0 38.9 %collective-permute-start.72 = (bf16[128,1024]{1,0:T(8,128)(2,1)S(1)}, bf16[128,1024]{1,0:T(8,128)(2,1)S(1)}, u32[]{:S(2)}, u32[]{:S(2)}) collective-permute-start(bf16[128,1024]{1,0:T(8,128)(2,1)S(1)} %slice.729), channel_id=1, source_target_pairs={{0,1},{1,2},{2,3},{3,0},{4,5},{5,6},{6,7},{7,4},{8,9},{9,10},{10,1... | collective-permute-start | bytes 786440 | tf_op jit(solution)/shard_map/ppermute | solution.py:405
  890.9 28.0 %collective-permute-start.91 = (bf16[256,512]{1,0:T(8,128)(2,1)S(1)}, bf16[256,512]{1,0:T(8,128)(2,1)S(1)}, u32[]{:S(2)}, u32[]{:S(2)}) collective-permute-start(bf16[256,512]{1,0:T(8,128)(2,1)S(1)} %get-tuple-element.241), channel_id=1, source_target_pairs={{0,16},{16,0},{1,17},{17,1},{2,18},{18,2},{3,19},{19,3},{4,20},{20... | collective-permute-start | bytes 786440 | tf_op jit(solution)/shard_map/ppermute | solution.py:410
  (100 other events, 1436.9 us)

commit v3 on v2

--- a/solution.py
+++ b/solution.py
@@ -398,6 +398,7 @@
 VMEM_LIMIT = 60 * 1024 * 1024
 ROW_BLOCK = 256
 CHUNKS = 2
+MICROSECOND = 1_000_000_000
 
 
 def ring(value, axis, by):
@@ -427,75 +428,64 @@
     return jnp.concatenate(picked, axis=-1)
 
 
-def after(values, *earlier):
-    return lax.optimization_barrier((values, earlier))[0]
-
-
-def exchange(blocks, own):
-    rows = blocks.shape[1]
-    half = rows // 2
+class Clock:
+    def __init__(self):
+        self.ended = ()
+
+    def hold(self, value):
+        return lax.optimization_barrier((value, self.ended))[0]
+
+    def tick(self, *ended):
+        self.ended = ended
+
+
+def exchange_near(blocks, own, hold):
+    half = blocks.shape[1] // 2
     far = pick(blocks, (own + 2) % 4)
     ahead = jnp.concatenate([pick(blocks, (own + 1) % 4), far[:half]], axis=0)
     behind = jnp.concatenate([pick(blocks, (own + 3) % 4), far[half:]], axis=0)
-    from_left = ring(ahead, "tensor", 1)
-    from_right = ring(behind, "tensor", -1)
-    first = ring(from_left[rows:], "tensor", 1)
-    second = ring(from_right[rows:], "tensor", -1)
+    return ring(hold(ahead), "tensor", 1), ring(hold(behind), "tensor", -1)
+
+
+def exchange_far(near, hold):
+    rows = near[0].shape[0] * 2 // 3
+    first = ring(hold(near[0][rows:]), "tensor", 1)
+    second = ring(hold(near[1][rows:]), "tensor", -1)
+    return first, second
+
+
+def exchanged(blocks, near, far, own):
+    rows = blocks.shape[1]
     result = jnp.zeros_like(blocks)
     result = place(result, pick(blocks, own), own)
-    result = place(result, from_left[:rows], (own + 3) % 4)
-    result = place(result, from_right[:rows], (own + 1) % 4)
-    return place(result, jnp.concatenate([first, second], axis=0), (own + 2) % 4)
-
-
-def with_other_core(pieces):
-    return tuple(pieces) + tuple(swap(piece, "dp", 1) for piece in pieces)
-
-
-def gather_across_first(shard):
-    pair = jnp.stack([shard, swap(shard, "dp", 2)])
-    left = ring(pair, "tensor", 1)
-    right = ring(pair, "tensor", -1)
-    far = jnp.stack([ring(left[0], "tensor", 1), ring(right[1], "tensor", -1)])
-    return with_other_core((pair, left, right, far))
-
-
-def gather_along_first(shard):
-    half = shard.shape[0] // 2
-    left = ring(shard, "tensor", 1)
-    right = ring(shard, "tensor", -1)
-    far = jnp.concatenate(
-        [ring(left[:half], "tensor", 1), ring(right[half:], "tensor", -1)], axis=0
-    )
-    pieces = [jnp.stack([part, swap(part, "dp", 2)]) for part in (shard, left, right, far)]
-    return with_other_core(pieces)
+    result = place(result, near[0][:rows], (own + 3) % 4)
+    result = place(result, near[1][:rows], (own + 1) % 4)
+    return place(result, jnp.concatenate(far, axis=0), (own + 2) % 4)
 
 
 def add_wide(left, right):
     return (left.astype(jnp.float32) + right.astype(jnp.float32)).astype(jnp.bfloat16)
 
 
-def reduce_ring(blocks):
-    own, left, right, far = blocks
-    half = own.shape[0] // 2
-    to_right = ring(far[:half], "tensor", 1)
-    to_left = ring(far[half:], "tensor", -1)
-    right = jnp.concatenate([add_wide(right[:half], to_right), right[half:]], axis=0)
-    left = jnp.concatenate([left[:half], add_wide(left[half:], to_left)], axis=0)
-    got_left = ring(right, "tensor", 1)
-    got_right = ring(left, "tensor", -1)
-    total = own.astype(jnp.float32) + got_left.astype(jnp.float32) + got_right.astype(jnp.float32)
+def ring_first(blocks, hold):
+    far = blocks[3]
+    half = far.shape[0] // 2
+    to_right = ring(hold(far[:half]), "tensor", 1)
+    to_left = ring(hold(far[half:]), "tensor", -1)
+    return to_right, to_left
+
+
+def ring_second(blocks, got, hold):
+    _, left, right, _ = blocks
+    half = left.shape[0] // 2
+    right = jnp.concatenate([add_wide(right[:half], got[0]), right[half:]], axis=0)
+    left = jnp.concatenate([left[:half], add_wide(left[half:], got[1])], axis=0)
+    return ring(hold(right), "tensor", 1), ring(hold(left), "tensor", -1)
+
+
+def ring_total(own, got):
+    total = own.astype(jnp.float32) + got[0].astype(jnp.float32) + got[1].astype(jnp.float32)
     return total.astype(jnp.bfloat16)
-
-
-def reduce_across_last(shared):
-    own = reduce_ring([shared[k] for k in range(4)])
-    return add_wide(own[0], swap(own[1], "dp", 2))
-
-
-def reduce_along_last(shared):
-    own = add_wide(shared[:, 0], swap(shared[:, 1], "dp", 2))
-    return reduce_ring([own[k] for k in range(4)])
 
 
 def normalised(x):
@@ -531,7 +521,7 @@
     )
 
 
-def call(body, name, grid, ins, outs, scratch=(), filled=()):
+def call(body, name, flops, grid, ins, outs, scratch=(), filled=()):
     count = len(ins)
 
     def run(*refs):
@@ -547,6 +537,7 @@
         out_shape=[jax.ShapeDtypeStruct(shape, kind) for shape, kind, _, _ in outs],
         scratch_shapes=list(scratch),
         input_output_aliases={count + i: i for i in range(len(filled))},
+        cost_estimate=pl.CostEstimate(flops=flops, bytes_accessed=1 << 20, transcendentals=0),
         compiler_params=pltpu.CompilerParams(
             vmem_limit_bytes=VMEM_LIMIT, dimension_semantics=("arbitrary",) * len(grid)
         ),
@@ -614,6 +605,7 @@
     return call(
         qkv_body,
         "norm_qkv",
+        rows * 13 * MICROSECOND // 1024,
         (rows // ROW_BLOCK,),
         [rows_of(x, first), whole(vecs), whole(shift)]
         + [rows_of(t, at) for t in tables]
@@ -658,6 +650,7 @@
     return call(
         attend_body,
         "attend",
+        length * 19 * MICROSECOND // 1024,
         (groups,),
         [
             (qkv, (length, 128), lambda i: (0, 3 * i)),
@@ -728,6 +721,7 @@
     return call(
         mlp_body,
         "mlp_out",
+        rows * 32 * MICROSECOND // 1024,
         (rows // ROW_BLOCK,),
         [rows_of(ctx, at), rows_of(ln_m, at), whole(shift)]
         + matrix(narrow, heads // 4, 3)
@@ -772,6 +766,7 @@
     return call(
         mlp_back_body,
         "mlp_back",
+        rows * 15 * MICROSECOND // 1024,
         (rows // ROW_BLOCK,),
         [rows_of(g, first), rows_of(slope, at)]
         + matrix(narrow, heads // 4, 3)
@@ -828,6 +823,7 @@
     return call(
         attend_back_body,
         "attend_back",
+        length * 26 * MICROSECOND // 1024,
         (groups,),
         [
             (qkv, (length, 128), lambda i: (0, 3 * i)),
@@ -872,6 +868,7 @@
     return call(
         norm_back_body,
         "norm_back",
+        rows * 21 * MICROSECOND // 1024,
         (rows // ROW_BLOCK,),
         [rows_of(x, first), rows_of(d_qkv, at), rows_of(d_up, at), whole(vecs)]
         + matrix(narrow, n_qkv, 0)
@@ -918,6 +915,7 @@
     return call(
         partial(weight_grad_body, tuple(len(group) for group in lefts)),
         "weight_grad",
+        length * 14 * MICROSECOND // 1024,
         (4,),
         [whole(left) for group in lefts for left in group]
         + [(r, (length, n), lambda i: (0, i)) for r, n in zip(rights, sizes)],
@@ -958,11 +956,8 @@
     down_halves = w_down[0].T.reshape(rows, 2, -1).transpose(1, 0, 2)
     n_qkv, n_out, n_up = qkv_halves.shape[2], out_halves.shape[2], up_halves.shape[2]
 
-    def both_layers(halves):
-        keep = pick(halves, section)
-        got = swap(pick(halves, 1 - section), "section", 1)
-        return jnp.where(first_section, keep, got), jnp.where(first_section, got, keep)
-
+    narrow = jnp.stack([jnp.concatenate([qkv_halves[h], out_halves[h]], axis=1) for h in (0, 1)])
+    broad = jnp.stack([jnp.concatenate([up_halves[h], down_halves[h]], axis=1) for h in (0, 1)])
     small = jnp.concatenate(
         [
             norm_gains[0].reshape(-1),
@@ -971,41 +966,84 @@
             b_up[0].reshape(-1).astype(jnp.float32),
         ]
     )
-    other = swap(small, "section", 1)
-    small = jnp.where(first_section, jnp.stack([small, other]), jnp.stack([other, small]))
-    small = jnp.stack([small, swap(small, "dp", 1)])
+    clock = Clock()
+    hold, tick = clock.hold, clock.tick
+
+    def pass_half(halves):
+        return swap(hold(pick(halves, 1 - section)), "section", 1)
+
+    def by_layer(halves, got):
+        keep = pick(halves, section)
+        return jnp.where(first_section, keep, got), jnp.where(first_section, got, keep)
+
+    def x_swap(value):
+        return swap(hold(value), "dp", 2)
+
+    def core_swap(value):
+        return swap(hold(value), "dp", 1)
+
+    def y_swap(value):
+        return swap(hold(value), "section", 1)
+
+    def both_ways(value):
+        value = hold(value)
+        return ring(value, "tensor", 1), ring(value, "tensor", -1)
+
+    def far_narrow(left, right):
+        return ring(hold(left[0]), "tensor", 1), ring(hold(right[1]), "tensor", -1)
+
+    def far_broad(left, right):
+        half = left.shape[0] // 2
+        return ring(hold(left[:half]), "tensor", 1), ring(hold(right[half:]), "tensor", -1)
+
+    got_narrow = pass_half(narrow)
+    got_small = swap(small, "section", 1)
+    tick(got_narrow, got_small)
+    narrow_shards = by_layer(narrow, got_narrow)
+    small = jnp.where(first_section, jnp.stack([small, got_small]), jnp.stack([got_small, small]))
+    blocks = acts_in[:, :, 0, :]
+    near = exchange_near(blocks, along, hold)
+    got_broad = pass_half(broad)
+    pair = jnp.stack([narrow_shards[0], x_swap(narrow_shards[0])])
+    small = jnp.stack([small, core_swap(small)])
     small = jnp.concatenate([small, swap(small, "dp", 2)])
-    small = jnp.stack(
-        [small, ring(small, "tensor", 1), ring(small, "tensor", -1), ring(small, "tensor", 2)]
-    )
-
-    narrow = jnp.stack([jnp.concatenate([qkv_halves[h], out_halves[h]], axis=1) for h in (0, 1)])
-    broad = jnp.stack([jnp.concatenate([up_halves[h], down_halves[h]], axis=1) for h in (0, 1)])
-    narrow_shards = both_layers(narrow)
-    acts = exchange(acts_in[:, :, 0, :], along).reshape(length, width)
+    tick(near, got_broad, pair, small)
+    broad_shards = by_layer(broad, got_broad)
+    far = exchange_far(near, hold)
+    left, right = both_ways(pair)
+    broad_own = jnp.stack([broad_shards[0], x_swap(broad_shards[0])])
+    small = jnp.stack([small, swap(hold(small), "tensor", 1)])
+    small = jnp.concatenate([small, swap(small, "tensor", 2)])
+    tick(far, left, right, broad_own, small)
+    acts = exchanged(blocks, near, far, along).reshape(length, width)
     acts = relative(acts, across)
-    broad_shards = both_layers(broad)
-
-    mats = [(gather_across_first(narrow_shards[0]), gather_along_first(broad_shards[0]))]
-    later = after((narrow_shards[1], broad_shards[1]), mats[0][1][:4])
-    mats.append((gather_across_first(later[0]), gather_along_first(later[1])))
+    narrow_far = far_narrow(left, right)
+    others = [core_swap(pair), core_swap(left), core_swap(right)]
+    tick(narrow_far, others)
+    narrow_far = jnp.stack(narrow_far)
+    others.append(core_swap(narrow_far))
+    narrow_zero = (pair, left, right, narrow_far, *others)
+    tick(others[3])
 
     share = norm_gains.shape[2]
     vec_part = small[..., : 6 * share].reshape(4, 4, 2, 6, share)
     offsets = jnp.array(FAR_ORDER, jnp.int32)
     order = jnp.stack([pick(offsets, (k - along) % 4) for k in range(4)])
-    vec_part = jnp.stack([pick(vec_part, order[k]) for k in range(4)])
+    slots = [jnp.bitwise_xor((along + k) % 4, along) for k in (0, 3, 1, 2)]
+    vec_part = jnp.stack([pick(vec_part, jnp.bitwise_xor(along, k)) for k in range(4)])
     vecs_full = vec_part.transpose(2, 3, 1, 0, 4).reshape(2, 6, width)
     at = 6 * share
     share_q = b_qkv.shape[2]
     dp_order = [jnp.bitwise_xor(across, k) for k in range(4)]
     qkv_bias = small[..., at : at + heads * share_q].reshape(4, 4, 2, heads, share_q)
+    qkv_bias = jnp.stack([pick(qkv_bias, k) for k in slots])
     qkv_bias = jnp.stack([pick(qkv_bias, i, 1) for i in dp_order], axis=1)
     qkv_bias = qkv_bias.transpose(2, 0, 3, 1, 4).reshape(2, 4, 2, heads // 2, 3, 64)
     qkv_bias = pick(qkv_bias, section, 2).transpose(0, 1, 3, 2, 4).reshape(2, 1, -1)
     at += heads * share_q
     bias_rows, share_u = b_up.shape[1], b_up.shape[2]
     up_bias = small[..., at : at + bias_rows * share_u].reshape(4, 4, 2, bias_rows, share_u)
+    up_bias = jnp.stack([pick(up_bias, k) for k in slots])
     up_bias = jnp.stack([pick(up_bias, i, 1) for i in dp_order], axis=1)
     up_bias = up_bias.transpose(2, 0, 3, 1, 4).reshape(2, 4, 2, bias_rows // 2, 4 * share_u)
     up_bias = pick(up_bias, section, 2).reshape(2, 1, -1)
@@ -1015,119 +1053,246 @@
     chunk = length // CHUNKS
     starts = [i * chunk for i in range(CHUNKS)]
 
-    sources = [(acts, a) for a in starts]
-    inputs = [acts[a : a + chunk] for a in starts]
-    kept = []
-    grads_in = None
-    for layer in (0, 1):
-        narrow, broad = mats[layer]
+    all_vecs = [
+        jnp.concatenate([v[0:1], v[2:3], v[1:2], v[3:4], zero_rows], axis=0) for v in vecs_full
+    ]
+
+    def project(layer, i, source, pieces, filled):
+        return run_qkv(
+            source, all_vecs[layer], qkv_bias[layer], tables, pieces, starts[i], chunk, filled
+        )
+
+    def feed(layer, i, ctx, ln_m, narrow, broad, filled):
+        *filled, part = run_mlp(
+            hold(ctx), ln_m, up_bias[layer], narrow, broad, starts[i], chunk, filled
+        )
+        return filled, part
+
+    def join(layer, before, part, got):
+        total = part.astype(jnp.float32) + got.astype(jnp.float32)
         full = vecs_full[layer]
-        vecs = jnp.concatenate(
-            [full[0:1], full[2:3], full[1:2], full[3:4], zero_rows], axis=0
-        )
-        first = ()
-        for i in range(CHUNKS):
-            first = run_qkv(
-                sources[i], vecs, qkv_bias[layer], tables, narrow, starts[i], chunk, first
-            )
-        ln_a, ln_m, qkv = first
-        if layer == 1:
-            qkv = after(qkv, grads_in)
-        ctx, lse = run_attend(qkv)
-        if layer == 0:
-            given = after(cotangent[:, :, 0, :], ctx, mats[1][1][:4])
-            grads_in = exchange(given, along).reshape(length, width)
-            grads_in = relative(grads_in, across)
-        outs, first = [], ()
-        for i in range(CHUNKS):
-            *first, part = run_mlp(
-                ctx, ln_m, up_bias[layer], narrow, broad, starts[i], chunk, first
-            )
-            got = swap(part, "section", 1)
-            total = part.astype(jnp.float32) + got.astype(jnp.float32)
-            total = inputs[i].astype(jnp.float32) + total + (full[4] + full[5])
-            outs.append(total.astype(bf))
-        kept.append((sources, vecs, ln_a, ln_m, qkv, ctx, lse, *first, outs))
-        inputs = outs
-        sources = [(out, 0) for out in outs]
-
-    def deliver(values):
-        return exchange(relative(values, across).reshape(4, positions, width), along)
-
-    acts_local = deliver(
-        jnp.where(first_section, jnp.concatenate(kept[0][9]), jnp.concatenate(kept[1][9]))
-    )
-
-    sources = [(grads_in, a) for a in starts]
-    upstream = [grads_in[a : a + chunk] for a in starts]
-    whole_up = [grads_in]
-    reduced = [None, None]
-    vectors = [None, None]
-    layer_grads = [None, None]
-    for layer in (1, 0):
-        narrow, broad = mats[layer]
-        x_list, vecs, ln_a, ln_m, qkv, ctx, lse, act, slope, _ = kept[layer]
-        first, sum_up, sum_g = (), 0.0, 0.0
-        if layer == 0:
-            sources = [(after(down, acts_local), at) for down, at in sources]
-        for i in range(CHUNKS):
-            *first, up_term, g_term = run_mlp_back(
-                sources[i], slope, narrow, broad, starts[i], chunk, ctx.shape[1], first
-            )
-            sum_up, sum_g = sum_up + up_term, sum_g + g_term
-        d_up, d_ctx = first
-        if layer == 0:
-            keep, send = run_weight_grad([[ln_m], whole_up], [d_up, act])
-            broad_sum = add_wide(keep, swap(send, "dp", 1))
-            d_ctx = after(d_ctx, keep)
-        d_qkv, sum_qkv = run_attend_back(qkv, d_ctx, lse, tables)
-        downs, norm_sums = [], 0.0
-        for i in range(CHUNKS):
-            part, sums = run_norm_back(
-                x_list[i], d_qkv, d_up, vecs, narrow, broad, starts[i], chunk
-            )
-            got = swap(part, "section", 1)
-            total = part.astype(jnp.float32) + got.astype(jnp.float32)
-            downs.append((upstream[i].astype(jnp.float32) + total).astype(bf))
-            norm_sums = norm_sums + sums[:4]
-        if layer == 1:
-            keep, send = run_weight_grad([[ln_m], whole_up], [d_up, act])
-            broad_sum = add_wide(keep, swap(send, "dp", 1))
-        keep, send = run_weight_grad([[ln_a], whole_up], [d_qkv, ctx])
-        narrow_sum = add_wide(keep, swap(send, "dp", 1))
-        reduced[layer] = (reduce_across_last(narrow_sum), reduce_along_last(broad_sum))
-        vectors[layer] = (norm_sums, sum_g, sum_qkv, sum_up)
-        layer_grads[layer] = jnp.concatenate(downs, axis=0)
-        upstream = downs
-        whole_up = downs
-        sources = [(down, 0) for down in downs]
-
-    grad_local = deliver(jnp.where(first_section, layer_grads[0], layer_grads[1]))
-
-    def whole_layer(first, second):
-        keep = jnp.where(first_section, first, second)
-        got = swap(jnp.where(first_section, second, first), "section", 1)
-        keep, got = keep.astype(jnp.float32), got.astype(jnp.float32)
-        return jnp.where(first_section, jnp.stack([keep, got], 1), jnp.stack([got, keep], 1))
-
-    narrow_out = whole_layer(reduced[0][0], reduced[1][0])
-    broad_out = whole_layer(reduced[0][1], reduced[1][1])
-    grad_qkv = narrow_out[..., :n_qkv].reshape(rows, 2, 3, 2, 64)
-    grad_qkv = grad_qkv.transpose(0, 1, 3, 2, 4).reshape(rows, -1)
-    grad_out = narrow_out[..., n_qkv:].reshape(rows, -1).T
-    grad_up = broad_out[..., :n_up].reshape(rows, -1)
-    grad_down = broad_out[..., n_up:].reshape(rows, -1).T
+        return (before.astype(jnp.float32) + total + (full[4] + full[5])).astype(bf)
+
+    acts = hold(acts)
+    first = project(0, 0, (acts, 0), narrow_zero, ())
+    first = project(0, 1, (acts, chunk), narrow_zero, first)
+    broad_left, broad_right = both_ways(broad_shards[0])
+    tick(first, broad_left, broad_right)
+    ln_a0, ln_m0, qkv0 = first
+    ctx0, lse0 = run_attend(hold(qkv0))
+    broad_far = far_broad(broad_left, broad_right)
+    got_left, got_right = x_swap(broad_left), x_swap(broad_right)
+    tick(ctx0, broad_far, got_left, got_right)
+    broad_left = jnp.stack([broad_left, got_left])
+    broad_right = jnp.stack([broad_right, got_right])
+    broad_far = jnp.concatenate(broad_far, axis=0)
+    got_far = x_swap(broad_far)
+    others = [core_swap(broad_own), core_swap(broad_left), core_swap(broad_right)]
+    tick(got_far, others)
+    broad_far = jnp.stack([broad_far, got_far])
+    others.append(core_swap(broad_far))
+    broad_zero = (broad_own, broad_left, broad_right, broad_far, *others)
+    pair = jnp.stack([narrow_shards[1], x_swap(narrow_shards[1])])
+    tick(others[3], pair)
+    first, part_a = feed(0, 0, ctx0, ln_m0, narrow_zero, broad_zero, ())
+    broad_left, broad_right = both_ways(broad_shards[1])
+    tick(part_a, broad_left, broad_right)
+    first, part_b = feed(0, 1, ctx0, ln_m0, narrow_zero, broad_zero, first)
+    act0, slope0 = first
+    got_a = y_swap(part_a)
+    left, right = both_ways(pair)
+    got_own = x_swap(broad_shards[1])
+    tick(part_b, got_a, left, right, got_own)
+    got_b = y_swap(part_b)
+    narrow_far = far_narrow(left, right)
+    got_left = x_swap(broad_left)
+    others = [core_swap(pair), core_swap(left), core_swap(right)]
+    x1_a = join(0, acts[:chunk], part_a, got_a)
+    tick(got_b, narrow_far, got_left, others)
+    x1_b = join(0, acts[chunk:], part_b, got_b)
+    narrow_far = jnp.stack(narrow_far)
+    others.append(core_swap(narrow_far))
+    narrow_one = (pair, left, right, narrow_far, *others)
+    tick(others[3], x1_a, x1_b)
+
+    first = project(1, 0, (hold(x1_a), 0), narrow_one, ())
+    first = project(1, 1, (x1_b, 0), narrow_one, first)
+    ln_a1, ln_m1, qkv1 = first
+    broad_far = far_broad(broad_left, broad_right)
+    got_right = x_swap(broad_right)
+    tick(first, broad_far, got_right)
+    ctx1, lse1 = run_attend(hold(qkv1))
+    broad_own = jnp.stack([broad_shards[1], got_own])
+    broad_left = jnp.stack([broad_left, got_left])
+    broad_right = jnp.stack([broad_right, got_right])
+    broad_far = jnp.concatenate(broad_far, axis=0)
+    got_far = x_swap(broad_far)
+    others = [core_swap(broad_own), core_swap(broad_left), core_swap(broad_right)]
+    tick(ctx1, got_far, others)
+    broad_far = jnp.stack([broad_far, got_far])
+    others.append(core_swap(broad_far))
+    broad_one = (broad_own, broad_left, broad_right, broad_far, *others)
+    tick(others[3])
+    first, part_a = feed(1, 0, ctx1, ln_m1, narrow_one, broad_one, ())
+    blocks = cotangent[:, :, 0, :]
+    near = exchange_near(blocks, along, hold)
+    tick(part_a, near)
+    first, part_b = feed(1, 1, ctx1, ln_m1, narrow_one, broad_one, first)
+    act1, slope1 = first
+    far = exchange_far(near, hold)
+    got_a = y_swap(part_a)
+    tick(part_b, far, got_a)
+
+    grads = exchanged(blocks, near, far, along).reshape(length, width)
+    grads = hold(relative(grads, across))
+    n_heads = ctx0.shape[1]
+
+    def back(i, source, slope, narrow, broad, filled):
+        *filled, up_term, g_term = run_mlp_back(
+            source, slope, narrow, broad, starts[i], chunk, n_heads, filled
+        )
+        return filled, up_term, g_term
+
+    first, up_a, g_a = back(0, (grads, 0), slope1, narrow_one, broad_one, ())
+    first, up_b, g_b = back(1, (grads, chunk), slope1, narrow_one, broad_one, first)
+    d_up1, d_ctx1 = first
+    sums_one = [None, g_a + g_b, None, up_a + up_b]
+    got_b = y_swap(part_b)
+    tick(first, got_b)
+    x2 = jnp.concatenate(
+        [join(1, x1_a, part_a, got_a), join(1, x1_b, part_b, got_b)], axis=0
+    )
+    x1 = jnp.concatenate([x1_a, x1_b], axis=0)
+
+    def to_blocks(values):
+        return relative(values, across).reshape(4, positions, width)
+
+    out_blocks = to_blocks(jnp.where(first_section, x1, x2))
+    d_qkv1, sums_one[2] = run_attend_back(qkv1, hold(d_ctx1), lse1, tables)
+    out_near = exchange_near(out_blocks, along, hold)
+    tick(d_qkv1, out_near)
+    part_a, sum_a = run_norm_back(
+        (x1_a, 0), hold(d_qkv1), d_up1, all_vecs[1], narrow_one, broad_one, 0, chunk
+    )
+    out_far = exchange_far(out_near, hold)
+    tick(part_a, out_far)
+    acts_local = exchanged(out_blocks, out_near, out_far, along)
+    part_b, sum_b = run_norm_back(
+        (x1_b, 0), hold(d_qkv1), d_up1, all_vecs[1], narrow_one, broad_one, chunk, chunk
+    )
+    sums_one[0] = (sum_a + sum_b)[:4]
+    keep_broad, send = run_weight_grad([[hold(ln_m1)], [grads]], [d_up1, act1])
+    got_a = y_swap(part_a)
+    tick(part_b, keep_broad, got_a)
+    keep_narrow, send_narrow = run_weight_grad([[hold(ln_a1)], [grads]], [d_qkv1, ctx1])
+    got_b = y_swap(part_b)
+    got_core = core_swap(send)
+    tick(keep_narrow, got_b, got_core)
+
+    def lower(above, part, got):
+        total = part.astype(jnp.float32) + got.astype(jnp.float32)
+        return (above.astype(jnp.float32) + total).astype(bf)
+
+    g1_a = hold(lower(grads[:chunk], part_a, got_a))
+    g1_b = hold(lower(grads[chunk:], part_b, got_b))
+    broad_sum = add_wide(keep_broad, got_core)
+    first, up_a, g_a = back(0, (g1_a, 0), slope0, narrow_zero, broad_zero, ())
+    first, up_b, g_b = back(1, (g1_b, 0), slope0, narrow_zero, broad_zero, first)
+    d_up0, d_ctx0 = first
+    sums_zero = [None, g_a + g_b, None, up_a + up_b]
+    got_core = core_swap(send_narrow)
+    got_x = [x_swap(broad_sum[2:, 1])]
+    tick(first, got_core, got_x)
+    narrow_sum = add_wide(keep_narrow, got_core)
+    narrow_sum = [narrow_sum[k] for k in range(4)]
+    keep_broad, send = run_weight_grad([[hold(ln_m0)], [g1_a, g1_b]], [d_up0, act0])
+    narrow_got = ring_first(narrow_sum, hold)
+    got_x.append(x_swap(broad_sum[:2, 1]))
+    tick(keep_broad, narrow_got, got_x)
+
+    def after_x(total, got):
+        late = add_wide(total[2:, 0], got[0])
+        early = add_wide(total[:2, 0], got[1])
+        return [early[0], early[1], late[0], late[1]]
+
+    broad_one_sum = after_x(broad_sum, got_x)
+    d_qkv0, sums_zero[2] = run_attend_back(qkv0, hold(d_ctx0), lse0, tables)
+    narrow_got = ring_second(narrow_sum, narrow_got, hold)
+    broad_got = ring_first(broad_one_sum, hold)
+    got_core = core_swap(send)
+    tick(d_qkv0, narrow_got, broad_got, got_core)
+    narrow_total = ring_total(narrow_sum[0], narrow_got)
+    broad_sum = add_wide(keep_broad, got_core)
+    part_a, sum_a = run_norm_back(
+        (acts, 0), hold(d_qkv0), d_up0, all_vecs[0], narrow_zero, broad_zero, 0, chunk
+    )
+    broad_got = ring_second(broad_one_sum, broad_got, hold)
+    got_x = x_swap(narrow_total[1])
+    tick(part_a, broad_got, got_x)
+    one_narrow = add_wide(narrow_total[0], got_x)
+    one_broad = ring_total(broad_one_sum[0], broad_got)
+    part_b, sum_b = run_norm_back(
+        (acts, chunk), hold(d_qkv0), d_up0, all_vecs[0], narrow_zero, broad_zero, chunk, chunk
+    )
+    sums_zero[0] = (sum_a + sum_b)[:4]
+    keep_narrow, send_narrow = run_weight_grad([[hold(ln_a0)], [g1_a, g1_b]], [d_qkv0, ctx0])
+    got_a = y_swap(part_a)
+    got_x = [x_swap(broad_sum[2:, 1])]
+    tick(part_b, keep_narrow, got_a, got_x)
 
     flat = []
-    for norm_sums, sum_g, sum_qkv, sum_up in vectors:
+    for norm_sums, sum_g, sum_qkv, sum_up in (sums_zero, sums_one):
         feature = relative(jnp.concatenate([norm_sums, sum_g], axis=0), across)
         q_sum = sum_qkv.reshape(4, 3, 2, 64).transpose(0, 2, 1, 3).reshape(4, -1)
         both = jnp.concatenate([q_sum, sum_up.reshape(4, -1)], axis=1)
         both = jnp.stack([pick(both, order[k]) for k in range(4)])
         flat.append(jnp.concatenate([feature.reshape(-1), both.reshape(-1)]))
     flat = jnp.stack(flat)
-    for axis, bit in (("dp", 1), ("dp", 2), ("tensor", 1), ("tensor", 2)):
-        flat = flat + swap(flat, axis, bit)
+    got_b = y_swap(part_b)
+    got_x.append(x_swap(broad_sum[:2, 1]))
+    late = add_wide(broad_sum[2:, 0], got_x[0])
+    broad_got = ring_first([None, None, late[0], late[1]], hold)
+    got_core = core_swap(send_narrow)
+    tick(got_b, got_x, broad_got, got_core)
+    flat = flat + core_swap(flat)
+    early = add_wide(broad_sum[:2, 0], got_x[1])
+    broad_zero_sum = [early[0], early[1], late[0], late[1]]
+    narrow_sum = add_wide(keep_narrow, got_core)
+    narrow_sum = [narrow_sum[k] for k in range(4)]
+    grads_low = jnp.concatenate([lower(g1_a, part_a, got_a), lower(g1_b, part_b, got_b)], axis=0)
+    g1 = jnp.concatenate([g1_a, g1_b], axis=0)
+    out_blocks = to_blocks(jnp.where(first_section, grads_low, g1))
+    narrow_got = ring_first(narrow_sum, hold)
+    broad_got = ring_second(broad_zero_sum, broad_got, hold)
+    tick(narrow_got, broad_got, flat)
+    flat = flat + x_swap(flat)
+    zero_broad = ring_total(broad_zero_sum[0], broad_got)
+    narrow_got = ring_second(narrow_sum, narrow_got, hold)
+    out_near = exchange_near(out_blocks, along, hold)
+    broad_send = y_swap(jnp.where(first_section, one_broad, zero_broad))
+    tick(narrow_got, out_near, broad_send, flat)
+    flat = flat + swap(hold(flat), "tensor", 1)
+    narrow_total = ring_total(narrow_sum[0], narrow_got)
+    out_far = exchange_far(out_near, hold)
+    zero_narrow = add_wide(narrow_total[0], x_swap(narrow_total[1]))
+    tick(out_far, zero_narrow, flat)
+    flat = flat + swap(hold(flat), "tensor", 2)
+    grad_local = exchanged(out_blocks, out_near, out_far, along)
+    narrow_send = y_swap(jnp.where(first_section, one_narrow, zero_narrow))
+
+    def whole_layer(keep_pair, got):
+        keep = jnp.where(first_section, *keep_pair).astype(jnp.float32)
+        got = got.astype(jnp.float32)
+        return jnp.where(first_section, jnp.stack([keep, got], 1), jnp.stack([got, keep], 1))
+
+    narrow_out = whole_layer((zero_narrow, one_narrow), narrow_send)
+    broad_out = whole_layer((zero_broad, one_broad), broad_send)
+    grad_qkv = narrow_out[..., :n_qkv].reshape(rows, 2, 3, 2, 64)
+    grad_qkv = grad_qkv.transpose(0, 1, 3, 2, 4).reshape(rows, -1)
+    grad_out = narrow_out[..., n_qkv:].reshape(rows, -1).T
+    grad_up = broad_out[..., :n_up].reshape(rows, -1)
+    grad_down = broad_out[..., n_up:].reshape(rows, -1).T
+
     keep = pick(flat, section)
     mine = pick(flat, 1 - section)
     got = swap(mine, "section", 1)

time: 939 us -> 902 us (0.961)
  waiting for transfers between devices: 335 us -> 269 us
  local copies, waits for them, and re-layouts: 74.3 us -> 100 us
  other arithmetic: 73.4 us -> 85.6 us
    ppermute x54 -> x58, waiting for transfers between devices: 152 us -> 112 us  [swap(): return lax.ppermute(value, axis, [(i, i ^ bit) for i in range(length)])]
    ppermute x51 -> x48, waiting for transfers between devices: 183 us -> 158 us  [ring(): lax.ppermute(value, axis, [(i, (i + by) % length) for i in range(length)])]
    ppermute x51 -> x48, starting transfers between devices: 88.2 us -> 74 us  [ring(): lax.ppermute(value, axis, [(i, (i + by) % length) for i in range(length)])]
    optimization_barrier x0 -> x2, local copies, waits for them, and re-layouts: none -> 9.84 us  [hold(): return lax.optimization_barrier((value, self.ended))[0]]
    ppermute x54 -> x58, starting transfers between devices: 39.1 us -> 45.6 us  [swap(): return lax.ppermute(value, axis, [(i, i ^ bit) for i in range(length)])]
    convert_element_type x10 -> x12, other arithmetic: 14.8 us -> 20.3 us  [add_wide(): (left.astype(jnp.float32) + right.astype(jnp.float32)).astype(jnp.bfloat16)]
  transfers between devices with their start and end apart: 105 -> 106, of which waited for: 43 -> 42; matrix products, arithmetic and copies ran while one was open for 14% -> 17% of each run, Pallas kernels for 30% -> 34%
where the time goes in v3:
time: 902 us; the launch traced here: 892 us
  Pallas kernels  306 us (34%)
  waiting for transfers between devices  269 us (30%)
  starting transfers between devices  120 us (13%)
  local copies, waits for them, and re-layouts  100 us (11%)
  other arithmetic  85.6 us (9%)
  between operations  11.1 us (1%)
    pallas_call x24, Pallas kernels, call(): pl.pallas_call(run, name=name, grid=grid, in_specs=[pl.BlockSpec(block, i...  306 us
    ppermute x48, waiting for transfers between devices, ring(): lax.ppermute(value, axis, [(i, (i + by) % length) for i in range(length)])  158 us
    ppermute x58, waiting for transfers between devices, swap(): return lax.ppermute(value, axis, [(i, i ^ bit) for i in range(length)])  112 us
    ppermute x48, starting transfers between devices, ring(): lax.ppermute(value, axis, [(i, (i + by) % length) for i in range(length)])  74 us
    ppermute x58, starting transfers between devices, swap(): return lax.ppermute(value, axis, [(i, i ^ bit) for i in range(length)])  45.6 us
    convert_element_type x12, other arithmetic, add_wide(): (left.astype(jnp.float32) + right.astype(jnp.float32)).astype(jnp.bfloat16)  20.3 us
    unnamed x171, local copies, waits for them, and re-layouts  18.5 us
  transfers between devices with their start and end apart: 106, of which 42 were waited for; matrix products, arithmetic and copies ran while one was open for 17% of the time, Pallas kernels for 34%

profile of v3, /device:TPU:0, one launch (start us, length us, event | category | flops | bytes accessed | tf_op | source)
XLA Modules:
  0.0 892.2 jit_solution(79177271299085938)
XLA Ops:
  4.0 3.0 collective-permute-start
  39.9 14.5 %collective-permute-done.3 = bf16[384,1024]{1,0:T(8,128)(2,1)} collective-permute-done((bf16[384,1024]{1,0:T(8,128)(2,1)}, bf16[384,1024]{1,0:T(8,128)(2,1)}, u32[]{:S(2)}, u32[]{:S(2)}) %collective-permute-start.3) | collective-permute-done | bytes 786464 | tf_op jit(solution)/shard_map/ppermute | solution.py:406
  64.6 17.9 %collective-permute-done.13 = f32[4,2,832]{2,1,0:T(2,128)S(1)} collective-permute-done((f32[4,2,832]{2,1,0:T(2,128)S(1)}, f32[4,2,832]{2,1,0:T(2,128)S(1)}, u32[]{:S(2)}, u32[]{:S(2)}) %collective-permute-start.13) | collective-permute-done | bytes 26656 | tf_op jit(solution)/shard_map/ppermute | solution.py:411
  90.3 7.8 collective-permute-done.9
  100.7 3.9 collective-permute-start.16
  105.2 5.4 collective-permute-done.15
  110.6 4.3 collective-permute-done.16
  127.9 6.4 norm_qkv.4
  134.3 6.4 norm_qkv.5
  140.7 9.2 %collective-permute-done.22 = bf16[256,1024]{1,0:T(8,128)(2,1)S(1)} collective-permute-done((bf16[256,1024]{1,0:T(8,128)(2,1)S(1)}, bf16[256,1024]{1,0:T(8,128)(2,1)S(1)}, u32[]{:S(2)}, u32[]{:S(2)}) %collective-permute-start.22) | collective-permute-done | bytes 524320 | tf_op jit(solution)/shard_map/ppermute | solution.py:406
  155.4 19.0 %attend.2 = (bf16[1024,512]{1,0:T(8,128)(2,1)}, f32[4,8,1024]{2,1,0:T(8,128)}) custom-call(bf16[1024,1536]{1,0:T(8,128)(2,1)} %get-tuple-element.216.refs_0_.refs_1_.refs_2_, bf16[1024,1536]{1,0:T(8,128)(2,1)} %get-tuple-element.216.refs_0_.refs_1_.refs_2_, bf16[1024,1536]{1,0:T(8,128)(2,1)} %get-tuple-element.216.refs_0_.refs_1_.refs_2_), custom_call_target="tpu_custom_call" | custom-call | flops 19000000512 | bytes 1048576 | tf_op jit(solution)/shard_map/attend/pallas_call | solution.py:530
  182.0 12.6 %collective-permute-done.27 = bf16[256,1024]{1,0:T(8,128)(2,1)S(1)} collective-permute-done((bf16[256,1024]{1,0:T(8,128)(2,1)S(1)}, bf16[256,1024]{1,0:T(8,128)(2,1)S(1)}, u32[]{:S(2)}, u32[]{:S(2)}) %collective-permute-start.27) | collective-permute-done | bytes 524320 | tf_op jit(solution)/shard_map/ppermute | solution.py:411
  203.2 6.0 collective-permute-done.32
  210.6 3.7 collective-permute-start.34
  214.3 15.7 %mlp_out.4 = (bf16[1024,2048]{1,0:T(8,128)(2,1)}, bf16[1024,2048]{1,0:T(8,128)(2,1)}, bf16[512,1024]{1,0:T(8,128)(2,1)}) custom-call(bf16[1024,512]{1,0:T(8,128)(2,1)} %get-tuple-element.232.refs_0_.refs_4_, bf16[1024,1024]{1,0:T(8,128)(2,1)} %get-tuple-element.311.refs_1_.refs_0_, f32[1,2048]{1,0:T(1,128)} %bitcast.435, ...), custom_call_target="tpu_custom_call" | custom-call | flops 16000000000 | bytes 1048576 | tf_op jit(solution)/shard_map/mlp_out/pallas_call | solution.py:530
  229.9 5.1 collective-permute-done.34
  241.9 15.8 %mlp_out.5 = (bf16[1024,2048]{1,0:T(8,128)(2,1)}, bf16[1024,2048]{1,0:T(8,128)(2,1)}, bf16[512,1024]{1,0:T(8,128)(2,1)}) custom-call(bf16[1024,512]{1,0:T(8,128)(2,1)} %get-tuple-element.232.refs_0_.refs_4_, bf16[1024,1024]{1,0:T(8,128)(2,1)} %get-tuple-element.311.refs_1_.refs_0_, ...), custom_call_target="tpu_custom_call", output_to_operand_aliasing={{0}: (27, {}), {1}: (28, {})} | custom-call | flops 16000000000 | bytes 1048576 | tf_op jit(solution)/shard_map/mlp_out/pallas_call | solution.py:530
  257.7 3.2 collective-permute-done.37.refs_8_.refs_5_.refs_4_.refs_6_
  271.5 5.7 collective-permute-done.40
  288.5 4.1 add_convert_fusion.11
  297.2 6.4 norm_qkv.6
  303.6 6.3 norm_qkv.7
  314.4 19.1 %attend.3 = (bf16[1024,512]{1,0:T(8,128)(2,1)}, f32[4,8,1024]{2,1,0:T(8,128)}) custom-call(bf16[1024,1536]{1,0:T(8,128)(2,1)} %get-tuple-element.256.refs_0_.refs_1_.refs_2_, bf16[1024,1536]{1,0:T(8,128)(2,1)} %get-tuple-element.256.refs_0_.refs_1_.refs_2_, bf16[1024,1536]{1,0:T(8,128)(2,1)} %get-tuple-element.256.refs_0_.refs_1_.refs_2_), custom_call_target="tpu_custom_call" | custom-call | flops 19000000512 | bytes 1048576 | tf_op jit(solution)/shard_map/attend/pallas_call | solution.py:530
  341.9 15.7 %mlp_out.6 = (bf16[1024,2048]{1,0:T(8,128)(2,1)}, bf16[1024,2048]{1,0:T(8,128)(2,1)}, bf16[512,1024]{1,0:T(8,128)(2,1)}) custom-call(bf16[1024,512]{1,0:T(8,128)(2,1)} %get-tuple-element.268.refs_0_.refs_3_, bf16[1024,1024]{1,0:T(8,128)(2,1)} %get-tuple-element.293.refs_1_.refs_0_, f32[1,2048]{1,0:T(1,128)} %bitcast.433, ...), custom_call_target="tpu_custom_call" | custom-call | flops 16000000000 | bytes 1048576 | tf_op jit(solution)/shard_map/mlp_out/pallas_call | solution.py:530
  357.5 18.5 %collective-permute-done.56 = bf16[384,1024]{1,0:T(8,128)(2,1)} collective-permute-done((bf16[384,1024]{1,0:T(8,128)(2,1)}, bf16[384,1024]{1,0:T(8,128)(2,1)}, u32[]{:S(2)}, u32[]{:S(2)}) %collective-permute-start.56) | collective-permute-done | bytes 786464 | tf_op jit(solution)/shard_map/ppermute | solution.py:406
  381.7 15.7 %mlp_out.7 = (bf16[1024,2048]{1,0:T(8,128)(2,1)}, bf16[1024,2048]{1,0:T(8,128)(2,1)}, bf16[512,1024]{1,0:T(8,128)(2,1)}) custom-call(bf16[1024,512]{1,0:T(8,128)(2,1)} %get-tuple-element.268.refs_0_.refs_3_, bf16[1024,1024]{1,0:T(8,128)(2,1)} %get-tuple-element.293.refs_1_.refs_0_, ...), custom_call_target="tpu_custom_call", output_to_operand_aliasing={{0}: (27, {}), {1}: (28, {})} | custom-call | flops 16000000000 | bytes 1048576 | tf_op jit(solution)/shard_map/mlp_out/pallas_call | solution.py:530
  406.4 7.5 mlp_back.4
  414.0 7.9 mlp_back.5
  421.9 6.9 collective-permute-done.60
  428.8 3.4 add_convert_fusion.9
  437.1 25.8 %attend_back.2 = (bf16[1024,1536]{1,0:T(8,128)(2,1)}, f32[1,1536]{1,0:T(1,128)}) custom-call(bf16[1024,1536]{1,0:T(8,128)(2,1)} %get-tuple-element.256.refs_0_.refs_1_.refs_2_, bf16[1024,1536]{1,0:T(8,128)(2,1)} %get-tuple-element.256.refs_0_.refs_1_.refs_2_, bf16[1024,1536]{1,0:T(8,128)(2,1)} %get-tuple-element.256.refs_0_.refs_1_.refs_2_, ...), custom_call_target="tpu_custom_call" | custom-call | flops 25999998976 | bytes 1048576 | tf_op jit(solution)/shard_map/attend_back/pallas_call | solution.py:530
  462.9 5.3 collective-permute-done.62
  474.0 10.8 %norm_back.4 = (bf16[512,1024]{1,0:T(8,128)(2,1)}, f32[8,1024]{1,0:T(8,128)}) custom-call(bf16[512,1024]{1,0:T(8,128)(2,1)} %get-tuple-element.246.refs_0_, bf16[1024,1536]{1,0:T(8,128)(2,1)} %get-tuple-element.291.refs_1_.refs_2_, bf16[1024,2048]{1,0:T(8,128)(2,1)} %get-tuple-element.279.refs_2_, f32[8,1024]{1,0:T(8,128)} %concatenate.192.refs_1_.refs_3_, ...), custom_call_target="tpu_custom_call" | custom-call | flops 10499999744 | bytes 1048576 | tf_op jit(solution)/shard_map/norm_back/pallas_call | solution.py:530
  487.1 14.8 %weight_grad.4 = (bf16[4,2,256,1024]{3,2,1,0:T(8,128)(2,1)}, bf16[4,2,256,1024]{3,2,1,0:T(8,128)(2,1)}) custom-call(bf16[1024,1024]{1,0:T(8,128)(2,1)} %get-tuple-element.293.refs_1_.refs_0_, bf16[1024,1024]{1,0:T(8,128)(2,1)} %pad_maximum_fusion.2.refs_0_.refs_1_, bf16[1024,2048]{1,0:T(8,128)(2,1)} %get-tuple-element.279.refs_2_, ...), custom_call_target="tpu_custom_call" | custom-call | flops 14000000000 | bytes 1048576 | tf_op jit(solution)/shard_map/weight_grad/pallas_call | solution.py:530
  501.9 10.6 %norm_back.5 = (bf16[512,1024]{1,0:T(8,128)(2,1)}, f32[8,1024]{1,0:T(8,128)}) custom-call(bf16[512,1024]{1,0:T(8,128)(2,1)} %get-tuple-element.409.refs_0_, bf16[1024,1536]{1,0:T(8,128)(2,1)} %get-tuple-element.291.refs_1_.refs_2_, bf16[1024,2048]{1,0:T(8,128)(2,1)} %get-tuple-element.279.refs_2_, f32[8,1024]{1,0:T(8,128)} %concatenate.192.refs_1_.refs_3_, ...), custom_call_target="tpu_custom_call" | custom-call | flops 10499999744 | bytes 1048576 | tf_op jit(solution)/shard_map/norm_back/pallas_call | solution.py:530
  512.6 5.0 copy.95
  534.0 12.4 %weight_grad.5 = (bf16[4,2,256,512]{3,2,1,0:T(8,128)(2,1)}, bf16[4,2,256,512]{3,2,1,0:T(8,128)(2,1)}) custom-call(bf16[1024,1024]{1,0:T(8,128)(2,1)} %get-tuple-element.296.refs_0_, bf16[1024,1024]{1,0:T(8,128)(2,1)} %pad_maximum_fusion.2.refs_0_.refs_1_, bf16[1024,1536]{1,0:T(8,128)(2,1)} %get-tuple-element.291.refs_1_.refs_2_, ...), custom_call_target="tpu_custom_call" | custom-call | flops 14000000000 | bytes 1048576 | tf_op jit(solution)/shard_map/weight_grad/pallas_call | solution.py:530
  546.5 13.0 %collective-permute-done.66 = bf16[512,1024]{1,0:T(8,128)(2,1)} collective-permute-done((bf16[512,1024]{1,0:T(8,128)(2,1)}, bf16[512,1024]{1,0:T(8,128)(2,1)}, u32[]{:S(2)}, u32[]{:S(2)}) %collective-permute-start.66) | collective-permute-done | bytes 1048608 | tf_op jit(solution)/shard_map/ppermute | solution.py:411
  559.4 4.8 add_convert_fusion.7
  564.3 4.3 add_convert_fusion.1
  572.1 7.5 mlp_back.6
  579.7 7.6 mlp_back.7
  588.8 8.2 collective-permute-done.69
  604.6 15.1 %weight_grad.6 = (bf16[4,2,256,1024]{3,2,1,0:T(8,128)(2,1)}, bf16[4,2,256,1024]{3,2,1,0:T(8,128)(2,1)}) custom-call(bf16[1024,1024]{1,0:T(8,128)(2,1)} %get-tuple-element.311.refs_1_.refs_0_, bf16[512,1024]{1,0:T(8,128)(2,1)} %get-tuple-element.301.refs_0_.refs_1_, bf16[512,1024]{1,0:T(8,128)(2,1)} %get-tuple-element.302.refs_0_.refs_2_, ...), custom_call_target="tpu_custom_call" | custom-call | flops 14000000000 | bytes 1048576 | tf_op jit(solution)/shard_map/weight_grad/pallas_call | solution.py:530
  623.8 4.9 copy.97
  637.4 25.9 %attend_back.3 = (bf16[1024,1536]{1,0:T(8,128)(2,1)}, f32[1,1536]{1,0:T(1,128)}) custom-call(bf16[1024,1536]{1,0:T(8,128)(2,1)} %get-tuple-element.216.refs_0_.refs_1_.refs_2_, bf16[1024,1536]{1,0:T(8,128)(2,1)} %get-tuple-element.216.refs_0_.refs_1_.refs_2_, bf16[1024,1536]{1,0:T(8,128)(2,1)} %get-tuple-element.216.refs_0_.refs_1_.refs_2_, ...), custom_call_target="tpu_custom_call" | custom-call | flops 25999998976 | bytes 1048576 | tf_op jit(solution)/shard_map/attend_back/pallas_call | solution.py:530
  675.6 10.8 %norm_back.6 = (bf16[512,1024]{1,0:T(8,128)(2,1)}, f32[8,1024]{1,0:T(8,128)}) custom-call(bf16[1024,1024]{1,0:T(8,128)(2,1)} %pad_maximum_fusion.refs_0_, bf16[1024,1536]{1,0:T(8,128)(2,1)} %get-tuple-element.332.refs_1_.refs_3_, bf16[1024,2048]{1,0:T(8,128)(2,1)} %get-tuple-element.307.refs_3_.refs_2_, f32[8,1024]{1,0:T(8,128)} %concatenate.186.refs_1_.refs_3_, ...), custom_call_target="tpu_custom_call" | custom-call | flops 10499999744 | bytes 1048576 | tf_op jit(solution)/shard_map/norm_back/pallas_call | solution.py:530
  686.4 5.6 add_convert_fusion
  694.7 3.6 collective-permute-done.78
  699.6 10.7 %norm_back.7 = (bf16[512,1024]{1,0:T(8,128)(2,1)}, f32[8,1024]{1,0:T(8,128)}) custom-call(bf16[1024,1024]{1,0:T(8,128)(2,1)} %pad_maximum_fusion.refs_0_, bf16[1024,1536]{1,0:T(8,128)(2,1)} %get-tuple-element.332.refs_1_.refs_3_, bf16[1024,2048]{1,0:T(8,128)(2,1)} %get-tuple-element.307.refs_3_.refs_2_, f32[8,1024]{1,0:T(8,128)} %concatenate.186.refs_1_.refs_3_, ...), custom_call_target="tpu_custom_call" | custom-call | flops 10499999744 | bytes 1048576 | tf_op jit(solution)/shard_map/norm_back/pallas_call | solution.py:530
  711.2 12.4 %weight_grad.7 = (bf16[4,2,256,512]{3,2,1,0:T(8,128)(2,1)}, bf16[4,2,256,512]{3,2,1,0:T(8,128)(2,1)}) custom-call(bf16[1024,1024]{1,0:T(8,128)(2,1)} %get-tuple-element.334.refs_0_, bf16[512,1024]{1,0:T(8,128)(2,1)} %get-tuple-element.301.refs_0_.refs_1_, bf16[512,1024]{1,0:T(8,128)(2,1)} %get-tuple-element.302.refs_0_.refs_2_, ...), custom_call_target="tpu_custom_call" | custom-call | flops 14000000000 | bytes 1048576 | tf_op jit(solution)/shard_map/weight_grad/pallas_call | solution.py:530
  728.8 18.1 %collective-permute-done.84 = bf16[2,256,1024]{2,1,0:T(8,128)(2,1)S(1)} collective-permute-done((bf16[2,256,1024]{2,1,0:T(8,128)(2,1)}, bf16[2,256,1024]{2,1,0:T(8,128)(2,1)S(1)}, u32[]{:S(2)}, u32[]{:S(2)}) %collective-permute-start.84) | collective-permute-done | bytes 1048608 | tf_op jit(solution)/shard_map/ppermute | solution.py:411
  763.7 3.8 collective-permute-start.91
  767.6 2.9 collective-permute-done.89
  770.5 6.9 collective-permute-done.88
  779.2 8.1 collective-permute-done.91
  787.3 12.2 %collective-permute-done.90 = bf16[256,1024]{1,0:T(8,128)(2,1)S(1)} collective-permute-done((bf16[256,1024]{1,0:T(8,128)(2,1)S(1)}, bf16[256,1024]{1,0:T(8,128)(2,1)S(1)}, u32[]{:S(2)}, u32[]{:S(2)}) %collective-permute-start.90) | collective-permute-done | bytes 524320 | tf_op jit(solution)/shard_map/ppermute | solution.py:406
  804.8 3.5 collective-permute-start.94
  808.4 7.6 collective-permute-done.97
  827.8 15.0 %collective-permute-done.94 = bf16[384,1024]{1,0:T(8,128)(2,1)} collective-permute-done((bf16[384,1024]{1,0:T(8,128)(2,1)}, bf16[384,1024]{1,0:T(8,128)(2,1)}, u32[]{:S(2)}, u32[]{:S(2)}) %collective-permute-start.94) | collective-permute-done | bytes 786464 | tf_op jit(solution)/shard_map/ppermute | solution.py:406
  842.8 15.7 %collective-permute-done.93 = bf16[384,1024]{1,0:T(8,128)(2,1)} collective-permute-done((bf16[384,1024]{1,0:T(8,128)(2,1)}, bf16[384,1024]{1,0:T(8,128)(2,1)}, u32[]{:S(2)}, u32[]{:S(2)}) %collective-permute-start.93) | collective-permute-done | bytes 786464 | tf_op jit(solution)/shard_map/ppermute | solution.py:406
  863.8 3.0 collective-permute-start.100
  873.0 2.9 collective-permute-done.100
  878.9 3.1 collective-permute-done.103
  (628 shorter events, 282.4 us)
Async XLA Ops:
  16.7 23.2 %collective-permute-start.2 = (bf16[384,1024]{1,0:T(8,128)(2,1)}, bf16[384,1024]{1,0:T(8,128)(2,1)}, u32[]{:S(2)}, u32[]{:S(2)}) collective-permute-start(bf16[384,1024]{1,0:T(8,128)(2,1)} %pad_maximum_fusion.12), channel_id=1, source_target_pairs={{0,1},{1,2},{2,3},{3,0},{4,5},{5,6},{6,7},{7,4},{8,9},{9,10},{10,1... | collective-permute-start | bytes 2359304 | tf_op jit(solution)/shard_map/ppermute | solution.py:406
  18.8 35.6 %collective-permute-start.3 = (bf16[384,1024]{1,0:T(8,128)(2,1)}, bf16[384,1024]{1,0:T(8,128)(2,1)}, u32[]{:S(2)}, u32[]{:S(2)}) collective-permute-start(bf16[384,1024]{1,0:T(8,128)(2,1)} %pad_maximum_fusion.13), channel_id=1, source_target_pairs={{0,3},{1,0},{2,1},{3,2},{4,7},{5,4},{6,5},{7,6},{8,11},{9,8},{10,9... | collective-permute-start | bytes 2359304 | tf_op jit(solution)/shard_map/ppermute | solution.py:406
  54.4 43.7 %collective-permute-start.10 = (bf16[2,256,512]{2,1,0:T(8,128)(2,1)}, bf16[2,256,512]{2,1,0:T(8,128)(2,1)}, u32[]{:S(2)}, u32[]{:S(2)}) collective-permute-start(bf16[2,256,512]{2,1,0:T(8,128)(2,1)} %pad_maximum_fusion.20.refs_6_.refs_3_.refs_2_.refs_4_), channel_id=1, source_target_pairs={{0,1},{1,2},{2,3},{3,0},{4,5},{5,6},{6,7},{7,4},{8,9},{9,10},{10,1... | collective-permute-start | bytes 1572872 | tf_op jit(solution)/shard_map/ppermute | solution.py:406
  55.5 42.6 %collective-permute-start.11 = (bf16[2,256,512]{2,1,0:T(8,128)(2,1)}, bf16[2,256,512]{2,1,0:T(8,128)(2,1)}, u32[]{:S(2)}, u32[]{:S(2)}) collective-permute-start(bf16[2,256,512]{2,1,0:T(8,128)(2,1)} %pad_maximum_fusion.20.refs_6_.refs_3_.refs_2_.refs_4_), channel_id=1, source_target_pairs={{0,3},{1,0},{2,1},{3,2},{4,7},{5,4},{6,5},{7,6},{8,11},{9,8},{10,9... | collective-permute-start | bytes 1572872 | tf_op jit(solution)/shard_map/ppermute | solution.py:406
  58.2 24.3 %collective-permute-start.13 = (f32[4,2,832]{2,1,0:T(2,128)S(1)}, f32[4,2,832]{2,1,0:T(2,128)S(1)}, u32[]{:S(2)}, u32[]{:S(2)}) collective-permute-start(f32[4,2,832]{2,1,0:T(2,128)S(1)} %pad_maximum_fusion.41), channel_id=1, source_target_pairs={{0,1},{1,0},{2,3},{3,2},{4,5},{5,4},{6,7},{7,6},{8,9},{9,8},{10,11... | collective-permute-start | bytes 79880 | tf_op jit(solution)/shard_map/ppermute | solution.py:411
  58.2 32.0 %collective-permute-start.12 = (bf16[256,1024]{1,0:T(8,128)(2,1)S(1)}, bf16[256,1024]{1,0:T(8,128)(2,1)S(1)}, u32[]{:S(2)}, u32[]{:S(2)}) collective-permute-start(bf16[256,1024]{1,0:T(8,128)(2,1)S(1)} %get-tuple-element.215), channel_id=1, source_target_pairs={{0,8},{4,12},{8,0},{12,4},{1,9},{5,13},{9,1},{13,5},{2,10},{6,14},... | collective-permute-start | bytes 1572872 | tf_op jit(solution)/shard_map/ppermute | solution.py:411
  60.7 29.6 %collective-permute-start.8 = (bf16[128,1024]{1,0:T(8,128)(2,1)S(1)}, bf16[128,1024]{1,0:T(8,128)(2,1)}, u32[]{:S(2)}, u32[]{:S(2)}) collective-permute-start(bf16[128,1024]{1,0:T(8,128)(2,1)S(1)} %slice.696), channel_id=1, source_target_pairs={{0,1},{1,2},{2,3},{3,0},{4,5},{5,6},{6,7},{7,4},{8,9},{9,10},{10,1... | collective-permute-start | bytes 786440 | tf_op jit(solution)/shard_map/ppermute | solution.py:406
  98.1 17.8 %collective-permute-start.19 = (bf16[2,256,512]{2,1,0:T(8,128)(2,1)}, bf16[2,256,512]{2,1,0:T(8,128)(2,1)S(1)}, u32[]{:S(2)}, u32[]{:S(2)}) collective-permute-start(bf16[2,256,512]{2,1,0:T(8,128)(2,1)} %collective-permute-done.11.refs_8_.refs_5_.refs_4_.refs_6_), channel_id=1, source_target_pairs={{0,4},{4,0},{8,12},{12,8},{1,5},{5,1},{9,13},{13,9},{2,6},{6,2},{1... | collective-permute-start | bytes 1572872 | tf_op jit(solution)/shard_map/ppermute | solution.py:411
  98.1 17.8 %collective-permute-start.18 = (bf16[2,256,512]{2,1,0:T(8,128)(2,1)}, bf16[2,256,512]{2,1,0:T(8,128)(2,1)S(1)}, u32[]{:S(2)}, u32[]{:S(2)}) collective-permute-start(bf16[2,256,512]{2,1,0:T(8,128)(2,1)} %collective-permute-done.10.refs_7_.refs_4_.refs_3_.refs_5_), channel_id=1, source_target_pairs={{0,4},{4,0},{8,12},{12,8},{1,5},{5,1},{9,13},{13,9},{2,6},{6,2},{1... | collective-permute-start | bytes 1572872 | tf_op jit(solution)/shard_map/ppermute | solution.py:411
  98.6 17.3 %collective-permute-start.17 = (bf16[2,256,512]{2,1,0:T(8,128)(2,1)}, bf16[2,256,512]{2,1,0:T(8,128)(2,1)S(1)}, u32[]{:S(2)}, u32[]{:S(2)}) collective-permute-start(bf16[2,256,512]{2,1,0:T(8,128)(2,1)} %pad_maximum_fusion.20.refs_6_.refs_3_.refs_2_.refs_4_), channel_id=1, source_target_pairs={{0,4},{4,0},{8,12},{12,8},{1,5},{5,1},{9,13},{13,9},{2,6},{6,2},{1... | collective-permute-start | bytes 1572872 | tf_op jit(solution)/shard_map/ppermute | solution.py:411
  123.9 16.8 %collective-permute-start.21 = (bf16[256,1024]{1,0:T(8,128)(2,1)S(1)}, bf16[256,1024]{1,0:T(8,128)(2,1)S(1)}, u32[]{:S(2)}, u32[]{:S(2)}) collective-permute-start(bf16[256,1024]{1,0:T(8,128)(2,1)S(1)} %get-tuple-element.215), channel_id=1, source_target_pairs={{0,1},{1,2},{2,3},{3,0},{4,5},{5,6},{6,7},{7,4},{8,9},{9,10},{10,1... | collective-permute-start | bytes 1572872 | tf_op jit(solution)/shard_map/ppermute | solution.py:406
  125.1 24.8 %collective-permute-start.22 = (bf16[256,1024]{1,0:T(8,128)(2,1)S(1)}, bf16[256,1024]{1,0:T(8,128)(2,1)S(1)}, u32[]{:S(2)}, u32[]{:S(2)}) collective-permute-start(bf16[256,1024]{1,0:T(8,128)(2,1)S(1)} %get-tuple-element.215), channel_id=1, source_target_pairs={{0,3},{1,0},{2,1},{3,2},{4,7},{5,4},{6,5},{7,6},{8,11},{9,8},{10,9... | collective-permute-start | bytes 1572872 | tf_op jit(solution)/shard_map/ppermute | solution.py:406
  149.9 24.5 %collective-permute-start.26 = (bf16[256,1024]{1,0:T(8,128)(2,1)S(1)}, bf16[256,1024]{1,0:T(8,128)(2,1)S(1)}, u32[]{:S(2)}, u32[]{:S(2)}) collective-permute-start(bf16[256,1024]{1,0:T(8,128)(2,1)S(1)} %collective-permute-done.22), channel_id=1, source_target_pairs={{0,8},{4,12},{8,0},{12,4},{1,9},{5,13},{9,1},{13,5},{2,10},{6,14},... | collective-permute-start | bytes 1572872 | tf_op jit(solution)/shard_map/ppermute | solution.py:411
  151.4 25.0 %collective-permute-start.25 = (bf16[256,1024]{1,0:T(8,128)(2,1)S(1)}, bf16[256,1024]{1,0:T(8,128)(2,1)}, u32[]{:S(2)}, u32[]{:S(2)}) collective-permute-start(bf16[256,1024]{1,0:T(8,128)(2,1)S(1)} %collective-permute-done.21), channel_id=1, source_target_pairs={{0,8},{4,12},{8,0},{12,4},{1,9},{5,13},{9,1},{13,5},{2,10},{6,14},... | collective-permute-start | bytes 1572872 | tf_op jit(solution)/shard_map/ppermute | solution.py:411
  152.7 23.7 %collective-permute-start.24 = (bf16[128,1024]{1,0:T(8,128)(2,1)}, bf16[128,1024]{1,0:T(8,128)(2,1)}, u32[]{:S(2)}, u32[]{:S(2)}) collective-permute-start(bf16[128,1024]{1,0:T(8,128)(2,1)} %slice.712), channel_id=1, source_target_pairs={{0,3},{1,0},{2,1},{3,2},{4,7},{5,4},{6,5},{7,6},{8,11},{9,8},{10,9... | collective-permute-start | bytes 786440 | tf_op jit(solution)/shard_map/ppermute | solution.py:406
  155.3 21.1 %collective-permute-start.23 = (bf16[128,1024]{1,0:T(8,128)(2,1)}, bf16[128,1024]{1,0:T(8,128)(2,1)}, u32[]{:S(2)}, u32[]{:S(2)}) collective-permute-start(bf16[128,1024]{1,0:T(8,128)(2,1)} %slice.711), channel_id=1, source_target_pairs={{0,1},{1,2},{2,3},{3,0},{4,5},{5,6},{6,7},{7,4},{8,9},{9,10},{10,1... | collective-permute-start | bytes 786440 | tf_op jit(solution)/shard_map/ppermute | solution.py:406
  176.5 19.2 %collective-permute-start.30 = (bf16[2,256,1024]{2,1,0:T(8,128)(2,1)S(1)}, bf16[2,256,1024]{2,1,0:T(8,128)(2,1)S(1)}, u32[]{:S(2)}, u32[]{:S(2)}) collective-permute-start(bf16[2,256,1024]{2,1,0:T(8,128)(2,1)S(1)} %pad_maximum_fusion.7.refs_13_.refs_21_.refs_12_.refs_14_), channel_id=1, source_target_pairs={{0,4},{4,0},{8,12},{12,8},{1,5},{5,1},{9,13},{13,9},{2,6},{6,2},{1... | collective-permute-start | bytes 3145736 | tf_op jit(solution)/shard_map/ppermute | solution.py:411
  178.0 17.7 %collective-permute-start.29 = (bf16[2,256,1024]{2,1,0:T(8,128)(2,1)S(1)}, bf16[2,256,1024]{2,1,0:T(8,128)(2,1)S(1)}, u32[]{:S(2)}, u32[]{:S(2)}) collective-permute-start(bf16[2,256,1024]{2,1,0:T(8,128)(2,1)S(1)} %pad_maximum_fusion.6.refs_12_.refs_20_.refs_11_.refs_13_), channel_id=1, source_target_pairs={{0,4},{4,0},{8,12},{12,8},{1,5},{5,1},{9,13},{13,9},{2,6},{6,2},{1... | collective-permute-start | bytes 3145736 | tf_op jit(solution)/shard_map/ppermute | solution.py:411
  178.3 17.5 %collective-permute-start.28 = (bf16[2,256,1024]{2,1,0:T(8,128)(2,1)S(1)}, bf16[2,256,1024]{2,1,0:T(8,128)(2,1)S(1)}, u32[]{:S(2)}, u32[]{:S(2)}) collective-permute-start(bf16[2,256,1024]{2,1,0:T(8,128)(2,1)S(1)} %pad_maximum_fusion.4.refs_11_.refs_19_.refs_10_.refs_12_), channel_id=1, source_target_pairs={{0,4},{4,0},{8,12},{12,8},{1,5},{5,1},{9,13},{13,9},{2,6},{6,2},{1... | collective-permute-start | bytes 3145736 | tf_op jit(solution)/shard_map/ppermute | solution.py:411
  210.1 19.9 %collective-permute-start.33 = (bf16[256,1024]{1,0:T(8,128)(2,1)S(1)}, bf16[256,1024]{1,0:T(8,128)(2,1)S(1)}, u32[]{:S(2)}, u32[]{:S(2)}) collective-permute-start(bf16[256,1024]{1,0:T(8,128)(2,1)S(1)} %get-tuple-element.237), channel_id=1, source_target_pairs={{0,1},{1,2},{2,3},{3,0},{4,5},{5,6},{6,7},{7,4},{8,9},{9,10},{10,1... | collective-permute-start | bytes 1572872 | tf_op jit(solution)/shard_map/ppermute | solution.py:406
  210.6 24.5 %collective-permute-start.34 = (bf16[256,1024]{1,0:T(8,128)(2,1)S(1)}, bf16[256,1024]{1,0:T(8,128)(2,1)S(1)}, u32[]{:S(2)}, u32[]{:S(2)}) collective-permute-start(bf16[256,1024]{1,0:T(8,128)(2,1)S(1)} %get-tuple-element.237), channel_id=1, source_target_pairs={{0,3},{1,0},{2,1},{3,2},{4,7},{5,4},{6,5},{7,6},{8,11},{9,8},{10,9... | collective-permute-start | bytes 1572872 | tf_op jit(solution)/shard_map/ppermute | solution.py:406
  235.1 22.7 %collective-permute-start.36 = (bf16[2,256,512]{2,1,0:T(8,128)(2,1)}, bf16[2,256,512]{2,1,0:T(8,128)(2,1)}, u32[]{:S(2)}, u32[]{:S(2)}) collective-permute-start(bf16[2,256,512]{2,1,0:T(8,128)(2,1)} %pad_maximum_fusion.22.refs_6_.refs_3_.refs_2_.refs_4_), channel_id=1, source_target_pairs={{0,1},{1,2},{2,3},{3,0},{4,5},{5,6},{6,7},{7,4},{8,9},{9,10},{10,1... | collective-permute-start | bytes 1572872 | tf_op jit(solution)/shard_map/ppermute | solution.py:406
  236.9 24.0 %collective-permute-start.37 = (bf16[2,256,512]{2,1,0:T(8,128)(2,1)}, bf16[2,256,512]{2,1,0:T(8,128)(2,1)}, u32[]{:S(2)}, u32[]{:S(2)}) collective-permute-start(bf16[2,256,512]{2,1,0:T(8,128)(2,1)} %pad_maximum_fusion.22.refs_6_.refs_3_.refs_2_.refs_4_), channel_id=1, source_target_pairs={{0,3},{1,0},{2,1},{3,2},{4,7},{5,4},{6,5},{7,6},{8,11},{9,8},{10,9... | collective-permute-start | bytes 1572872 | tf_op jit(solution)/shard_map/ppermute | solution.py:406
  238.9 18.8 %collective-permute-start.38 = (bf16[256,1024]{1,0:T(8,128)(2,1)S(1)}, bf16[256,1024]{1,0:T(8,128)(2,1)S(1)}, u32[]{:S(2)}, u32[]{:S(2)}) collective-permute-start(bf16[256,1024]{1,0:T(8,128)(2,1)S(1)} %get-tuple-element.237), channel_id=1, source_target_pairs={{0,8},{4,12},{8,0},{12,4},{1,9},{5,13},{9,1},{13,5},{2,10},{6,14},... | collective-permute-start | bytes 1572872 | tf_op jit(solution)/shard_map/ppermute | solution.py:411
  240.4 23.1 %collective-permute-start.35 = (bf16[512,1024]{1,0:T(8,128)(2,1)}, bf16[512,1024]{1,0:T(8,128)(2,1)S(1)}, u32[]{:S(2)}, u32[]{:S(2)}) collective-permute-start(bf16[512,1024]{1,0:T(8,128)(2,1)} %get-tuple-element.231), channel_id=1, source_target_pairs={{0,16},{16,0},{1,17},{17,1},{2,18},{18,2},{3,19},{19,3},{4,20},{20... | collective-permute-start | bytes 3145736 | tf_op jit(solution)/shard_map/ppermute | solution.py:411
  263.5 22.8 %collective-permute-start.39 = (bf16[512,1024]{1,0:T(8,128)(2,1)}, bf16[512,1024]{1,0:T(8,128)(2,1)}, u32[]{:S(2)}, u32[]{:S(2)}) collective-permute-start(bf16[512,1024]{1,0:T(8,128)(2,1)} %get-tuple-element.238), channel_id=1, source_target_pairs={{0,16},{16,0},{1,17},{17,1},{2,18},{18,2},{3,19},{19,3},{4,20},{20... | collective-permute-start | bytes 3145736 | tf_op jit(solution)/shard_map/ppermute | solution.py:411
  293.3 18.6 %collective-permute-start.49 = (bf16[256,1024]{1,0:T(8,128)(2,1)S(1)}, bf16[256,1024]{1,0:T(8,128)(2,1)S(1)}, u32[]{:S(2)}, u32[]{:S(2)}) collective-permute-start(bf16[256,1024]{1,0:T(8,128)(2,1)S(1)} %collective-permute-done.34), channel_id=1, source_target_pairs={{0,8},{4,12},{8,0},{12,4},{1,9},{5,13},{9,1},{13,5},{2,10},{6,14},... | collective-permute-start | bytes 1572872 | tf_op jit(solution)/shard_map/ppermute | solution.py:411
  313.0 21.5 %collective-permute-start.53 = (bf16[2,256,1024]{2,1,0:T(8,128)(2,1)}, bf16[2,256,1024]{2,1,0:T(8,128)(2,1)}, u32[]{:S(2)}, u32[]{:S(2)}) collective-permute-start(bf16[2,256,1024]{2,1,0:T(8,128)(2,1)} %pad_maximum_fusion.11.refs_13_.refs_21_.refs_12_.refs_14_), channel_id=1, source_target_pairs={{0,4},{4,0},{8,12},{12,8},{1,5},{5,1},{9,13},{13,9},{2,6},{6,2},{1... | collective-permute-start | bytes 3145736 | tf_op jit(solution)/shard_map/ppermute | solution.py:411
  313.0 21.5 %collective-permute-start.52 = (bf16[2,256,1024]{2,1,0:T(8,128)(2,1)S(1)}, bf16[2,256,1024]{2,1,0:T(8,128)(2,1)}, u32[]{:S(2)}, u32[]{:S(2)}) collective-permute-start(bf16[2,256,1024]{2,1,0:T(8,128)(2,1)S(1)} %copy-done.23), channel_id=1, source_target_pairs={{0,4},{4,0},{8,12},{12,8},{1,5},{5,1},{9,13},{13,9},{2,6},{6,2},{1... | collective-permute-start | bytes 3145736 | tf_op jit(solution)/shard_map/ppermute | solution.py:411
  313.6 21.0 %collective-permute-start.51 = (bf16[2,256,1024]{2,1,0:T(8,128)(2,1)S(1)}, bf16[2,256,1024]{2,1,0:T(8,128)(2,1)}, u32[]{:S(2)}, u32[]{:S(2)}) collective-permute-start(bf16[2,256,1024]{2,1,0:T(8,128)(2,1)S(1)} %pad_maximum_fusion.9.refs_11_.refs_19_.refs_10_.refs_12_), channel_id=1, source_target_pairs={{0,4},{4,0},{8,12},{12,8},{1,5},{5,1},{9,13},{13,9},{2,6},{6,2},{1... | collective-permute-start | bytes 3145736 | tf_op jit(solution)/shard_map/ppermute | solution.py:411
  313.6 19.9 %collective-permute-start.50 = (bf16[256,1024]{1,0:T(8,128)(2,1)S(1)}, bf16[256,1024]{1,0:T(8,128)(2,1)S(1)}, u32[]{:S(2)}, u32[]{:S(2)}) collective-permute-start(bf16[256,1024]{1,0:T(8,128)(2,1)S(1)} %constant_dynamic-update-slice_fusion.2), channel_id=1, source_target_pairs={{0,8},{4,12},{8,0},{12,4},{1,9},{5,13},{9,1},{13,5},{2,10},{6,14},... | collective-permute-start | bytes 1572872 | tf_op jit(solution)/shard_map/ppermute | solution.py:411
  337.6 39.4 %collective-permute-start.55 = (bf16[384,1024]{1,0:T(8,128)(2,1)S(1)}, bf16[384,1024]{1,0:T(8,128)(2,1)}, u32[]{:S(2)}, u32[]{:S(2)}) collective-permute-start(bf16[384,1024]{1,0:T(8,128)(2,1)S(1)} %pad_maximum_fusion.14), channel_id=1, source_target_pairs={{0,1},{1,2},{2,3},{3,0},{4,5},{5,6},{6,7},{7,4},{8,9},{9,10},{10,1... | collective-permute-start | bytes 2359304 | tf_op jit(solution)/shard_map/ppermute | solution.py:406
  339.3 36.8 %collective-permute-start.56 = (bf16[384,1024]{1,0:T(8,128)(2,1)}, bf16[384,1024]{1,0:T(8,128)(2,1)}, u32[]{:S(2)}, u32[]{:S(2)}) collective-permute-start(bf16[384,1024]{1,0:T(8,128)(2,1)} %pad_maximum_fusion.15), channel_id=1, source_target_pairs={{0,3},{1,0},{2,1},{3,2},{4,7},{5,4},{6,5},{7,6},{8,11},{9,8},{10,9... | collective-permute-start | bytes 2359304 | tf_op jit(solution)/shard_map/ppermute | solution.py:406
  377.0 22.5 %collective-permute-start.59 = (bf16[128,1024]{1,0:T(8,128)(2,1)S(1)}, bf16[128,1024]{1,0:T(8,128)(2,1)S(1)}, u32[]{:S(2)}, u32[]{:S(2)}) collective-permute-start(bf16[128,1024]{1,0:T(8,128)(2,1)S(1)} %slice.728), channel_id=1, source_target_pairs={{0,3},{1,0},{2,1},{3,2},{4,7},{5,4},{6,5},{7,6},{8,11},{9,8},{10,9... | collective-permute-start | bytes 786440 | tf_op jit(solution)/shard_map/ppermute | solution.py:406
  379.8 19.8 %collective-permute-start.58 = (bf16[128,1024]{1,0:T(8,128)(2,1)S(1)}, bf16[128,1024]{1,0:T(8,128)(2,1)}, u32[]{:S(2)}, u32[]{:S(2)}) collective-permute-start(bf16[128,1024]{1,0:T(8,128)(2,1)S(1)} %slice.727), channel_id=1, source_target_pairs={{0,1},{1,2},{2,3},{3,0},{4,5},{5,6},{6,7},{7,4},{8,9},{9,10},{10,1... | collective-permute-start | bytes 786440 | tf_op jit(solution)/shard_map/ppermute | solution.py:406
  380.2 24.7 %collective-permute-start.57 = (bf16[512,1024]{1,0:T(8,128)(2,1)}, bf16[512,1024]{1,0:T(8,128)(2,1)S(1)}, u32[]{:S(2)}, u32[]{:S(2)}) collective-permute-start(bf16[512,1024]{1,0:T(8,128)(2,1)} %get-tuple-element.267), channel_id=1, source_target_pairs={{0,16},{16,0},{1,17},{17,1},{2,18},{18,2},{3,19},{19,3},{4,20},{20... | collective-permute-start | bytes 3145736 | tf_op jit(solution)/shard_map/ppermute | solution.py:411
  404.9 23.9 %collective-permute-start.60 = (bf16[512,1024]{1,0:T(8,128)(2,1)}, bf16[512,1024]{1,0:T(8,128)(2,1)}, u32[]{:S(2)}, u32[]{:S(2)}) collective-permute-start(bf16[512,1024]{1,0:T(8,128)(2,1)} %get-tuple-element.274), channel_id=1, source_target_pairs={{0,16},{16,0},{1,17},{17,1},{2,18},{18,2},{3,19},{19,3},{4,20},{20... | collective-permute-start | bytes 3145736 | tf_op jit(solution)/shard_map/ppermute | solution.py:411
  434.1 34.1 %collective-permute-start.62 = (bf16[384,1024]{1,0:T(8,128)(2,1)S(1)}, bf16[384,1024]{1,0:T(8,128)(2,1)}, u32[]{:S(2)}, u32[]{:S(2)}) collective-permute-start(bf16[384,1024]{1,0:T(8,128)(2,1)S(1)} %pad_maximum_fusion.17), channel_id=1, source_target_pairs={{0,3},{1,0},{2,1},{3,2},{4,7},{5,4},{6,5},{7,6},{8,11},{9,8},{10,9... | collective-permute-start | bytes 2359304 | tf_op jit(solution)/shard_map/ppermute | solution.py:406
  437.0 31.2 %collective-permute-start.61 = (bf16[384,1024]{1,0:T(8,128)(2,1)}, bf16[384,1024]{1,0:T(8,128)(2,1)}, u32[]{:S(2)}, u32[]{:S(2)}) collective-permute-start(bf16[384,1024]{1,0:T(8,128)(2,1)} %pad_maximum_fusion.16), channel_id=1, source_target_pairs={{0,1},{1,2},{2,3},{3,0},{4,5},{5,6},{6,7},{7,4},{8,9},{9,10},{10,1... | collective-permute-start | bytes 2359304 | tf_op jit(solution)/shard_map/ppermute | solution.py:406
  485.5 27.0 %collective-permute-start.65 = (bf16[512,1024]{1,0:T(8,128)(2,1)}, bf16[512,1024]{1,0:T(8,128)(2,1)S(1)}, u32[]{:S(2)}, u32[]{:S(2)}) collective-permute-start(bf16[512,1024]{1,0:T(8,128)(2,1)} %get-tuple-element.290), channel_id=1, source_target_pairs={{0,16},{16,0},{1,17},{17,1},{2,18},{18,2},{3,19},{19,3},{4,20},{20... | collective-permute-start | bytes 3145736 | tf_op jit(solution)/shard_map/ppermute | solution.py:411
  517.6 46.7 %collective-permute-start.67 = (bf16[4,2,256,1024]{3,2,0,1:T(8,128)(2,1)}, bf16[4,2,256,1024]{3,2,0,1:T(8,128)(2,1)}, u32[]{:S(2)}, u32[]{:S(2)}) collective-permute-start(bf16[4,2,256,1024]{3,2,0,1:T(8,128)(2,1)} %copy.95), channel_id=1, source_target_pairs={{0,4},{4,0},{8,12},{12,8},{1,5},{5,1},{9,13},{13,9},{2,6},{6,2},{1... | collective-permute-start | bytes 12582920 | tf_op jit(solution)/shard_map/ppermute | solution.py:411
  533.5 25.9 %collective-permute-start.66 = (bf16[512,1024]{1,0:T(8,128)(2,1)}, bf16[512,1024]{1,0:T(8,128)(2,1)}, u32[]{:S(2)}, u32[]{:S(2)}) collective-permute-start(bf16[512,1024]{1,0:T(8,128)(2,1)} %get-tuple-element.298), channel_id=1, source_target_pairs={{0,16},{16,0},{1,17},{17,1},{2,18},{18,2},{3,19},{19,3},{4,20},{20... | collective-permute-start | bytes 3145736 | tf_op jit(solution)/shard_map/ppermute | solution.py:411
  564.3 32.7 %collective-permute-start.68 = (bf16[4,2,256,512]{3,2,1,0:T(8,128)(2,1)}, bf16[4,2,256,512]{3,2,1,0:T(8,128)(2,1)S(1)}, u32[]{:S(2)}, u32[]{:S(2)}) collective-permute-start(bf16[4,2,256,512]{3,2,1,0:T(8,128)(2,1)} %get-tuple-element.309), channel_id=1, source_target_pairs={{0,4},{4,0},{8,12},{12,8},{1,5},{5,1},{9,13},{13,9},{2,6},{6,2},{1... | collective-permute-start | bytes 6291464 | tf_op jit(solution)/shard_map/ppermute | solution.py:411
  571.2 25.8 %collective-permute-start.69 = (bf16[2,256,1024]{2,1,0:T(8,128)(2,1)}, bf16[2,256,1024]{2,1,0:T(8,128)(2,1)S(1)}, u32[]{:S(2)}, u32[]{:S(2)}) collective-permute-start(bf16[2,256,1024]{2,1,0:T(8,128)(2,1)} %get-tuple-element.310), channel_id=1, source_target_pairs={{0,8},{4,12},{8,0},{12,4},{1,9},{5,13},{9,1},{13,5},{2,10},{6,14},... | collective-permute-start | bytes 3145736 | tf_op jit(solution)/shard_map/ppermute | solution.py:411
  598.7 25.1 %collective-permute-start.72 = (bf16[2,256,1024]{2,1,0:T(8,128)(2,1)}, bf16[2,256,1024]{2,1,0:T(8,128)(2,1)}, u32[]{:S(2)}, u32[]{:S(2)}) collective-permute-start(bf16[2,256,1024]{2,1,0:T(8,128)(2,1)} %get-tuple-element.316), channel_id=1, source_target_pairs={{0,8},{4,12},{8,0},{12,4},{1,9},{5,13},{9,1},{13,5},{2,10},{6,14},... | collective-permute-start | bytes 3145736 | tf_op jit(solution)/shard_map/ppermute | solution.py:411
  602.6 17.2 %collective-permute-start.71 = (bf16[1,256,512]{2,1,0:T(8,128)(2,1)S(1)}, bf16[1,256,512]{2,1,0:T(8,128)(2,1)S(1)}, u32[]{:S(2)}, u32[]{:S(2)}) collective-permute-start(bf16[1,256,512]{2,1,0:T(8,128)(2,1)S(1)} %get-tuple-element.315), channel_id=1, source_target_pairs={{0,3},{1,0},{2,1},{3,2},{4,7},{5,4},{6,5},{7,6},{8,11},{9,8},{10,9... | collective-permute-start | bytes 786440 | tf_op jit(solution)/shard_map/ppermute | solution.py:406
  628.7 43.2 %collective-permute-start.77 = (bf16[4,2,256,1024]{3,2,0,1:T(8,128)(2,1)}, bf16[4,2,256,1024]{3,2,0,1:T(8,128)(2,1)}, u32[]{:S(2)}, u32[]{:S(2)}) collective-permute-start(bf16[4,2,256,1024]{3,2,0,1:T(8,128)(2,1)} %copy.97), channel_id=1, source_target_pairs={{0,4},{4,0},{8,12},{12,8},{1,5},{5,1},{9,13},{13,9},{2,6},{6,2},{1... | collective-permute-start | bytes 12582920 | tf_op jit(solution)/shard_map/ppermute | solution.py:411
  628.7 41.0 %collective-permute-start.74 = (bf16[2,256,512]{2,1,0:T(8,128)(2,1)}, bf16[2,256,512]{2,1,0:T(8,128)(2,1)}, u32[]{:S(2)}, u32[]{:S(2)}) collective-permute-start(bf16[2,256,512]{2,1,0:T(8,128)(2,1)} %pad_maximum_fusion.25), channel_id=1, source_target_pairs={{0,3},{1,0},{2,1},{3,2},{4,7},{5,4},{6,5},{7,6},{8,11},{9,8},{10,9... | collective-permute-start | bytes 1572872 | tf_op jit(solution)/shard_map/ppermute | solution.py:406
  629.6 40.1 %collective-permute-start.73 = (bf16[2,256,512]{2,1,0:T(8,128)(2,1)}, bf16[2,256,512]{2,1,0:T(8,128)(2,1)}, u32[]{:S(2)}, u32[]{:S(2)}) collective-permute-start(bf16[2,256,512]{2,1,0:T(8,128)(2,1)} %pad_maximum_fusion.24), channel_id=1, source_target_pairs={{0,1},{1,2},{2,3},{3,0},{4,5},{5,6},{6,7},{7,4},{8,9},{9,10},{10,1... | collective-permute-start | bytes 1572872 | tf_op jit(solution)/shard_map/ppermute | solution.py:406
  634.8 31.1 %collective-permute-start.76 = (bf16[128,1024]{1,0:T(8,128)(2,1)}, bf16[128,1024]{1,0:T(8,128)(2,1)}, u32[]{:S(2)}, u32[]{:S(2)}) collective-permute-start(bf16[128,1024]{1,0:T(8,128)(2,1)} %get-tuple-element.323), channel_id=1, source_target_pairs={{0,3},{1,0},{2,1},{3,2},{4,7},{5,4},{6,5},{7,6},{8,11},{9,8},{10,9... | collective-permute-start | bytes 786440 | tf_op jit(solution)/shard_map/ppermute | solution.py:406
  637.4 30.3 %collective-permute-start.75 = (bf16[128,1024]{1,0:T(8,128)(2,1)}, bf16[128,1024]{1,0:T(8,128)(2,1)}, u32[]{:S(2)}, u32[]{:S(2)}) collective-permute-start(bf16[128,1024]{1,0:T(8,128)(2,1)} %get-tuple-element.322), channel_id=1, source_target_pairs={{0,1},{1,2},{2,3},{3,0},{4,5},{5,6},{6,7},{7,4},{8,9},{9,10},{10,1... | collective-permute-start | bytes 786440 | tf_op jit(solution)/shard_map/ppermute | solution.py:406
  671.9 22.7 %collective-permute-start.80 = (bf16[256,512]{1,0:T(8,128)(2,1)S(1)}, bf16[256,512]{1,0:T(8,128)(2,1)S(1)}, u32[]{:S(2)}, u32[]{:S(2)}) collective-permute-start(bf16[256,512]{1,0:T(8,128)(2,1)S(1)} %slice_bitcast_fusion.35), channel_id=1, source_target_pairs={{0,8},{4,12},{8,0},{12,4},{1,9},{5,13},{9,1},{13,5},{2,10},{6,14},... | collective-permute-start | bytes 786440 | tf_op jit(solution)/shard_map/ppermute | solution.py:411
  672.9 21.7 %collective-permute-start.79 = (bf16[256,1024]{1,0:T(8,128)(2,1)}, bf16[256,1024]{1,0:T(8,128)(2,1)S(1)}, u32[]{:S(2)}, u32[]{:S(2)}) collective-permute-start(bf16[256,1024]{1,0:T(8,128)(2,1)} %pad_maximum_fusion.27), channel_id=1, source_target_pairs={{0,3},{1,0},{2,1},{3,2},{4,7},{5,4},{6,5},{7,6},{8,11},{9,8},{10,9... | collective-permute-start | bytes 1572872 | tf_op jit(solution)/shard_map/ppermute | solution.py:406
  675.6 22.6 %collective-permute-start.78 = (bf16[256,1024]{1,0:T(8,128)(2,1)}, bf16[256,1024]{1,0:T(8,128)(2,1)S(1)}, u32[]{:S(2)}, u32[]{:S(2)}) collective-permute-start(bf16[256,1024]{1,0:T(8,128)(2,1)} %pad_maximum_fusion.26), channel_id=1, source_target_pairs={{0,1},{1,2},{2,3},{3,0},{4,5},{5,6},{6,7},{7,4},{8,9},{9,10},{10,1... | collective-permute-start | bytes 1572872 | tf_op jit(solution)/shard_map/ppermute | solution.py:406
  698.2 25.4 %collective-permute-start.82 = (bf16[2,256,1024]{2,1,0:T(8,128)(2,1)}, bf16[2,256,1024]{2,1,0:T(8,128)(2,1)}, u32[]{:S(2)}, u32[]{:S(2)}) collective-permute-start(bf16[2,256,1024]{2,1,0:T(8,128)(2,1)} %get-tuple-element.336), channel_id=1, source_target_pairs={{0,8},{4,12},{8,0},{12,4},{1,9},{5,13},{9,1},{13,5},{2,10},{6,14},... | collective-permute-start | bytes 3145736 | tf_op jit(solution)/shard_map/ppermute | solution.py:411
  699.0 24.6 %collective-permute-start.81 = (bf16[512,1024]{1,0:T(8,128)(2,1)}, bf16[512,1024]{1,0:T(8,128)(2,1)}, u32[]{:S(2)}, u32[]{:S(2)}) collective-permute-start(bf16[512,1024]{1,0:T(8,128)(2,1)} %get-tuple-element.331), channel_id=1, source_target_pairs={{0,16},{16,0},{1,17},{17,1},{2,18},{18,2},{3,19},{19,3},{4,20},{20... | collective-permute-start | bytes 3145736 | tf_op jit(solution)/shard_map/ppermute | solution.py:411
  723.6 23.2 %collective-permute-start.84 = (bf16[2,256,1024]{2,1,0:T(8,128)(2,1)}, bf16[2,256,1024]{2,1,0:T(8,128)(2,1)S(1)}, u32[]{:S(2)}, u32[]{:S(2)}) collective-permute-start(bf16[2,256,1024]{2,1,0:T(8,128)(2,1)} %get-tuple-element.339), channel_id=1, source_target_pairs={{0,8},{4,12},{8,0},{12,4},{1,9},{5,13},{9,1},{13,5},{2,10},{6,14},... | collective-permute-start | bytes 3145736 | tf_op jit(solution)/shard_map/ppermute | solution.py:411
  724.9 26.3 %collective-permute-start.83 = (bf16[512,1024]{1,0:T(8,128)(2,1)S(1)}, bf16[512,1024]{1,0:T(8,128)(2,1)S(1)}, u32[]{:S(2)}, u32[]{:S(2)}) collective-permute-start(bf16[512,1024]{1,0:T(8,128)(2,1)S(1)} %copy-done.26), channel_id=1, source_target_pairs={{0,16},{16,0},{1,17},{17,1},{2,18},{18,2},{3,19},{19,3},{4,20},{20... | collective-permute-start | bytes 3145736 | tf_op jit(solution)/shard_map/ppermute | solution.py:411
  763.7 23.6 %collective-permute-start.91 = (bf16[256,1024]{1,0:T(8,128)(2,1)S(1)}, bf16[256,1024]{1,0:T(8,128)(2,1)S(1)}, u32[]{:S(2)}, u32[]{:S(2)}) collective-permute-start(bf16[256,1024]{1,0:T(8,128)(2,1)S(1)} %pad_maximum_fusion.29), channel_id=1, source_target_pairs={{0,3},{1,0},{2,1},{3,2},{4,7},{5,4},{6,5},{7,6},{8,11},{9,8},{10,9... | collective-permute-start | bytes 1572872 | tf_op jit(solution)/shard_map/ppermute | solution.py:406
  767.5 31.9 %collective-permute-start.90 = (bf16[256,1024]{1,0:T(8,128)(2,1)S(1)}, bf16[256,1024]{1,0:T(8,128)(2,1)S(1)}, u32[]{:S(2)}, u32[]{:S(2)}) collective-permute-start(bf16[256,1024]{1,0:T(8,128)(2,1)S(1)} %pad_maximum_fusion.28), channel_id=1, source_target_pairs={{0,1},{1,2},{2,3},{3,0},{4,5},{5,6},{6,7},{7,4},{8,9},{9,10},{10,1... | collective-permute-start | bytes 1572872 | tf_op jit(solution)/shard_map/ppermute | solution.py:406
  799.4 25.8 %collective-permute-start.96 = (bf16[2,256,512]{2,1,0:T(8,128)(2,1)}, bf16[2,256,512]{2,1,0:T(8,128)(2,1)}, u32[]{:S(2)}, u32[]{:S(2)}) collective-permute-start(bf16[2,256,512]{2,1,0:T(8,128)(2,1)} %pad_maximum_fusion.31), channel_id=1, source_target_pairs={{0,3},{1,0},{2,1},{3,2},{4,7},{5,4},{6,5},{7,6},{8,11},{9,8},{10,9... | collective-permute-start | bytes 1572872 | tf_op jit(solution)/shard_map/ppermute | solution.py:406
  801.1 25.2 %collective-permute-start.95 = (bf16[2,256,512]{2,1,0:T(8,128)(2,1)}, bf16[2,256,512]{2,1,0:T(8,128)(2,1)}, u32[]{:S(2)}, u32[]{:S(2)}) collective-permute-start(bf16[2,256,512]{2,1,0:T(8,128)(2,1)} %pad_maximum_fusion.30), channel_id=1, source_target_pairs={{0,1},{1,2},{2,3},{3,0},{4,5},{5,6},{6,7},{7,4},{8,9},{9,10},{10,1... | collective-permute-start | bytes 1572872 | tf_op jit(solution)/shard_map/ppermute | solution.py:406
  804.8 38.0 %collective-permute-start.94 = (bf16[384,1024]{1,0:T(8,128)(2,1)}, bf16[384,1024]{1,0:T(8,128)(2,1)}, u32[]{:S(2)}, u32[]{:S(2)}) collective-permute-start(bf16[384,1024]{1,0:T(8,128)(2,1)} %pad_maximum_fusion.19), channel_id=1, source_target_pairs={{0,3},{1,0},{2,1},{3,2},{4,7},{5,4},{6,5},{7,6},{8,11},{9,8},{10,9... | collective-permute-start | bytes 2359304 | tf_op jit(solution)/shard_map/ppermute | solution.py:406
  808.3 50.2 %collective-permute-start.93 = (bf16[384,1024]{1,0:T(8,128)(2,1)}, bf16[384,1024]{1,0:T(8,128)(2,1)}, u32[]{:S(2)}, u32[]{:S(2)}) collective-permute-start(bf16[384,1024]{1,0:T(8,128)(2,1)} %pad_maximum_fusion.18), channel_id=1, source_target_pairs={{0,1},{1,2},{2,3},{3,0},{4,5},{5,6},{6,7},{7,4},{8,9},{9,10},{10,1... | collective-permute-start | bytes 2359304 | tf_op jit(solution)/shard_map/ppermute | solution.py:406
  (124 other events, 1419.5 us)

commit v4 on v3

--- a/solution.py
+++ b/solution.py
@@ -989,40 +989,60 @@
         value = hold(value)
         return ring(value, "tensor", 1), ring(value, "tensor", -1)
 
-    def far_narrow(left, right):
-        return ring(hold(left[0]), "tensor", 1), ring(hold(right[1]), "tensor", -1)
-
-    def far_broad(left, right):
+    def far_halves(left, right):
         half = left.shape[0] // 2
         return ring(hold(left[:half]), "tensor", 1), ring(hold(right[half:]), "tensor", -1)
 
+    def own_half(blocks):
+        return lax.dynamic_slice_in_dim(blocks, section * (width // 2), width // 2, 2)
+
+    def both_halves(own, got):
+        own = own.reshape(length, width // 2)
+        got = got.reshape(length, width // 2)
+        low = jnp.where(first_section, own, got)
+        high = jnp.where(first_section, got, own)
+        return relative(jnp.concatenate([low, high], axis=1), across)
+
+    def stacked(own, got):
+        return jnp.stack([own, got])
+
     got_narrow = pass_half(narrow)
     got_small = swap(small, "section", 1)
-    tick(got_narrow, got_small)
+    blocks = own_half(acts_in[:, :, 0, :])
+    near = exchange_near(blocks, along, hold)
+    tick(got_narrow, got_small, near)
     narrow_shards = by_layer(narrow, got_narrow)
     small = jnp.where(first_section, jnp.stack([small, got_small]), jnp.stack([got_small, small]))
-    blocks = acts_in[:, :, 0, :]
-    near = exchange_near(blocks, along, hold)
+    left, right = both_ways(narrow_shards[0])
+    far = exchange_far(near, hold)
     got_broad = pass_half(broad)
-    pair = jnp.stack([narrow_shards[0], x_swap(narrow_shards[0])])
+    got_own = x_swap(narrow_shards[0])
     small = jnp.stack([small, core_swap(small)])
     small = jnp.concatenate([small, swap(small, "dp", 2)])
-    tick(near, got_broad, pair, small)
+    tick(left, right, far, got_broad, got_own, small)
+    own_acts = exchanged(blocks, near, far, along)
+    got_acts = y_swap(own_acts)
+    narrow_far = far_halves(left, right)
+    got_left, got_right = x_swap(left), x_swap(right)
+    small = jnp.stack([small, swap(hold(small), "tensor", 1)])
+    tick(narrow_far, got_left, got_right, small)
     broad_shards = by_layer(broad, got_broad)
-    far = exchange_far(near, hold)
-    left, right = both_ways(pair)
-    broad_own = jnp.stack([broad_shards[0], x_swap(broad_shards[0])])
-    small = jnp.stack([small, swap(hold(small), "tensor", 1)])
-    small = jnp.concatenate([small, swap(small, "tensor", 2)])
-    tick(far, left, right, broad_own, small)
-    acts = exchanged(blocks, near, far, along).reshape(length, width)
-    acts = relative(acts, across)
-    narrow_far = far_narrow(left, right)
-    others = [core_swap(pair), core_swap(left), core_swap(right)]
-    tick(narrow_far, others)
-    narrow_far = jnp.stack(narrow_far)
-    others.append(core_swap(narrow_far))
-    narrow_zero = (pair, left, right, narrow_far, *others)
+    small = jnp.concatenate([small, swap(hold(small), "tensor", 2)])
+    broad_left, broad_right = both_ways(broad_shards[0])
+    narrow_far = jnp.concatenate(narrow_far, axis=0)
+    got_far = x_swap(narrow_far)
+    pieces = [
+        stacked(narrow_shards[0], got_own),
+        stacked(left, got_left),
+        stacked(right, got_right),
+    ]
+    others = [core_swap(piece) for piece in pieces]
+    tick(got_far, others, got_acts, small)
+    acts = both_halves(own_acts, got_acts)
+    pieces.append(stacked(narrow_far, got_far))
+    others.append(core_swap(pieces[3]))
+    got_own = x_swap(broad_shards[0])
+    narrow_zero = (*pieces, *others)
     tick(others[3])
 
     share = norm_gains.shape[2]
@@ -1075,76 +1095,87 @@
 
     acts = hold(acts)
     first = project(0, 0, (acts, 0), narrow_zero, ())
+    tick(first, broad_left, broad_right)
+    got_left = x_swap(broad_left)
     first = project(0, 1, (acts, chunk), narrow_zero, first)
-    broad_left, broad_right = both_ways(broad_shards[0])
-    tick(first, broad_left, broad_right)
+    tick(first, got_own)
     ln_a0, ln_m0, qkv0 = first
+    broad_far = far_halves(broad_left, broad_right)
+    got_right = x_swap(broad_right)
     ctx0, lse0 = run_attend(hold(qkv0))
-    broad_far = far_broad(broad_left, broad_right)
-    got_left, got_right = x_swap(broad_left), x_swap(broad_right)
     tick(ctx0, broad_far, got_left, got_right)
-    broad_left = jnp.stack([broad_left, got_left])
-    broad_right = jnp.stack([broad_right, got_right])
     broad_far = jnp.concatenate(broad_far, axis=0)
     got_far = x_swap(broad_far)
-    others = [core_swap(broad_own), core_swap(broad_left), core_swap(broad_right)]
+    pieces = [
+        stacked(broad_shards[0], got_own),
+        stacked(broad_left, got_left),
+        stacked(broad_right, got_right),
+    ]
+    others = [core_swap(piece) for piece in pieces]
     tick(got_far, others)
-    broad_far = jnp.stack([broad_far, got_far])
-    others.append(core_swap(broad_far))
-    broad_zero = (broad_own, broad_left, broad_right, broad_far, *others)
-    pair = jnp.stack([narrow_shards[1], x_swap(narrow_shards[1])])
-    tick(others[3], pair)
+    pieces.append(stacked(broad_far, got_far))
+    others.append(core_swap(pieces[3]))
+    broad_zero = (*pieces, *others)
+    tick(others[3])
     first, part_a = feed(0, 0, ctx0, ln_m0, narrow_zero, broad_zero, ())
-    broad_left, broad_right = both_ways(broad_shards[1])
-    tick(part_a, broad_left, broad_right)
+    left, right = both_ways(narrow_shards[1])
+    got_own = x_swap(narrow_shards[1])
+    broad_own = x_swap(broad_shards[1])
+    tick(part_a, left, right, got_own, broad_own)
     first, part_b = feed(0, 1, ctx0, ln_m0, narrow_zero, broad_zero, first)
     act0, slope0 = first
     got_a = y_swap(part_a)
-    left, right = both_ways(pair)
-    got_own = x_swap(broad_shards[1])
-    tick(part_b, got_a, left, right, got_own)
+    narrow_far = far_halves(left, right)
+    broad_left, broad_right = both_ways(broad_shards[1])
+    tick(part_b, got_a, narrow_far, broad_left, broad_right)
     got_b = y_swap(part_b)
-    narrow_far = far_narrow(left, right)
+    got_left, got_right = x_swap(left), x_swap(right)
+    x1_a = join(0, acts[:chunk], part_a, got_a)
+    tick(got_left, got_right)
+    narrow_far = jnp.concatenate(narrow_far, axis=0)
+    got_far = x_swap(narrow_far)
+    pieces = [
+        stacked(narrow_shards[1], got_own),
+        stacked(left, got_left),
+        stacked(right, got_right),
+    ]
+    others = [core_swap(piece) for piece in pieces]
+    tick(got_b, got_far, others)
+    x1_b = join(0, acts[chunk:], part_b, got_b)
+    pieces.append(stacked(narrow_far, got_far))
+    others.append(core_swap(pieces[3]))
+    narrow_one = (*pieces, *others)
+    tick(others[3], x1_a, x1_b)
+
+    broad_far = far_halves(broad_left, broad_right)
     got_left = x_swap(broad_left)
-    others = [core_swap(pair), core_swap(left), core_swap(right)]
-    x1_a = join(0, acts[:chunk], part_a, got_a)
-    tick(got_b, narrow_far, got_left, others)
-    x1_b = join(0, acts[chunk:], part_b, got_b)
-    narrow_far = jnp.stack(narrow_far)
-    others.append(core_swap(narrow_far))
-    narrow_one = (pair, left, right, narrow_far, *others)
-    tick(others[3], x1_a, x1_b)
-
     first = project(1, 0, (hold(x1_a), 0), narrow_one, ())
     first = project(1, 1, (x1_b, 0), narrow_one, first)
     ln_a1, ln_m1, qkv1 = first
-    broad_far = far_broad(broad_left, broad_right)
-    got_right = x_swap(broad_right)
-    tick(first, broad_far, got_right)
+    tick(first, broad_far, got_left)
+    broad_far = jnp.concatenate(broad_far, axis=0)
+    got_right, got_far = x_swap(broad_right), x_swap(broad_far)
+    pieces = [stacked(broad_shards[1], broad_own), stacked(broad_left, got_left)]
+    others = [core_swap(piece) for piece in pieces]
     ctx1, lse1 = run_attend(hold(qkv1))
-    broad_own = jnp.stack([broad_shards[1], got_own])
-    broad_left = jnp.stack([broad_left, got_left])
-    broad_right = jnp.stack([broad_right, got_right])
-    broad_far = jnp.concatenate(broad_far, axis=0)
-    got_far = x_swap(broad_far)
-    others = [core_swap(broad_own), core_swap(broad_left), core_swap(broad_right)]
-    tick(ctx1, got_far, others)
-    broad_far = jnp.stack([broad_far, got_far])
-    others.append(core_swap(broad_far))
-    broad_one = (broad_own, broad_left, broad_right, broad_far, *others)
-    tick(others[3])
+    tick(ctx1, got_right, got_far, others)
+    pieces += [stacked(broad_right, got_right), stacked(broad_far, got_far)]
+    others += [core_swap(piece) for piece in pieces[2:]]
+    broad_one = (*pieces, *others)
+    tick(others[2:])
     first, part_a = feed(1, 0, ctx1, ln_m1, narrow_one, broad_one, ())
-    blocks = cotangent[:, :, 0, :]
+    blocks = own_half(cotangent[:, :, 0, :])
     near = exchange_near(blocks, along, hold)
     tick(part_a, near)
     first, part_b = feed(1, 1, ctx1, ln_m1, narrow_one, broad_one, first)
     act1, slope1 = first
     far = exchange_far(near, hold)
-    got_a = y_swap(part_a)
-    tick(part_b, far, got_a)
-
-    grads = exchanged(blocks, near, far, along).reshape(length, width)
-    grads = hold(relative(grads, across))
+    tick(far)
+    own_grads = exchanged(blocks, near, far, along)
+    got_grads = y_swap(own_grads)
+    tick(part_b, got_grads)
+
+    grads = hold(both_halves(own_grads, got_grads))
     n_heads = ctx0.shape[1]
 
     def back(i, source, slope, narrow, broad, filled):
@@ -1157,88 +1188,91 @@
     first, up_b, g_b = back(1, (grads, chunk), slope1, narrow_one, broad_one, first)
     d_up1, d_ctx1 = first
     sums_one = [None, g_a + g_b, None, up_a + up_b]
-    got_b = y_swap(part_b)
-    tick(first, got_b)
-    x2 = jnp.concatenate(
-        [join(1, x1_a, part_a, got_a), join(1, x1_b, part_b, got_b)], axis=0
-    )
+    got_a = y_swap(part_a)
+    tick(first, got_a)
     x1 = jnp.concatenate([x1_a, x1_b], axis=0)
 
     def to_blocks(values):
         return relative(values, across).reshape(4, positions, width)
 
+    d_qkv1, sums_one[2] = run_attend_back(qkv1, hold(d_ctx1), lse1, tables)
+    got_b = y_swap(part_b)
+    tick(d_qkv1, got_b)
+    x2 = jnp.concatenate(
+        [join(1, x1_a, part_a, got_a), join(1, x1_b, hold(part_b), got_b)], axis=0
+    )
     out_blocks = to_blocks(jnp.where(first_section, x1, x2))
-    d_qkv1, sums_one[2] = run_attend_back(qkv1, hold(d_ctx1), lse1, tables)
-    out_near = exchange_near(out_blocks, along, hold)
-    tick(d_qkv1, out_near)
     part_a, sum_a = run_norm_back(
         (x1_a, 0), hold(d_qkv1), d_up1, all_vecs[1], narrow_one, broad_one, 0, chunk
     )
-    out_far = exchange_far(out_near, hold)
-    tick(part_a, out_far)
-    acts_local = exchanged(out_blocks, out_near, out_far, along)
+    tick(part_a, out_blocks)
+    got_a = y_swap(part_a)
     part_b, sum_b = run_norm_back(
         (x1_b, 0), hold(d_qkv1), d_up1, all_vecs[1], narrow_one, broad_one, chunk, chunk
     )
     sums_one[0] = (sum_a + sum_b)[:4]
     keep_broad, send = run_weight_grad([[hold(ln_m1)], [grads]], [d_up1, act1])
-    got_a = y_swap(part_a)
     tick(part_b, keep_broad, got_a)
-    keep_narrow, send_narrow = run_weight_grad([[hold(ln_a1)], [grads]], [d_qkv1, ctx1])
     got_b = y_swap(part_b)
     got_core = core_swap(send)
+    out_near = exchange_near(out_blocks, along, hold)
+    keep_narrow, send_narrow = run_weight_grad([[hold(ln_a1)], [grads]], [d_qkv1, ctx1])
     tick(keep_narrow, got_b, got_core)
 
     def lower(above, part, got):
         total = part.astype(jnp.float32) + got.astype(jnp.float32)
         return (above.astype(jnp.float32) + total).astype(bf)
 
-    g1_a = hold(lower(grads[:chunk], part_a, got_a))
-    g1_b = hold(lower(grads[chunk:], part_b, got_b))
-    broad_sum = add_wide(keep_broad, got_core)
-    first, up_a, g_a = back(0, (g1_a, 0), slope0, narrow_zero, broad_zero, ())
+    g1_a = lower(grads[:chunk], hold(part_a), got_a)
+    g1_b = lower(grads[chunk:], hold(part_b), got_b)
+    broad_sum = add_wide(hold(keep_broad), got_core)
+    got_core = core_swap(send_narrow)
+    got_x = [x_swap(broad_sum[2:, 1])]
+    first, up_a, g_a = back(0, (hold(g1_a), 0), slope0, narrow_zero, broad_zero, ())
     first, up_b, g_b = back(1, (g1_b, 0), slope0, narrow_zero, broad_zero, first)
     d_up0, d_ctx0 = first
     sums_zero = [None, g_a + g_b, None, up_a + up_b]
-    got_core = core_swap(send_narrow)
-    got_x = [x_swap(broad_sum[2:, 1])]
-    tick(first, got_core, got_x)
-    narrow_sum = add_wide(keep_narrow, got_core)
-    narrow_sum = [narrow_sum[k] for k in range(4)]
+    tick(first, got_core, got_x, out_near)
+    out_far = exchange_far(out_near, hold)
+    narrow_sum = add_wide(hold(keep_narrow), got_core)
+    got_narrow = x_swap(narrow_sum[:, 1])
+    got_x.append(x_swap(broad_sum[:2, 1]))
     keep_broad, send = run_weight_grad([[hold(ln_m0)], [g1_a, g1_b]], [d_up0, act0])
-    narrow_got = ring_first(narrow_sum, hold)
-    got_x.append(x_swap(broad_sum[:2, 1]))
-    tick(keep_broad, narrow_got, got_x)
+    tick(keep_broad, out_far)
 
     def after_x(total, got):
         late = add_wide(total[2:, 0], got[0])
         early = add_wide(total[:2, 0], got[1])
         return [early[0], early[1], late[0], late[1]]
 
-    broad_one_sum = after_x(broad_sum, got_x)
+    got_core = core_swap(send)
+    late = add_wide(hold(broad_sum[2:, 0]), got_x[0])
+    broad_got = ring_first([None, None, late[0], late[1]], hold)
     d_qkv0, sums_zero[2] = run_attend_back(qkv0, hold(d_ctx0), lse0, tables)
-    narrow_got = ring_second(narrow_sum, narrow_got, hold)
-    broad_got = ring_first(broad_one_sum, hold)
-    got_core = core_swap(send)
-    tick(d_qkv0, narrow_got, broad_got, got_core)
-    narrow_total = ring_total(narrow_sum[0], narrow_got)
-    broad_sum = add_wide(keep_broad, got_core)
+    tick(d_qkv0, broad_got, got_core, got_x, got_narrow)
+    early = add_wide(hold(broad_sum[:2, 0]), got_x[1])
+    broad_one_sum = [early[0], early[1], late[0], late[1]]
+    narrow_sum = add_wide(hold(narrow_sum[:, 0]), got_narrow)
+    narrow_sum = [narrow_sum[k] for k in range(4)]
+    broad_sum = add_wide(hold(keep_broad), got_core)
+    got_x = [x_swap(broad_sum[2:, 1])]
+    broad_got = ring_second(broad_one_sum, broad_got, hold)
     part_a, sum_a = run_norm_back(
         (acts, 0), hold(d_qkv0), d_up0, all_vecs[0], narrow_zero, broad_zero, 0, chunk
     )
-    broad_got = ring_second(broad_one_sum, broad_got, hold)
-    got_x = x_swap(narrow_total[1])
-    tick(part_a, broad_got, got_x)
-    one_narrow = add_wide(narrow_total[0], got_x)
-    one_broad = ring_total(broad_one_sum[0], broad_got)
+    tick(part_a, broad_got)
+    got_a = y_swap(part_a)
+    narrow_got = ring_first(narrow_sum, hold)
     part_b, sum_b = run_norm_back(
         (acts, chunk), hold(d_qkv0), d_up0, all_vecs[0], narrow_zero, broad_zero, chunk, chunk
     )
     sums_zero[0] = (sum_a + sum_b)[:4]
+    tick(part_b, got_x, narrow_got)
+    got_b = y_swap(part_b)
+    narrow_got = ring_second(narrow_sum, narrow_got, hold)
+    got_x.append(x_swap(broad_sum[:2, 1]))
     keep_narrow, send_narrow = run_weight_grad([[hold(ln_a0)], [g1_a, g1_b]], [d_qkv0, ctx0])
-    got_a = y_swap(part_a)
-    got_x = [x_swap(broad_sum[2:, 1])]
-    tick(part_b, keep_narrow, got_a, got_x)
+    tick(keep_narrow, got_a, narrow_got)
 
     flat = []
     for norm_sums, sum_g, sum_qkv, sum_up in (sums_zero, sums_one):
@@ -1248,37 +1282,42 @@
         both = jnp.stack([pick(both, order[k]) for k in range(4)])
         flat.append(jnp.concatenate([feature.reshape(-1), both.reshape(-1)]))
     flat = jnp.stack(flat)
-    got_b = y_swap(part_b)
-    got_x.append(x_swap(broad_sum[:2, 1]))
-    late = add_wide(broad_sum[2:, 0], got_x[0])
-    broad_got = ring_first([None, None, late[0], late[1]], hold)
     got_core = core_swap(send_narrow)
-    tick(got_b, got_x, broad_got, got_core)
+    late = add_wide(hold(broad_sum[2:, 0]), got_x[0])
+    broad_next = ring_first([None, None, late[0], late[1]], hold)
+    tick(got_b, got_x, broad_next, got_core)
+    early = add_wide(hold(broad_sum[:2, 0]), got_x[1])
+    broad_zero_sum = [early[0], early[1], late[0], late[1]]
+    grads_low = jnp.concatenate(
+        [lower(g1_a, hold(part_a), got_a), lower(g1_b, hold(part_b), got_b)], axis=0
+    )
+    g1 = jnp.concatenate([g1_a, g1_b], axis=0)
+    grad_blocks = to_blocks(jnp.where(first_section, grads_low, g1))
+    tick(grad_blocks)
+    grad_near = exchange_near(grad_blocks, along, hold)
+    zero_sum = add_wide(keep_narrow, got_core)
+    got_narrow = x_swap(zero_sum[:, 1])
     flat = flat + core_swap(flat)
-    early = add_wide(broad_sum[:2, 0], got_x[1])
-    broad_zero_sum = [early[0], early[1], late[0], late[1]]
-    narrow_sum = add_wide(keep_narrow, got_core)
-    narrow_sum = [narrow_sum[k] for k in range(4)]
-    grads_low = jnp.concatenate([lower(g1_a, part_a, got_a), lower(g1_b, part_b, got_b)], axis=0)
-    g1 = jnp.concatenate([g1_a, g1_b], axis=0)
-    out_blocks = to_blocks(jnp.where(first_section, grads_low, g1))
-    narrow_got = ring_first(narrow_sum, hold)
-    broad_got = ring_second(broad_zero_sum, broad_got, hold)
-    tick(narrow_got, broad_got, flat)
+    one_broad = ring_total(hold(broad_one_sum[0]), broad_got)
+    one_narrow = ring_total(hold(narrow_sum[0]), narrow_got)
+    acts_local = exchanged(hold(out_blocks), out_near, out_far, along)
+    tick(grad_near, got_narrow, flat, acts_local)
+    broad_next = ring_second(broad_zero_sum, broad_next, hold)
+    zero_sum = add_wide(hold(zero_sum[:, 0]), got_narrow)
+    zero_sum = [zero_sum[k] for k in range(4)]
+    narrow_next = ring_first(zero_sum, hold)
     flat = flat + x_swap(flat)
-    zero_broad = ring_total(broad_zero_sum[0], broad_got)
-    narrow_got = ring_second(narrow_sum, narrow_got, hold)
-    out_near = exchange_near(out_blocks, along, hold)
+    tick(narrow_next, broad_next, flat)
+    zero_broad = ring_total(broad_zero_sum[0], broad_next)
     broad_send = y_swap(jnp.where(first_section, one_broad, zero_broad))
-    tick(narrow_got, out_near, broad_send, flat)
+    narrow_next = ring_second(zero_sum, narrow_next, hold)
+    grad_far = exchange_far(grad_near, hold)
     flat = flat + swap(hold(flat), "tensor", 1)
-    narrow_total = ring_total(narrow_sum[0], narrow_got)
-    out_far = exchange_far(out_near, hold)
-    zero_narrow = add_wide(narrow_total[0], x_swap(narrow_total[1]))
-    tick(out_far, zero_narrow, flat)
+    tick(narrow_next, grad_far, broad_send, flat)
+    zero_narrow = ring_total(zero_sum[0], narrow_next)
+    narrow_send = y_swap(jnp.where(first_section, one_narrow, zero_narrow))
     flat = flat + swap(hold(flat), "tensor", 2)
-    grad_local = exchanged(out_blocks, out_near, out_far, along)
-    narrow_send = y_swap(jnp.where(first_section, one_narrow, zero_narrow))
+    grad_local = exchanged(grad_blocks, grad_near, grad_far, along)
 
     def whole_layer(keep_pair, got):
         keep = jnp.where(first_section, *keep_pair).astype(jnp.float32)

time: 902 us -> 860 us (0.953)
  waiting for transfers between devices: 269 us -> 245 us
  local copies, waits for them, and re-layouts: 100 us -> 88.7 us
    ppermute x48, waiting for transfers between devices: 158 us -> 111 us  [ring(): lax.ppermute(value, axis, [(i, (i + by) % length) for i in range(length)])]
    ppermute x58 -> x66, waiting for transfers between devices: 112 us -> 134 us  [swap(): return lax.ppermute(value, axis, [(i, i ^ bit) for i in range(length)])]
    unnamed x171 -> x191, local copies, waits for them, and re-layouts: 18.5 us -> 15.3 us
    ppermute x58 -> x66, starting transfers between devices: 45.6 us -> 45.7 us  [swap(): return lax.ppermute(value, axis, [(i, i ^ bit) for i in range(length)])]
    convert_element_type x12 -> x16, other arithmetic: 20.3 us -> 20.3 us  [add_wide(): (left.astype(jnp.float32) + right.astype(jnp.float32)).astype(jnp.bfloat16)]
  transfers between devices with their start and end apart: 106 -> 114, of which waited for: 42 -> 37; matrix products, arithmetic and copies ran while one was open for 17% -> 15% of each run, Pallas kernels for 34% -> 35%
where the time goes in v4:
time: 860 us; the launch traced here: 851 us
  Pallas kernels  307 us (36%)
  waiting for transfers between devices  245 us (28%)
  starting transfers between devices  118 us (14%)
  local copies, waits for them, and re-layouts  88.7 us (10%)
  other arithmetic  81.8 us (10%)
  between operations  11.6 us (1%)
    pallas_call x24, Pallas kernels, call(): pl.pallas_call(run, name=name, grid=grid, in_specs=[pl.BlockSpec(block, i...  307 us
    ppermute x66, waiting for transfers between devices, swap(): return lax.ppermute(value, axis, [(i, i ^ bit) for i in range(length)])  134 us
    ppermute x48, waiting for transfers between devices, ring(): lax.ppermute(value, axis, [(i, (i + by) % length) for i in range(length)])  111 us
    ppermute x48, starting transfers between devices, ring(): lax.ppermute(value, axis, [(i, (i + by) % length) for i in range(length)])  72.1 us
    ppermute x66, starting transfers between devices, swap(): return lax.ppermute(value, axis, [(i, i ^ bit) for i in range(length)])  45.7 us
    convert_element_type x16, other arithmetic, add_wide(): (left.astype(jnp.float32) + right.astype(jnp.float32)).astype(jnp.bfloat16)  20.3 us
  transfers between devices with their start and end apart: 114, of which 37 were waited for; matrix products, arithmetic and copies ran while one was open for 15% of the time, Pallas kernels for 35%

profile of v4, /device:TPU:0, one launch (start us, length us, event | category | flops | bytes accessed | tf_op | source)
XLA Modules:
  0.0 851.5 jit_solution(17164017739879997817)
XLA Ops:
  4.1 3.0 collective-permute-start
  28.0 3.8 collective-permute-start.7
  41.4 4.1 collective-permute-done.4
  45.6 4.9 collective-permute-done.5
  58.0 4.9 collective-permute-done.13
  71.0 19.4 %collective-permute-done.22 = f32[2,4,2,832]{3,2,1,0:T(2,128)S(1)} collective-permute-done((f32[2,4,2,832]{3,2,1,0:T(2,128)S(1)}, f32[2,4,2,832]{3,2,1,0:T(2,128)S(1)}, u32[]{:S(2)}, u32[]{:S(2)}) %collective-permute-start.22) | collective-permute-done | bytes 53280 | tf_op jit(solution)/shard_map/ppermute | solution.py:411
  111.7 6.4 norm_qkv.4
  119.4 6.4 norm_qkv.5
  129.3 19.0 %attend.2 = (bf16[1024,512]{1,0:T(8,128)(2,1)}, f32[4,8,1024]{2,1,0:T(8,128)}) custom-call(bf16[1024,1536]{1,0:T(8,128)(2,1)} %get-tuple-element.238.refs_0_.refs_1_.refs_2_, bf16[1024,1536]{1,0:T(8,128)(2,1)} %get-tuple-element.238.refs_0_.refs_1_.refs_2_, bf16[1024,1536]{1,0:T(8,128)(2,1)} %get-tuple-element.238.refs_0_.refs_1_.refs_2_), custom_call_target="tpu_custom_call" | custom-call | flops 19000000512 | bytes 1048576 | tf_op jit(solution)/shard_map/attend/pallas_call | solution.py:530
  156.0 13.0 %collective-permute-done.31 = bf16[256,1024]{1,0:T(8,128)(2,1)S(1)} collective-permute-done((bf16[256,1024]{1,0:T(8,128)(2,1)S(1)}, bf16[256,1024]{1,0:T(8,128)(2,1)S(1)}, u32[]{:S(2)}, u32[]{:S(2)}) %collective-permute-start.31) | collective-permute-done | bytes 524320 | tf_op jit(solution)/shard_map/ppermute | solution.py:411
  175.0 4.3 collective-permute-start.37
  181.3 15.8 %mlp_out.4 = (bf16[1024,2048]{1,0:T(8,128)(2,1)}, bf16[1024,2048]{1,0:T(8,128)(2,1)}, bf16[512,1024]{1,0:T(8,128)(2,1)}) custom-call(bf16[1024,512]{1,0:T(8,128)(2,1)} %get-tuple-element.255.refs_0_.refs_4_, bf16[1024,1024]{1,0:T(8,128)(2,1)} %get-tuple-element.339.refs_1_.refs_0_, f32[1,2048]{1,0:T(1,128)} %bitcast.421, ...), custom_call_target="tpu_custom_call" | custom-call | flops 16000000000 | bytes 1048576 | tf_op jit(solution)/shard_map/mlp_out/pallas_call | solution.py:530
  198.6 3.8 collective-permute-start.44
  204.5 15.8 %mlp_out.5 = (bf16[1024,2048]{1,0:T(8,128)(2,1)}, bf16[1024,2048]{1,0:T(8,128)(2,1)}, bf16[512,1024]{1,0:T(8,128)(2,1)}) custom-call(bf16[1024,512]{1,0:T(8,128)(2,1)} %get-tuple-element.255.refs_0_.refs_4_, bf16[1024,1024]{1,0:T(8,128)(2,1)} %get-tuple-element.339.refs_1_.refs_0_, ...), custom_call_target="tpu_custom_call", output_to_operand_aliasing={{0}: (27, {}), {1}: (28, {})} | custom-call | flops 16000000000 | bytes 1048576 | tf_op jit(solution)/shard_map/mlp_out/pallas_call | solution.py:530
  220.3 5.4 collective-permute-done.42
  225.6 4.5 collective-permute-done.41
  233.3 5.7 collective-permute-done.47
  255.6 4.7 add_convert_fusion.17
  263.3 6.4 norm_qkv.6
  269.7 6.3 norm_qkv.7
  280.7 19.1 %attend.3 = (bf16[1024,512]{1,0:T(8,128)(2,1)}, f32[4,8,1024]{2,1,0:T(8,128)}) custom-call(bf16[1024,1536]{1,0:T(8,128)(2,1)} %get-tuple-element.280.refs_0_.refs_1_.refs_2_, bf16[1024,1536]{1,0:T(8,128)(2,1)} %get-tuple-element.280.refs_0_.refs_1_.refs_2_, bf16[1024,1536]{1,0:T(8,128)(2,1)} %get-tuple-element.280.refs_0_.refs_1_.refs_2_), custom_call_target="tpu_custom_call" | custom-call | flops 19000000512 | bytes 1048576 | tf_op jit(solution)/shard_map/attend/pallas_call | solution.py:530
  311.4 15.7 %mlp_out.6 = (bf16[1024,2048]{1,0:T(8,128)(2,1)}, bf16[1024,2048]{1,0:T(8,128)(2,1)}, bf16[512,1024]{1,0:T(8,128)(2,1)}) custom-call(bf16[1024,512]{1,0:T(8,128)(2,1)} %get-tuple-element.292.refs_0_.refs_3_, bf16[1024,1024]{1,0:T(8,128)(2,1)} %get-tuple-element.315.refs_1_.refs_0_, f32[1,2048]{1,0:T(1,128)} %bitcast.419, bf16[2,256,512]{2,1,0:T(8,128)(2,1)} %copy-done.46, ...), custom_call_target="tpu_custom_call" | custom-call | flops 16000000000 | bytes 1048576 | tf_op jit(solution)/shard_map/mlp_out/pallas_call | solution.py:530
  333.7 3.9 collective-permute-done.64
  339.2 15.7 %mlp_out.7 = (bf16[1024,2048]{1,0:T(8,128)(2,1)}, bf16[1024,2048]{1,0:T(8,128)(2,1)}, bf16[512,1024]{1,0:T(8,128)(2,1)}) custom-call(bf16[1024,512]{1,0:T(8,128)(2,1)} %get-tuple-element.292.refs_0_.refs_3_, bf16[1024,1024]{1,0:T(8,128)(2,1)} %get-tuple-element.315.refs_1_.refs_0_, ...), custom_call_target="tpu_custom_call", output_to_operand_aliasing={{0}: (27, {}), {1}: (28, {})} | custom-call | flops 16000000000 | bytes 1048576 | tf_op jit(solution)/shard_map/mlp_out/pallas_call | solution.py:530
  354.9 8.9 %collective-permute-done.66 = bf16[4,256,512]{2,1,0:T(8,128)(2,1)S(1)} collective-permute-done((bf16[4,256,512]{2,1,0:T(8,128)(2,1)S(1)}, bf16[4,256,512]{2,1,0:T(8,128)(2,1)S(1)}, u32[]{:S(2)}, u32[]{:S(2)}) %collective-permute-start.66) | collective-permute-done | bytes 1048608 | tf_op jit(solution)/shard_map/ppermute | solution.py:411
  366.7 7.6 mlp_back.4
  374.3 7.7 mlp_back.5
  381.9 8.5 collective-permute-done.67
  391.3 26.1 %attend_back.2 = (bf16[1024,1536]{1,0:T(8,128)(2,1)}, f32[1,1536]{1,0:T(1,128)}) custom-call(bf16[1024,1536]{1,0:T(8,128)(2,1)} %get-tuple-element.280.refs_0_.refs_1_.refs_2_, bf16[1024,1536]{1,0:T(8,128)(2,1)} %get-tuple-element.280.refs_0_.refs_1_.refs_2_, bf16[1024,1536]{1,0:T(8,128)(2,1)} %get-tuple-element.280.refs_0_.refs_1_.refs_2_, ...), custom_call_target="tpu_custom_call" | custom-call | flops 25999998976 | bytes 1048576 | tf_op jit(solution)/shard_map/attend_back/pallas_call | solution.py:530
  417.5 3.4 add_convert_fusion.15
  422.6 11.3 %norm_back.4 = (bf16[512,1024]{1,0:T(8,128)(2,1)}, f32[8,1024]{1,0:T(8,128)}) custom-call(bf16[512,1024]{1,0:T(8,128)(2,1)} %get-tuple-element.270.refs_0_, bf16[1024,1536]{1,0:T(8,128)(2,1)} %get-tuple-element.313.refs_1_.refs_2_, bf16[1024,2048]{1,0:T(8,128)(2,1)} %get-tuple-element.305.refs_2_, f32[8,1024]{1,0:T(8,128)} %concatenate.206.refs_1_.refs_3_, ...), custom_call_target="tpu_custom_call" | custom-call | flops 10499999744 | bytes 1048576 | tf_op jit(solution)/shard_map/norm_back/pallas_call | solution.py:530
  435.0 15.0 %weight_grad.4 = (bf16[4,2,256,1024]{3,2,1,0:T(8,128)(2,1)}, bf16[4,2,256,1024]{3,2,1,0:T(8,128)(2,1)}) custom-call(bf16[1024,1024]{1,0:T(8,128)(2,1)} %get-tuple-element.315.refs_1_.refs_0_, bf16[1024,1024]{1,0:T(8,128)(2,1)} %pad_maximum_fusion.1.refs_0_.refs_1_, bf16[1024,2048]{1,0:T(8,128)(2,1)} %get-tuple-element.305.refs_2_, ...), custom_call_target="tpu_custom_call" | custom-call | flops 14000000000 | bytes 1048576 | tf_op jit(solution)/shard_map/weight_grad/pallas_call | solution.py:530
  450.0 10.7 %norm_back.5 = (bf16[512,1024]{1,0:T(8,128)(2,1)}, f32[8,1024]{1,0:T(8,128)}) custom-call(bf16[512,1024]{1,0:T(8,128)(2,1)} %get-tuple-element.451.refs_0_, bf16[1024,1536]{1,0:T(8,128)(2,1)} %get-tuple-element.313.refs_1_.refs_2_, bf16[1024,2048]{1,0:T(8,128)(2,1)} %get-tuple-element.305.refs_2_, f32[8,1024]{1,0:T(8,128)} %concatenate.206.refs_1_.refs_3_, ...), custom_call_target="tpu_custom_call" | custom-call | flops 10499999744 | bytes 1048576 | tf_op jit(solution)/shard_map/norm_back/pallas_call | solution.py:530
  460.9 5.0 copy.101
  479.6 12.4 %weight_grad.5 = (bf16[4,2,256,512]{3,2,1,0:T(8,128)(2,1)}, bf16[4,2,256,512]{3,2,1,0:T(8,128)(2,1)}) custom-call(bf16[1024,1024]{1,0:T(8,128)(2,1)} %get-tuple-element.319.refs_0_, bf16[1024,1024]{1,0:T(8,128)(2,1)} %pad_maximum_fusion.1.refs_0_.refs_1_, bf16[1024,1536]{1,0:T(8,128)(2,1)} %get-tuple-element.313.refs_1_.refs_2_, ...), custom_call_target="tpu_custom_call" | custom-call | flops 14000000000 | bytes 1048576 | tf_op jit(solution)/shard_map/weight_grad/pallas_call | solution.py:530
  492.0 11.6 %collective-permute-done.70 = bf16[512,1024]{1,0:T(8,128)(2,1)S(1)} collective-permute-done((bf16[512,1024]{1,0:T(8,128)(2,1)S(1)}, bf16[512,1024]{1,0:T(8,128)(2,1)S(1)}, u32[]{:S(2)}, u32[]{:S(2)}) %collective-permute-start.70) | collective-permute-done | bytes 1048608 | tf_op jit(solution)/shard_map/ppermute | solution.py:411
  504.6 3.2 copy.102
  507.8 4.3 add_convert_fusion.1
  518.9 7.6 mlp_back.6
  526.5 7.6 mlp_back.7
  534.1 5.8 collective-permute-done.73
  547.6 17.4 %collective-permute-done.76 = bf16[2,256,1024]{2,1,0:T(8,128)(2,1)} collective-permute-done((bf16[2,256,1024]{2,1,0:T(8,128)(2,1)}, bf16[2,256,1024]{2,1,0:T(8,128)(2,1)}, u32[]{:S(2)}, u32[]{:S(2)}) %collective-permute-start.76) | collective-permute-done | bytes 1048608 | tf_op jit(solution)/shard_map/ppermute | solution.py:411
  565.0 15.0 %weight_grad.6 = (bf16[4,2,256,1024]{3,2,1,0:T(8,128)(2,1)}, bf16[4,2,256,1024]{3,2,1,0:T(8,128)(2,1)}) custom-call(bf16[1024,1024]{1,0:T(8,128)(2,1)} %get-tuple-element.339.refs_1_.refs_0_, bf16[512,1024]{1,0:T(8,128)(2,1)} %get-tuple-element.327.refs_0_.refs_1_, bf16[512,1024]{1,0:T(8,128)(2,1)} %get-tuple-element.471.refs_0_.refs_2_, ...), custom_call_target="tpu_custom_call" | custom-call | flops 14000000000 | bytes 1048576 | tf_op jit(solution)/shard_map/weight_grad/pallas_call | solution.py:530
  580.0 4.8 copy.104
  592.5 25.9 %attend_back.3 = (bf16[1024,1536]{1,0:T(8,128)(2,1)}, f32[1,1536]{1,0:T(1,128)}) custom-call(bf16[1024,1536]{1,0:T(8,128)(2,1)} %get-tuple-element.238.refs_0_.refs_1_.refs_2_, bf16[1024,1536]{1,0:T(8,128)(2,1)} %get-tuple-element.238.refs_0_.refs_1_.refs_2_, bf16[1024,1536]{1,0:T(8,128)(2,1)} %get-tuple-element.238.refs_0_.refs_1_.refs_2_, ...), custom_call_target="tpu_custom_call" | custom-call | flops 25999998976 | bytes 1048576 | tf_op jit(solution)/shard_map/attend_back/pallas_call | solution.py:530
  625.8 3.8 collective-permute-start.84
  629.8 4.3 add_convert_fusion
  636.5 10.6 %norm_back.6 = (bf16[512,1024]{1,0:T(8,128)(2,1)}, f32[8,1024]{1,0:T(8,128)}) custom-call(bf16[1024,1024]{1,0:T(8,128)(2,1)} %pad_maximum_fusion.refs_0_, bf16[1024,1536]{1,0:T(8,128)(2,1)} %get-tuple-element.359.refs_1_.refs_3_, bf16[1024,2048]{1,0:T(8,128)(2,1)} %get-tuple-element.331.refs_3_.refs_2_, f32[8,1024]{1,0:T(8,128)} %concatenate.200.refs_1_.refs_3_, ...), custom_call_target="tpu_custom_call" | custom-call | flops 10499999744 | bytes 1048576 | tf_op jit(solution)/shard_map/norm_back/pallas_call | solution.py:530
  649.4 3.5 collective-permute-done.83
  654.9 10.6 %norm_back.7 = (bf16[512,1024]{1,0:T(8,128)(2,1)}, f32[8,1024]{1,0:T(8,128)}) custom-call(bf16[1024,1024]{1,0:T(8,128)(2,1)} %pad_maximum_fusion.refs_0_, bf16[1024,1536]{1,0:T(8,128)(2,1)} %get-tuple-element.359.refs_1_.refs_3_, bf16[1024,2048]{1,0:T(8,128)(2,1)} %get-tuple-element.331.refs_3_.refs_2_, f32[8,1024]{1,0:T(8,128)} %concatenate.200.refs_1_.refs_3_, ...), custom_call_target="tpu_custom_call" | custom-call | flops 10499999744 | bytes 1048576 | tf_op jit(solution)/shard_map/norm_back/pallas_call | solution.py:530
  673.2 3.7 collective-permute-start.92
  677.2 12.8 %collective-permute-done.89 = bf16[2,256,1024]{2,1,0:T(8,128)(2,1)S(1)} collective-permute-done((bf16[2,256,1024]{2,1,0:T(8,128)(2,1)}, bf16[2,256,1024]{2,1,0:T(8,128)(2,1)S(1)}, u32[]{:S(2)}, u32[]{:S(2)}) %collective-permute-start.89) | collective-permute-done | bytes 1048608 | tf_op jit(solution)/shard_map/ppermute | solution.py:411
  690.0 12.0 %weight_grad.7 = (bf16[4,2,256,512]{3,2,1,0:T(8,128)(2,1)}, bf16[4,2,256,512]{3,2,1,0:T(8,128)(2,1)}) custom-call(bf16[1024,1024]{1,0:T(8,128)(2,1)} %get-tuple-element.368.refs_0_, bf16[512,1024]{1,0:T(8,128)(2,1)} %get-tuple-element.327.refs_0_.refs_1_, bf16[512,1024]{1,0:T(8,128)(2,1)} %get-tuple-element.471.refs_0_.refs_2_, ...), custom_call_target="tpu_custom_call" | custom-call | flops 14000000000 | bytes 1048576 | tf_op jit(solution)/shard_map/weight_grad/pallas_call | solution.py:530
  709.5 7.1 collective-permute-done.93
  716.7 11.2 %collective-permute-done.88 = bf16[512,1024]{1,0:T(8,128)(2,1)S(1)} collective-permute-done((bf16[512,1024]{1,0:T(8,128)(2,1)}, bf16[512,1024]{1,0:T(8,128)(2,1)S(1)}, u32[]{:S(2)}, u32[]{:S(2)}) %collective-permute-start.88) | collective-permute-done | bytes 1048608 | tf_op jit(solution)/shard_map/ppermute | solution.py:411
  735.7 3.5 collective-permute-start.97
  743.5 29.4 %collective-permute-done.96 = bf16[384,1024]{1,0:T(8,128)(2,1)S(1)} collective-permute-done((bf16[384,1024]{1,0:T(8,128)(2,1)S(1)}, bf16[384,1024]{1,0:T(8,128)(2,1)S(1)}, u32[]{:S(2)}, u32[]{:S(2)}) %collective-permute-start.96) | collective-permute-done | bytes 786464 | tf_op jit(solution)/shard_map/ppermute | solution.py:406
  776.7 3.7 collective-permute-start.101
  780.5 20.3 %collective-permute-done.101 = bf16[128,512]{1,0:T(8,128)(2,1)S(1)} collective-permute-done((bf16[128,512]{1,0:T(8,128)(2,1)S(1)}, bf16[128,512]{1,0:T(8,128)(2,1)S(1)}, u32[]{:S(2)}, u32[]{:S(2)}) %collective-permute-start.101) | collective-permute-done | bytes 131104 | tf_op jit(solution)/shard_map/ppermute | solution.py:406
  805.2 2.9 collective-permute-start.106
  815.3 4.2 collective-permute-done.106
  819.5 4.3 collective-permute-done.109
  823.8 7.2 collective-permute-done.108
  832.6 4.8 collective-permute-done.111
  (676 shorter events, 248.3 us)
Async XLA Ops:
  4.1 23.8 %collective-permute-start = (bf16[384,512]{1,0:T(8,128)(2,1)}, bf16[384,512]{1,0:T(8,128)(2,1)}, u32[]{:S(2)}, u32[]{:S(2)}) collective-permute-start(bf16[384,512]{1,0:T(8,128)(2,1)} %pad_maximum_fusion.28), channel_id=1, source_target_pairs={{0,1},{1,2},{2,3},{3,0},{4,5},{5,6},{6,7},{7,4},{8,9},{9,10},{10,1... | collective-permute-start | bytes 1179656 | tf_op jit(solution)/shard_map/ppermute | solution.py:406
  7.9 20.0 %collective-permute-start.1 = (bf16[384,512]{1,0:T(8,128)(2,1)}, bf16[384,512]{1,0:T(8,128)(2,1)}, u32[]{:S(2)}, u32[]{:S(2)}) collective-permute-start(bf16[384,512]{1,0:T(8,128)(2,1)} %pad_maximum_fusion.29), channel_id=1, source_target_pairs={{0,3},{1,0},{2,1},{3,2},{4,7},{5,4},{6,5},{7,6},{8,11},{9,8},{10,9... | collective-permute-start | bytes 1179656 | tf_op jit(solution)/shard_map/ppermute | solution.py:406
  27.9 23.3 %collective-permute-start.6 = (bf16[256,512]{1,0:T(8,128)(2,1)S(1)}, bf16[256,512]{1,0:T(8,128)(2,1)S(1)}, u32[]{:S(2)}, u32[]{:S(2)}) collective-permute-start(bf16[256,512]{1,0:T(8,128)(2,1)S(1)} %get-tuple-element.215), channel_id=1, source_target_pairs={{0,1},{1,2},{2,3},{3,0},{4,5},{5,6},{6,7},{7,4},{8,9},{9,10},{10,1... | collective-permute-start | bytes 786440 | tf_op jit(solution)/shard_map/ppermute | solution.py:406
  28.0 23.3 %collective-permute-start.7 = (bf16[256,512]{1,0:T(8,128)(2,1)S(1)}, bf16[256,512]{1,0:T(8,128)(2,1)S(1)}, u32[]{:S(2)}, u32[]{:S(2)}) collective-permute-start(bf16[256,512]{1,0:T(8,128)(2,1)S(1)} %get-tuple-element.215), channel_id=1, source_target_pairs={{0,3},{1,0},{2,1},{3,2},{4,7},{5,4},{6,5},{7,6},{8,11},{9,8},{10,9... | collective-permute-start | bytes 786440 | tf_op jit(solution)/shard_map/ppermute | solution.py:406
  31.8 20.4 %collective-permute-start.8 = (bf16[256,1024]{1,0:T(8,128)(2,1)S(1)}, bf16[256,1024]{1,0:T(8,128)(2,1)S(1)}, u32[]{:S(2)}, u32[]{:S(2)}) collective-permute-start(bf16[256,1024]{1,0:T(8,128)(2,1)S(1)} %copy-done.48), channel_id=1, source_target_pairs={{0,16},{16,0},{1,17},{17,1},{2,18},{18,2},{3,19},{19,3},{4,20},{20... | collective-permute-start | bytes 1572872 | tf_op jit(solution)/shard_map/ppermute | solution.py:411
  56.4 49.7 %collective-permute-start.12 = (bf16[4,256,512]{2,1,0:T(8,128)(2,1)}, bf16[4,256,512]{2,1,0:T(8,128)(2,1)S(1)}, u32[]{:S(2)}, u32[]{:S(2)}) collective-permute-start(bf16[4,256,512]{2,1,0:T(8,128)(2,1)} %fusion.34), channel_id=1, source_target_pairs={{0,16},{16,0},{1,17},{17,1},{2,18},{18,2},{3,19},{19,3},{4,20},{20... | collective-permute-start | bytes 3145736 | tf_op jit(solution)/shard_map/ppermute | solution.py:411
  63.0 42.3 %collective-permute-start.25 = (bf16[256,1024]{1,0:T(8,128)(2,1)S(1)}, bf16[256,1024]{1,0:T(8,128)(2,1)S(1)}, u32[]{:S(2)}, u32[]{:S(2)}) collective-permute-start(bf16[256,1024]{1,0:T(8,128)(2,1)S(1)} %get-tuple-element.237), channel_id=1, source_target_pairs={{0,1},{1,2},{2,3},{3,0},{4,5},{5,6},{6,7},{7,4},{8,9},{9,10},{10,1... | collective-permute-start | bytes 1572872 | tf_op jit(solution)/shard_map/ppermute | solution.py:406
  64.7 35.2 %collective-permute-start.27 = (bf16[256,1024]{1,0:T(8,128)(2,1)S(1)}, bf16[256,1024]{1,0:T(8,128)(2,1)S(1)}, u32[]{:S(2)}, u32[]{:S(2)}) collective-permute-start(bf16[256,1024]{1,0:T(8,128)(2,1)S(1)} %get-tuple-element.237), channel_id=1, source_target_pairs={{0,3},{1,0},{2,1},{3,2},{4,7},{5,4},{6,5},{7,6},{8,11},{9,8},{10,9... | collective-permute-start | bytes 1572872 | tf_op jit(solution)/shard_map/ppermute | solution.py:406
  67.0 23.4 %collective-permute-start.22 = (f32[2,4,2,832]{3,2,1,0:T(2,128)S(1)}, f32[2,4,2,832]{3,2,1,0:T(2,128)S(1)}, u32[]{:S(2)}, u32[]{:S(2)}) collective-permute-start(f32[2,4,2,832]{3,2,1,0:T(2,128)S(1)} %pad_maximum_fusion.40), channel_id=1, source_target_pairs={{0,2},{1,3},{2,0},{3,1},{4,6},{5,7},{6,4},{7,5},{8,10},{9,11},{10,... | collective-permute-start | bytes 159752 | tf_op jit(solution)/shard_map/ppermute | solution.py:411
  70.1 36.0 %collective-permute-start.21 = (bf16[2,256,512]{2,1,0:T(8,128)(2,1)}, bf16[2,256,512]{2,1,0:T(8,128)(2,1)}, u32[]{:S(2)}, u32[]{:S(2)}) collective-permute-start(bf16[2,256,512]{2,1,0:T(8,128)(2,1)} %pad_maximum_fusion.19.refs_8_.refs_5_.refs_4_.refs_6_), channel_id=1, source_target_pairs={{0,4},{4,0},{8,12},{12,8},{1,5},{5,1},{9,13},{13,9},{2,6},{6,2},{1... | collective-permute-start | bytes 1572872 | tf_op jit(solution)/shard_map/ppermute | solution.py:411
  118.1 30.3 %collective-permute-start.29 = (bf16[256,1024]{1,0:T(8,128)(2,1)S(1)}, bf16[256,1024]{1,0:T(8,128)(2,1)S(1)}, u32[]{:S(2)}, u32[]{:S(2)}) collective-permute-start(bf16[256,1024]{1,0:T(8,128)(2,1)S(1)} %collective-permute-done.25), channel_id=1, source_target_pairs={{0,8},{4,12},{8,0},{12,4},{1,9},{5,13},{9,1},{13,5},{2,10},{6,14},... | collective-permute-start | bytes 1572872 | tf_op jit(solution)/shard_map/ppermute | solution.py:411
  125.8 24.6 %collective-permute-start.30 = (bf16[256,1024]{1,0:T(8,128)(2,1)S(1)}, bf16[256,1024]{1,0:T(8,128)(2,1)}, u32[]{:S(2)}, u32[]{:S(2)}) collective-permute-start(bf16[256,1024]{1,0:T(8,128)(2,1)S(1)} %collective-permute-done.27), channel_id=1, source_target_pairs={{0,8},{4,12},{8,0},{12,4},{1,9},{5,13},{9,1},{13,5},{2,10},{6,14},... | collective-permute-start | bytes 1572872 | tf_op jit(solution)/shard_map/ppermute | solution.py:411
  126.6 25.3 %collective-permute-start.28 = (bf16[128,1024]{1,0:T(8,128)(2,1)S(1)}, bf16[128,1024]{1,0:T(8,128)(2,1)}, u32[]{:S(2)}, u32[]{:S(2)}) collective-permute-start(bf16[128,1024]{1,0:T(8,128)(2,1)S(1)} %slice.712), channel_id=1, source_target_pairs={{0,3},{1,0},{2,1},{3,2},{4,7},{5,4},{6,5},{7,6},{8,11},{9,8},{10,9... | collective-permute-start | bytes 786440 | tf_op jit(solution)/shard_map/ppermute | solution.py:406
  129.3 22.7 %collective-permute-start.26 = (bf16[128,1024]{1,0:T(8,128)(2,1)}, bf16[128,1024]{1,0:T(8,128)(2,1)}, u32[]{:S(2)}, u32[]{:S(2)}) collective-permute-start(bf16[128,1024]{1,0:T(8,128)(2,1)} %slice.711), channel_id=1, source_target_pairs={{0,1},{1,2},{2,3},{3,0},{4,5},{5,6},{6,7},{7,4},{8,9},{9,10},{10,1... | collective-permute-start | bytes 786440 | tf_op jit(solution)/shard_map/ppermute | solution.py:406
  174.1 23.1 %collective-permute-start.36 = (bf16[256,512]{1,0:T(8,128)(2,1)S(1)}, bf16[256,512]{1,0:T(8,128)(2,1)S(1)}, u32[]{:S(2)}, u32[]{:S(2)}) collective-permute-start(bf16[256,512]{1,0:T(8,128)(2,1)S(1)} %copy-done.27), channel_id=1, source_target_pairs={{0,1},{1,2},{2,3},{3,0},{4,5},{5,6},{6,7},{7,4},{8,9},{9,10},{10,1... | collective-permute-start | bytes 786440 | tf_op jit(solution)/shard_map/ppermute | solution.py:406
  175.0 22.1 %collective-permute-start.37 = (bf16[256,512]{1,0:T(8,128)(2,1)S(1)}, bf16[256,512]{1,0:T(8,128)(2,1)S(1)}, u32[]{:S(2)}, u32[]{:S(2)}) collective-permute-start(bf16[256,512]{1,0:T(8,128)(2,1)S(1)} %copy-done.27), channel_id=1, source_target_pairs={{0,3},{1,0},{2,1},{3,2},{4,7},{5,4},{6,5},{7,6},{8,11},{9,8},{10,9... | collective-permute-start | bytes 786440 | tf_op jit(solution)/shard_map/ppermute | solution.py:406
  179.3 18.5 %collective-permute-start.38 = (bf16[256,512]{1,0:T(8,128)(2,1)S(1)}, bf16[256,512]{1,0:T(8,128)(2,1)S(1)}, u32[]{:S(2)}, u32[]{:S(2)}) collective-permute-start(bf16[256,512]{1,0:T(8,128)(2,1)S(1)} %copy-done.27), channel_id=1, source_target_pairs={{0,8},{4,12},{8,0},{12,4},{1,9},{5,13},{9,1},{13,5},{2,10},{6,14},... | collective-permute-start | bytes 786440 | tf_op jit(solution)/shard_map/ppermute | solution.py:411
  198.6 31.5 %collective-permute-start.43 = (bf16[256,1024]{1,0:T(8,128)(2,1)S(1)}, bf16[256,1024]{1,0:T(8,128)(2,1)S(1)}, u32[]{:S(2)}, u32[]{:S(2)}) collective-permute-start(bf16[256,1024]{1,0:T(8,128)(2,1)S(1)} %get-tuple-element.261), channel_id=1, source_target_pairs={{0,1},{1,2},{2,3},{3,0},{4,5},{5,6},{6,7},{7,4},{8,9},{9,10},{10,1... | collective-permute-start | bytes 1572872 | tf_op jit(solution)/shard_map/ppermute | solution.py:406
  198.6 31.5 %collective-permute-start.44 = (bf16[256,1024]{1,0:T(8,128)(2,1)S(1)}, bf16[256,1024]{1,0:T(8,128)(2,1)S(1)}, u32[]{:S(2)}, u32[]{:S(2)}) collective-permute-start(bf16[256,1024]{1,0:T(8,128)(2,1)S(1)} %get-tuple-element.261), channel_id=1, source_target_pairs={{0,3},{1,0},{2,1},{3,2},{4,7},{5,4},{6,5},{7,6},{8,11},{9,8},{10,9... | collective-permute-start | bytes 1572872 | tf_op jit(solution)/shard_map/ppermute | solution.py:406
  202.4 23.2 %collective-permute-start.42 = (bf16[128,512]{1,0:T(8,128)(2,1)S(1)}, bf16[128,512]{1,0:T(8,128)(2,1)S(1)}, u32[]{:S(2)}, u32[]{:S(2)}) collective-permute-start(bf16[128,512]{1,0:T(8,128)(2,1)S(1)} %slice.717), channel_id=1, source_target_pairs={{0,3},{1,0},{2,1},{3,2},{4,7},{5,4},{6,5},{7,6},{8,11},{9,8},{10,9... | collective-permute-start | bytes 393224 | tf_op jit(solution)/shard_map/ppermute | solution.py:406
  202.5 27.6 %collective-permute-start.41 = (bf16[128,512]{1,0:T(8,128)(2,1)}, bf16[128,512]{1,0:T(8,128)(2,1)S(1)}, u32[]{:S(2)}, u32[]{:S(2)}) collective-permute-start(bf16[128,512]{1,0:T(8,128)(2,1)} %slice.716), channel_id=1, source_target_pairs={{0,1},{1,2},{2,3},{3,0},{4,5},{5,6},{6,7},{7,4},{8,9},{9,10},{10,1... | collective-permute-start | bytes 393224 | tf_op jit(solution)/shard_map/ppermute | solution.py:406
  204.5 25.7 %collective-permute-start.40 = (bf16[512,1024]{1,0:T(8,128)(2,1)}, bf16[512,1024]{1,0:T(8,128)(2,1)S(1)}, u32[]{:S(2)}, u32[]{:S(2)}) collective-permute-start(bf16[512,1024]{1,0:T(8,128)(2,1)} %get-tuple-element.254), channel_id=1, source_target_pairs={{0,16},{16,0},{1,17},{17,1},{2,18},{18,2},{3,19},{19,3},{4,20},{20... | collective-permute-start | bytes 3145736 | tf_op jit(solution)/shard_map/ppermute | solution.py:411
  231.5 22.9 %collective-permute-start.45 = (bf16[512,1024]{1,0:T(8,128)(2,1)}, bf16[512,1024]{1,0:T(8,128)(2,1)}, u32[]{:S(2)}, u32[]{:S(2)}) collective-permute-start(bf16[512,1024]{1,0:T(8,128)(2,1)} %get-tuple-element.262), channel_id=1, source_target_pairs={{0,16},{16,0},{1,17},{17,1},{2,18},{18,2},{3,19},{19,3},{4,20},{20... | collective-permute-start | bytes 3145736 | tf_op jit(solution)/shard_map/ppermute | solution.py:411
  277.0 22.8 %collective-permute-start.57 = (bf16[256,1024]{1,0:T(8,128)(2,1)S(1)}, bf16[256,1024]{1,0:T(8,128)(2,1)S(1)}, u32[]{:S(2)}, u32[]{:S(2)}) collective-permute-start(bf16[256,1024]{1,0:T(8,128)(2,1)S(1)} %constant_dynamic-update-slice_fusion.6), channel_id=1, source_target_pairs={{0,8},{4,12},{8,0},{12,4},{1,9},{5,13},{9,1},{13,5},{2,10},{6,14},... | collective-permute-start | bytes 1572872 | tf_op jit(solution)/shard_map/ppermute | solution.py:411
  279.5 24.6 %collective-permute-start.59 = (bf16[2,256,1024]{2,1,0:T(8,128)(2,1)}, bf16[2,256,1024]{2,1,0:T(8,128)(2,1)}, u32[]{:S(2)}, u32[]{:S(2)}) collective-permute-start(bf16[2,256,1024]{2,1,0:T(8,128)(2,1)} %pad_maximum_fusion.10.refs_12_.refs_20_.refs_11_.refs_13_), channel_id=1, source_target_pairs={{0,4},{4,0},{8,12},{12,8},{1,5},{5,1},{9,13},{13,9},{2,6},{6,2},{1... | collective-permute-start | bytes 3145736 | tf_op jit(solution)/shard_map/ppermute | solution.py:411
  279.5 24.6 %collective-permute-start.58 = (bf16[2,256,1024]{2,1,0:T(8,128)(2,1)S(1)}, bf16[2,256,1024]{2,1,0:T(8,128)(2,1)}, u32[]{:S(2)}, u32[]{:S(2)}) collective-permute-start(bf16[2,256,1024]{2,1,0:T(8,128)(2,1)S(1)} %pad_maximum_fusion.9.refs_11_.refs_19_.refs_10_.refs_12_), channel_id=1, source_target_pairs={{0,4},{4,0},{8,12},{12,8},{1,5},{5,1},{9,13},{13,9},{2,6},{6,2},{1... | collective-permute-start | bytes 3145736 | tf_op jit(solution)/shard_map/ppermute | solution.py:411
  280.0 22.0 %collective-permute-start.56 = (bf16[256,1024]{1,0:T(8,128)(2,1)S(1)}, bf16[256,1024]{1,0:T(8,128)(2,1)}, u32[]{:S(2)}, u32[]{:S(2)}) collective-permute-start(bf16[256,1024]{1,0:T(8,128)(2,1)S(1)} %collective-permute-done.44), channel_id=1, source_target_pairs={{0,8},{4,12},{8,0},{12,4},{1,9},{5,13},{9,1},{13,5},{2,10},{6,14},... | collective-permute-start | bytes 1572872 | tf_op jit(solution)/shard_map/ppermute | solution.py:411
  308.6 20.7 %collective-permute-start.63 = (bf16[384,512]{1,0:T(8,128)(2,1)S(1)}, bf16[384,512]{1,0:T(8,128)(2,1)S(1)}, u32[]{:S(2)}, u32[]{:S(2)}) collective-permute-start(bf16[384,512]{1,0:T(8,128)(2,1)S(1)} %pad_maximum_fusion.31), channel_id=1, source_target_pairs={{0,3},{1,0},{2,1},{3,2},{4,7},{5,4},{6,5},{7,6},{8,11},{9,8},{10,9... | collective-permute-start | bytes 1179656 | tf_op jit(solution)/shard_map/ppermute | solution.py:406
  338.9 24.9 %collective-permute-start.66 = (bf16[4,256,512]{2,1,0:T(8,128)(2,1)S(1)}, bf16[4,256,512]{2,1,0:T(8,128)(2,1)S(1)}, u32[]{:S(2)}, u32[]{:S(2)}) collective-permute-start(bf16[4,256,512]{2,1,0:T(8,128)(2,1)S(1)} %fusion.35), channel_id=1, source_target_pairs={{0,16},{16,0},{1,17},{17,1},{2,18},{18,2},{3,19},{19,3},{4,20},{20... | collective-permute-start | bytes 3145736 | tf_op jit(solution)/shard_map/ppermute | solution.py:411
  366.4 24.0 %collective-permute-start.67 = (bf16[512,1024]{1,0:T(8,128)(2,1)S(1)}, bf16[512,1024]{1,0:T(8,128)(2,1)S(1)}, u32[]{:S(2)}, u32[]{:S(2)}) collective-permute-start(bf16[512,1024]{1,0:T(8,128)(2,1)S(1)} %copy-done.36), channel_id=1, source_target_pairs={{0,16},{16,0},{1,17},{17,1},{2,18},{18,2},{3,19},{19,3},{4,20},{20... | collective-permute-start | bytes 3145736 | tf_op jit(solution)/shard_map/ppermute | solution.py:411
  390.4 27.1 %collective-permute-start.68 = (bf16[512,1024]{1,0:T(8,128)(2,1)}, bf16[512,1024]{1,0:T(8,128)(2,1)}, u32[]{:S(2)}, u32[]{:S(2)}) collective-permute-start(bf16[512,1024]{1,0:T(8,128)(2,1)} %get-tuple-element.310), channel_id=1, source_target_pairs={{0,16},{16,0},{1,17},{17,1},{2,18},{18,2},{3,19},{19,3},{4,20},{20... | collective-permute-start | bytes 3145736 | tf_op jit(solution)/shard_map/ppermute | solution.py:411
  433.9 26.9 %collective-permute-start.69 = (bf16[512,1024]{1,0:T(8,128)(2,1)}, bf16[512,1024]{1,0:T(8,128)(2,1)S(1)}, u32[]{:S(2)}, u32[]{:S(2)}) collective-permute-start(bf16[512,1024]{1,0:T(8,128)(2,1)} %get-tuple-element.324), channel_id=1, source_target_pairs={{0,16},{16,0},{1,17},{17,1},{2,18},{18,2},{3,19},{19,3},{4,20},{20... | collective-permute-start | bytes 3145736 | tf_op jit(solution)/shard_map/ppermute | solution.py:411
  465.8 37.8 %collective-permute-start.71 = (bf16[4,2,256,1024]{3,2,0,1:T(8,128)(2,1)}, bf16[4,2,256,1024]{3,2,0,1:T(8,128)(2,1)}, u32[]{:S(2)}, u32[]{:S(2)}) collective-permute-start(bf16[4,2,256,1024]{3,2,0,1:T(8,128)(2,1)} %copy.101), channel_id=1, source_target_pairs={{0,4},{4,0},{8,12},{12,8},{1,5},{5,1},{9,13},{13,9},{2,6},{6,2},{1... | collective-permute-start | bytes 12582920 | tf_op jit(solution)/shard_map/ppermute | solution.py:411
  476.6 57.5 %collective-permute-start.75 = (bf16[384,1024]{1,0:T(8,128)(2,1)}, bf16[384,1024]{1,0:T(8,128)(2,1)}, u32[]{:S(2)}, u32[]{:S(2)}) collective-permute-start(bf16[384,1024]{1,0:T(8,128)(2,1)} %pad_maximum_fusion.13), channel_id=1, source_target_pairs={{0,3},{1,0},{2,1},{3,2},{4,7},{5,4},{6,5},{7,6},{8,11},{9,8},{10,9... | collective-permute-start | bytes 2359304 | tf_op jit(solution)/shard_map/ppermute | solution.py:406
  476.8 57.4 %collective-permute-start.74 = (bf16[384,1024]{1,0:T(8,128)(2,1)}, bf16[384,1024]{1,0:T(8,128)(2,1)}, u32[]{:S(2)}, u32[]{:S(2)}) collective-permute-start(bf16[384,1024]{1,0:T(8,128)(2,1)} %pad_maximum_fusion.12), channel_id=1, source_target_pairs={{0,1},{1,2},{2,3},{3,0},{4,5},{5,6},{6,7},{7,4},{8,9},{9,10},{10,1... | collective-permute-start | bytes 2359304 | tf_op jit(solution)/shard_map/ppermute | solution.py:406
  478.6 25.0 %collective-permute-start.70 = (bf16[512,1024]{1,0:T(8,128)(2,1)S(1)}, bf16[512,1024]{1,0:T(8,128)(2,1)S(1)}, u32[]{:S(2)}, u32[]{:S(2)}) collective-permute-start(bf16[512,1024]{1,0:T(8,128)(2,1)S(1)} %copy-done.31), channel_id=1, source_target_pairs={{0,16},{16,0},{1,17},{17,1},{2,18},{18,2},{3,19},{19,3},{4,20},{20... | collective-permute-start | bytes 3145736 | tf_op jit(solution)/shard_map/ppermute | solution.py:411
  507.8 32.0 %collective-permute-start.72 = (bf16[4,2,256,512]{3,2,0,1:T(8,128)(2,1)}, bf16[4,2,256,512]{3,2,0,1:T(8,128)(2,1)S(1)}, u32[]{:S(2)}, u32[]{:S(2)}) collective-permute-start(bf16[4,2,256,512]{3,2,0,1:T(8,128)(2,1)} %copy.102), channel_id=1, source_target_pairs={{0,4},{4,0},{8,12},{12,8},{1,5},{5,1},{9,13},{13,9},{2,6},{6,2},{1... | collective-permute-start | bytes 6291464 | tf_op jit(solution)/shard_map/ppermute | solution.py:411
  514.0 25.9 %collective-permute-start.73 = (bf16[2,256,1024]{2,1,0:T(8,128)(2,1)}, bf16[2,256,1024]{2,1,0:T(8,128)(2,1)}, u32[]{:S(2)}, u32[]{:S(2)}) collective-permute-start(bf16[2,256,1024]{2,1,0:T(8,128)(2,1)} %get-tuple-element.335), channel_id=1, source_target_pairs={{0,8},{4,12},{8,0},{12,4},{1,9},{5,13},{9,1},{13,5},{2,10},{6,14},... | collective-permute-start | bytes 3145736 | tf_op jit(solution)/shard_map/ppermute | solution.py:411
  539.9 25.1 %collective-permute-start.76 = (bf16[2,256,1024]{2,1,0:T(8,128)(2,1)}, bf16[2,256,1024]{2,1,0:T(8,128)(2,1)}, u32[]{:S(2)}, u32[]{:S(2)}) collective-permute-start(bf16[2,256,1024]{2,1,0:T(8,128)(2,1)} %get-tuple-element.338), channel_id=1, source_target_pairs={{0,8},{4,12},{8,0},{12,4},{1,9},{5,13},{9,1},{13,5},{2,10},{6,14},... | collective-permute-start | bytes 3145736 | tf_op jit(solution)/shard_map/ppermute | solution.py:411
  545.5 34.5 %collective-permute-start.78 = (bf16[128,1024]{1,0:T(8,128)(2,1)}, bf16[128,1024]{1,0:T(8,128)(2,1)S(1)}, u32[]{:S(2)}, u32[]{:S(2)}) collective-permute-start(bf16[128,1024]{1,0:T(8,128)(2,1)} %slice.734), channel_id=1, source_target_pairs={{0,3},{1,0},{2,1},{3,2},{4,7},{5,4},{6,5},{7,6},{8,11},{9,8},{10,9... | collective-permute-start | bytes 786440 | tf_op jit(solution)/shard_map/ppermute | solution.py:406
  547.6 32.4 %collective-permute-start.77 = (bf16[128,1024]{1,0:T(8,128)(2,1)S(1)}, bf16[128,1024]{1,0:T(8,128)(2,1)S(1)}, u32[]{:S(2)}, u32[]{:S(2)}) collective-permute-start(bf16[128,1024]{1,0:T(8,128)(2,1)S(1)} %slice.733), channel_id=1, source_target_pairs={{0,1},{1,2},{2,3},{3,0},{4,5},{5,6},{6,7},{7,4},{8,9},{9,10},{10,1... | collective-permute-start | bytes 786440 | tf_op jit(solution)/shard_map/ppermute | solution.py:406
  584.8 36.4 %collective-permute-start.81 = (bf16[4,2,256,1024]{3,2,0,1:T(8,128)(2,1)}, bf16[4,2,256,1024]{3,2,0,1:T(8,128)(2,1)}, u32[]{:S(2)}, u32[]{:S(2)}) collective-permute-start(bf16[4,2,256,1024]{3,2,0,1:T(8,128)(2,1)} %copy.104), channel_id=1, source_target_pairs={{0,4},{4,0},{8,12},{12,8},{1,5},{5,1},{9,13},{13,9},{2,6},{6,2},{1... | collective-permute-start | bytes 12582920 | tf_op jit(solution)/shard_map/ppermute | solution.py:411
  586.7 34.5 %collective-permute-start.82 = (bf16[4,256,512]{2,1,0:T(8,128)(2,1)}, bf16[4,256,512]{2,1,0:T(8,128)(2,1)}, u32[]{:S(2)}, u32[]{:S(2)}) collective-permute-start(bf16[4,256,512]{2,1,0:T(8,128)(2,1)} %get-tuple-element.353), channel_id=1, source_target_pairs={{0,8},{4,12},{8,0},{12,4},{1,9},{5,13},{9,1},{13,5},{2,10},{6,14},... | collective-permute-start | bytes 3145736 | tf_op jit(solution)/shard_map/ppermute | solution.py:411
  590.5 30.8 %collective-permute-start.80 = (bf16[128,1024]{1,0:T(8,128)(2,1)}, bf16[128,1024]{1,0:T(8,128)(2,1)}, u32[]{:S(2)}, u32[]{:S(2)}) collective-permute-start(bf16[128,1024]{1,0:T(8,128)(2,1)} %get-tuple-element.349), channel_id=1, source_target_pairs={{0,3},{1,0},{2,1},{3,2},{4,7},{5,4},{6,5},{7,6},{8,11},{9,8},{10,9... | collective-permute-start | bytes 786440 | tf_op jit(solution)/shard_map/ppermute | solution.py:406
  592.5 26.8 %collective-permute-start.79 = (bf16[128,1024]{1,0:T(8,128)(2,1)}, bf16[128,1024]{1,0:T(8,128)(2,1)}, u32[]{:S(2)}, u32[]{:S(2)}) collective-permute-start(bf16[128,1024]{1,0:T(8,128)(2,1)} %get-tuple-element.348), channel_id=1, source_target_pairs={{0,1},{1,2},{2,3},{3,0},{4,5},{5,6},{6,7},{7,4},{8,9},{9,10},{10,1... | collective-permute-start | bytes 786440 | tf_op jit(solution)/shard_map/ppermute | solution.py:406
  625.8 23.6 %collective-permute-start.84 = (bf16[256,1024]{1,0:T(8,128)(2,1)}, bf16[256,1024]{1,0:T(8,128)(2,1)S(1)}, u32[]{:S(2)}, u32[]{:S(2)}) collective-permute-start(bf16[256,1024]{1,0:T(8,128)(2,1)} %pad_maximum_fusion.25), channel_id=1, source_target_pairs={{0,3},{1,0},{2,1},{3,2},{4,7},{5,4},{6,5},{7,6},{8,11},{9,8},{10,9... | collective-permute-start | bytes 1572872 | tf_op jit(solution)/shard_map/ppermute | solution.py:406
  629.6 23.3 %collective-permute-start.83 = (bf16[256,1024]{1,0:T(8,128)(2,1)}, bf16[256,1024]{1,0:T(8,128)(2,1)}, u32[]{:S(2)}, u32[]{:S(2)}) collective-permute-start(bf16[256,1024]{1,0:T(8,128)(2,1)} %pad_maximum_fusion.24), channel_id=1, source_target_pairs={{0,1},{1,2},{2,3},{3,0},{4,5},{5,6},{6,7},{7,4},{8,9},{9,10},{10,1... | collective-permute-start | bytes 1572872 | tf_op jit(solution)/shard_map/ppermute | solution.py:406
  635.8 29.8 %collective-permute-start.85 = (bf16[2,256,1024]{2,1,0:T(8,128)(2,1)}, bf16[2,256,1024]{2,1,0:T(8,128)(2,1)}, u32[]{:S(2)}, u32[]{:S(2)}) collective-permute-start(bf16[2,256,1024]{2,1,0:T(8,128)(2,1)} %get-tuple-element.362), channel_id=1, source_target_pairs={{0,8},{4,12},{8,0},{12,4},{1,9},{5,13},{9,1},{13,5},{2,10},{6,14},... | collective-permute-start | bytes 3145736 | tf_op jit(solution)/shard_map/ppermute | solution.py:411
  666.2 23.8 %collective-permute-start.89 = (bf16[2,256,1024]{2,1,0:T(8,128)(2,1)}, bf16[2,256,1024]{2,1,0:T(8,128)(2,1)S(1)}, u32[]{:S(2)}, u32[]{:S(2)}) collective-permute-start(bf16[2,256,1024]{2,1,0:T(8,128)(2,1)} %get-tuple-element.367), channel_id=1, source_target_pairs={{0,8},{4,12},{8,0},{12,4},{1,9},{5,13},{9,1},{13,5},{2,10},{6,14},... | collective-permute-start | bytes 3145736 | tf_op jit(solution)/shard_map/ppermute | solution.py:411
  667.0 35.0 %collective-permute-start.90 = (bf16[512,1024]{1,0:T(8,128)(2,1)}, bf16[512,1024]{1,0:T(8,128)(2,1)}, u32[]{:S(2)}, u32[]{:S(2)}) collective-permute-start(bf16[512,1024]{1,0:T(8,128)(2,1)} %get-tuple-element.378), channel_id=1, source_target_pairs={{0,16},{16,0},{1,17},{17,1},{2,18},{18,2},{3,19},{19,3},{4,20},{20... | collective-permute-start | bytes 3145736 | tf_op jit(solution)/shard_map/ppermute | solution.py:411
  673.2 28.8 %collective-permute-start.92 = (bf16[256,512]{1,0:T(8,128)(2,1)}, bf16[256,512]{1,0:T(8,128)(2,1)S(1)}, u32[]{:S(2)}, u32[]{:S(2)}) collective-permute-start(bf16[256,512]{1,0:T(8,128)(2,1)} %pad_maximum_fusion.33), channel_id=1, source_target_pairs={{0,3},{1,0},{2,1},{3,2},{4,7},{5,4},{6,5},{7,6},{8,11},{9,8},{10,9... | collective-permute-start | bytes 786440 | tf_op jit(solution)/shard_map/ppermute | solution.py:406
  676.9 25.1 %collective-permute-start.91 = (bf16[256,512]{1,0:T(8,128)(2,1)}, bf16[256,512]{1,0:T(8,128)(2,1)S(1)}, u32[]{:S(2)}, u32[]{:S(2)}) collective-permute-start(bf16[256,512]{1,0:T(8,128)(2,1)} %pad_maximum_fusion.32), channel_id=1, source_target_pairs={{0,1},{1,2},{2,3},{3,0},{4,5},{5,6},{6,7},{7,4},{8,9},{9,10},{10,1... | collective-permute-start | bytes 786440 | tf_op jit(solution)/shard_map/ppermute | solution.py:406
  702.0 26.0 %collective-permute-start.95 = (bf16[4,2,256,512]{3,2,1,0:T(8,128)(2,1)}, bf16[4,2,256,512]{3,2,1,0:T(8,128)(2,1)S(1)}, u32[]{:S(2)}, u32[]{:S(2)}) collective-permute-start(bf16[4,2,256,512]{3,2,1,0:T(8,128)(2,1)} %get-tuple-element.377), channel_id=1, source_target_pairs={{0,4},{4,0},{8,12},{12,8},{1,5},{5,1},{9,13},{13,9},{2,6},{6,2},{1... | collective-permute-start | bytes 6291464 | tf_op jit(solution)/shard_map/ppermute | solution.py:411
  702.7 25.3 %collective-permute-start.88 = (bf16[512,1024]{1,0:T(8,128)(2,1)}, bf16[512,1024]{1,0:T(8,128)(2,1)S(1)}, u32[]{:S(2)}, u32[]{:S(2)}) collective-permute-start(bf16[512,1024]{1,0:T(8,128)(2,1)} %get-tuple-element.379), channel_id=1, source_target_pairs={{0,16},{16,0},{1,17},{17,1},{2,18},{18,2},{3,19},{19,3},{4,20},{20... | collective-permute-start | bytes 3145736 | tf_op jit(solution)/shard_map/ppermute | solution.py:411
  707.1 20.9 %collective-permute-start.94 = (bf16[128,1024]{1,0:T(8,128)(2,1)S(1)}, bf16[128,1024]{1,0:T(8,128)(2,1)S(1)}, u32[]{:S(2)}, u32[]{:S(2)}) collective-permute-start(bf16[128,1024]{1,0:T(8,128)(2,1)S(1)} %get-tuple-element.375), channel_id=1, source_target_pairs={{0,3},{1,0},{2,1},{3,2},{4,7},{5,4},{6,5},{7,6},{8,11},{9,8},{10,9... | collective-permute-start | bytes 786440 | tf_op jit(solution)/shard_map/ppermute | solution.py:406
  734.8 38.2 %collective-permute-start.98 = (bf16[4,256,512]{2,1,0:T(8,128)(2,1)S(1)}, bf16[4,256,512]{2,1,0:T(8,128)(2,1)S(1)}, u32[]{:S(2)}, u32[]{:S(2)}) collective-permute-start(bf16[4,256,512]{2,1,0:T(8,128)(2,1)S(1)} %get-tuple-element.383), channel_id=1, source_target_pairs={{0,8},{4,12},{8,0},{12,4},{1,9},{5,13},{9,1},{13,5},{2,10},{6,14},... | collective-permute-start | bytes 3145736 | tf_op jit(solution)/shard_map/ppermute | solution.py:411
  735.7 37.2 %collective-permute-start.97 = (bf16[384,1024]{1,0:T(8,128)(2,1)S(1)}, bf16[384,1024]{1,0:T(8,128)(2,1)S(1)}, u32[]{:S(2)}, u32[]{:S(2)}) collective-permute-start(bf16[384,1024]{1,0:T(8,128)(2,1)S(1)} %pad_maximum_fusion.15), channel_id=1, source_target_pairs={{0,3},{1,0},{2,1},{3,2},{4,7},{5,4},{6,5},{7,6},{8,11},{9,8},{10,9... | collective-permute-start | bytes 2359304 | tf_op jit(solution)/shard_map/ppermute | solution.py:406
  739.2 33.7 %collective-permute-start.96 = (bf16[384,1024]{1,0:T(8,128)(2,1)S(1)}, bf16[384,1024]{1,0:T(8,128)(2,1)S(1)}, u32[]{:S(2)}, u32[]{:S(2)}) collective-permute-start(bf16[384,1024]{1,0:T(8,128)(2,1)S(1)} %pad_maximum_fusion.14), channel_id=1, source_target_pairs={{0,1},{1,2},{2,3},{3,0},{4,5},{5,6},{6,7},{7,4},{8,9},{9,10},{10,1... | collective-permute-start | bytes 2359304 | tf_op jit(solution)/shard_map/ppermute | solution.py:406
  773.0 30.0 %collective-permute-start.103 = (bf16[256,1024]{1,0:T(8,128)(2,1)S(1)}, bf16[256,1024]{1,0:T(8,128)(2,1)S(1)}, u32[]{:S(2)}, u32[]{:S(2)}) collective-permute-start(bf16[256,1024]{1,0:T(8,128)(2,1)S(1)} %pad_maximum_fusion.27), channel_id=1, source_target_pairs={{0,3},{1,0},{2,1},{3,2},{4,7},{5,4},{6,5},{7,6},{8,11},{9,8},{10,9... | collective-permute-start | bytes 1572872 | tf_op jit(solution)/shard_map/ppermute | solution.py:406
  775.0 28.1 %collective-permute-start.102 = (bf16[256,1024]{1,0:T(8,128)(2,1)S(1)}, bf16[256,1024]{1,0:T(8,128)(2,1)S(1)}, u32[]{:S(2)}, u32[]{:S(2)}) collective-permute-start(bf16[256,1024]{1,0:T(8,128)(2,1)S(1)} %pad_maximum_fusion.26), channel_id=1, source_target_pairs={{0,1},{1,2},{2,3},{3,0},{4,5},{5,6},{6,7},{7,4},{8,9},{9,10},{10,1... | collective-permute-start | bytes 1572872 | tf_op jit(solution)/shard_map/ppermute | solution.py:406
  776.7 24.2 %collective-permute-start.101 = (bf16[128,512]{1,0:T(8,128)(2,1)S(1)}, bf16[128,512]{1,0:T(8,128)(2,1)S(1)}, u32[]{:S(2)}, u32[]{:S(2)}) collective-permute-start(bf16[128,512]{1,0:T(8,128)(2,1)S(1)} %get-tuple-element.401), channel_id=1, source_target_pairs={{0,3},{1,0},{2,1},{3,2},{4,7},{5,4},{6,5},{7,6},{8,11},{9,8},{10,9... | collective-permute-start | bytes 393224 | tf_op jit(solution)/shard_map/ppermute | solution.py:406
  780.4 22.5 %collective-permute-start.100 = (bf16[128,512]{1,0:T(8,128)(2,1)S(1)}, bf16[128,512]{1,0:T(8,128)(2,1)S(1)}, u32[]{:S(2)}, u32[]{:S(2)}) collective-permute-start(bf16[128,512]{1,0:T(8,128)(2,1)S(1)} %get-tuple-element.400), channel_id=1, source_target_pairs={{0,1},{1,2},{2,3},{3,0},{4,5},{5,6},{6,7},{7,4},{8,9},{9,10},{10,1... | collective-permute-start | bytes 393224 | tf_op jit(solution)/shard_map/ppermute | solution.py:406
  809.7 22.4 %collective-permute-start.110 = (bf16[256,1024]{1,0:T(8,128)(2,1)S(1)}, bf16[256,1024]{1,0:T(8,128)(2,1)S(1)}, u32[]{:S(2)}, u32[]{:S(2)}) collective-permute-start(bf16[256,1024]{1,0:T(8,128)(2,1)S(1)} %get-tuple-element.412), channel_id=1, source_target_pairs={{0,16},{16,0},{1,17},{17,1},{2,18},{18,2},{3,19},{19,3},{4,20},{20... | collective-permute-start | bytes 1572872 | tf_op jit(solution)/shard_map/ppermute | solution.py:411
  811.3 19.8 %collective-permute-start.108 = (bf16[256,512]{1,0:T(8,128)(2,1)S(1)}, bf16[256,512]{1,0:T(8,128)(2,1)S(1)}, u32[]{:S(2)}, u32[]{:S(2)}) collective-permute-start(bf16[256,512]{1,0:T(8,128)(2,1)S(1)} %pad_maximum_fusion.34), channel_id=1, source_target_pairs={{0,1},{1,2},{2,3},{3,0},{4,5},{5,6},{6,7},{7,4},{8,9},{9,10},{10,1... | collective-permute-start | bytes 786440 | tf_op jit(solution)/shard_map/ppermute | solution.py:406
  (141 other events, 1425.8 us)

commit v5 on v4

--- a/solution.py
+++ b/solution.py
@@ -398,6 +398,7 @@
 VMEM_LIMIT = 60 * 1024 * 1024
 ROW_BLOCK = 256
 CHUNKS = 2
+COLUMN_STEP = 512
 MICROSECOND = 1_000_000_000
 
 
@@ -436,7 +437,7 @@
         return lax.optimization_barrier((value, self.ended))[0]
 
     def tick(self, *ended):
-        self.ended = ended
+        self.ended = tuple(jax.tree.leaves(ended))
 
 
 def exchange_near(blocks, own, hold):
@@ -465,6 +466,11 @@
 
 def add_wide(left, right):
     return (left.astype(jnp.float32) + right.astype(jnp.float32)).astype(jnp.bfloat16)
+
+
+def add_three(first, second, third):
+    total = first.astype(jnp.float32) + second.astype(jnp.float32) + third.astype(jnp.float32)
+    return total.astype(jnp.bfloat16)
 
 
 def ring_first(blocks, hold):
@@ -638,8 +644,8 @@
             top = jnp.max(scores, axis=1, keepdims=True)
             power = jnp.exp(scores - top)
             total = jnp.sum(power, axis=1, keepdims=True)
-            probs = (power * (1.0 / total)).astype(jnp.bfloat16)
-            ctx[at:end, lanes] = nn_dot(probs, vals[:end]).astype(jnp.bfloat16)
+            mixed = nn_dot(power.astype(jnp.bfloat16), vals[:end]) * (1.0 / total)
+            ctx[at:end, lanes] = mixed.astype(jnp.bfloat16)
             level = jnp.broadcast_to(top + jnp.log(total), (step, 128))
             lse[0, head : head + 1, at:end] = level.T[0:1]
 
@@ -703,13 +709,19 @@
         assemble(rest[8:16], w_up)
         assemble(rest[16:24], w_down)
 
-    up = nn_dot(ln_m[...], w_up[...]) + shift[...]
-    half_erf = 0.5 * erf(up * (2.0**-0.5)) + 0.5
-    bell = jnp.exp(up * up * -0.5) * ((2.0 * math.pi) ** -0.5)
-    active = (up * half_erf).astype(jnp.bfloat16)
-    act[...] = active
-    slope[...] = (half_erf + up * bell).astype(jnp.bfloat16)
-    part[...] = (nt_dot(ctx[...], w_out[...]) + nt_dot(active, w_down[...])).astype(jnp.bfloat16)
+    total = nt_dot(ctx[...], w_out[...])
+    values = ln_m[...]
+    size = min(COLUMN_STEP, act.shape[1])
+    for at in range(0, act.shape[1], size):
+        cols = slice(at, at + size)
+        up = nn_dot(values, w_up[:, cols]) + shift[:, cols]
+        half_erf = 0.5 * erf(up * (2.0**-0.5)) + 0.5
+        bell = jnp.exp(up * up * -0.5) * ((2.0 * math.pi) ** -0.5)
+        active = (up * half_erf).astype(jnp.bfloat16)
+        act[:, cols] = active
+        slope[:, cols] = (half_erf + up * bell).astype(jnp.bfloat16)
+        total = total + nt_dot(active, w_down[:, cols])
+    part[...] = total.astype(jnp.bfloat16)
 
 
 def run_mlp(ctx, ln_m, shift, narrow, broad, at, rows, filled):
@@ -748,10 +760,14 @@
         sum_g[...] = jnp.zeros_like(sum_g)
 
     grad = g[...]
-    du = (nn_dot(grad, w_down[...]) * slope[...].astype(jnp.float32)).astype(jnp.bfloat16)
-    d_up[...] = du
+    size = min(COLUMN_STEP, d_up.shape[1])
+    for at in range(0, d_up.shape[1], size):
+        cols = slice(at, at + size)
+        du = nn_dot(grad, w_down[:, cols]) * slope[:, cols].astype(jnp.float32)
+        du = du.astype(jnp.bfloat16)
+        d_up[:, cols] = du
+        sum_up[:, cols] += jnp.sum(du.astype(jnp.float32), axis=0, keepdims=True)
     d_ctx[...] = nn_dot(grad, w_out[...]).astype(jnp.bfloat16)
-    sum_up[...] += jnp.sum(du.astype(jnp.float32), axis=0, keepdims=True)
     sum_g[...] += jnp.sum(grad.astype(jnp.float32), axis=0, keepdims=True)
 
 
@@ -1225,57 +1241,58 @@
 
     g1_a = lower(grads[:chunk], hold(part_a), got_a)
     g1_b = lower(grads[chunk:], hold(part_b), got_b)
-    broad_sum = add_wide(hold(keep_broad), got_core)
+    keep_one, core_one = hold(keep_broad), got_core
     got_core = core_swap(send_narrow)
-    got_x = [x_swap(broad_sum[2:, 1])]
+    got_x = [x_swap(add_wide(keep_one[2:, 1], core_one[2:, 1]))]
     first, up_a, g_a = back(0, (hold(g1_a), 0), slope0, narrow_zero, broad_zero, ())
     first, up_b, g_b = back(1, (g1_b, 0), slope0, narrow_zero, broad_zero, first)
     d_up0, d_ctx0 = first
     sums_zero = [None, g_a + g_b, None, up_a + up_b]
     tick(first, got_core, got_x, out_near)
+    core_narrow = got_core
     out_far = exchange_far(out_near, hold)
-    narrow_sum = add_wide(hold(keep_narrow), got_core)
-    got_narrow = x_swap(narrow_sum[:, 1])
-    got_x.append(x_swap(broad_sum[:2, 1]))
+    got_x.append(x_swap(add_wide(hold(keep_one[:2, 1]), core_one[:2, 1])))
     keep_broad, send = run_weight_grad([[hold(ln_m0)], [g1_a, g1_b]], [d_up0, act0])
-    tick(keep_broad, out_far)
-
-    def after_x(total, got):
-        late = add_wide(total[2:, 0], got[0])
-        early = add_wide(total[:2, 0], got[1])
-        return [early[0], early[1], late[0], late[1]]
+    tick(keep_broad, out_far, got_x)
+
+    def late_blocks(keep, core, got):
+        late = add_three(hold(keep[2:, 0]), core[2:, 0], got)
+        return [late[0], late[1]]
+
+    def early_blocks(keep, core, got):
+        early = add_three(hold(keep[:2, 0]), core[:2, 0], got)
+        return [early[0], early[1]]
 
     got_core = core_swap(send)
-    late = add_wide(hold(broad_sum[2:, 0]), got_x[0])
-    broad_got = ring_first([None, None, late[0], late[1]], hold)
+    late = late_blocks(keep_one, core_one, got_x[0])
+    broad_got = ring_first([None, None, *late], hold)
+    got_narrow = x_swap(add_wide(hold(keep_narrow[:, 1]), core_narrow[:, 1]))
     d_qkv0, sums_zero[2] = run_attend_back(qkv0, hold(d_ctx0), lse0, tables)
-    tick(d_qkv0, broad_got, got_core, got_x, got_narrow)
-    early = add_wide(hold(broad_sum[:2, 0]), got_x[1])
-    broad_one_sum = [early[0], early[1], late[0], late[1]]
-    narrow_sum = add_wide(hold(narrow_sum[:, 0]), got_narrow)
+    tick(d_qkv0, broad_got, got_core, got_narrow)
+    broad_one_sum = early_blocks(keep_one, core_one, got_x[1]) + late
+    narrow_sum = add_three(hold(keep_narrow[:, 0]), core_narrow[:, 0], got_narrow)
     narrow_sum = [narrow_sum[k] for k in range(4)]
-    broad_sum = add_wide(hold(keep_broad), got_core)
-    got_x = [x_swap(broad_sum[2:, 1])]
+    keep_zero, core_zero = hold(keep_broad), got_core
+    got_x = [x_swap(add_wide(keep_zero[2:, 1], core_zero[2:, 1]))]
     broad_got = ring_second(broad_one_sum, broad_got, hold)
     part_a, sum_a = run_norm_back(
         (acts, 0), hold(d_qkv0), d_up0, all_vecs[0], narrow_zero, broad_zero, 0, chunk
     )
-    tick(part_a, broad_got)
+    tick(part_a)
     got_a = y_swap(part_a)
-    narrow_got = ring_first(narrow_sum, hold)
     part_b, sum_b = run_norm_back(
         (acts, chunk), hold(d_qkv0), d_up0, all_vecs[0], narrow_zero, broad_zero, chunk, chunk
     )
     sums_zero[0] = (sum_a + sum_b)[:4]
-    tick(part_b, got_x, narrow_got)
+    tick(part_b, got_x, broad_got)
     got_b = y_swap(part_b)
-    narrow_got = ring_second(narrow_sum, narrow_got, hold)
-    got_x.append(x_swap(broad_sum[:2, 1]))
+    got_x.append(x_swap(add_wide(hold(keep_zero[:2, 1]), core_zero[:2, 1])))
+    narrow_got = ring_first(narrow_sum, hold)
     keep_narrow, send_narrow = run_weight_grad([[hold(ln_a0)], [g1_a, g1_b]], [d_qkv0, ctx0])
-    tick(keep_narrow, got_a, narrow_got)
+    tick(keep_narrow, got_a, got_b, got_x, narrow_got)
 
     flat = []
-    for norm_sums, sum_g, sum_qkv, sum_up in (sums_zero, sums_one):
+    for norm_sums, sum_g, sum_qkv, sum_up in hold((sums_zero, sums_one)):
         feature = relative(jnp.concatenate([norm_sums, sum_g], axis=0), across)
         q_sum = sum_qkv.reshape(4, 3, 2, 64).transpose(0, 2, 1, 3).reshape(4, -1)
         both = jnp.concatenate([q_sum, sum_up.reshape(4, -1)], axis=1)
@@ -1283,37 +1300,35 @@
         flat.append(jnp.concatenate([feature.reshape(-1), both.reshape(-1)]))
     flat = jnp.stack(flat)
     got_core = core_swap(send_narrow)
-    late = add_wide(hold(broad_sum[2:, 0]), got_x[0])
-    broad_next = ring_first([None, None, late[0], late[1]], hold)
-    tick(got_b, got_x, broad_next, got_core)
-    early = add_wide(hold(broad_sum[:2, 0]), got_x[1])
-    broad_zero_sum = [early[0], early[1], late[0], late[1]]
+    late = late_blocks(keep_zero, core_zero, got_x[0])
+    broad_next = ring_first([None, None, *late], hold)
     grads_low = jnp.concatenate(
         [lower(g1_a, hold(part_a), got_a), lower(g1_b, hold(part_b), got_b)], axis=0
     )
     g1 = jnp.concatenate([g1_a, g1_b], axis=0)
     grad_blocks = to_blocks(jnp.where(first_section, grads_low, g1))
-    tick(grad_blocks)
-    grad_near = exchange_near(grad_blocks, along, hold)
-    zero_sum = add_wide(keep_narrow, got_core)
-    got_narrow = x_swap(zero_sum[:, 1])
+    tick(broad_next, got_core, grad_blocks)
+    broad_zero_sum = early_blocks(keep_zero, core_zero, got_x[1]) + late
+    broad_next = ring_second(broad_zero_sum, broad_next, hold)
+    narrow_got = ring_second(narrow_sum, narrow_got, hold)
+    got_narrow = x_swap(add_wide(hold(keep_narrow[:, 1]), got_core[:, 1]))
     flat = flat + core_swap(flat)
-    one_broad = ring_total(hold(broad_one_sum[0]), broad_got)
-    one_narrow = ring_total(hold(narrow_sum[0]), narrow_got)
     acts_local = exchanged(hold(out_blocks), out_near, out_far, along)
-    tick(grad_near, got_narrow, flat, acts_local)
-    broad_next = ring_second(broad_zero_sum, broad_next, hold)
-    zero_sum = add_wide(hold(zero_sum[:, 0]), got_narrow)
+    tick(broad_next, got_narrow, flat, narrow_got, acts_local)
+    zero_sum = add_three(hold(keep_narrow[:, 0]), got_core[:, 0], got_narrow)
     zero_sum = [zero_sum[k] for k in range(4)]
     narrow_next = ring_first(zero_sum, hold)
     flat = flat + x_swap(flat)
-    tick(narrow_next, broad_next, flat)
-    zero_broad = ring_total(broad_zero_sum[0], broad_next)
+    tick(narrow_next, flat)
+    grad_near = exchange_near(grad_blocks, along, hold)
+    narrow_next = ring_second(zero_sum, narrow_next, hold)
+    one_broad = ring_total(hold(broad_one_sum[0]), broad_got)
+    one_narrow = ring_total(hold(narrow_sum[0]), narrow_got)
+    zero_broad = ring_total(hold(broad_zero_sum[0]), broad_next)
     broad_send = y_swap(jnp.where(first_section, one_broad, zero_broad))
-    narrow_next = ring_second(zero_sum, narrow_next, hold)
+    flat = flat + swap(hold(flat), "tensor", 1)
+    tick(narrow_next, grad_near, broad_send, flat)
     grad_far = exchange_far(grad_near, hold)
-    flat = flat + swap(hold(flat), "tensor", 1)
-    tick(narrow_next, grad_far, broad_send, flat)
     zero_narrow = ring_total(zero_sum[0], narrow_next)
     narrow_send = y_swap(jnp.where(first_section, one_narrow, zero_narrow))
     flat = flat + swap(hold(flat), "tensor", 2)

time: 860 us -> 843 us (0.980)
  waiting for transfers between devices: 245 us -> 206 us
  other arithmetic: 81.8 us -> 100 us
    ppermute x66, waiting for transfers between devices: 134 us -> 94.5 us  [swap(): return lax.ppermute(value, axis, [(i, i ^ bit) for i in range(length)])]
    convert_element_type x0 -> x6, other arithmetic: none -> 12.2 us  [add_three(): return total.astype(jnp.bfloat16)]
    convert_element_type x16 -> x12, other arithmetic: 20.3 us -> 18.7 us  [add_wide(): (left.astype(jnp.float32) + right.astype(jnp.float32)).astype(jnp.bfloat16)]
  transfers between devices with their start and end apart: 114 -> 114, of which waited for: 37 -> 39; matrix products, arithmetic and copies ran while one was open for 15% -> 19% of each run, Pallas kernels for 35% -> 34%
where the time goes in v5:
time: 843 us; the launch traced here: 834 us
  Pallas kernels  305 us (36%)
  waiting for transfers between devices  206 us (24%)
  starting transfers between devices  114 us (14%)
  other arithmetic  100 us (12%)
  local copies, waits for them, and re-layouts  96.3 us (11%)
  between operations  11.3 us (1%)
    pallas_call x24, Pallas kernels, call(): pl.pallas_call(run, name=name, grid=grid, in_specs=[pl.BlockSpec(block, i...  305 us
    ppermute x48, waiting for transfers between devices, ring(): lax.ppermute(value, axis, [(i, (i + by) % length) for i in range(length)])  112 us
    ppermute x66, waiting for transfers between devices, swap(): return lax.ppermute(value, axis, [(i, i ^ bit) for i in range(length)])  94.5 us
    ppermute x48, starting transfers between devices, ring(): lax.ppermute(value, axis, [(i, (i + by) % length) for i in range(length)])  70.4 us
    ppermute x66, starting transfers between devices, swap(): return lax.ppermute(value, axis, [(i, i ^ bit) for i in range(length)])  43.9 us
    convert_element_type x12, other arithmetic, add_wide(): (left.astype(jnp.float32) + right.astype(jnp.float32)).astype(jnp.bfloat16)  18.7 us
  transfers between devices with their start and end apart: 114, of which 39 were waited for; matrix products, arithmetic and copies ran while one was open for 19% of the time, Pallas kernels for 34%

profile of v5, /device:TPU:0, one launch (start us, length us, event | category | flops | bytes accessed | tf_op | source)
XLA Modules:
  0.0 833.6 jit_solution(14226709991122517056)
XLA Ops:
  4.1 3.0 collective-permute-start
  28.0 3.8 collective-permute-start.7
  41.4 4.1 collective-permute-done.4
  45.6 4.9 collective-permute-done.5
  58.0 4.9 collective-permute-done.13
  71.1 19.5 %collective-permute-done.22 = f32[2,4,2,832]{3,2,1,0:T(2,128)S(1)} collective-permute-done((f32[2,4,2,832]{3,2,1,0:T(2,128)S(1)}, f32[2,4,2,832]{3,2,1,0:T(2,128)S(1)}, u32[]{:S(2)}, u32[]{:S(2)}) %collective-permute-start.22) | collective-permute-done | bytes 53280 | tf_op jit(solution)/shard_map/ppermute | solution.py:412
  111.0 6.4 norm_qkv.4
  117.4 6.4 norm_qkv.5
  128.6 17.2 %attend.2 = (bf16[1024,512]{1,0:T(8,128)(2,1)}, f32[4,8,1024]{2,1,0:T(8,128)}) custom-call(bf16[1024,1536]{1,0:T(8,128)(2,1)} %get-tuple-element.250.refs_0_.refs_1_.refs_2_, bf16[1024,1536]{1,0:T(8,128)(2,1)} %get-tuple-element.250.refs_0_.refs_1_.refs_2_, bf16[1024,1536]{1,0:T(8,128)(2,1)} %get-tuple-element.250.refs_0_.refs_1_.refs_2_), custom_call_target="tpu_custom_call" | custom-call | flops 19000000512 | bytes 1048576 | tf_op jit(solution)/shard_map/attend/pallas_call | solution.py:536
  153.4 13.2 %collective-permute-done.31 = bf16[256,1024]{1,0:T(8,128)(2,1)S(1)} collective-permute-done((bf16[256,1024]{1,0:T(8,128)(2,1)S(1)}, bf16[256,1024]{1,0:T(8,128)(2,1)S(1)}, u32[]{:S(2)}, u32[]{:S(2)}) %collective-permute-start.31) | collective-permute-done | bytes 524320 | tf_op jit(solution)/shard_map/ppermute | solution.py:412
  173.0 4.3 collective-permute-start.37
  179.3 16.4 %mlp_out.4 = (bf16[1024,2048]{1,0:T(8,128)(2,1)}, bf16[1024,2048]{1,0:T(8,128)(2,1)}, bf16[512,1024]{1,0:T(8,128)(2,1)}) custom-call(bf16[1024,512]{1,0:T(8,128)(2,1)} %get-tuple-element.267.refs_0_.refs_4_, bf16[1024,1024]{1,0:T(8,128)(2,1)} %get-tuple-element.350.refs_1_.refs_0_, f32[1,2048]{1,0:T(1,128)} %bitcast.463, ...), custom_call_target="tpu_custom_call" | custom-call | flops 16000000000 | bytes 1048576 | tf_op jit(solution)/shard_map/mlp_out/pallas_call | solution.py:536
  197.8 3.8 collective-permute-start.44
  203.6 16.4 %mlp_out.5 = (bf16[1024,2048]{1,0:T(8,128)(2,1)}, bf16[1024,2048]{1,0:T(8,128)(2,1)}, bf16[512,1024]{1,0:T(8,128)(2,1)}) custom-call(bf16[1024,512]{1,0:T(8,128)(2,1)} %get-tuple-element.267.refs_0_.refs_4_, bf16[1024,1024]{1,0:T(8,128)(2,1)} %get-tuple-element.350.refs_1_.refs_0_, ...), custom_call_target="tpu_custom_call", output_to_operand_aliasing={{0}: (27, {}), {1}: (28, {})} | custom-call | flops 16000000000 | bytes 1048576 | tf_op jit(solution)/shard_map/mlp_out/pallas_call | solution.py:536
  220.1 4.7 collective-permute-done.42
  224.8 4.6 collective-permute-done.41
  233.3 5.0 collective-permute-done.47
  254.8 4.7 add_convert_fusion.9
  262.7 6.4 norm_qkv.6
  269.1 6.3 norm_qkv.7
  279.2 17.2 %attend.3 = (bf16[1024,512]{1,0:T(8,128)(2,1)}, f32[4,8,1024]{2,1,0:T(8,128)}) custom-call(bf16[1024,1536]{1,0:T(8,128)(2,1)} %get-tuple-element.292.refs_0_.refs_1_.refs_2_, bf16[1024,1536]{1,0:T(8,128)(2,1)} %get-tuple-element.292.refs_0_.refs_1_.refs_2_, bf16[1024,1536]{1,0:T(8,128)(2,1)} %get-tuple-element.292.refs_0_.refs_1_.refs_2_), custom_call_target="tpu_custom_call" | custom-call | flops 19000000512 | bytes 1048576 | tf_op jit(solution)/shard_map/attend/pallas_call | solution.py:536
  296.5 3.8 collective-permute-done.56
  309.8 16.5 %mlp_out.6 = (bf16[1024,2048]{1,0:T(8,128)(2,1)}, bf16[1024,2048]{1,0:T(8,128)(2,1)}, bf16[512,1024]{1,0:T(8,128)(2,1)}) custom-call(bf16[1024,512]{1,0:T(8,128)(2,1)} %get-tuple-element.304.refs_0_.refs_3_, bf16[1024,1024]{1,0:T(8,128)(2,1)} %get-tuple-element.327.refs_1_.refs_0_, f32[1,2048]{1,0:T(1,128)} %bitcast.461, ...), custom_call_target="tpu_custom_call" | custom-call | flops 16000000000 | bytes 1048576 | tf_op jit(solution)/shard_map/mlp_out/pallas_call | solution.py:536
  332.1 3.9 collective-permute-done.64
  337.6 16.4 %mlp_out.7 = (bf16[1024,2048]{1,0:T(8,128)(2,1)}, bf16[1024,2048]{1,0:T(8,128)(2,1)}, bf16[512,1024]{1,0:T(8,128)(2,1)}) custom-call(bf16[1024,512]{1,0:T(8,128)(2,1)} %get-tuple-element.304.refs_0_.refs_3_, bf16[1024,1024]{1,0:T(8,128)(2,1)} %get-tuple-element.327.refs_1_.refs_0_, ...), custom_call_target="tpu_custom_call", output_to_operand_aliasing={{0}: (27, {}), {1}: (28, {})} | custom-call | flops 16000000000 | bytes 1048576 | tf_op jit(solution)/shard_map/mlp_out/pallas_call | solution.py:536
  354.0 8.2 collective-permute-done.66
  365.1 7.6 mlp_back.4
  372.7 7.6 mlp_back.5
  380.3 8.5 %collective-permute-done.67 = bf16[512,1024]{1,0:T(8,128)(2,1)S(1)} collective-permute-done((bf16[512,1024]{1,0:T(8,128)(2,1)S(1)}, bf16[512,1024]{1,0:T(8,128)(2,1)S(1)}, u32[]{:S(2)}, u32[]{:S(2)}) %collective-permute-start.67) | collective-permute-done | bytes 1048608 | tf_op jit(solution)/shard_map/ppermute | solution.py:412
  389.8 26.1 %attend_back.2 = (bf16[1024,1536]{1,0:T(8,128)(2,1)}, f32[1,1536]{1,0:T(1,128)}) custom-call(bf16[1024,1536]{1,0:T(8,128)(2,1)} %get-tuple-element.292.refs_0_.refs_1_.refs_2_, bf16[1024,1536]{1,0:T(8,128)(2,1)} %get-tuple-element.292.refs_0_.refs_1_.refs_2_, bf16[1024,1536]{1,0:T(8,128)(2,1)} %get-tuple-element.292.refs_0_.refs_1_.refs_2_, ...), custom_call_target="tpu_custom_call" | custom-call | flops 25999998976 | bytes 1048576 | tf_op jit(solution)/shard_map/attend_back/pallas_call | solution.py:536
  415.9 3.4 add_convert_fusion.7
  421.0 10.9 %norm_back.4 = (bf16[512,1024]{1,0:T(8,128)(2,1)}, f32[8,1024]{1,0:T(8,128)}) custom-call(bf16[512,1024]{1,0:T(8,128)(2,1)} %get-tuple-element.282.refs_0_, bf16[1024,1536]{1,0:T(8,128)(2,1)} %get-tuple-element.325.refs_1_.refs_2_, bf16[1024,2048]{1,0:T(8,128)(2,1)} %get-tuple-element.317.refs_2_, f32[8,1024]{1,0:T(8,128)} %concatenate.206.refs_1_.refs_3_, ...), custom_call_target="tpu_custom_call" | custom-call | flops 10499999744 | bytes 1048576 | tf_op jit(solution)/shard_map/norm_back/pallas_call | solution.py:536
  433.0 15.2 %weight_grad.4 = (bf16[4,2,256,1024]{3,2,1,0:T(8,128)(2,1)}, bf16[4,2,256,1024]{3,2,1,0:T(8,128)(2,1)}) custom-call(bf16[1024,1024]{1,0:T(8,128)(2,1)} %get-tuple-element.327.refs_1_.refs_0_, bf16[1024,1024]{1,0:T(8,128)(2,1)} %pad_maximum_fusion.1.refs_0_.refs_1_, bf16[1024,2048]{1,0:T(8,128)(2,1)} %get-tuple-element.317.refs_2_, ...), custom_call_target="tpu_custom_call" | custom-call | flops 14000000000 | bytes 1048576 | tf_op jit(solution)/shard_map/weight_grad/pallas_call | solution.py:536
  448.2 10.7 %norm_back.5 = (bf16[512,1024]{1,0:T(8,128)(2,1)}, f32[8,1024]{1,0:T(8,128)}) custom-call(bf16[512,1024]{1,0:T(8,128)(2,1)} %get-tuple-element.473.refs_0_, bf16[1024,1536]{1,0:T(8,128)(2,1)} %get-tuple-element.325.refs_1_.refs_2_, bf16[1024,2048]{1,0:T(8,128)(2,1)} %get-tuple-element.317.refs_2_, f32[8,1024]{1,0:T(8,128)} %concatenate.206.refs_1_.refs_3_, ...), custom_call_target="tpu_custom_call" | custom-call | flops 10499999744 | bytes 1048576 | tf_op jit(solution)/shard_map/norm_back/pallas_call | solution.py:536
  459.0 4.6 copy.119
  478.2 12.0 %weight_grad.5 = (bf16[4,2,256,512]{3,2,1,0:T(8,128)(2,1)}, bf16[4,2,256,512]{3,2,1,0:T(8,128)(2,1)}) custom-call(bf16[1024,1024]{1,0:T(8,128)(2,1)} %get-tuple-element.331.refs_0_, bf16[1024,1024]{1,0:T(8,128)(2,1)} %pad_maximum_fusion.1.refs_0_.refs_1_, bf16[1024,1536]{1,0:T(8,128)(2,1)} %get-tuple-element.325.refs_1_.refs_2_, ...), custom_call_target="tpu_custom_call" | custom-call | flops 14000000000 | bytes 1048576 | tf_op jit(solution)/shard_map/weight_grad/pallas_call | solution.py:536
  490.3 22.1 %collective-permute-done.75 = bf16[384,1024]{1,0:T(8,128)(2,1)} collective-permute-done((bf16[384,1024]{1,0:T(8,128)(2,1)}, bf16[384,1024]{1,0:T(8,128)(2,1)}, u32[]{:S(2)}, u32[]{:S(2)}) %collective-permute-start.75) | collective-permute-done | bytes 786464 | tf_op jit(solution)/shard_map/ppermute | solution.py:407
  514.3 2.9 fusion.16
  521.1 4.3 add_convert_fusion.4
  525.4 7.6 mlp_back.6
  533.0 3.7 slice_bitcast_fusion.12
  536.7 7.6 mlp_back.7
  549.8 14.8 %weight_grad.6 = (bf16[4,2,256,1024]{3,2,1,0:T(8,128)(2,1)}, bf16[4,2,256,1024]{3,2,1,0:T(8,128)(2,1)}) custom-call(bf16[1024,1024]{1,0:T(8,128)(2,1)} %get-tuple-element.350.refs_1_.refs_0_, bf16[512,1024]{1,0:T(8,128)(2,1)} %get-tuple-element.339.refs_0_.refs_1_, bf16[512,1024]{1,0:T(8,128)(2,1)} %get-tuple-element.493.refs_0_.refs_2_, ...), custom_call_target="tpu_custom_call" | custom-call | flops 14000000000 | bytes 1048576 | tf_op jit(solution)/shard_map/weight_grad/pallas_call | solution.py:536
  564.6 7.1 collective-permute-done.78
  571.7 5.0 copy.124
  586.9 26.0 %attend_back.3 = (bf16[1024,1536]{1,0:T(8,128)(2,1)}, f32[1,1536]{1,0:T(1,128)}) custom-call(bf16[1024,1536]{1,0:T(8,128)(2,1)} %get-tuple-element.250.refs_0_.refs_1_.refs_2_, bf16[1024,1536]{1,0:T(8,128)(2,1)} %get-tuple-element.250.refs_0_.refs_1_.refs_2_, bf16[1024,1536]{1,0:T(8,128)(2,1)} %get-tuple-element.250.refs_0_.refs_1_.refs_2_, ...), custom_call_target="tpu_custom_call" | custom-call | flops 25999998976 | bytes 1048576 | tf_op jit(solution)/shard_map/attend_back/pallas_call | solution.py:536
  613.9 10.7 %norm_back.6 = (bf16[512,1024]{1,0:T(8,128)(2,1)}, f32[8,1024]{1,0:T(8,128)}) custom-call(bf16[1024,1024]{1,0:T(8,128)(2,1)} %pad_maximum_fusion.refs_0_, bf16[1024,1536]{1,0:T(8,128)(2,1)} %get-tuple-element.370.refs_1_.refs_3_, bf16[1024,2048]{1,0:T(8,128)(2,1)} %get-tuple-element.342.refs_3_.refs_2_, f32[8,1024]{1,0:T(8,128)} %concatenate.200.refs_1_.refs_3_, ...), custom_call_target="tpu_custom_call" | custom-call | flops 10499999744 | bytes 1048576 | tf_op jit(solution)/shard_map/norm_back/pallas_call | solution.py:536
  632.4 3.0 fusion.17
  637.6 10.9 %norm_back.7 = (bf16[512,1024]{1,0:T(8,128)(2,1)}, f32[8,1024]{1,0:T(8,128)}) custom-call(bf16[1024,1024]{1,0:T(8,128)(2,1)} %pad_maximum_fusion.refs_0_, bf16[1024,1536]{1,0:T(8,128)(2,1)} %get-tuple-element.370.refs_1_.refs_3_, bf16[1024,2048]{1,0:T(8,128)(2,1)} %get-tuple-element.342.refs_3_.refs_2_, f32[8,1024]{1,0:T(8,128)} %concatenate.200.refs_1_.refs_3_, ...), custom_call_target="tpu_custom_call" | custom-call | flops 10499999744 | bytes 1048576 | tf_op jit(solution)/shard_map/norm_back/pallas_call | solution.py:536
  651.0 3.3 slice_bitcast_fusion.4
  655.7 4.5 collective-permute-done.83
  660.2 3.5 collective-permute-start.90
  668.5 12.0 %weight_grad.7 = (bf16[4,2,256,512]{3,2,1,0:T(8,128)(2,1)}, bf16[4,2,256,512]{3,2,1,0:T(8,128)(2,1)}) custom-call(bf16[1024,1024]{1,0:T(8,128)(2,1)} %get-tuple-element.376.refs_0_, bf16[512,1024]{1,0:T(8,128)(2,1)} %get-tuple-element.339.refs_0_.refs_1_, bf16[512,1024]{1,0:T(8,128)(2,1)} %get-tuple-element.493.refs_0_.refs_2_, ...), custom_call_target="tpu_custom_call" | custom-call | flops 14000000000 | bytes 1048576 | tf_op jit(solution)/shard_map/weight_grad/pallas_call | solution.py:536
  680.5 3.0 slice_bitcast_fusion.5
  686.2 3.7 collective-permute-done.88
  694.9 3.5 collective-permute-start.92
  718.0 3.9 collective-permute-start.95
  729.7 10.8 %collective-permute-done.95 = bf16[256,1024]{1,0:T(8,128)(2,1)S(1)} collective-permute-done((bf16[256,1024]{1,0:T(8,128)(2,1)S(1)}, bf16[256,1024]{1,0:T(8,128)(2,1)S(1)}, u32[]{:S(2)}, u32[]{:S(2)}) %collective-permute-start.95) | collective-permute-done | bytes 524320 | tf_op jit(solution)/shard_map/ppermute | solution.py:407
  740.5 11.1 %collective-permute-done.94 = bf16[256,1024]{1,0:T(8,128)(2,1)S(1)} collective-permute-done((bf16[256,1024]{1,0:T(8,128)(2,1)S(1)}, bf16[256,1024]{1,0:T(8,128)(2,1)S(1)}, u32[]{:S(2)}, u32[]{:S(2)}) %collective-permute-start.94) | collective-permute-done | bytes 524320 | tf_op jit(solution)/shard_map/ppermute | solution.py:407
  755.0 3.6 collective-permute-start.101
  758.7 3.0 collective-permute-done.101
  761.7 4.8 collective-permute-done.100
  774.6 7.4 collective-permute-done.108
  787.8 25.3 %collective-permute-done.104 = bf16[384,1024]{1,0:T(8,128)(2,1)} collective-permute-done((bf16[384,1024]{1,0:T(8,128)(2,1)}, bf16[384,1024]{1,0:T(8,128)(2,1)}, u32[]{:S(2)}, u32[]{:S(2)}) %collective-permute-start.104) | collective-permute-done | bytes 786464 | tf_op jit(solution)/shard_map/ppermute | solution.py:407
  (664 shorter events, 264.5 us)
Async XLA Ops:
  4.1 23.8 %collective-permute-start = (bf16[384,512]{1,0:T(8,128)(2,1)}, bf16[384,512]{1,0:T(8,128)(2,1)}, u32[]{:S(2)}, u32[]{:S(2)}) collective-permute-start(bf16[384,512]{1,0:T(8,128)(2,1)} %pad_maximum_fusion.28), channel_id=1, source_target_pairs={{0,1},{1,2},{2,3},{3,0},{4,5},{5,6},{6,7},{7,4},{8,9},{9,10},{10,1... | collective-permute-start | bytes 1179656 | tf_op jit(solution)/shard_map/ppermute | solution.py:407
  7.9 20.1 %collective-permute-start.1 = (bf16[384,512]{1,0:T(8,128)(2,1)}, bf16[384,512]{1,0:T(8,128)(2,1)}, u32[]{:S(2)}, u32[]{:S(2)}) collective-permute-start(bf16[384,512]{1,0:T(8,128)(2,1)} %pad_maximum_fusion.29), channel_id=1, source_target_pairs={{0,3},{1,0},{2,1},{3,2},{4,7},{5,4},{6,5},{7,6},{8,11},{9,8},{10,9... | collective-permute-start | bytes 1179656 | tf_op jit(solution)/shard_map/ppermute | solution.py:407
  27.9 23.3 %collective-permute-start.6 = (bf16[256,512]{1,0:T(8,128)(2,1)S(1)}, bf16[256,512]{1,0:T(8,128)(2,1)S(1)}, u32[]{:S(2)}, u32[]{:S(2)}) collective-permute-start(bf16[256,512]{1,0:T(8,128)(2,1)S(1)} %get-tuple-element.227), channel_id=1, source_target_pairs={{0,1},{1,2},{2,3},{3,0},{4,5},{5,6},{6,7},{7,4},{8,9},{9,10},{10,1... | collective-permute-start | bytes 786440 | tf_op jit(solution)/shard_map/ppermute | solution.py:407
  28.0 23.2 %collective-permute-start.7 = (bf16[256,512]{1,0:T(8,128)(2,1)S(1)}, bf16[256,512]{1,0:T(8,128)(2,1)S(1)}, u32[]{:S(2)}, u32[]{:S(2)}) collective-permute-start(bf16[256,512]{1,0:T(8,128)(2,1)S(1)} %get-tuple-element.227), channel_id=1, source_target_pairs={{0,3},{1,0},{2,1},{3,2},{4,7},{5,4},{6,5},{7,6},{8,11},{9,8},{10,9... | collective-permute-start | bytes 786440 | tf_op jit(solution)/shard_map/ppermute | solution.py:407
  31.8 20.3 %collective-permute-start.8 = (bf16[256,1024]{1,0:T(8,128)(2,1)S(1)}, bf16[256,1024]{1,0:T(8,128)(2,1)S(1)}, u32[]{:S(2)}, u32[]{:S(2)}) collective-permute-start(bf16[256,1024]{1,0:T(8,128)(2,1)S(1)} %copy-done.45), channel_id=1, source_target_pairs={{0,16},{16,0},{1,17},{17,1},{2,18},{18,2},{3,19},{19,3},{4,20},{20... | collective-permute-start | bytes 1572872 | tf_op jit(solution)/shard_map/ppermute | solution.py:412
  56.4 49.7 %collective-permute-start.12 = (bf16[4,256,512]{2,1,0:T(8,128)(2,1)}, bf16[4,256,512]{2,1,0:T(8,128)(2,1)S(1)}, u32[]{:S(2)}, u32[]{:S(2)}) collective-permute-start(bf16[4,256,512]{2,1,0:T(8,128)(2,1)} %fusion.50), channel_id=1, source_target_pairs={{0,16},{16,0},{1,17},{17,1},{2,18},{18,2},{3,19},{19,3},{4,20},{20... | collective-permute-start | bytes 3145736 | tf_op jit(solution)/shard_map/ppermute | solution.py:412
  63.0 42.3 %collective-permute-start.25 = (bf16[256,1024]{1,0:T(8,128)(2,1)S(1)}, bf16[256,1024]{1,0:T(8,128)(2,1)S(1)}, u32[]{:S(2)}, u32[]{:S(2)}) collective-permute-start(bf16[256,1024]{1,0:T(8,128)(2,1)S(1)} %get-tuple-element.249), channel_id=1, source_target_pairs={{0,1},{1,2},{2,3},{3,0},{4,5},{5,6},{6,7},{7,4},{8,9},{9,10},{10,1... | collective-permute-start | bytes 1572872 | tf_op jit(solution)/shard_map/ppermute | solution.py:407
  64.7 35.3 %collective-permute-start.27 = (bf16[256,1024]{1,0:T(8,128)(2,1)S(1)}, bf16[256,1024]{1,0:T(8,128)(2,1)S(1)}, u32[]{:S(2)}, u32[]{:S(2)}) collective-permute-start(bf16[256,1024]{1,0:T(8,128)(2,1)S(1)} %get-tuple-element.249), channel_id=1, source_target_pairs={{0,3},{1,0},{2,1},{3,2},{4,7},{5,4},{6,5},{7,6},{8,11},{9,8},{10,9... | collective-permute-start | bytes 1572872 | tf_op jit(solution)/shard_map/ppermute | solution.py:407
  67.1 23.6 %collective-permute-start.22 = (f32[2,4,2,832]{3,2,1,0:T(2,128)S(1)}, f32[2,4,2,832]{3,2,1,0:T(2,128)S(1)}, u32[]{:S(2)}, u32[]{:S(2)}) collective-permute-start(f32[2,4,2,832]{3,2,1,0:T(2,128)S(1)} %pad_maximum_fusion.40), channel_id=1, source_target_pairs={{0,2},{1,3},{2,0},{3,1},{4,6},{5,7},{6,4},{7,5},{8,10},{9,11},{10,... | collective-permute-start | bytes 159752 | tf_op jit(solution)/shard_map/ppermute | solution.py:412
  70.2 35.9 %collective-permute-start.21 = (bf16[2,256,512]{2,1,0:T(8,128)(2,1)}, bf16[2,256,512]{2,1,0:T(8,128)(2,1)}, u32[]{:S(2)}, u32[]{:S(2)}) collective-permute-start(bf16[2,256,512]{2,1,0:T(8,128)(2,1)} %pad_maximum_fusion.19.refs_8_.refs_5_.refs_4_.refs_6_), channel_id=1, source_target_pairs={{0,4},{4,0},{8,12},{12,8},{1,5},{5,1},{9,13},{13,9},{2,6},{6,2},{1... | collective-permute-start | bytes 1572872 | tf_op jit(solution)/shard_map/ppermute | solution.py:412
  106.2 17.6 %collective-permute-start.24 = (bf16[256,1024]{1,0:T(8,128)(2,1)S(1)}, bf16[256,1024]{1,0:T(8,128)(2,1)}, u32[]{:S(2)}, u32[]{:S(2)}) collective-permute-start(bf16[256,1024]{1,0:T(8,128)(2,1)S(1)} %get-tuple-element.249), channel_id=1, source_target_pairs={{0,8},{4,12},{8,0},{12,4},{1,9},{5,13},{9,1},{13,5},{2,10},{6,14},... | collective-permute-start | bytes 1572872 | tf_op jit(solution)/shard_map/ppermute | solution.py:412
  123.8 23.1 %collective-permute-start.30 = (bf16[256,1024]{1,0:T(8,128)(2,1)S(1)}, bf16[256,1024]{1,0:T(8,128)(2,1)}, u32[]{:S(2)}, u32[]{:S(2)}) collective-permute-start(bf16[256,1024]{1,0:T(8,128)(2,1)S(1)} %collective-permute-done.27), channel_id=1, source_target_pairs={{0,8},{4,12},{8,0},{12,4},{1,9},{5,13},{9,1},{13,5},{2,10},{6,14},... | collective-permute-start | bytes 1572872 | tf_op jit(solution)/shard_map/ppermute | solution.py:412
  125.0 23.4 %collective-permute-start.28 = (bf16[128,1024]{1,0:T(8,128)(2,1)S(1)}, bf16[128,1024]{1,0:T(8,128)(2,1)}, u32[]{:S(2)}, u32[]{:S(2)}) collective-permute-start(bf16[128,1024]{1,0:T(8,128)(2,1)S(1)} %slice.760), channel_id=1, source_target_pairs={{0,3},{1,0},{2,1},{3,2},{4,7},{5,4},{6,5},{7,6},{8,11},{9,8},{10,9... | collective-permute-start | bytes 786440 | tf_op jit(solution)/shard_map/ppermute | solution.py:407
  127.6 20.8 %collective-permute-start.26 = (bf16[128,1024]{1,0:T(8,128)(2,1)}, bf16[128,1024]{1,0:T(8,128)(2,1)}, u32[]{:S(2)}, u32[]{:S(2)}) collective-permute-start(bf16[128,1024]{1,0:T(8,128)(2,1)} %slice.759), channel_id=1, source_target_pairs={{0,1},{1,2},{2,3},{3,0},{4,5},{5,6},{6,7},{7,4},{8,9},{9,10},{10,1... | collective-permute-start | bytes 786440 | tf_op jit(solution)/shard_map/ppermute | solution.py:407
  127.6 21.8 %collective-permute-start.29 = (bf16[256,1024]{1,0:T(8,128)(2,1)S(1)}, bf16[256,1024]{1,0:T(8,128)(2,1)S(1)}, u32[]{:S(2)}, u32[]{:S(2)}) collective-permute-start(bf16[256,1024]{1,0:T(8,128)(2,1)S(1)} %collective-permute-done.25), channel_id=1, source_target_pairs={{0,8},{4,12},{8,0},{12,4},{1,9},{5,13},{9,1},{13,5},{2,10},{6,14},... | collective-permute-start | bytes 1572872 | tf_op jit(solution)/shard_map/ppermute | solution.py:412
  149.5 18.2 %collective-permute-start.34 = (bf16[2,256,1024]{2,1,0:T(8,128)(2,1)S(1)}, bf16[2,256,1024]{2,1,0:T(8,128)(2,1)S(1)}, u32[]{:S(2)}, u32[]{:S(2)}) collective-permute-start(bf16[2,256,1024]{2,1,0:T(8,128)(2,1)S(1)} %pad_maximum_fusion.7.refs_13_.refs_21_.refs_12_.refs_14_), channel_id=1, source_target_pairs={{0,4},{4,0},{8,12},{12,8},{1,5},{5,1},{9,13},{13,9},{2,6},{6,2},{1... | collective-permute-start | bytes 3145736 | tf_op jit(solution)/shard_map/ppermute | solution.py:412
  149.6 18.1 %collective-permute-start.33 = (bf16[2,256,1024]{2,1,0:T(8,128)(2,1)S(1)}, bf16[2,256,1024]{2,1,0:T(8,128)(2,1)S(1)}, u32[]{:S(2)}, u32[]{:S(2)}) collective-permute-start(bf16[2,256,1024]{2,1,0:T(8,128)(2,1)S(1)} %pad_maximum_fusion.6.refs_12_.refs_20_.refs_11_.refs_13_), channel_id=1, source_target_pairs={{0,4},{4,0},{8,12},{12,8},{1,5},{5,1},{9,13},{13,9},{2,6},{6,2},{1... | collective-permute-start | bytes 3145736 | tf_op jit(solution)/shard_map/ppermute | solution.py:412
  150.1 17.5 %collective-permute-start.32 = (bf16[2,256,1024]{2,1,0:T(8,128)(2,1)S(1)}, bf16[2,256,1024]{2,1,0:T(8,128)(2,1)S(1)}, u32[]{:S(2)}, u32[]{:S(2)}) collective-permute-start(bf16[2,256,1024]{2,1,0:T(8,128)(2,1)S(1)} %pad_maximum_fusion.5.refs_11_.refs_19_.refs_10_.refs_12_), channel_id=1, source_target_pairs={{0,4},{4,0},{8,12},{12,8},{1,5},{5,1},{9,13},{13,9},{2,6},{6,2},{1... | collective-permute-start | bytes 3145736 | tf_op jit(solution)/shard_map/ppermute | solution.py:412
  173.0 23.4 %collective-permute-start.36 = (bf16[256,512]{1,0:T(8,128)(2,1)S(1)}, bf16[256,512]{1,0:T(8,128)(2,1)S(1)}, u32[]{:S(2)}, u32[]{:S(2)}) collective-permute-start(bf16[256,512]{1,0:T(8,128)(2,1)S(1)} %copy-done.29), channel_id=1, source_target_pairs={{0,1},{1,2},{2,3},{3,0},{4,5},{5,6},{6,7},{7,4},{8,9},{9,10},{10,1... | collective-permute-start | bytes 786440 | tf_op jit(solution)/shard_map/ppermute | solution.py:407
  173.0 22.7 %collective-permute-start.37 = (bf16[256,512]{1,0:T(8,128)(2,1)S(1)}, bf16[256,512]{1,0:T(8,128)(2,1)S(1)}, u32[]{:S(2)}, u32[]{:S(2)}) collective-permute-start(bf16[256,512]{1,0:T(8,128)(2,1)S(1)} %copy-done.29), channel_id=1, source_target_pairs={{0,3},{1,0},{2,1},{3,2},{4,7},{5,4},{6,5},{7,6},{8,11},{9,8},{10,9... | collective-permute-start | bytes 786440 | tf_op jit(solution)/shard_map/ppermute | solution.py:407
  177.2 19.8 %collective-permute-start.38 = (bf16[256,512]{1,0:T(8,128)(2,1)S(1)}, bf16[256,512]{1,0:T(8,128)(2,1)S(1)}, u32[]{:S(2)}, u32[]{:S(2)}) collective-permute-start(bf16[256,512]{1,0:T(8,128)(2,1)S(1)} %copy-done.29), channel_id=1, source_target_pairs={{0,8},{4,12},{8,0},{12,4},{1,9},{5,13},{9,1},{13,5},{2,10},{6,14},... | collective-permute-start | bytes 786440 | tf_op jit(solution)/shard_map/ppermute | solution.py:412
  178.3 18.7 %collective-permute-start.39 = (bf16[256,1024]{1,0:T(8,128)(2,1)S(1)}, bf16[256,1024]{1,0:T(8,128)(2,1)S(1)}, u32[]{:S(2)}, u32[]{:S(2)}) collective-permute-start(bf16[256,1024]{1,0:T(8,128)(2,1)S(1)} %get-tuple-element.273), channel_id=1, source_target_pairs={{0,8},{4,12},{8,0},{12,4},{1,9},{5,13},{9,1},{13,5},{2,10},{6,14},... | collective-permute-start | bytes 1572872 | tf_op jit(solution)/shard_map/ppermute | solution.py:412
  197.8 31.6 %collective-permute-start.43 = (bf16[256,1024]{1,0:T(8,128)(2,1)S(1)}, bf16[256,1024]{1,0:T(8,128)(2,1)S(1)}, u32[]{:S(2)}, u32[]{:S(2)}) collective-permute-start(bf16[256,1024]{1,0:T(8,128)(2,1)S(1)} %get-tuple-element.273), channel_id=1, source_target_pairs={{0,1},{1,2},{2,3},{3,0},{4,5},{5,6},{6,7},{7,4},{8,9},{9,10},{10,1... | collective-permute-start | bytes 1572872 | tf_op jit(solution)/shard_map/ppermute | solution.py:407
  197.8 31.6 %collective-permute-start.44 = (bf16[256,1024]{1,0:T(8,128)(2,1)S(1)}, bf16[256,1024]{1,0:T(8,128)(2,1)S(1)}, u32[]{:S(2)}, u32[]{:S(2)}) collective-permute-start(bf16[256,1024]{1,0:T(8,128)(2,1)S(1)} %get-tuple-element.273), channel_id=1, source_target_pairs={{0,3},{1,0},{2,1},{3,2},{4,7},{5,4},{6,5},{7,6},{8,11},{9,8},{10,9... | collective-permute-start | bytes 1572872 | tf_op jit(solution)/shard_map/ppermute | solution.py:407
  201.6 23.2 %collective-permute-start.42 = (bf16[128,512]{1,0:T(8,128)(2,1)}, bf16[128,512]{1,0:T(8,128)(2,1)S(1)}, u32[]{:S(2)}, u32[]{:S(2)}) collective-permute-start(bf16[128,512]{1,0:T(8,128)(2,1)} %slice.765), channel_id=1, source_target_pairs={{0,3},{1,0},{2,1},{3,2},{4,7},{5,4},{6,5},{7,6},{8,11},{9,8},{10,9... | collective-permute-start | bytes 393224 | tf_op jit(solution)/shard_map/ppermute | solution.py:407
  201.6 27.8 %collective-permute-start.41 = (bf16[128,512]{1,0:T(8,128)(2,1)}, bf16[128,512]{1,0:T(8,128)(2,1)}, u32[]{:S(2)}, u32[]{:S(2)}) collective-permute-start(bf16[128,512]{1,0:T(8,128)(2,1)} %slice.764), channel_id=1, source_target_pairs={{0,1},{1,2},{2,3},{3,0},{4,5},{5,6},{6,7},{7,4},{8,9},{9,10},{10,1... | collective-permute-start | bytes 393224 | tf_op jit(solution)/shard_map/ppermute | solution.py:407
  203.6 25.8 %collective-permute-start.40 = (bf16[512,1024]{1,0:T(8,128)(2,1)}, bf16[512,1024]{1,0:T(8,128)(2,1)S(1)}, u32[]{:S(2)}, u32[]{:S(2)}) collective-permute-start(bf16[512,1024]{1,0:T(8,128)(2,1)} %get-tuple-element.266), channel_id=1, source_target_pairs={{0,16},{16,0},{1,17},{17,1},{2,18},{18,2},{3,19},{19,3},{4,20},{20... | collective-permute-start | bytes 3145736 | tf_op jit(solution)/shard_map/ppermute | solution.py:412
  230.6 23.0 %collective-permute-start.45 = (bf16[512,1024]{1,0:T(8,128)(2,1)}, bf16[512,1024]{1,0:T(8,128)(2,1)}, u32[]{:S(2)}, u32[]{:S(2)}) collective-permute-start(bf16[512,1024]{1,0:T(8,128)(2,1)} %get-tuple-element.274), channel_id=1, source_target_pairs={{0,16},{16,0},{1,17},{17,1},{2,18},{18,2},{3,19},{19,3},{4,20},{20... | collective-permute-start | bytes 3145736 | tf_op jit(solution)/shard_map/ppermute | solution.py:412
  275.6 20.8 %collective-permute-start.57 = (bf16[256,1024]{1,0:T(8,128)(2,1)S(1)}, bf16[256,1024]{1,0:T(8,128)(2,1)S(1)}, u32[]{:S(2)}, u32[]{:S(2)}) collective-permute-start(bf16[256,1024]{1,0:T(8,128)(2,1)S(1)} %constant_dynamic-update-slice_fusion.6), channel_id=1, source_target_pairs={{0,8},{4,12},{8,0},{12,4},{1,9},{5,13},{9,1},{13,5},{2,10},{6,14},... | collective-permute-start | bytes 1572872 | tf_op jit(solution)/shard_map/ppermute | solution.py:412
  277.7 24.7 %collective-permute-start.59 = (bf16[2,256,1024]{2,1,0:T(8,128)(2,1)}, bf16[2,256,1024]{2,1,0:T(8,128)(2,1)}, u32[]{:S(2)}, u32[]{:S(2)}) collective-permute-start(bf16[2,256,1024]{2,1,0:T(8,128)(2,1)} %pad_maximum_fusion.10.refs_12_.refs_20_.refs_11_.refs_13_), channel_id=1, source_target_pairs={{0,4},{4,0},{8,12},{12,8},{1,5},{5,1},{9,13},{13,9},{2,6},{6,2},{1... | collective-permute-start | bytes 3145736 | tf_op jit(solution)/shard_map/ppermute | solution.py:412
  277.7 24.7 %collective-permute-start.58 = (bf16[2,256,1024]{2,1,0:T(8,128)(2,1)S(1)}, bf16[2,256,1024]{2,1,0:T(8,128)(2,1)}, u32[]{:S(2)}, u32[]{:S(2)}) collective-permute-start(bf16[2,256,1024]{2,1,0:T(8,128)(2,1)S(1)} %pad_maximum_fusion.9.refs_11_.refs_19_.refs_10_.refs_12_), channel_id=1, source_target_pairs={{0,4},{4,0},{8,12},{12,8},{1,5},{5,1},{9,13},{13,9},{2,6},{6,2},{1... | collective-permute-start | bytes 3145736 | tf_op jit(solution)/shard_map/ppermute | solution.py:412
  278.2 22.1 %collective-permute-start.56 = (bf16[256,1024]{1,0:T(8,128)(2,1)S(1)}, bf16[256,1024]{1,0:T(8,128)(2,1)}, u32[]{:S(2)}, u32[]{:S(2)}) collective-permute-start(bf16[256,1024]{1,0:T(8,128)(2,1)S(1)} %collective-permute-done.44), channel_id=1, source_target_pairs={{0,8},{4,12},{8,0},{12,4},{1,9},{5,13},{9,1},{13,5},{2,10},{6,14},... | collective-permute-start | bytes 1572872 | tf_op jit(solution)/shard_map/ppermute | solution.py:412
  306.9 20.7 %collective-permute-start.63 = (bf16[384,512]{1,0:T(8,128)(2,1)S(1)}, bf16[384,512]{1,0:T(8,128)(2,1)S(1)}, u32[]{:S(2)}, u32[]{:S(2)}) collective-permute-start(bf16[384,512]{1,0:T(8,128)(2,1)S(1)} %pad_maximum_fusion.31), channel_id=1, source_target_pairs={{0,3},{1,0},{2,1},{3,2},{4,7},{5,4},{6,5},{7,6},{8,11},{9,8},{10,9... | collective-permute-start | bytes 1179656 | tf_op jit(solution)/shard_map/ppermute | solution.py:407
  309.8 17.8 %collective-permute-start.62 = (bf16[384,512]{1,0:T(8,128)(2,1)S(1)}, bf16[384,512]{1,0:T(8,128)(2,1)S(1)}, u32[]{:S(2)}, u32[]{:S(2)}) collective-permute-start(bf16[384,512]{1,0:T(8,128)(2,1)S(1)} %pad_maximum_fusion.30), channel_id=1, source_target_pairs={{0,1},{1,2},{2,3},{3,0},{4,5},{5,6},{6,7},{7,4},{8,9},{9,10},{10,1... | collective-permute-start | bytes 1179656 | tf_op jit(solution)/shard_map/ppermute | solution.py:407
  337.2 24.9 %collective-permute-start.66 = (bf16[4,256,512]{2,1,0:T(8,128)(2,1)S(1)}, bf16[4,256,512]{2,1,0:T(8,128)(2,1)S(1)}, u32[]{:S(2)}, u32[]{:S(2)}) collective-permute-start(bf16[4,256,512]{2,1,0:T(8,128)(2,1)S(1)} %fusion.51), channel_id=1, source_target_pairs={{0,16},{16,0},{1,17},{17,1},{2,18},{18,2},{3,19},{19,3},{4,20},{20... | collective-permute-start | bytes 3145736 | tf_op jit(solution)/shard_map/ppermute | solution.py:412
  364.8 24.0 %collective-permute-start.67 = (bf16[512,1024]{1,0:T(8,128)(2,1)S(1)}, bf16[512,1024]{1,0:T(8,128)(2,1)S(1)}, u32[]{:S(2)}, u32[]{:S(2)}) collective-permute-start(bf16[512,1024]{1,0:T(8,128)(2,1)S(1)} %copy-done.35), channel_id=1, source_target_pairs={{0,16},{16,0},{1,17},{17,1},{2,18},{18,2},{3,19},{19,3},{4,20},{20... | collective-permute-start | bytes 3145736 | tf_op jit(solution)/shard_map/ppermute | solution.py:412
  388.8 27.1 %collective-permute-start.68 = (bf16[512,1024]{1,0:T(8,128)(2,1)}, bf16[512,1024]{1,0:T(8,128)(2,1)}, u32[]{:S(2)}, u32[]{:S(2)}) collective-permute-start(bf16[512,1024]{1,0:T(8,128)(2,1)} %get-tuple-element.322), channel_id=1, source_target_pairs={{0,16},{16,0},{1,17},{17,1},{2,18},{18,2},{3,19},{19,3},{4,20},{20... | collective-permute-start | bytes 3145736 | tf_op jit(solution)/shard_map/ppermute | solution.py:412
  431.9 27.1 %collective-permute-start.69 = (bf16[512,1024]{1,0:T(8,128)(2,1)}, bf16[512,1024]{1,0:T(8,128)(2,1)S(1)}, u32[]{:S(2)}, u32[]{:S(2)}) collective-permute-start(bf16[512,1024]{1,0:T(8,128)(2,1)} %get-tuple-element.338), channel_id=1, source_target_pairs={{0,16},{16,0},{1,17},{17,1},{2,18},{18,2},{3,19},{19,3},{4,20},{20... | collective-permute-start | bytes 3145736 | tf_op jit(solution)/shard_map/ppermute | solution.py:412
  463.6 50.7 %collective-permute-start.71 = (bf16[4,2,256,1024]{3,2,0,1:T(8,128)(2,1)}, bf16[4,2,256,1024]{3,2,0,1:T(8,128)(2,1)}, u32[]{:S(2)}, u32[]{:S(2)}) collective-permute-start(bf16[4,2,256,1024]{3,2,0,1:T(8,128)(2,1)} %copy.119), channel_id=1, source_target_pairs={{0,4},{4,0},{8,12},{12,8},{1,5},{5,1},{9,13},{13,9},{2,6},{6,2},{1... | collective-permute-start | bytes 12582920 | tf_op jit(solution)/shard_map/ppermute | solution.py:412
  475.2 37.1 %collective-permute-start.75 = (bf16[384,1024]{1,0:T(8,128)(2,1)}, bf16[384,1024]{1,0:T(8,128)(2,1)}, u32[]{:S(2)}, u32[]{:S(2)}) collective-permute-start(bf16[384,1024]{1,0:T(8,128)(2,1)} %pad_maximum_fusion.13), channel_id=1, source_target_pairs={{0,3},{1,0},{2,1},{3,2},{4,7},{5,4},{6,5},{7,6},{8,11},{9,8},{10,9... | collective-permute-start | bytes 2359304 | tf_op jit(solution)/shard_map/ppermute | solution.py:407
  475.4 37.9 %collective-permute-start.74 = (bf16[384,1024]{1,0:T(8,128)(2,1)}, bf16[384,1024]{1,0:T(8,128)(2,1)}, u32[]{:S(2)}, u32[]{:S(2)}) collective-permute-start(bf16[384,1024]{1,0:T(8,128)(2,1)} %pad_maximum_fusion.12), channel_id=1, source_target_pairs={{0,1},{1,2},{2,3},{3,0},{4,5},{5,6},{6,7},{7,4},{8,9},{9,10},{10,1... | collective-permute-start | bytes 2359304 | tf_op jit(solution)/shard_map/ppermute | solution.py:407
  477.3 37.1 %collective-permute-start.70 = (bf16[512,1024]{1,0:T(8,128)(2,1)}, bf16[512,1024]{1,0:T(8,128)(2,1)}, u32[]{:S(2)}, u32[]{:S(2)}) collective-permute-start(bf16[512,1024]{1,0:T(8,128)(2,1)} %get-tuple-element.336), channel_id=1, source_target_pairs={{0,16},{16,0},{1,17},{17,1},{2,18},{18,2},{3,19},{19,3},{4,20},{20... | collective-permute-start | bytes 3145736 | tf_op jit(solution)/shard_map/ppermute | solution.py:412
  517.3 27.0 %collective-permute-start.73 = (bf16[2,256,1024]{2,1,0:T(8,128)(2,1)}, bf16[2,256,1024]{2,1,0:T(8,128)(2,1)}, u32[]{:S(2)}, u32[]{:S(2)}) collective-permute-start(bf16[2,256,1024]{2,1,0:T(8,128)(2,1)} %fusion.16), channel_id=1, source_target_pairs={{0,8},{4,12},{8,0},{12,4},{1,9},{5,13},{9,1},{13,5},{2,10},{6,14},... | collective-permute-start | bytes 3145736 | tf_op jit(solution)/shard_map/ppermute | solution.py:412
  520.0 24.2 %collective-permute-start.72 = (bf16[4,2,256,512]{3,2,0,1:T(8,128)(2,1)}, bf16[4,2,256,512]{3,2,0,1:T(8,128)(2,1)}, u32[]{:S(2)}, u32[]{:S(2)}) collective-permute-start(bf16[4,2,256,512]{3,2,0,1:T(8,128)(2,1)} %copy.120), channel_id=1, source_target_pairs={{0,4},{4,0},{8,12},{12,8},{1,5},{5,1},{9,13},{13,9},{2,6},{6,2},{1... | collective-permute-start | bytes 6291464 | tf_op jit(solution)/shard_map/ppermute | solution.py:412
  546.9 24.8 %collective-permute-start.78 = (bf16[2,256,1024]{2,1,0:T(8,128)(2,1)}, bf16[2,256,1024]{2,1,0:T(8,128)(2,1)S(1)}, u32[]{:S(2)}, u32[]{:S(2)}) collective-permute-start(bf16[2,256,1024]{2,1,0:T(8,128)(2,1)} %fusion.15), channel_id=1, source_target_pairs={{0,8},{4,12},{8,0},{12,4},{1,9},{5,13},{9,1},{13,5},{2,10},{6,14},... | collective-permute-start | bytes 3145736 | tf_op jit(solution)/shard_map/ppermute | solution.py:412
  576.7 37.2 %collective-permute-start.81 = (bf16[4,2,256,1024]{3,2,0,1:T(8,128)(2,1)}, bf16[4,2,256,1024]{3,2,0,1:T(8,128)(2,1)}, u32[]{:S(2)}, u32[]{:S(2)}) collective-permute-start(bf16[4,2,256,1024]{3,2,0,1:T(8,128)(2,1)} %copy.124), channel_id=1, source_target_pairs={{0,4},{4,0},{8,12},{12,8},{1,5},{5,1},{9,13},{13,9},{2,6},{6,2},{1... | collective-permute-start | bytes 12582920 | tf_op jit(solution)/shard_map/ppermute | solution.py:412
  581.0 32.8 %collective-permute-start.82 = (bf16[4,256,512]{2,1,0:T(8,128)(2,1)}, bf16[4,256,512]{2,1,0:T(8,128)(2,1)}, u32[]{:S(2)}, u32[]{:S(2)}) collective-permute-start(bf16[4,256,512]{2,1,0:T(8,128)(2,1)} %fusion.12), channel_id=1, source_target_pairs={{0,8},{4,12},{8,0},{12,4},{1,9},{5,13},{9,1},{13,5},{2,10},{6,14},... | collective-permute-start | bytes 3145736 | tf_op jit(solution)/shard_map/ppermute | solution.py:412
  584.9 29.0 %collective-permute-start.80 = (bf16[128,1024]{1,0:T(8,128)(2,1)}, bf16[128,1024]{1,0:T(8,128)(2,1)S(1)}, u32[]{:S(2)}, u32[]{:S(2)}) collective-permute-start(bf16[128,1024]{1,0:T(8,128)(2,1)} %get-tuple-element.362), channel_id=1, source_target_pairs={{0,3},{1,0},{2,1},{3,2},{4,7},{5,4},{6,5},{7,6},{8,11},{9,8},{10,9... | collective-permute-start | bytes 786440 | tf_op jit(solution)/shard_map/ppermute | solution.py:407
  584.9 28.0 %collective-permute-start.79 = (bf16[128,1024]{1,0:T(8,128)(2,1)}, bf16[128,1024]{1,0:T(8,128)(2,1)S(1)}, u32[]{:S(2)}, u32[]{:S(2)}) collective-permute-start(bf16[128,1024]{1,0:T(8,128)(2,1)} %get-tuple-element.361), channel_id=1, source_target_pairs={{0,1},{1,2},{2,3},{3,0},{4,5},{5,6},{6,7},{7,4},{8,9},{9,10},{10,1... | collective-permute-start | bytes 786440 | tf_op jit(solution)/shard_map/ppermute | solution.py:407
  630.4 23.9 %collective-permute-start.85 = (bf16[256,1024]{1,0:T(8,128)(2,1)}, bf16[256,1024]{1,0:T(8,128)(2,1)S(1)}, u32[]{:S(2)}, u32[]{:S(2)}) collective-permute-start(bf16[256,1024]{1,0:T(8,128)(2,1)} %pad_maximum_fusion.25), channel_id=1, source_target_pairs={{0,3},{1,0},{2,1},{3,2},{4,7},{5,4},{6,5},{7,6},{8,11},{9,8},{10,9... | collective-permute-start | bytes 1572872 | tf_op jit(solution)/shard_map/ppermute | solution.py:407
  632.2 23.6 %collective-permute-start.84 = (bf16[256,1024]{1,0:T(8,128)(2,1)}, bf16[256,1024]{1,0:T(8,128)(2,1)}, u32[]{:S(2)}, u32[]{:S(2)}) collective-permute-start(bf16[256,1024]{1,0:T(8,128)(2,1)} %pad_maximum_fusion.24), channel_id=1, source_target_pairs={{0,1},{1,2},{2,3},{3,0},{4,5},{5,6},{6,7},{7,4},{8,9},{9,10},{10,1... | collective-permute-start | bytes 1572872 | tf_op jit(solution)/shard_map/ppermute | solution.py:407
  635.4 24.8 %collective-permute-start.83 = (bf16[2,256,1024]{2,1,0:T(8,128)(2,1)}, bf16[2,256,1024]{2,1,0:T(8,128)(2,1)}, u32[]{:S(2)}, u32[]{:S(2)}) collective-permute-start(bf16[2,256,1024]{2,1,0:T(8,128)(2,1)} %fusion.17), channel_id=1, source_target_pairs={{0,8},{4,12},{8,0},{12,4},{1,9},{5,13},{9,1},{13,5},{2,10},{6,14},... | collective-permute-start | bytes 3145736 | tf_op jit(solution)/shard_map/ppermute | solution.py:412
  636.6 49.6 %collective-permute-start.86 = (bf16[512,1024]{1,0:T(8,128)(2,1)}, bf16[512,1024]{1,0:T(8,128)(2,1)}, u32[]{:S(2)}, u32[]{:S(2)}) collective-permute-start(bf16[512,1024]{1,0:T(8,128)(2,1)} %get-tuple-element.390), channel_id=1, source_target_pairs={{0,16},{16,0},{1,17},{17,1},{2,18},{18,2},{3,19},{19,3},{4,20},{20... | collective-permute-start | bytes 3145736 | tf_op jit(solution)/shard_map/ppermute | solution.py:412
  660.2 23.4 %collective-permute-start.90 = (bf16[128,512]{1,0:T(8,128)(2,1)}, bf16[128,512]{1,0:T(8,128)(2,1)}, u32[]{:S(2)}, u32[]{:S(2)}) collective-permute-start(bf16[128,512]{1,0:T(8,128)(2,1)} %get-tuple-element.384), channel_id=1, source_target_pairs={{0,3},{1,0},{2,1},{3,2},{4,7},{5,4},{6,5},{7,6},{8,11},{9,8},{10,9... | collective-permute-start | bytes 393224 | tf_op jit(solution)/shard_map/ppermute | solution.py:407
  663.8 19.8 %collective-permute-start.89 = (bf16[128,512]{1,0:T(8,128)(2,1)}, bf16[128,512]{1,0:T(8,128)(2,1)}, u32[]{:S(2)}, u32[]{:S(2)}) collective-permute-start(bf16[128,512]{1,0:T(8,128)(2,1)} %get-tuple-element.383), channel_id=1, source_target_pairs={{0,1},{1,2},{2,3},{3,0},{4,5},{5,6},{6,7},{7,4},{8,9},{9,10},{10,1... | collective-permute-start | bytes 393224 | tf_op jit(solution)/shard_map/ppermute | solution.py:407
  666.4 23.5 %collective-permute-start.88 = (bf16[2,256,1024]{2,1,0:T(8,128)(2,1)}, bf16[2,256,1024]{2,1,0:T(8,128)(2,1)}, u32[]{:S(2)}, u32[]{:S(2)}) collective-permute-start(bf16[2,256,1024]{2,1,0:T(8,128)(2,1)} %fusion.9), channel_id=1, source_target_pairs={{0,8},{4,12},{8,0},{12,4},{1,9},{5,13},{9,1},{13,5},{2,10},{6,14},... | collective-permute-start | bytes 3145736 | tf_op jit(solution)/shard_map/ppermute | solution.py:412
  667.5 23.3 %collective-permute-start.87 = (bf16[512,1024]{1,0:T(8,128)(2,1)}, bf16[512,1024]{1,0:T(8,128)(2,1)}, u32[]{:S(2)}, u32[]{:S(2)}) collective-permute-start(bf16[512,1024]{1,0:T(8,128)(2,1)} %get-tuple-element.391), channel_id=1, source_target_pairs={{0,16},{16,0},{1,17},{17,1},{2,18},{18,2},{3,19},{19,3},{4,20},{20... | collective-permute-start | bytes 3145736 | tf_op jit(solution)/shard_map/ppermute | solution.py:412
  690.8 21.7 %collective-permute-start.93 = (bf16[4,2,256,512]{3,2,1,0:T(8,128)(2,1)}, bf16[4,2,256,512]{3,2,1,0:T(8,128)(2,1)}, u32[]{:S(2)}, u32[]{:S(2)}) collective-permute-start(bf16[4,2,256,512]{3,2,1,0:T(8,128)(2,1)} %get-tuple-element.389), channel_id=1, source_target_pairs={{0,4},{4,0},{8,12},{12,8},{1,5},{5,1},{9,13},{13,9},{2,6},{6,2},{1... | collective-permute-start | bytes 6291464 | tf_op jit(solution)/shard_map/ppermute | solution.py:412
  694.9 17.6 %collective-permute-start.92 = (bf16[128,1024]{1,0:T(8,128)(2,1)}, bf16[128,1024]{1,0:T(8,128)(2,1)}, u32[]{:S(2)}, u32[]{:S(2)}) collective-permute-start(bf16[128,1024]{1,0:T(8,128)(2,1)} %get-tuple-element.387), channel_id=1, source_target_pairs={{0,3},{1,0},{2,1},{3,2},{4,7},{5,4},{6,5},{7,6},{8,11},{9,8},{10,9... | collective-permute-start | bytes 786440 | tf_op jit(solution)/shard_map/ppermute | solution.py:407
  718.0 22.5 %collective-permute-start.95 = (bf16[256,1024]{1,0:T(8,128)(2,1)S(1)}, bf16[256,1024]{1,0:T(8,128)(2,1)S(1)}, u32[]{:S(2)}, u32[]{:S(2)}) collective-permute-start(bf16[256,1024]{1,0:T(8,128)(2,1)S(1)} %pad_maximum_fusion.27), channel_id=1, source_target_pairs={{0,3},{1,0},{2,1},{3,2},{4,7},{5,4},{6,5},{7,6},{8,11},{9,8},{10,9... | collective-permute-start | bytes 1572872 | tf_op jit(solution)/shard_map/ppermute | solution.py:407
  721.9 29.7 %collective-permute-start.94 = (bf16[256,1024]{1,0:T(8,128)(2,1)S(1)}, bf16[256,1024]{1,0:T(8,128)(2,1)S(1)}, u32[]{:S(2)}, u32[]{:S(2)}) collective-permute-start(bf16[256,1024]{1,0:T(8,128)(2,1)S(1)} %pad_maximum_fusion.26), channel_id=1, source_target_pairs={{0,1},{1,2},{2,3},{3,0},{4,5},{5,6},{6,7},{7,4},{8,9},{9,10},{10,1... | collective-permute-start | bytes 1572872 | tf_op jit(solution)/shard_map/ppermute | solution.py:407
  727.0 25.4 %collective-permute-start.96 = (bf16[4,256,512]{2,1,0:T(8,128)(2,1)S(1)}, bf16[4,256,512]{2,1,0:T(8,128)(2,1)S(1)}, u32[]{:S(2)}, u32[]{:S(2)}) collective-permute-start(bf16[4,256,512]{2,1,0:T(8,128)(2,1)S(1)} %fusion.2), channel_id=1, source_target_pairs={{0,8},{4,12},{8,0},{12,4},{1,9},{5,13},{9,1},{13,5},{2,10},{6,14},... | collective-permute-start | bytes 3145736 | tf_op jit(solution)/shard_map/ppermute | solution.py:412
  772.8 40.3 %collective-permute-start.104 = (bf16[384,1024]{1,0:T(8,128)(2,1)}, bf16[384,1024]{1,0:T(8,128)(2,1)}, u32[]{:S(2)}, u32[]{:S(2)}) collective-permute-start(bf16[384,1024]{1,0:T(8,128)(2,1)} %pad_maximum_fusion.15), channel_id=1, source_target_pairs={{0,3},{1,0},{2,1},{3,2},{4,7},{5,4},{6,5},{7,6},{8,11},{9,8},{10,9... | collective-permute-start | bytes 2359304 | tf_op jit(solution)/shard_map/ppermute | solution.py:407
  782.0 31.1 %collective-permute-start.103 = (bf16[384,1024]{1,0:T(8,128)(2,1)}, bf16[384,1024]{1,0:T(8,128)(2,1)}, u32[]{:S(2)}, u32[]{:S(2)}) collective-permute-start(bf16[384,1024]{1,0:T(8,128)(2,1)} %pad_maximum_fusion.14), channel_id=1, source_target_pairs={{0,1},{1,2},{2,3},{3,0},{4,5},{5,6},{6,7},{7,4},{8,9},{9,10},{10,1... | collective-permute-start | bytes 2359304 | tf_op jit(solution)/shard_map/ppermute | solution.py:407
  (132 other events, 1241.2 us)

commit v6 on v5

--- a/solution.py
+++ b/solution.py
@@ -442,9 +442,9 @@
 
 def exchange_near(blocks, own, hold):
     half = blocks.shape[1] // 2
-    far = pick(blocks, (own + 2) % 4)
-    ahead = jnp.concatenate([pick(blocks, (own + 1) % 4), far[:half]], axis=0)
-    behind = jnp.concatenate([pick(blocks, (own + 3) % 4), far[half:]], axis=0)
+    far = pick(blocks, (own + 2) & 3)
+    ahead = jnp.concatenate([pick(blocks, (own + 1) & 3), far[:half]], axis=0)
+    behind = jnp.concatenate([pick(blocks, (own + 3) & 3), far[half:]], axis=0)
     return ring(hold(ahead), "tensor", 1), ring(hold(behind), "tensor", -1)
 
 
@@ -459,9 +459,9 @@
     rows = blocks.shape[1]
     result = jnp.zeros_like(blocks)
     result = place(result, pick(blocks, own), own)
-    result = place(result, near[0][:rows], (own + 3) % 4)
-    result = place(result, near[1][:rows], (own + 1) % 4)
-    return place(result, jnp.concatenate(far, axis=0), (own + 2) % 4)
+    result = place(result, near[0][:rows], (own + 3) & 3)
+    result = place(result, near[1][:rows], (own + 1) & 3)
+    return place(result, jnp.concatenate(far, axis=0), (own + 2) & 3)
 
 
 def add_wide(left, right):
@@ -917,16 +917,16 @@
         grad = nn_dot(turned[...], right[...]).astype(jnp.bfloat16)
         for side in range(2):
             first = 2 * side * rows
-            keep[0, side, :, at : at + size] = grad[first : first + rows]
-            send[0, side, :, at : at + size] = grad[first + rows : first + 2 * rows]
+            keep[side, 0, :, at : at + size] = grad[first : first + rows]
+            send[side, 0, :, at : at + size] = grad[first + rows : first + 2 * rows]
         at += size
 
 
 def run_weight_grad(lefts, rights):
     length, width = rights[0].shape[0], lefts[0][0].shape[1]
     sizes = [right.shape[1] // 4 for right in rights]
-    shape = (4, 2, width // 4, sum(sizes))
-    out = (shape, jnp.bfloat16, (1,) + shape[1:], lambda i: (i, 0, 0, 0))
+    shape = (2, 4, width // 4, sum(sizes))
+    out = (shape, jnp.bfloat16, (2, 1) + shape[2:], lambda i: (0, i, 0, 0))
     turned = pltpu.VMEM((width, length), jnp.bfloat16)
     return call(
         partial(weight_grad_body, tuple(len(group) for group in lefts)),
@@ -953,9 +953,9 @@
 def by_sequence(
     acts_in, cotangent, norm_gains, vec_bias, w_qkv, b_qkv, w_out, w_up, b_up, w_down
 ):
-    section = lax.axis_index("section")
-    across = lax.axis_index("dp")
-    along = lax.axis_index("tensor")
+    section = lax.axis_index("section").astype(jnp.uint32)
+    across = lax.axis_index("dp").astype(jnp.uint32)
+    along = lax.axis_index("tensor").astype(jnp.uint32)
     first_section = section == 0
     width = acts_in.shape[3]
     rows = w_qkv.shape[1]
@@ -1041,9 +1041,9 @@
     narrow_far = far_halves(left, right)
     got_left, got_right = x_swap(left), x_swap(right)
     small = jnp.stack([small, swap(hold(small), "tensor", 1)])
+    small = jnp.concatenate([small, swap(small, "tensor", 2)])
     tick(narrow_far, got_left, got_right, small)
     broad_shards = by_layer(broad, got_broad)
-    small = jnp.concatenate([small, swap(hold(small), "tensor", 2)])
     broad_left, broad_right = both_ways(broad_shards[0])
     narrow_far = jnp.concatenate(narrow_far, axis=0)
     got_far = x_swap(narrow_far)
@@ -1053,7 +1053,7 @@
         stacked(right, got_right),
     ]
     others = [core_swap(piece) for piece in pieces]
-    tick(got_far, others, got_acts, small)
+    tick(got_far, others, got_acts)
     acts = both_halves(own_acts, got_acts)
     pieces.append(stacked(narrow_far, got_far))
     others.append(core_swap(pieces[3]))
@@ -1064,8 +1064,8 @@
     share = norm_gains.shape[2]
     vec_part = small[..., : 6 * share].reshape(4, 4, 2, 6, share)
     offsets = jnp.array(FAR_ORDER, jnp.int32)
-    order = jnp.stack([pick(offsets, (k - along) % 4) for k in range(4)])
-    slots = [jnp.bitwise_xor((along + k) % 4, along) for k in (0, 3, 1, 2)]
+    order = jnp.stack([pick(offsets, (k - along) & 3) for k in range(4)])
+    slots = [jnp.bitwise_xor((along + k) & 3, along) for k in (0, 3, 1, 2)]
     vec_part = jnp.stack([pick(vec_part, jnp.bitwise_xor(along, k)) for k in range(4)])
     vecs_full = vec_part.transpose(2, 3, 1, 0, 4).reshape(2, 6, width)
     at = 6 * share
@@ -1223,17 +1223,19 @@
     )
     tick(part_a, out_blocks)
     got_a = y_swap(part_a)
+    out_parts = out_blocks[..., : width // 2], out_blocks[..., width // 2 :]
+    out_near = [exchange_near(out_parts[0], along, hold)]
     part_b, sum_b = run_norm_back(
         (x1_b, 0), hold(d_qkv1), d_up1, all_vecs[1], narrow_one, broad_one, chunk, chunk
     )
     sums_one[0] = (sum_a + sum_b)[:4]
     keep_broad, send = run_weight_grad([[hold(ln_m1)], [grads]], [d_up1, act1])
-    tick(part_b, keep_broad, got_a)
+    tick(part_b, keep_broad, got_a, out_near)
     got_b = y_swap(part_b)
     got_core = core_swap(send)
-    out_near = exchange_near(out_blocks, along, hold)
+    out_near.append(exchange_near(out_parts[1], along, hold))
     keep_narrow, send_narrow = run_weight_grad([[hold(ln_a1)], [grads]], [d_qkv1, ctx1])
-    tick(keep_narrow, got_b, got_core)
+    tick(keep_narrow, got_b, got_core, out_near)
 
     def lower(above, part, got):
         total = part.astype(jnp.float32) + got.astype(jnp.float32)
@@ -1243,37 +1245,37 @@
     g1_b = lower(grads[chunk:], hold(part_b), got_b)
     keep_one, core_one = hold(keep_broad), got_core
     got_core = core_swap(send_narrow)
-    got_x = [x_swap(add_wide(keep_one[2:, 1], core_one[2:, 1]))]
+    got_x = [x_swap(add_wide(keep_one[1, 2:], core_one[1, 2:]))]
     first, up_a, g_a = back(0, (hold(g1_a), 0), slope0, narrow_zero, broad_zero, ())
     first, up_b, g_b = back(1, (g1_b, 0), slope0, narrow_zero, broad_zero, first)
     d_up0, d_ctx0 = first
     sums_zero = [None, g_a + g_b, None, up_a + up_b]
-    tick(first, got_core, got_x, out_near)
+    out_far = [exchange_far(near, hold) for near in out_near]
+    tick(first, got_core, got_x, out_far)
     core_narrow = got_core
-    out_far = exchange_far(out_near, hold)
-    got_x.append(x_swap(add_wide(hold(keep_one[:2, 1]), core_one[:2, 1])))
+    got_x.append(x_swap(add_wide(hold(keep_one[1, :2]), core_one[1, :2])))
     keep_broad, send = run_weight_grad([[hold(ln_m0)], [g1_a, g1_b]], [d_up0, act0])
-    tick(keep_broad, out_far, got_x)
+    tick(keep_broad, got_x)
 
     def late_blocks(keep, core, got):
-        late = add_three(hold(keep[2:, 0]), core[2:, 0], got)
+        late = add_three(hold(keep[0, 2:]), core[0, 2:], got)
         return [late[0], late[1]]
 
     def early_blocks(keep, core, got):
-        early = add_three(hold(keep[:2, 0]), core[:2, 0], got)
+        early = add_three(hold(keep[0, :2]), core[0, :2], got)
         return [early[0], early[1]]
 
     got_core = core_swap(send)
     late = late_blocks(keep_one, core_one, got_x[0])
     broad_got = ring_first([None, None, *late], hold)
-    got_narrow = x_swap(add_wide(hold(keep_narrow[:, 1]), core_narrow[:, 1]))
+    got_narrow = x_swap(add_wide(hold(keep_narrow[1]), core_narrow[1]))
     d_qkv0, sums_zero[2] = run_attend_back(qkv0, hold(d_ctx0), lse0, tables)
     tick(d_qkv0, broad_got, got_core, got_narrow)
     broad_one_sum = early_blocks(keep_one, core_one, got_x[1]) + late
-    narrow_sum = add_three(hold(keep_narrow[:, 0]), core_narrow[:, 0], got_narrow)
+    narrow_sum = add_three(hold(keep_narrow[0]), core_narrow[0], got_narrow)
     narrow_sum = [narrow_sum[k] for k in range(4)]
     keep_zero, core_zero = hold(keep_broad), got_core
-    got_x = [x_swap(add_wide(keep_zero[2:, 1], core_zero[2:, 1]))]
+    got_x = [x_swap(add_wide(keep_zero[1, 2:], core_zero[1, 2:]))]
     broad_got = ring_second(broad_one_sum, broad_got, hold)
     part_a, sum_a = run_norm_back(
         (acts, 0), hold(d_qkv0), d_up0, all_vecs[0], narrow_zero, broad_zero, 0, chunk
@@ -1286,7 +1288,7 @@
     sums_zero[0] = (sum_a + sum_b)[:4]
     tick(part_b, got_x, broad_got)
     got_b = y_swap(part_b)
-    got_x.append(x_swap(add_wide(hold(keep_zero[:2, 1]), core_zero[:2, 1])))
+    got_x.append(x_swap(add_wide(hold(keep_zero[1, :2]), core_zero[1, :2])))
     narrow_got = ring_first(narrow_sum, hold)
     keep_narrow, send_narrow = run_weight_grad([[hold(ln_a0)], [g1_a, g1_b]], [d_qkv0, ctx0])
     tick(keep_narrow, got_a, got_b, got_x, narrow_got)
@@ -1307,18 +1309,23 @@
     )
     g1 = jnp.concatenate([g1_a, g1_b], axis=0)
     grad_blocks = to_blocks(jnp.where(first_section, grads_low, g1))
-    tick(broad_next, got_core, grad_blocks)
+    flat = flat + swap(flat, "dp", 1)
+    tick(broad_next, got_core, grad_blocks, flat)
     broad_zero_sum = early_blocks(keep_zero, core_zero, got_x[1]) + late
     broad_next = ring_second(broad_zero_sum, broad_next, hold)
     narrow_got = ring_second(narrow_sum, narrow_got, hold)
-    got_narrow = x_swap(add_wide(hold(keep_narrow[:, 1]), got_core[:, 1]))
-    flat = flat + core_swap(flat)
-    acts_local = exchanged(hold(out_blocks), out_near, out_far, along)
+    got_narrow = x_swap(add_wide(hold(keep_narrow[1]), got_core[1]))
+    flat = flat + x_swap(flat)
+    acts_local = [
+        exchanged(part, near, far, along)
+        for part, near, far in zip(hold(out_parts), out_near, out_far)
+    ]
+    acts_local = jnp.concatenate(acts_local, axis=-1)
     tick(broad_next, got_narrow, flat, narrow_got, acts_local)
-    zero_sum = add_three(hold(keep_narrow[:, 0]), got_core[:, 0], got_narrow)
+    zero_sum = add_three(hold(keep_narrow[0]), got_core[0], got_narrow)
     zero_sum = [zero_sum[k] for k in range(4)]
     narrow_next = ring_first(zero_sum, hold)
-    flat = flat + x_swap(flat)
+    flat = flat + swap(hold(flat), "tensor", 1)
     tick(narrow_next, flat)
     grad_near = exchange_near(grad_blocks, along, hold)
     narrow_next = ring_second(zero_sum, narrow_next, hold)
@@ -1326,8 +1333,7 @@
     one_narrow = ring_total(hold(narrow_sum[0]), narrow_got)
     zero_broad = ring_total(hold(broad_zero_sum[0]), broad_next)
     broad_send = y_swap(jnp.where(first_section, one_broad, zero_broad))
-    flat = flat + swap(hold(flat), "tensor", 1)
-    tick(narrow_next, grad_near, broad_send, flat)
+    tick(narrow_next, grad_near, broad_send)
     grad_far = exchange_far(grad_near, hold)
     zero_narrow = ring_total(zero_sum[0], narrow_next)
     narrow_send = y_swap(jnp.where(first_section, one_narrow, zero_narrow))

time: 843 us -> 819 us (0.972)
  local copies, waits for them, and re-layouts: 96.3 us -> 82.1 us
  waiting for transfers between devices: 206 us -> 195 us
    ppermute x66, waiting for transfers between devices: 94.5 us -> 82.2 us  [swap(): return lax.ppermute(value, axis, [(i, i ^ bit) for i in range(length)])]
    optimization_barrier x4 -> x1, local copies, waits for them, and re-layouts: 11.7 us -> 0.51 us  [hold(): return lax.optimization_barrier((value, self.ended))[0]]
    ppermute x48 -> x52, starting transfers between devices: 70.4 us -> 77.9 us  [ring(): lax.ppermute(value, axis, [(i, (i + by) % length) for i in range(length)])]
    ppermute x48 -> x52, waiting for transfers between devices: 112 us -> 113 us  [ring(): lax.ppermute(value, axis, [(i, (i + by) % length) for i in range(length)])]
  transfers between devices with their start and end apart: 114 -> 118, of which waited for: 39 -> 41; matrix products, arithmetic and copies ran while one was open for 19% -> 17% of each run, Pallas kernels for 34% -> 35%
where the time goes in v6:
time: 819 us; the launch traced here: 810 us
  Pallas kernels  305 us (37%)
  waiting for transfers between devices  195 us (24%)
  starting transfers between devices  122 us (15%)
  other arithmetic  94.6 us (12%)
  local copies, waits for them, and re-layouts  82.1 us (10%)
  between operations  11.5 us (1%)
    pallas_call x24, Pallas kernels, call(): pl.pallas_call(run, name=name, grid=grid, in_specs=[pl.BlockSpec(block, i...  305 us
    ppermute x52, waiting for transfers between devices, ring(): lax.ppermute(value, axis, [(i, (i + by) % length) for i in range(length)])  113 us
    ppermute x66, waiting for transfers between devices, swap(): return lax.ppermute(value, axis, [(i, i ^ bit) for i in range(length)])  82.2 us
    ppermute x52, starting transfers between devices, ring(): lax.ppermute(value, axis, [(i, (i + by) % length) for i in range(length)])  77.9 us
    ppermute x66, starting transfers between devices, swap(): return lax.ppermute(value, axis, [(i, i ^ bit) for i in range(length)])  44.6 us
  transfers between devices with their start and end apart: 118, of which 41 were waited for; matrix products, arithmetic and copies ran while one was open for 17% of the time, Pallas kernels for 35%

profile of v6, /device:TPU:0, one launch (start us, length us, event | category | flops | bytes accessed | tf_op | source)
XLA Modules:
  0.0 810.4 jit_solution(8466788845725126622)
XLA Ops:
  27.9 3.8 collective-permute-start.7
  41.4 4.1 collective-permute-done.4
  45.5 4.9 collective-permute-done.5
  60.2 4.8 collective-permute-done.18
  67.1 3.5 collective-permute-start.27
  78.0 4.0 collective-permute-done.27
  85.5 3.5 collective-permute-done.25
  95.2 6.4 norm_qkv.4
  101.6 6.4 norm_qkv.5
  112.8 17.2 %attend.2 = (bf16[1024,512]{1,0:T(8,128)(2,1)}, f32[4,8,1024]{2,1,0:T(8,128)}) custom-call(bf16[1024,1536]{1,0:T(8,128)(2,1)} %get-tuple-element.252.refs_0_.refs_1_.refs_2_, bf16[1024,1536]{1,0:T(8,128)(2,1)} %get-tuple-element.252.refs_0_.refs_1_.refs_2_, bf16[1024,1536]{1,0:T(8,128)(2,1)} %get-tuple-element.252.refs_0_.refs_1_.refs_2_), custom_call_target="tpu_custom_call" | custom-call | flops 19000000512 | bytes 1048576 | tf_op jit(solution)/shard_map/attend/pallas_call | solution.py:536
  136.9 13.8 %collective-permute-done.31 = bf16[256,1024]{1,0:T(8,128)(2,1)S(1)} collective-permute-done((bf16[256,1024]{1,0:T(8,128)(2,1)S(1)}, bf16[256,1024]{1,0:T(8,128)(2,1)S(1)}, u32[]{:S(2)}, u32[]{:S(2)}) %collective-permute-start.31) | collective-permute-done | bytes 524320 | tf_op jit(solution)/shard_map/ppermute | solution.py:412
  162.1 16.4 %mlp_out.4 = (bf16[1024,2048]{1,0:T(8,128)(2,1)}, bf16[1024,2048]{1,0:T(8,128)(2,1)}, bf16[512,1024]{1,0:T(8,128)(2,1)}) custom-call(bf16[1024,512]{1,0:T(8,128)(2,1)} %get-tuple-element.269.refs_0_.refs_4_, bf16[1024,1024]{1,0:T(8,128)(2,1)} %get-tuple-element.358.refs_1_.refs_0_, f32[1,2048]{1,0:T(1,128)} %bitcast.476, ...), custom_call_target="tpu_custom_call" | custom-call | flops 16000000000 | bytes 1048576 | tf_op jit(solution)/shard_map/mlp_out/pallas_call | solution.py:536
  179.3 3.8 collective-permute-start.44
  186.2 16.4 %mlp_out.5 = (bf16[1024,2048]{1,0:T(8,128)(2,1)}, bf16[1024,2048]{1,0:T(8,128)(2,1)}, bf16[512,1024]{1,0:T(8,128)(2,1)}) custom-call(bf16[1024,512]{1,0:T(8,128)(2,1)} %get-tuple-element.269.refs_0_.refs_4_, bf16[1024,1024]{1,0:T(8,128)(2,1)} %get-tuple-element.358.refs_1_.refs_0_, ...), custom_call_target="tpu_custom_call", output_to_operand_aliasing={{0}: (27, {}), {1}: (28, {})} | custom-call | flops 16000000000 | bytes 1048576 | tf_op jit(solution)/shard_map/mlp_out/pallas_call | solution.py:536
  202.6 3.8 collective-permute-done.42
  206.5 4.4 collective-permute-done.41
  214.4 5.4 collective-permute-done.47
  236.0 4.7 add_convert_fusion.9
  244.1 6.4 norm_qkv.6
  250.5 6.3 norm_qkv.7
  260.5 17.2 %attend.3 = (bf16[1024,512]{1,0:T(8,128)(2,1)}, f32[4,8,1024]{2,1,0:T(8,128)}) custom-call(bf16[1024,1536]{1,0:T(8,128)(2,1)} %get-tuple-element.294.refs_0_.refs_1_.refs_2_, bf16[1024,1536]{1,0:T(8,128)(2,1)} %get-tuple-element.294.refs_0_.refs_1_.refs_2_, bf16[1024,1536]{1,0:T(8,128)(2,1)} %get-tuple-element.294.refs_0_.refs_1_.refs_2_), custom_call_target="tpu_custom_call" | custom-call | flops 19000000512 | bytes 1048576 | tf_op jit(solution)/shard_map/attend/pallas_call | solution.py:536
  277.9 3.9 collective-permute-done.56
  291.3 16.5 %mlp_out.6 = (bf16[1024,2048]{1,0:T(8,128)(2,1)}, bf16[1024,2048]{1,0:T(8,128)(2,1)}, bf16[512,1024]{1,0:T(8,128)(2,1)}) custom-call(bf16[1024,512]{1,0:T(8,128)(2,1)} %get-tuple-element.306.refs_0_.refs_3_, bf16[1024,1024]{1,0:T(8,128)(2,1)} %get-tuple-element.329.refs_1_.refs_0_, f32[1,2048]{1,0:T(1,128)} %bitcast.474, ...), custom_call_target="tpu_custom_call" | custom-call | flops 16000000000 | bytes 1048576 | tf_op jit(solution)/shard_map/mlp_out/pallas_call | solution.py:536
  313.5 3.9 collective-permute-done.64
  319.4 16.5 %mlp_out.7 = (bf16[1024,2048]{1,0:T(8,128)(2,1)}, bf16[1024,2048]{1,0:T(8,128)(2,1)}, bf16[512,1024]{1,0:T(8,128)(2,1)}) custom-call(bf16[1024,512]{1,0:T(8,128)(2,1)} %get-tuple-element.306.refs_0_.refs_3_, bf16[1024,1024]{1,0:T(8,128)(2,1)} %get-tuple-element.329.refs_1_.refs_0_, ...), custom_call_target="tpu_custom_call", output_to_operand_aliasing={{0}: (27, {}), {1}: (28, {})} | custom-call | flops 16000000000 | bytes 1048576 | tf_op jit(solution)/shard_map/mlp_out/pallas_call | solution.py:536
  335.8 7.8 collective-permute-done.66
  346.9 7.6 mlp_back.4
  354.5 7.6 mlp_back.5
  362.1 8.2 %collective-permute-done.67 = bf16[512,1024]{1,0:T(8,128)(2,1)S(1)} collective-permute-done((bf16[512,1024]{1,0:T(8,128)(2,1)S(1)}, bf16[512,1024]{1,0:T(8,128)(2,1)S(1)}, u32[]{:S(2)}, u32[]{:S(2)}) %collective-permute-start.67) | collective-permute-done | bytes 1048608 | tf_op jit(solution)/shard_map/ppermute | solution.py:412
  371.3 26.1 %attend_back.2 = (bf16[1024,1536]{1,0:T(8,128)(2,1)}, f32[1,1536]{1,0:T(1,128)}) custom-call(bf16[1024,1536]{1,0:T(8,128)(2,1)} %get-tuple-element.294.refs_0_.refs_1_.refs_2_, bf16[1024,1536]{1,0:T(8,128)(2,1)} %get-tuple-element.294.refs_0_.refs_1_.refs_2_, bf16[1024,1536]{1,0:T(8,128)(2,1)} %get-tuple-element.294.refs_0_.refs_1_.refs_2_, ...), custom_call_target="tpu_custom_call" | custom-call | flops 25999998976 | bytes 1048576 | tf_op jit(solution)/shard_map/attend_back/pallas_call | solution.py:536
  397.4 3.4 add_convert_fusion.7
  403.7 10.6 %norm_back.4 = (bf16[512,1024]{1,0:T(8,128)(2,1)}, f32[8,1024]{1,0:T(8,128)}) custom-call(bf16[512,1024]{1,0:T(8,128)(2,1)} %get-tuple-element.284.refs_0_, bf16[1024,1536]{1,0:T(8,128)(2,1)} %get-tuple-element.327.refs_1_.refs_2_, bf16[1024,2048]{1,0:T(8,128)(2,1)} %get-tuple-element.319.refs_2_, f32[8,1024]{1,0:T(8,128)} %concatenate.218.refs_1_.refs_3_, ...), custom_call_target="tpu_custom_call" | custom-call | flops 10499999744 | bytes 1048576 | tf_op jit(solution)/shard_map/norm_back/pallas_call | solution.py:536
  419.2 14.9 %weight_grad.4 = (bf16[2,4,256,1024]{3,2,1,0:T(8,128)(2,1)}, bf16[2,4,256,1024]{3,2,1,0:T(8,128)(2,1)}) custom-call(bf16[1024,1024]{1,0:T(8,128)(2,1)} %get-tuple-element.329.refs_1_.refs_0_, bf16[1024,1024]{1,0:T(8,128)(2,1)} %pad_maximum_fusion.1.refs_0_.refs_1_, bf16[1024,2048]{1,0:T(8,128)(2,1)} %get-tuple-element.319.refs_2_, ...), custom_call_target="tpu_custom_call" | custom-call | flops 14000000000 | bytes 1048576 | tf_op jit(solution)/shard_map/weight_grad/pallas_call | solution.py:536
  434.1 10.7 %norm_back.5 = (bf16[512,1024]{1,0:T(8,128)(2,1)}, f32[8,1024]{1,0:T(8,128)}) custom-call(bf16[512,1024]{1,0:T(8,128)(2,1)} %get-tuple-element.479.refs_0_, bf16[1024,1536]{1,0:T(8,128)(2,1)} %get-tuple-element.327.refs_1_.refs_2_, bf16[1024,2048]{1,0:T(8,128)(2,1)} %get-tuple-element.319.refs_2_, f32[8,1024]{1,0:T(8,128)} %concatenate.218.refs_1_.refs_3_, ...), custom_call_target="tpu_custom_call" | custom-call | flops 10499999744 | bytes 1048576 | tf_op jit(solution)/shard_map/norm_back/pallas_call | solution.py:536
  463.6 12.1 %weight_grad.5 = (bf16[2,4,256,512]{3,2,1,0:T(8,128)(2,1)}, bf16[2,4,256,512]{3,2,1,0:T(8,128)(2,1)}) custom-call(bf16[1024,1024]{1,0:T(8,128)(2,1)} %get-tuple-element.335.refs_0_, bf16[1024,1024]{1,0:T(8,128)(2,1)} %pad_maximum_fusion.1.refs_0_.refs_1_, bf16[1024,1536]{1,0:T(8,128)(2,1)} %get-tuple-element.327.refs_1_.refs_2_, ...), custom_call_target="tpu_custom_call" | custom-call | flops 14000000000 | bytes 1048576 | tf_op jit(solution)/shard_map/weight_grad/pallas_call | solution.py:536
  476.4 4.6 collective-permute-done.74
  481.9 6.0 collective-permute-done.72
  487.9 3.5 collective-permute-start.81
  491.4 4.2 collective-permute-start.79
  498.5 4.7 add_convert_fusion.4
  503.2 7.5 mlp_back.6
  510.8 7.6 mlp_back.7
  518.5 3.3 slice_bitcast_fusion.15
  521.9 4.3 collective-permute-done.78
  529.2 15.0 %weight_grad.6 = (bf16[2,4,256,1024]{3,2,1,0:T(8,128)(2,1)}, bf16[2,4,256,1024]{3,2,1,0:T(8,128)(2,1)}) custom-call(bf16[1024,1024]{1,0:T(8,128)(2,1)} %get-tuple-element.358.refs_1_.refs_0_, bf16[512,1024]{1,0:T(8,128)(2,1)} %get-tuple-element.345.refs_0_.refs_1_, bf16[512,1024]{1,0:T(8,128)(2,1)} %get-tuple-element.497.refs_0_.refs_2_, ...), custom_call_target="tpu_custom_call" | custom-call | flops 14000000000 | bytes 1048576 | tf_op jit(solution)/shard_map/weight_grad/pallas_call | solution.py:536
  544.2 8.7 %collective-permute-done.82 = bf16[2,256,1024]{2,1,0:T(8,128)(2,1)} collective-permute-done((bf16[2,256,1024]{2,1,0:T(8,128)(2,1)S(1)}, bf16[2,256,1024]{2,1,0:T(8,128)(2,1)}, u32[]{:S(2)}, u32[]{:S(2)}) %collective-permute-start.82) | collective-permute-done | bytes 1048608 | tf_op jit(solution)/shard_map/ppermute | solution.py:412
  564.5 25.8 %attend_back.3 = (bf16[1024,1536]{1,0:T(8,128)(2,1)}, f32[1,1536]{1,0:T(1,128)}) custom-call(bf16[1024,1536]{1,0:T(8,128)(2,1)} %get-tuple-element.252.refs_0_.refs_1_.refs_2_, bf16[1024,1536]{1,0:T(8,128)(2,1)} %get-tuple-element.252.refs_0_.refs_1_.refs_2_, bf16[1024,1536]{1,0:T(8,128)(2,1)} %get-tuple-element.252.refs_0_.refs_1_.refs_2_, ...), custom_call_target="tpu_custom_call" | custom-call | flops 25999998976 | bytes 1048576 | tf_op jit(solution)/shard_map/attend_back/pallas_call | solution.py:536
  591.2 10.7 %norm_back.6 = (bf16[512,1024]{1,0:T(8,128)(2,1)}, f32[8,1024]{1,0:T(8,128)}) custom-call(bf16[1024,1024]{1,0:T(8,128)(2,1)} %pad_maximum_fusion.refs_0_, bf16[1024,1536]{1,0:T(8,128)(2,1)} %get-tuple-element.376.refs_1_.refs_3_, bf16[1024,2048]{1,0:T(8,128)(2,1)} %get-tuple-element.348.refs_3_.refs_2_, f32[8,1024]{1,0:T(8,128)} %concatenate.212.refs_1_.refs_3_, ...), custom_call_target="tpu_custom_call" | custom-call | flops 10499999744 | bytes 1048576 | tf_op jit(solution)/shard_map/norm_back/pallas_call | solution.py:536
  613.9 10.6 %norm_back.7 = (bf16[512,1024]{1,0:T(8,128)(2,1)}, f32[8,1024]{1,0:T(8,128)}) custom-call(bf16[1024,1024]{1,0:T(8,128)(2,1)} %pad_maximum_fusion.refs_0_, bf16[1024,1536]{1,0:T(8,128)(2,1)} %get-tuple-element.376.refs_1_.refs_3_, bf16[1024,2048]{1,0:T(8,128)(2,1)} %get-tuple-element.348.refs_3_.refs_2_, f32[8,1024]{1,0:T(8,128)} %concatenate.212.refs_1_.refs_3_, ...), custom_call_target="tpu_custom_call" | custom-call | flops 10499999744 | bytes 1048576 | tf_op jit(solution)/shard_map/norm_back/pallas_call | solution.py:536
  626.1 3.5 slice_bitcast_fusion.11
  630.5 4.5 collective-permute-done.87
  635.0 3.5 collective-permute-start.94
  642.3 12.1 %weight_grad.7 = (bf16[2,4,256,512]{3,2,1,0:T(8,128)(2,1)}, bf16[2,4,256,512]{3,2,1,0:T(8,128)(2,1)}) custom-call(bf16[1024,1024]{1,0:T(8,128)(2,1)} %get-tuple-element.382.refs_0_, bf16[512,1024]{1,0:T(8,128)(2,1)} %get-tuple-element.345.refs_0_.refs_1_, bf16[512,1024]{1,0:T(8,128)(2,1)} %get-tuple-element.497.refs_0_.refs_2_, ...), custom_call_target="tpu_custom_call" | custom-call | flops 14000000000 | bytes 1048576 | tf_op jit(solution)/shard_map/weight_grad/pallas_call | solution.py:536
  654.4 3.1 slice_bitcast_fusion.12
  660.0 3.8 collective-permute-done.92
  679.4 3.6 collective-permute-start.96
  684.0 11.1 %collective-permute-done.95 = bf16[128,1024]{1,0:T(8,128)(2,1)S(1)} collective-permute-done((bf16[128,1024]{1,0:T(8,128)(2,1)S(1)}, bf16[128,1024]{1,0:T(8,128)(2,1)S(1)}, u32[]{:S(2)}, u32[]{:S(2)}) %collective-permute-start.95) | collective-permute-done | bytes 262176 | tf_op jit(solution)/shard_map/ppermute | solution.py:407
  700.9 3.7 collective-permute-start.100
  710.6 20.6 %collective-permute-done.100 = bf16[256,1024]{1,0:T(8,128)(2,1)S(1)} collective-permute-done((bf16[256,1024]{1,0:T(8,128)(2,1)S(1)}, bf16[256,1024]{1,0:T(8,128)(2,1)S(1)}, u32[]{:S(2)}, u32[]{:S(2)}) %collective-permute-start.100) | collective-permute-done | bytes 524320 | tf_op jit(solution)/shard_map/ppermute | solution.py:407
  733.3 3.6 collective-permute-start.106
  739.7 5.6 collective-permute-done.105
  753.9 4.4 collective-permute-done.111
  763.0 27.4 %collective-permute-done.109 = bf16[384,1024]{1,0:T(8,128)(2,1)} collective-permute-done((bf16[384,1024]{1,0:T(8,128)(2,1)}, bf16[384,1024]{1,0:T(8,128)(2,1)}, u32[]{:S(2)}, u32[]{:S(2)}) %collective-permute-start.109) | collective-permute-done | bytes 786464 | tf_op jit(solution)/shard_map/ppermute | solution.py:407
  793.8 3.5 collective-permute-start.114
  (708 shorter events, 261.1 us)
Async XLA Ops:
  4.0 23.8 %collective-permute-start = (bf16[384,512]{1,0:T(8,128)(2,1)}, bf16[384,512]{1,0:T(8,128)(2,1)}, u32[]{:S(2)}, u32[]{:S(2)}) collective-permute-start(bf16[384,512]{1,0:T(8,128)(2,1)} %pad_maximum_fusion.27), channel_id=1, source_target_pairs={{0,1},{1,2},{2,3},{3,0},{4,5},{5,6},{6,7},{7,4},{8,9},{9,10},{10,1... | collective-permute-start | bytes 1179656 | tf_op jit(solution)/shard_map/ppermute | solution.py:407
  7.9 20.0 %collective-permute-start.1 = (bf16[384,512]{1,0:T(8,128)(2,1)}, bf16[384,512]{1,0:T(8,128)(2,1)}, u32[]{:S(2)}, u32[]{:S(2)}) collective-permute-start(bf16[384,512]{1,0:T(8,128)(2,1)} %pad_maximum_fusion.28), channel_id=1, source_target_pairs={{0,3},{1,0},{2,1},{3,2},{4,7},{5,4},{6,5},{7,6},{8,11},{9,8},{10,9... | collective-permute-start | bytes 1179656 | tf_op jit(solution)/shard_map/ppermute | solution.py:407
  27.9 23.3 %collective-permute-start.6 = (bf16[256,512]{1,0:T(8,128)(2,1)S(1)}, bf16[256,512]{1,0:T(8,128)(2,1)S(1)}, u32[]{:S(2)}, u32[]{:S(2)}) collective-permute-start(bf16[256,512]{1,0:T(8,128)(2,1)S(1)} %get-tuple-element.230), channel_id=1, source_target_pairs={{0,1},{1,2},{2,3},{3,0},{4,5},{5,6},{6,7},{7,4},{8,9},{9,10},{10,1... | collective-permute-start | bytes 786440 | tf_op jit(solution)/shard_map/ppermute | solution.py:407
  27.9 23.2 %collective-permute-start.7 = (bf16[256,512]{1,0:T(8,128)(2,1)S(1)}, bf16[256,512]{1,0:T(8,128)(2,1)S(1)}, u32[]{:S(2)}, u32[]{:S(2)}) collective-permute-start(bf16[256,512]{1,0:T(8,128)(2,1)S(1)} %get-tuple-element.230), channel_id=1, source_target_pairs={{0,3},{1,0},{2,1},{3,2},{4,7},{5,4},{6,5},{7,6},{8,11},{9,8},{10,9... | collective-permute-start | bytes 786440 | tf_op jit(solution)/shard_map/ppermute | solution.py:407
  32.8 18.5 %collective-permute-start.8 = (bf16[256,1024]{1,0:T(8,128)(2,1)S(1)}, bf16[256,1024]{1,0:T(8,128)(2,1)S(1)}, u32[]{:S(2)}, u32[]{:S(2)}) collective-permute-start(bf16[256,1024]{1,0:T(8,128)(2,1)S(1)} %copy-done.45), channel_id=1, source_target_pairs={{0,16},{16,0},{1,17},{17,1},{2,18},{18,2},{3,19},{19,3},{4,20},{20... | collective-permute-start | bytes 1572872 | tf_op jit(solution)/shard_map/ppermute | solution.py:412
  65.0 24.8 %collective-permute-start.12 = (bf16[4,256,512]{2,1,0:T(8,128)(2,1)}, bf16[4,256,512]{2,1,0:T(8,128)(2,1)S(1)}, u32[]{:S(2)}, u32[]{:S(2)}) collective-permute-start(bf16[4,256,512]{2,1,0:T(8,128)(2,1)} %fusion.51), channel_id=1, source_target_pairs={{0,16},{16,0},{1,17},{17,1},{2,18},{18,2},{3,19},{19,3},{4,20},{20... | collective-permute-start | bytes 3145736 | tf_op jit(solution)/shard_map/ppermute | solution.py:412
  89.8 18.2 %collective-permute-start.24 = (bf16[256,1024]{1,0:T(8,128)(2,1)S(1)}, bf16[256,1024]{1,0:T(8,128)(2,1)}, u32[]{:S(2)}, u32[]{:S(2)}) collective-permute-start(bf16[256,1024]{1,0:T(8,128)(2,1)S(1)} %get-tuple-element.251), channel_id=1, source_target_pairs={{0,8},{4,12},{8,0},{12,4},{1,9},{5,13},{9,1},{13,5},{2,10},{6,14},... | collective-permute-start | bytes 1572872 | tf_op jit(solution)/shard_map/ppermute | solution.py:412
  108.0 23.2 %collective-permute-start.30 = (bf16[256,1024]{1,0:T(8,128)(2,1)S(1)}, bf16[256,1024]{1,0:T(8,128)(2,1)}, u32[]{:S(2)}, u32[]{:S(2)}) collective-permute-start(bf16[256,1024]{1,0:T(8,128)(2,1)S(1)} %collective-permute-done.27), channel_id=1, source_target_pairs={{0,8},{4,12},{8,0},{12,4},{1,9},{5,13},{9,1},{13,5},{2,10},{6,14},... | collective-permute-start | bytes 1572872 | tf_op jit(solution)/shard_map/ppermute | solution.py:412
  108.6 24.1 %collective-permute-start.28 = (bf16[128,1024]{1,0:T(8,128)(2,1)S(1)}, bf16[128,1024]{1,0:T(8,128)(2,1)}, u32[]{:S(2)}, u32[]{:S(2)}) collective-permute-start(bf16[128,1024]{1,0:T(8,128)(2,1)S(1)} %slice.800), channel_id=1, source_target_pairs={{0,3},{1,0},{2,1},{3,2},{4,7},{5,4},{6,5},{7,6},{8,11},{9,8},{10,9... | collective-permute-start | bytes 786440 | tf_op jit(solution)/shard_map/ppermute | solution.py:407
  111.4 21.4 %collective-permute-start.26 = (bf16[128,1024]{1,0:T(8,128)(2,1)}, bf16[128,1024]{1,0:T(8,128)(2,1)}, u32[]{:S(2)}, u32[]{:S(2)}) collective-permute-start(bf16[128,1024]{1,0:T(8,128)(2,1)} %slice.799), channel_id=1, source_target_pairs={{0,1},{1,2},{2,3},{3,0},{4,5},{5,6},{6,7},{7,4},{8,9},{9,10},{10,1... | collective-permute-start | bytes 786440 | tf_op jit(solution)/shard_map/ppermute | solution.py:407
  111.4 22.3 %collective-permute-start.29 = (bf16[256,1024]{1,0:T(8,128)(2,1)S(1)}, bf16[256,1024]{1,0:T(8,128)(2,1)S(1)}, u32[]{:S(2)}, u32[]{:S(2)}) collective-permute-start(bf16[256,1024]{1,0:T(8,128)(2,1)S(1)} %collective-permute-done.25), channel_id=1, source_target_pairs={{0,8},{4,12},{8,0},{12,4},{1,9},{5,13},{9,1},{13,5},{2,10},{6,14},... | collective-permute-start | bytes 1572872 | tf_op jit(solution)/shard_map/ppermute | solution.py:412
  133.6 17.2 %collective-permute-start.34 = (bf16[2,256,1024]{2,1,0:T(8,128)(2,1)S(1)}, bf16[2,256,1024]{2,1,0:T(8,128)(2,1)S(1)}, u32[]{:S(2)}, u32[]{:S(2)}) collective-permute-start(bf16[2,256,1024]{2,1,0:T(8,128)(2,1)S(1)} %pad_maximum_fusion.8.refs_13_.refs_21_.refs_12_.refs_14_), channel_id=1, source_target_pairs={{0,4},{4,0},{8,12},{12,8},{1,5},{5,1},{9,13},{13,9},{2,6},{6,2},{1... | collective-permute-start | bytes 3145736 | tf_op jit(solution)/shard_map/ppermute | solution.py:412
  133.8 17.1 %collective-permute-start.33 = (bf16[2,256,1024]{2,1,0:T(8,128)(2,1)S(1)}, bf16[2,256,1024]{2,1,0:T(8,128)(2,1)S(1)}, u32[]{:S(2)}, u32[]{:S(2)}) collective-permute-start(bf16[2,256,1024]{2,1,0:T(8,128)(2,1)S(1)} %pad_maximum_fusion.7.refs_12_.refs_20_.refs_11_.refs_13_), channel_id=1, source_target_pairs={{0,4},{4,0},{8,12},{12,8},{1,5},{5,1},{9,13},{13,9},{2,6},{6,2},{1... | collective-permute-start | bytes 3145736 | tf_op jit(solution)/shard_map/ppermute | solution.py:412
  134.3 16.6 %collective-permute-start.32 = (bf16[2,256,1024]{2,1,0:T(8,128)(2,1)S(1)}, bf16[2,256,1024]{2,1,0:T(8,128)(2,1)S(1)}, u32[]{:S(2)}, u32[]{:S(2)}) collective-permute-start(bf16[2,256,1024]{2,1,0:T(8,128)(2,1)S(1)} %pad_maximum_fusion.6.refs_11_.refs_19_.refs_10_.refs_12_), channel_id=1, source_target_pairs={{0,4},{4,0},{8,12},{12,8},{1,5},{5,1},{9,13},{13,9},{2,6},{6,2},{1... | collective-permute-start | bytes 3145736 | tf_op jit(solution)/shard_map/ppermute | solution.py:412
  156.0 22.6 %collective-permute-start.36 = (bf16[256,512]{1,0:T(8,128)(2,1)S(1)}, bf16[256,512]{1,0:T(8,128)(2,1)S(1)}, u32[]{:S(2)}, u32[]{:S(2)}) collective-permute-start(bf16[256,512]{1,0:T(8,128)(2,1)S(1)} %copy-done.27), channel_id=1, source_target_pairs={{0,1},{1,2},{2,3},{3,0},{4,5},{5,6},{6,7},{7,4},{8,9},{9,10},{10,1... | collective-permute-start | bytes 786440 | tf_op jit(solution)/shard_map/ppermute | solution.py:407
  157.1 21.5 %collective-permute-start.37 = (bf16[256,512]{1,0:T(8,128)(2,1)S(1)}, bf16[256,512]{1,0:T(8,128)(2,1)S(1)}, u32[]{:S(2)}, u32[]{:S(2)}) collective-permute-start(bf16[256,512]{1,0:T(8,128)(2,1)S(1)} %copy-done.27), channel_id=1, source_target_pairs={{0,3},{1,0},{2,1},{3,2},{4,7},{5,4},{6,5},{7,6},{8,11},{9,8},{10,9... | collective-permute-start | bytes 786440 | tf_op jit(solution)/shard_map/ppermute | solution.py:407
  160.1 19.2 %collective-permute-start.38 = (bf16[256,512]{1,0:T(8,128)(2,1)S(1)}, bf16[256,512]{1,0:T(8,128)(2,1)S(1)}, u32[]{:S(2)}, u32[]{:S(2)}) collective-permute-start(bf16[256,512]{1,0:T(8,128)(2,1)S(1)} %copy-done.27), channel_id=1, source_target_pairs={{0,8},{4,12},{8,0},{12,4},{1,9},{5,13},{9,1},{13,5},{2,10},{6,14},... | collective-permute-start | bytes 786440 | tf_op jit(solution)/shard_map/ppermute | solution.py:412
  160.6 18.7 %collective-permute-start.39 = (bf16[256,1024]{1,0:T(8,128)(2,1)S(1)}, bf16[256,1024]{1,0:T(8,128)(2,1)S(1)}, u32[]{:S(2)}, u32[]{:S(2)}) collective-permute-start(bf16[256,1024]{1,0:T(8,128)(2,1)S(1)} %get-tuple-element.275), channel_id=1, source_target_pairs={{0,8},{4,12},{8,0},{12,4},{1,9},{5,13},{9,1},{13,5},{2,10},{6,14},... | collective-permute-start | bytes 1572872 | tf_op jit(solution)/shard_map/ppermute | solution.py:412
  179.3 31.6 %collective-permute-start.43 = (bf16[256,1024]{1,0:T(8,128)(2,1)S(1)}, bf16[256,1024]{1,0:T(8,128)(2,1)S(1)}, u32[]{:S(2)}, u32[]{:S(2)}) collective-permute-start(bf16[256,1024]{1,0:T(8,128)(2,1)S(1)} %get-tuple-element.275), channel_id=1, source_target_pairs={{0,1},{1,2},{2,3},{3,0},{4,5},{5,6},{6,7},{7,4},{8,9},{9,10},{10,1... | collective-permute-start | bytes 1572872 | tf_op jit(solution)/shard_map/ppermute | solution.py:407
  179.3 31.5 %collective-permute-start.44 = (bf16[256,1024]{1,0:T(8,128)(2,1)S(1)}, bf16[256,1024]{1,0:T(8,128)(2,1)S(1)}, u32[]{:S(2)}, u32[]{:S(2)}) collective-permute-start(bf16[256,1024]{1,0:T(8,128)(2,1)S(1)} %get-tuple-element.275), channel_id=1, source_target_pairs={{0,3},{1,0},{2,1},{3,2},{4,7},{5,4},{6,5},{7,6},{8,11},{9,8},{10,9... | collective-permute-start | bytes 1572872 | tf_op jit(solution)/shard_map/ppermute | solution.py:407
  183.2 23.3 %collective-permute-start.42 = (bf16[128,512]{1,0:T(8,128)(2,1)S(1)}, bf16[128,512]{1,0:T(8,128)(2,1)S(1)}, u32[]{:S(2)}, u32[]{:S(2)}) collective-permute-start(bf16[128,512]{1,0:T(8,128)(2,1)S(1)} %slice.805), channel_id=1, source_target_pairs={{0,3},{1,0},{2,1},{3,2},{4,7},{5,4},{6,5},{7,6},{8,11},{9,8},{10,9... | collective-permute-start | bytes 393224 | tf_op jit(solution)/shard_map/ppermute | solution.py:407
  183.2 27.7 %collective-permute-start.41 = (bf16[128,512]{1,0:T(8,128)(2,1)}, bf16[128,512]{1,0:T(8,128)(2,1)S(1)}, u32[]{:S(2)}, u32[]{:S(2)}) collective-permute-start(bf16[128,512]{1,0:T(8,128)(2,1)} %slice.804), channel_id=1, source_target_pairs={{0,1},{1,2},{2,3},{3,0},{4,5},{5,6},{6,7},{7,4},{8,9},{9,10},{10,1... | collective-permute-start | bytes 393224 | tf_op jit(solution)/shard_map/ppermute | solution.py:407
  185.6 25.3 %collective-permute-start.40 = (bf16[512,1024]{1,0:T(8,128)(2,1)}, bf16[512,1024]{1,0:T(8,128)(2,1)S(1)}, u32[]{:S(2)}, u32[]{:S(2)}) collective-permute-start(bf16[512,1024]{1,0:T(8,128)(2,1)} %get-tuple-element.268), channel_id=1, source_target_pairs={{0,16},{16,0},{1,17},{17,1},{2,18},{18,2},{3,19},{19,3},{4,20},{20... | collective-permute-start | bytes 3145736 | tf_op jit(solution)/shard_map/ppermute | solution.py:412
  211.5 23.2 %collective-permute-start.45 = (bf16[512,1024]{1,0:T(8,128)(2,1)}, bf16[512,1024]{1,0:T(8,128)(2,1)}, u32[]{:S(2)}, u32[]{:S(2)}) collective-permute-start(bf16[512,1024]{1,0:T(8,128)(2,1)} %get-tuple-element.276), channel_id=1, source_target_pairs={{0,16},{16,0},{1,17},{17,1},{2,18},{18,2},{3,19},{19,3},{4,20},{20... | collective-permute-start | bytes 3145736 | tf_op jit(solution)/shard_map/ppermute | solution.py:412
  256.9 20.9 %collective-permute-start.57 = (bf16[256,1024]{1,0:T(8,128)(2,1)S(1)}, bf16[256,1024]{1,0:T(8,128)(2,1)S(1)}, u32[]{:S(2)}, u32[]{:S(2)}) collective-permute-start(bf16[256,1024]{1,0:T(8,128)(2,1)S(1)} %constant_dynamic-update-slice_fusion.6), channel_id=1, source_target_pairs={{0,8},{4,12},{8,0},{12,4},{1,9},{5,13},{9,1},{13,5},{2,10},{6,14},... | collective-permute-start | bytes 1572872 | tf_op jit(solution)/shard_map/ppermute | solution.py:412
  259.0 25.0 %collective-permute-start.59 = (bf16[2,256,1024]{2,1,0:T(8,128)(2,1)}, bf16[2,256,1024]{2,1,0:T(8,128)(2,1)}, u32[]{:S(2)}, u32[]{:S(2)}) collective-permute-start(bf16[2,256,1024]{2,1,0:T(8,128)(2,1)} %pad_maximum_fusion.11.refs_12_.refs_20_.refs_11_.refs_13_), channel_id=1, source_target_pairs={{0,4},{4,0},{8,12},{12,8},{1,5},{5,1},{9,13},{13,9},{2,6},{6,2},{1... | collective-permute-start | bytes 3145736 | tf_op jit(solution)/shard_map/ppermute | solution.py:412
  259.0 25.0 %collective-permute-start.58 = (bf16[2,256,1024]{2,1,0:T(8,128)(2,1)S(1)}, bf16[2,256,1024]{2,1,0:T(8,128)(2,1)}, u32[]{:S(2)}, u32[]{:S(2)}) collective-permute-start(bf16[2,256,1024]{2,1,0:T(8,128)(2,1)S(1)} %pad_maximum_fusion.10.refs_11_.refs_19_.refs_10_.refs_12_), channel_id=1, source_target_pairs={{0,4},{4,0},{8,12},{12,8},{1,5},{5,1},{9,13},{13,9},{2,6},{6,2},{1... | collective-permute-start | bytes 3145736 | tf_op jit(solution)/shard_map/ppermute | solution.py:412
  259.5 22.3 %collective-permute-start.56 = (bf16[256,1024]{1,0:T(8,128)(2,1)S(1)}, bf16[256,1024]{1,0:T(8,128)(2,1)}, u32[]{:S(2)}, u32[]{:S(2)}) collective-permute-start(bf16[256,1024]{1,0:T(8,128)(2,1)S(1)} %collective-permute-done.44), channel_id=1, source_target_pairs={{0,8},{4,12},{8,0},{12,4},{1,9},{5,13},{9,1},{13,5},{2,10},{6,14},... | collective-permute-start | bytes 1572872 | tf_op jit(solution)/shard_map/ppermute | solution.py:412
  288.4 20.7 %collective-permute-start.63 = (bf16[384,512]{1,0:T(8,128)(2,1)S(1)}, bf16[384,512]{1,0:T(8,128)(2,1)S(1)}, u32[]{:S(2)}, u32[]{:S(2)}) collective-permute-start(bf16[384,512]{1,0:T(8,128)(2,1)S(1)} %pad_maximum_fusion.30), channel_id=1, source_target_pairs={{0,3},{1,0},{2,1},{3,2},{4,7},{5,4},{6,5},{7,6},{8,11},{9,8},{10,9... | collective-permute-start | bytes 1179656 | tf_op jit(solution)/shard_map/ppermute | solution.py:407
  291.3 17.8 %collective-permute-start.62 = (bf16[384,512]{1,0:T(8,128)(2,1)S(1)}, bf16[384,512]{1,0:T(8,128)(2,1)S(1)}, u32[]{:S(2)}, u32[]{:S(2)}) collective-permute-start(bf16[384,512]{1,0:T(8,128)(2,1)S(1)} %pad_maximum_fusion.29), channel_id=1, source_target_pairs={{0,1},{1,2},{2,3},{3,0},{4,5},{5,6},{6,7},{7,4},{8,9},{9,10},{10,1... | collective-permute-start | bytes 1179656 | tf_op jit(solution)/shard_map/ppermute | solution.py:407
  318.7 24.9 %collective-permute-start.66 = (bf16[4,256,512]{2,1,0:T(8,128)(2,1)S(1)}, bf16[4,256,512]{2,1,0:T(8,128)(2,1)S(1)}, u32[]{:S(2)}, u32[]{:S(2)}) collective-permute-start(bf16[4,256,512]{2,1,0:T(8,128)(2,1)S(1)} %fusion.52), channel_id=1, source_target_pairs={{0,16},{16,0},{1,17},{17,1},{2,18},{18,2},{3,19},{19,3},{4,20},{20... | collective-permute-start | bytes 3145736 | tf_op jit(solution)/shard_map/ppermute | solution.py:412
  346.3 24.0 %collective-permute-start.67 = (bf16[512,1024]{1,0:T(8,128)(2,1)S(1)}, bf16[512,1024]{1,0:T(8,128)(2,1)S(1)}, u32[]{:S(2)}, u32[]{:S(2)}) collective-permute-start(bf16[512,1024]{1,0:T(8,128)(2,1)S(1)} %copy-done.34), channel_id=1, source_target_pairs={{0,16},{16,0},{1,17},{17,1},{2,18},{18,2},{3,19},{19,3},{4,20},{20... | collective-permute-start | bytes 3145736 | tf_op jit(solution)/shard_map/ppermute | solution.py:412
  370.3 27.1 %collective-permute-start.68 = (bf16[512,1024]{1,0:T(8,128)(2,1)}, bf16[512,1024]{1,0:T(8,128)(2,1)}, u32[]{:S(2)}, u32[]{:S(2)}) collective-permute-start(bf16[512,1024]{1,0:T(8,128)(2,1)} %get-tuple-element.324), channel_id=1, source_target_pairs={{0,16},{16,0},{1,17},{17,1},{2,18},{18,2},{3,19},{19,3},{4,20},{20... | collective-permute-start | bytes 3145736 | tf_op jit(solution)/shard_map/ppermute | solution.py:412
  415.2 29.6 %collective-permute-start.71 = (bf16[384,512]{1,0:T(8,128)(2,1)}, bf16[384,512]{1,0:T(8,128)(2,1)S(1)}, u32[]{:S(2)}, u32[]{:S(2)}) collective-permute-start(bf16[384,512]{1,0:T(8,128)(2,1)} %pad_maximum_fusion.32), channel_id=1, source_target_pairs={{0,3},{1,0},{2,1},{3,2},{4,7},{5,4},{6,5},{7,6},{8,11},{9,8},{10,9... | collective-permute-start | bytes 1179656 | tf_op jit(solution)/shard_map/ppermute | solution.py:407
  416.3 28.5 %collective-permute-start.70 = (bf16[384,512]{1,0:T(8,128)(2,1)}, bf16[384,512]{1,0:T(8,128)(2,1)S(1)}, u32[]{:S(2)}, u32[]{:S(2)}) collective-permute-start(bf16[384,512]{1,0:T(8,128)(2,1)} %pad_maximum_fusion.31), channel_id=1, source_target_pairs={{0,1},{1,2},{2,3},{3,0},{4,5},{5,6},{6,7},{7,4},{8,9},{9,10},{10,1... | collective-permute-start | bytes 1179656 | tf_op jit(solution)/shard_map/ppermute | solution.py:407
  418.1 26.7 %collective-permute-start.69 = (bf16[512,1024]{1,0:T(8,128)(2,1)}, bf16[512,1024]{1,0:T(8,128)(2,1)S(1)}, u32[]{:S(2)}, u32[]{:S(2)}) collective-permute-start(bf16[512,1024]{1,0:T(8,128)(2,1)} %get-tuple-element.344), channel_id=1, source_target_pairs={{0,16},{16,0},{1,17},{17,1},{2,18},{18,2},{3,19},{19,3},{4,20},{20... | collective-permute-start | bytes 3145736 | tf_op jit(solution)/shard_map/ppermute | solution.py:412
  445.6 42.3 %collective-permute-start.73 = (bf16[2,4,256,1024]{3,2,1,0:T(8,128)(2,1)}, bf16[2,4,256,1024]{3,2,1,0:T(8,128)(2,1)}, u32[]{:S(2)}, u32[]{:S(2)}) collective-permute-start(bf16[2,4,256,1024]{3,2,1,0:T(8,128)(2,1)} %get-tuple-element.339), channel_id=1, source_target_pairs={{0,4},{4,0},{8,12},{12,8},{1,5},{5,1},{9,13},{13,9},{2,6},{6,2},{1... | collective-permute-start | bytes 12582920 | tf_op jit(solution)/shard_map/ppermute | solution.py:412
  462.5 18.5 %collective-permute-start.74 = (bf16[384,512]{1,0:T(8,128)(2,1)}, bf16[384,512]{1,0:T(8,128)(2,1)}, u32[]{:S(2)}, u32[]{:S(2)}) collective-permute-start(bf16[384,512]{1,0:T(8,128)(2,1)} %pad_maximum_fusion.33), channel_id=1, source_target_pairs={{0,1},{1,2},{2,3},{3,0},{4,5},{5,6},{6,7},{7,4},{8,9},{9,10},{10,1... | collective-permute-start | bytes 1179656 | tf_op jit(solution)/shard_map/ppermute | solution.py:407
  462.6 25.3 %collective-permute-start.72 = (bf16[512,1024]{1,0:T(8,128)(2,1)S(1)}, bf16[512,1024]{1,0:T(8,128)(2,1)}, u32[]{:S(2)}, u32[]{:S(2)}) collective-permute-start(bf16[512,1024]{1,0:T(8,128)(2,1)S(1)} %copy-done.30), channel_id=1, source_target_pairs={{0,16},{16,0},{1,17},{17,1},{2,18},{18,2},{3,19},{19,3},{4,20},{20... | collective-permute-start | bytes 3145736 | tf_op jit(solution)/shard_map/ppermute | solution.py:412
  487.9 30.5 %collective-permute-start.81 = (bf16[128,512]{1,0:T(8,128)(2,1)}, bf16[128,512]{1,0:T(8,128)(2,1)S(1)}, u32[]{:S(2)}, u32[]{:S(2)}) collective-permute-start(bf16[128,512]{1,0:T(8,128)(2,1)} %slice.825), channel_id=1, source_target_pairs={{0,3},{1,0},{2,1},{3,2},{4,7},{5,4},{6,5},{7,6},{8,11},{9,8},{10,9... | collective-permute-start | bytes 393224 | tf_op jit(solution)/shard_map/ppermute | solution.py:407
  491.4 30.4 %collective-permute-start.80 = (bf16[128,512]{1,0:T(8,128)(2,1)S(1)}, bf16[128,512]{1,0:T(8,128)(2,1)S(1)}, u32[]{:S(2)}, u32[]{:S(2)}) collective-permute-start(bf16[128,512]{1,0:T(8,128)(2,1)S(1)} %slice.824), channel_id=1, source_target_pairs={{0,1},{1,2},{2,3},{3,0},{4,5},{5,6},{6,7},{7,4},{8,9},{9,10},{10,1... | collective-permute-start | bytes 393224 | tf_op jit(solution)/shard_map/ppermute | solution.py:407
  491.4 30.4 %collective-permute-start.79 = (bf16[128,512]{1,0:T(8,128)(2,1)}, bf16[128,512]{1,0:T(8,128)(2,1)S(1)}, u32[]{:S(2)}, u32[]{:S(2)}) collective-permute-start(bf16[128,512]{1,0:T(8,128)(2,1)} %slice.823), channel_id=1, source_target_pairs={{0,3},{1,0},{2,1},{3,2},{4,7},{5,4},{6,5},{7,6},{8,11},{9,8},{10,9... | collective-permute-start | bytes 393224 | tf_op jit(solution)/shard_map/ppermute | solution.py:407
  497.6 28.6 %collective-permute-start.77 = (bf16[2,256,1024]{2,1,0:T(8,128)(2,1)S(1)}, bf16[2,256,1024]{2,1,0:T(8,128)(2,1)}, u32[]{:S(2)}, u32[]{:S(2)}) collective-permute-start(bf16[2,256,1024]{2,1,0:T(8,128)(2,1)S(1)} %fusion.16), channel_id=1, source_target_pairs={{0,8},{4,12},{8,0},{12,4},{1,9},{5,13},{9,1},{13,5},{2,10},{6,14},... | collective-permute-start | bytes 3145736 | tf_op jit(solution)/shard_map/ppermute | solution.py:412
  498.5 27.7 %collective-permute-start.76 = (bf16[2,4,256,512]{3,2,1,0:T(8,128)(2,1)}, bf16[2,4,256,512]{3,2,1,0:T(8,128)(2,1)}, u32[]{:S(2)}, u32[]{:S(2)}) collective-permute-start(bf16[2,4,256,512]{3,2,1,0:T(8,128)(2,1)} %get-tuple-element.351), channel_id=1, source_target_pairs={{0,4},{4,0},{8,12},{12,8},{1,5},{5,1},{9,13},{13,9},{2,6},{6,2},{1... | collective-permute-start | bytes 6291464 | tf_op jit(solution)/shard_map/ppermute | solution.py:412
  527.9 25.0 %collective-permute-start.82 = (bf16[2,256,1024]{2,1,0:T(8,128)(2,1)S(1)}, bf16[2,256,1024]{2,1,0:T(8,128)(2,1)}, u32[]{:S(2)}, u32[]{:S(2)}) collective-permute-start(bf16[2,256,1024]{2,1,0:T(8,128)(2,1)S(1)} %fusion.15), channel_id=1, source_target_pairs={{0,8},{4,12},{8,0},{12,4},{1,9},{5,13},{9,1},{13,5},{2,10},{6,14},... | collective-permute-start | bytes 3145736 | tf_op jit(solution)/shard_map/ppermute | solution.py:412
  552.9 38.4 %collective-permute-start.85 = (bf16[2,4,256,1024]{3,2,1,0:T(8,128)(2,1)}, bf16[2,4,256,1024]{3,2,1,0:T(8,128)(2,1)}, u32[]{:S(2)}, u32[]{:S(2)}) collective-permute-start(bf16[2,4,256,1024]{3,2,1,0:T(8,128)(2,1)} %get-tuple-element.370), channel_id=1, source_target_pairs={{0,4},{4,0},{8,12},{12,8},{1,5},{5,1},{9,13},{13,9},{2,6},{6,2},{1... | collective-permute-start | bytes 12582920 | tf_op jit(solution)/shard_map/ppermute | solution.py:412
  558.8 32.4 %collective-permute-start.86 = (bf16[4,256,512]{2,1,0:T(8,128)(2,1)}, bf16[4,256,512]{2,1,0:T(8,128)(2,1)}, u32[]{:S(2)}, u32[]{:S(2)}) collective-permute-start(bf16[4,256,512]{2,1,0:T(8,128)(2,1)} %fusion.12), channel_id=1, source_target_pairs={{0,8},{4,12},{8,0},{12,4},{1,9},{5,13},{9,1},{13,5},{2,10},{6,14},... | collective-permute-start | bytes 3145736 | tf_op jit(solution)/shard_map/ppermute | solution.py:412
  562.3 29.0 %collective-permute-start.84 = (bf16[128,1024]{1,0:T(8,128)(2,1)S(1)}, bf16[128,1024]{1,0:T(8,128)(2,1)S(1)}, u32[]{:S(2)}, u32[]{:S(2)}) collective-permute-start(bf16[128,1024]{1,0:T(8,128)(2,1)S(1)} %get-tuple-element.368), channel_id=1, source_target_pairs={{0,3},{1,0},{2,1},{3,2},{4,7},{5,4},{6,5},{7,6},{8,11},{9,8},{10,9... | collective-permute-start | bytes 786440 | tf_op jit(solution)/shard_map/ppermute | solution.py:407
  562.4 27.9 %collective-permute-start.83 = (bf16[128,1024]{1,0:T(8,128)(2,1)S(1)}, bf16[128,1024]{1,0:T(8,128)(2,1)S(1)}, u32[]{:S(2)}, u32[]{:S(2)}) collective-permute-start(bf16[128,1024]{1,0:T(8,128)(2,1)S(1)} %get-tuple-element.367), channel_id=1, source_target_pairs={{0,1},{1,2},{2,3},{3,0},{4,5},{5,6},{6,7},{7,4},{8,9},{9,10},{10,1... | collective-permute-start | bytes 786440 | tf_op jit(solution)/shard_map/ppermute | solution.py:407
  605.1 24.6 %collective-permute-start.89 = (bf16[256,1024]{1,0:T(8,128)(2,1)}, bf16[256,1024]{1,0:T(8,128)(2,1)S(1)}, u32[]{:S(2)}, u32[]{:S(2)}) collective-permute-start(bf16[256,1024]{1,0:T(8,128)(2,1)} %pad_maximum_fusion.24), channel_id=1, source_target_pairs={{0,3},{1,0},{2,1},{3,2},{4,7},{5,4},{6,5},{7,6},{8,11},{9,8},{10,9... | collective-permute-start | bytes 1572872 | tf_op jit(solution)/shard_map/ppermute | solution.py:407
  607.0 23.6 %collective-permute-start.88 = (bf16[256,1024]{1,0:T(8,128)(2,1)}, bf16[256,1024]{1,0:T(8,128)(2,1)}, u32[]{:S(2)}, u32[]{:S(2)}) collective-permute-start(bf16[256,1024]{1,0:T(8,128)(2,1)} %pad_maximum_fusion.23), channel_id=1, source_target_pairs={{0,1},{1,2},{2,3},{3,0},{4,5},{5,6},{6,7},{7,4},{8,9},{9,10},{10,1... | collective-permute-start | bytes 1572872 | tf_op jit(solution)/shard_map/ppermute | solution.py:407
  610.1 24.9 %collective-permute-start.87 = (bf16[2,256,1024]{2,1,0:T(8,128)(2,1)}, bf16[2,256,1024]{2,1,0:T(8,128)(2,1)}, u32[]{:S(2)}, u32[]{:S(2)}) collective-permute-start(bf16[2,256,1024]{2,1,0:T(8,128)(2,1)} %fusion.17), channel_id=1, source_target_pairs={{0,8},{4,12},{8,0},{12,4},{1,9},{5,13},{9,1},{13,5},{2,10},{6,14},... | collective-permute-start | bytes 3145736 | tf_op jit(solution)/shard_map/ppermute | solution.py:412
  610.9 49.0 %collective-permute-start.90 = (bf16[512,1024]{1,0:T(8,128)(2,1)}, bf16[512,1024]{1,0:T(8,128)(2,1)}, u32[]{:S(2)}, u32[]{:S(2)}) collective-permute-start(bf16[512,1024]{1,0:T(8,128)(2,1)} %get-tuple-element.396), channel_id=1, source_target_pairs={{0,16},{16,0},{1,17},{17,1},{2,18},{18,2},{3,19},{19,3},{4,20},{20... | collective-permute-start | bytes 3145736 | tf_op jit(solution)/shard_map/ppermute | solution.py:412
  635.0 22.5 %collective-permute-start.94 = (bf16[128,512]{1,0:T(8,128)(2,1)}, bf16[128,512]{1,0:T(8,128)(2,1)}, u32[]{:S(2)}, u32[]{:S(2)}) collective-permute-start(bf16[128,512]{1,0:T(8,128)(2,1)} %get-tuple-element.390), channel_id=1, source_target_pairs={{0,3},{1,0},{2,1},{3,2},{4,7},{5,4},{6,5},{7,6},{8,11},{9,8},{10,9... | collective-permute-start | bytes 393224 | tf_op jit(solution)/shard_map/ppermute | solution.py:407
  638.5 18.9 %collective-permute-start.93 = (bf16[128,512]{1,0:T(8,128)(2,1)}, bf16[128,512]{1,0:T(8,128)(2,1)}, u32[]{:S(2)}, u32[]{:S(2)}) collective-permute-start(bf16[128,512]{1,0:T(8,128)(2,1)} %get-tuple-element.389), channel_id=1, source_target_pairs={{0,1},{1,2},{2,3},{3,0},{4,5},{5,6},{6,7},{7,4},{8,9},{9,10},{10,1... | collective-permute-start | bytes 393224 | tf_op jit(solution)/shard_map/ppermute | solution.py:407
  640.4 23.4 %collective-permute-start.92 = (bf16[2,256,1024]{2,1,0:T(8,128)(2,1)S(1)}, bf16[2,256,1024]{2,1,0:T(8,128)(2,1)}, u32[]{:S(2)}, u32[]{:S(2)}) collective-permute-start(bf16[2,256,1024]{2,1,0:T(8,128)(2,1)S(1)} %fusion.9), channel_id=1, source_target_pairs={{0,8},{4,12},{8,0},{12,4},{1,9},{5,13},{9,1},{13,5},{2,10},{6,14},... | collective-permute-start | bytes 3145736 | tf_op jit(solution)/shard_map/ppermute | solution.py:412
  641.3 23.3 %collective-permute-start.91 = (bf16[512,1024]{1,0:T(8,128)(2,1)}, bf16[512,1024]{1,0:T(8,128)(2,1)}, u32[]{:S(2)}, u32[]{:S(2)}) collective-permute-start(bf16[512,1024]{1,0:T(8,128)(2,1)} %get-tuple-element.397), channel_id=1, source_target_pairs={{0,16},{16,0},{1,17},{17,1},{2,18},{18,2},{3,19},{19,3},{4,20},{20... | collective-permute-start | bytes 3145736 | tf_op jit(solution)/shard_map/ppermute | solution.py:412
  676.2 19.0 %collective-permute-start.97 = (bf16[2,4,256,512]{3,2,1,0:T(8,128)(2,1)}, bf16[2,4,256,512]{3,2,1,0:T(8,128)(2,1)S(1)}, u32[]{:S(2)}, u32[]{:S(2)}) collective-permute-start(bf16[2,4,256,512]{3,2,1,0:T(8,128)(2,1)} %get-tuple-element.395), channel_id=1, source_target_pairs={{0,4},{4,0},{8,12},{12,8},{1,5},{5,1},{9,13},{13,9},{2,6},{6,2},{1... | collective-permute-start | bytes 6291464 | tf_op jit(solution)/shard_map/ppermute | solution.py:412
  700.9 30.3 %collective-permute-start.100 = (bf16[256,1024]{1,0:T(8,128)(2,1)S(1)}, bf16[256,1024]{1,0:T(8,128)(2,1)S(1)}, u32[]{:S(2)}, u32[]{:S(2)}) collective-permute-start(bf16[256,1024]{1,0:T(8,128)(2,1)S(1)} %pad_maximum_fusion.26), channel_id=1, source_target_pairs={{0,3},{1,0},{2,1},{3,2},{4,7},{5,4},{6,5},{7,6},{8,11},{9,8},{10,9... | collective-permute-start | bytes 1572872 | tf_op jit(solution)/shard_map/ppermute | solution.py:407
  704.5 26.6 %collective-permute-start.99 = (bf16[256,1024]{1,0:T(8,128)(2,1)S(1)}, bf16[256,1024]{1,0:T(8,128)(2,1)S(1)}, u32[]{:S(2)}, u32[]{:S(2)}) collective-permute-start(bf16[256,1024]{1,0:T(8,128)(2,1)S(1)} %pad_maximum_fusion.25), channel_id=1, source_target_pairs={{0,1},{1,2},{2,3},{3,0},{4,5},{5,6},{6,7},{7,4},{8,9},{9,10},{10,1... | collective-permute-start | bytes 1572872 | tf_op jit(solution)/shard_map/ppermute | solution.py:407
  709.6 23.2 %collective-permute-start.101 = (bf16[4,256,512]{2,1,0:T(8,128)(2,1)S(1)}, bf16[4,256,512]{2,1,0:T(8,128)(2,1)S(1)}, u32[]{:S(2)}, u32[]{:S(2)}) collective-permute-start(bf16[4,256,512]{2,1,0:T(8,128)(2,1)S(1)} %fusion.2), channel_id=1, source_target_pairs={{0,8},{4,12},{8,0},{12,4},{1,9},{5,13},{9,1},{13,5},{2,10},{6,14},... | collective-permute-start | bytes 3145736 | tf_op jit(solution)/shard_map/ppermute | solution.py:412
  751.9 38.5 %collective-permute-start.109 = (bf16[384,1024]{1,0:T(8,128)(2,1)}, bf16[384,1024]{1,0:T(8,128)(2,1)}, u32[]{:S(2)}, u32[]{:S(2)}) collective-permute-start(bf16[384,1024]{1,0:T(8,128)(2,1)} %pad_maximum_fusion.14), channel_id=1, source_target_pairs={{0,3},{1,0},{2,1},{3,2},{4,7},{5,4},{6,5},{7,6},{8,11},{9,8},{10,9... | collective-permute-start | bytes 2359304 | tf_op jit(solution)/shard_map/ppermute | solution.py:407
  753.8 36.6 %collective-permute-start.108 = (bf16[384,1024]{1,0:T(8,128)(2,1)}, bf16[384,1024]{1,0:T(8,128)(2,1)}, u32[]{:S(2)}, u32[]{:S(2)}) collective-permute-start(bf16[384,1024]{1,0:T(8,128)(2,1)} %pad_maximum_fusion.13), channel_id=1, source_target_pairs={{0,1},{1,2},{2,3},{3,0},{4,5},{5,6},{6,7},{7,4},{8,9},{9,10},{10,1... | collective-permute-start | bytes 2359304 | tf_op jit(solution)/shard_map/ppermute | solution.py:407
  792.4 16.7 %collective-permute-start.113 = (bf16[128,1024]{1,0:T(8,128)(2,1)S(1)}, bf16[128,1024]{1,0:T(8,128)(2,1)S(1)}, u32[]{:S(2)}, u32[]{:S(2)}) collective-permute-start(bf16[128,1024]{1,0:T(8,128)(2,1)S(1)} %slice.867), channel_id=1, source_target_pairs={{0,1},{1,2},{2,3},{3,0},{4,5},{5,6},{6,7},{7,4},{8,9},{9,10},{10,1... | collective-permute-start | bytes 786440 | tf_op jit(solution)/shard_map/ppermute | solution.py:407
  (149 other events, 1481.9 us)

commit v7 on v6

--- a/solution.py
+++ b/solution.py
@@ -1168,28 +1168,30 @@
     first = project(1, 0, (hold(x1_a), 0), narrow_one, ())
     first = project(1, 1, (x1_b, 0), narrow_one, first)
     ln_a1, ln_m1, qkv1 = first
-    tick(first, broad_far, got_left)
+    pieces = [stacked(broad_shards[1], broad_own)]
+    others = [core_swap(pieces[0])]
+    tick(first, broad_far, got_left, others)
     broad_far = jnp.concatenate(broad_far, axis=0)
     got_right, got_far = x_swap(broad_right), x_swap(broad_far)
-    pieces = [stacked(broad_shards[1], broad_own), stacked(broad_left, got_left)]
-    others = [core_swap(piece) for piece in pieces]
+    pieces.append(stacked(broad_left, got_left))
+    others.append(core_swap(pieces[1]))
     ctx1, lse1 = run_attend(hold(qkv1))
-    tick(ctx1, got_right, got_far, others)
+    blocks = own_half(cotangent[:, :, 0, :])
+    near = exchange_near(blocks, along, hold)
+    tick(ctx1, got_right, got_far, others, near)
+    far = exchange_far(near, hold)
     pieces += [stacked(broad_right, got_right), stacked(broad_far, got_far)]
     others += [core_swap(piece) for piece in pieces[2:]]
     broad_one = (*pieces, *others)
-    tick(others[2:])
+    tick(others[2:], far)
+    own_grads = exchanged(blocks, near, far, along)
+    got_grads = y_swap(own_grads)
     first, part_a = feed(1, 0, ctx1, ln_m1, narrow_one, broad_one, ())
-    blocks = own_half(cotangent[:, :, 0, :])
-    near = exchange_near(blocks, along, hold)
-    tick(part_a, near)
+    tick(part_a, got_grads)
+    got_a = y_swap(part_a)
     first, part_b = feed(1, 1, ctx1, ln_m1, narrow_one, broad_one, first)
     act1, slope1 = first
-    far = exchange_far(near, hold)
-    tick(far)
-    own_grads = exchanged(blocks, near, far, along)
-    got_grads = y_swap(own_grads)
-    tick(part_b, got_grads)
+    tick(part_b, got_a)
 
     grads = hold(both_halves(own_grads, got_grads))
     n_heads = ctx0.shape[1]
@@ -1204,7 +1206,6 @@
     first, up_b, g_b = back(1, (grads, chunk), slope1, narrow_one, broad_one, first)
     d_up1, d_ctx1 = first
     sums_one = [None, g_a + g_b, None, up_a + up_b]
-    got_a = y_swap(part_a)
     tick(first, got_a)
     x1 = jnp.concatenate([x1_a, x1_b], axis=0)
 

time: 819 us -> 819 us (level)
  transfers between devices with their start and end apart: 118 -> 118, of which waited for: 41 -> 37; matrix products, arithmetic and copies ran while one was open for 17% -> 18% of each run, Pallas kernels for 35% -> 33%
where the time goes in v7:
time: 819 us; the launch traced here: 811 us
  Pallas kernels  306 us (37%)
  waiting for transfers between devices  191 us (23%)
  starting transfers between devices  121 us (15%)
  other arithmetic  94.1 us (11%)
  local copies, waits for them, and re-layouts  87 us (11%)
  between operations  11.5 us (1%)
    pallas_call x24, Pallas kernels, call(): pl.pallas_call(run, name=name, grid=grid, in_specs=[pl.BlockSpec(block, i...  306 us
    ppermute x52, waiting for transfers between devices, ring(): lax.ppermute(value, axis, [(i, (i + by) % length) for i in range(length)])  114 us
    ppermute x52, starting transfers between devices, ring(): lax.ppermute(value, axis, [(i, (i + by) % length) for i in range(length)])  78.2 us
    ppermute x66, waiting for transfers between devices, swap(): return lax.ppermute(value, axis, [(i, i ^ bit) for i in range(length)])  77 us
    ppermute x66, starting transfers between devices, swap(): return lax.ppermute(value, axis, [(i, i ^ bit) for i in range(length)])  42.5 us
  transfers between devices with their start and end apart: 118, of which 37 were waited for; matrix products, arithmetic and copies ran while one was open for 18% of the time, Pallas kernels for 33%

profile of v7, /device:TPU:0, one launch (start us, length us, event | category | flops | bytes accessed | tf_op | source)
XLA Modules:
  0.0 810.6 jit_solution(14538648570281969646)
XLA Ops:
  27.9 3.8 collective-permute-start.7
  41.4 4.1 collective-permute-done.4
  45.5 4.9 collective-permute-done.5
  60.3 4.8 collective-permute-done.18
  67.2 3.5 collective-permute-start.27
  78.0 4.0 collective-permute-done.27
  85.5 3.6 collective-permute-done.25
  95.3 6.4 norm_qkv.4
  101.6 6.4 norm_qkv.5
  112.8 17.2 %attend.2 = (bf16[1024,512]{1,0:T(8,128)(2,1)}, f32[4,8,1024]{2,1,0:T(8,128)}) custom-call(bf16[1024,1536]{1,0:T(8,128)(2,1)} %get-tuple-element.252.refs_0_.refs_1_.refs_2_, bf16[1024,1536]{1,0:T(8,128)(2,1)} %get-tuple-element.252.refs_0_.refs_1_.refs_2_, bf16[1024,1536]{1,0:T(8,128)(2,1)} %get-tuple-element.252.refs_0_.refs_1_.refs_2_), custom_call_target="tpu_custom_call" | custom-call | flops 19000000512 | bytes 1048576 | tf_op jit(solution)/shard_map/attend/pallas_call | solution.py:536
  136.9 13.8 %collective-permute-done.31 = bf16[256,1024]{1,0:T(8,128)(2,1)S(1)} collective-permute-done((bf16[256,1024]{1,0:T(8,128)(2,1)S(1)}, bf16[256,1024]{1,0:T(8,128)(2,1)S(1)}, u32[]{:S(2)}, u32[]{:S(2)}) %collective-permute-start.31) | collective-permute-done | bytes 524320 | tf_op jit(solution)/shard_map/ppermute | solution.py:412
  162.1 16.4 %mlp_out.4 = (bf16[1024,2048]{1,0:T(8,128)(2,1)}, bf16[1024,2048]{1,0:T(8,128)(2,1)}, bf16[512,1024]{1,0:T(8,128)(2,1)}) custom-call(bf16[1024,512]{1,0:T(8,128)(2,1)} %get-tuple-element.269.refs_0_.refs_4_, bf16[1024,1024]{1,0:T(8,128)(2,1)} %get-tuple-element.358.refs_1_.refs_0_, f32[1,2048]{1,0:T(1,128)} %bitcast.478, ...), custom_call_target="tpu_custom_call" | custom-call | flops 16000000000 | bytes 1048576 | tf_op jit(solution)/shard_map/mlp_out/pallas_call | solution.py:536
  179.3 3.8 collective-permute-start.44
  186.2 16.5 %mlp_out.5 = (bf16[1024,2048]{1,0:T(8,128)(2,1)}, bf16[1024,2048]{1,0:T(8,128)(2,1)}, bf16[512,1024]{1,0:T(8,128)(2,1)}) custom-call(bf16[1024,512]{1,0:T(8,128)(2,1)} %get-tuple-element.269.refs_0_.refs_4_, bf16[1024,1024]{1,0:T(8,128)(2,1)} %get-tuple-element.358.refs_1_.refs_0_, ...), custom_call_target="tpu_custom_call", output_to_operand_aliasing={{0}: (27, {}), {1}: (28, {})} | custom-call | flops 16000000000 | bytes 1048576 | tf_op jit(solution)/shard_map/mlp_out/pallas_call | solution.py:536
  202.6 3.8 collective-permute-done.42
  206.5 4.4 collective-permute-done.41
  229.0 3.7 collective-permute-done.48
  232.9 4.2 collective-permute-done.45
  238.3 4.8 add_convert_fusion.9
  246.7 6.4 norm_qkv.6
  253.1 6.3 norm_qkv.7
  262.5 3.8 collective-permute-start.61
  268.4 17.2 %attend.3 = (bf16[1024,512]{1,0:T(8,128)(2,1)}, f32[4,8,1024]{2,1,0:T(8,128)}) custom-call(bf16[1024,1536]{1,0:T(8,128)(2,1)} %get-tuple-element.295.refs_0_.refs_1_.refs_2_, bf16[1024,1536]{1,0:T(8,128)(2,1)} %get-tuple-element.295.refs_0_.refs_1_.refs_2_, bf16[1024,1536]{1,0:T(8,128)(2,1)} %get-tuple-element.295.refs_0_.refs_1_.refs_2_), custom_call_target="tpu_custom_call" | custom-call | flops 19000000512 | bytes 1048576 | tf_op jit(solution)/shard_map/attend/pallas_call | solution.py:536
  285.7 6.2 collective-permute-done.57
  299.8 5.3 collective-permute-done.65
  305.8 16.9 %mlp_out.6 = (bf16[1024,2048]{1,0:T(8,128)(2,1)}, bf16[1024,2048]{1,0:T(8,128)(2,1)}, bf16[512,1024]{1,0:T(8,128)(2,1)}) custom-call(bf16[1024,512]{1,0:T(8,128)(2,1)} %get-tuple-element.310.refs_0_.refs_3_, bf16[1024,1024]{1,0:T(8,128)(2,1)} %get-tuple-element.329.refs_1_.refs_0_, f32[1,2048]{1,0:T(1,128)} %bitcast.476, ...), custom_call_target="tpu_custom_call" | custom-call | flops 16000000000 | bytes 1048576 | tf_op jit(solution)/shard_map/mlp_out/pallas_call | solution.py:536
  322.6 5.9 collective-permute-done.66
  331.8 16.6 %mlp_out.7 = (bf16[1024,2048]{1,0:T(8,128)(2,1)}, bf16[1024,2048]{1,0:T(8,128)(2,1)}, bf16[512,1024]{1,0:T(8,128)(2,1)}) custom-call(bf16[1024,512]{1,0:T(8,128)(2,1)} %get-tuple-element.310.refs_0_.refs_3_, bf16[1024,1024]{1,0:T(8,128)(2,1)} %get-tuple-element.329.refs_1_.refs_0_, ...), custom_call_target="tpu_custom_call", output_to_operand_aliasing={{0}: (27, {}), {1}: (28, {})} | custom-call | flops 16000000000 | bytes 1048576 | tf_op jit(solution)/shard_map/mlp_out/pallas_call | solution.py:536
  351.2 7.9 mlp_back.4
  359.1 7.6 mlp_back.5
  367.3 26.0 %attend_back.2 = (bf16[1024,1536]{1,0:T(8,128)(2,1)}, f32[1,1536]{1,0:T(1,128)}) custom-call(bf16[1024,1536]{1,0:T(8,128)(2,1)} %get-tuple-element.295.refs_0_.refs_1_.refs_2_, bf16[1024,1536]{1,0:T(8,128)(2,1)} %get-tuple-element.295.refs_0_.refs_1_.refs_2_, bf16[1024,1536]{1,0:T(8,128)(2,1)} %get-tuple-element.295.refs_0_.refs_1_.refs_2_, ...), custom_call_target="tpu_custom_call" | custom-call | flops 25999998976 | bytes 1048576 | tf_op jit(solution)/shard_map/attend_back/pallas_call | solution.py:536
  393.4 3.4 add_convert_fusion.7
  399.7 10.6 %norm_back.4 = (bf16[512,1024]{1,0:T(8,128)(2,1)}, f32[8,1024]{1,0:T(8,128)}) custom-call(bf16[512,1024]{1,0:T(8,128)(2,1)} %get-tuple-element.284.refs_0_, bf16[1024,1536]{1,0:T(8,128)(2,1)} %get-tuple-element.327.refs_1_.refs_2_, bf16[1024,2048]{1,0:T(8,128)(2,1)} %get-tuple-element.319.refs_2_, f32[8,1024]{1,0:T(8,128)} %concatenate.218.refs_1_.refs_3_, ...), custom_call_target="tpu_custom_call" | custom-call | flops 10499999744 | bytes 1048576 | tf_op jit(solution)/shard_map/norm_back/pallas_call | solution.py:536
  416.2 15.1 %weight_grad.4 = (bf16[2,4,256,1024]{3,2,1,0:T(8,128)(2,1)}, bf16[2,4,256,1024]{3,2,1,0:T(8,128)(2,1)}) custom-call(bf16[1024,1024]{1,0:T(8,128)(2,1)} %get-tuple-element.329.refs_1_.refs_0_, bf16[1024,1024]{1,0:T(8,128)(2,1)} %pad_maximum_fusion.1.refs_0_.refs_1_, bf16[1024,2048]{1,0:T(8,128)(2,1)} %get-tuple-element.319.refs_2_, ...), custom_call_target="tpu_custom_call" | custom-call | flops 14000000000 | bytes 1048576 | tf_op jit(solution)/shard_map/weight_grad/pallas_call | solution.py:536
  431.3 10.6 %norm_back.5 = (bf16[512,1024]{1,0:T(8,128)(2,1)}, f32[8,1024]{1,0:T(8,128)}) custom-call(bf16[512,1024]{1,0:T(8,128)(2,1)} %get-tuple-element.479.refs_0_, bf16[1024,1536]{1,0:T(8,128)(2,1)} %get-tuple-element.327.refs_1_.refs_2_, bf16[1024,2048]{1,0:T(8,128)(2,1)} %get-tuple-element.319.refs_2_, f32[8,1024]{1,0:T(8,128)} %concatenate.218.refs_1_.refs_3_, ...), custom_call_target="tpu_custom_call" | custom-call | flops 10499999744 | bytes 1048576 | tf_op jit(solution)/shard_map/norm_back/pallas_call | solution.py:536
  457.8 3.3 collective-permute-start.75
  461.6 12.1 %weight_grad.5 = (bf16[2,4,256,512]{3,2,1,0:T(8,128)(2,1)}, bf16[2,4,256,512]{3,2,1,0:T(8,128)(2,1)}) custom-call(bf16[1024,1024]{1,0:T(8,128)(2,1)} %get-tuple-element.335.refs_0_, bf16[1024,1024]{1,0:T(8,128)(2,1)} %pad_maximum_fusion.1.refs_0_.refs_1_, bf16[1024,1536]{1,0:T(8,128)(2,1)} %get-tuple-element.327.refs_1_.refs_2_, ...), custom_call_target="tpu_custom_call" | custom-call | flops 14000000000 | bytes 1048576 | tf_op jit(solution)/shard_map/weight_grad/pallas_call | solution.py:536
  474.5 6.8 collective-permute-done.74
  482.2 4.2 collective-permute-done.72
  486.5 3.5 collective-permute-start.81
  490.0 3.8 collective-permute-start.79
  497.1 4.7 add_convert_fusion.4
  501.8 8.0 mlp_back.6
  509.7 7.6 mlp_back.7
  520.8 4.4 collective-permute-done.78
  527.8 14.9 %weight_grad.6 = (bf16[2,4,256,1024]{3,2,1,0:T(8,128)(2,1)}, bf16[2,4,256,1024]{3,2,1,0:T(8,128)(2,1)}) custom-call(bf16[1024,1024]{1,0:T(8,128)(2,1)} %get-tuple-element.358.refs_1_.refs_0_, bf16[512,1024]{1,0:T(8,128)(2,1)} %get-tuple-element.345.refs_0_.refs_1_, bf16[512,1024]{1,0:T(8,128)(2,1)} %get-tuple-element.497.refs_0_.refs_2_, ...), custom_call_target="tpu_custom_call" | custom-call | flops 14000000000 | bytes 1048576 | tf_op jit(solution)/shard_map/weight_grad/pallas_call | solution.py:536
  542.7 9.1 %collective-permute-done.82 = bf16[2,256,1024]{2,1,0:T(8,128)(2,1)} collective-permute-done((bf16[2,256,1024]{2,1,0:T(8,128)(2,1)S(1)}, bf16[2,256,1024]{2,1,0:T(8,128)(2,1)}, u32[]{:S(2)}, u32[]{:S(2)}) %collective-permute-start.82) | collective-permute-done | bytes 1048608 | tf_op jit(solution)/shard_map/ppermute | solution.py:412
  563.0 26.0 %attend_back.3 = (bf16[1024,1536]{1,0:T(8,128)(2,1)}, f32[1,1536]{1,0:T(1,128)}) custom-call(bf16[1024,1536]{1,0:T(8,128)(2,1)} %get-tuple-element.252.refs_0_.refs_1_.refs_2_, bf16[1024,1536]{1,0:T(8,128)(2,1)} %get-tuple-element.252.refs_0_.refs_1_.refs_2_, bf16[1024,1536]{1,0:T(8,128)(2,1)} %get-tuple-element.252.refs_0_.refs_1_.refs_2_, ...), custom_call_target="tpu_custom_call" | custom-call | flops 25999998976 | bytes 1048576 | tf_op jit(solution)/shard_map/attend_back/pallas_call | solution.py:536
  589.9 10.7 %norm_back.6 = (bf16[512,1024]{1,0:T(8,128)(2,1)}, f32[8,1024]{1,0:T(8,128)}) custom-call(bf16[1024,1024]{1,0:T(8,128)(2,1)} %pad_maximum_fusion.refs_0_, bf16[1024,1536]{1,0:T(8,128)(2,1)} %get-tuple-element.376.refs_1_.refs_3_, bf16[1024,2048]{1,0:T(8,128)(2,1)} %get-tuple-element.348.refs_3_.refs_2_, f32[8,1024]{1,0:T(8,128)} %concatenate.212.refs_1_.refs_3_, ...), custom_call_target="tpu_custom_call" | custom-call | flops 10499999744 | bytes 1048576 | tf_op jit(solution)/shard_map/norm_back/pallas_call | solution.py:536
  612.4 10.8 %norm_back.7 = (bf16[512,1024]{1,0:T(8,128)(2,1)}, f32[8,1024]{1,0:T(8,128)}) custom-call(bf16[1024,1024]{1,0:T(8,128)(2,1)} %pad_maximum_fusion.refs_0_, bf16[1024,1536]{1,0:T(8,128)(2,1)} %get-tuple-element.376.refs_1_.refs_3_, bf16[1024,2048]{1,0:T(8,128)(2,1)} %get-tuple-element.348.refs_3_.refs_2_, f32[8,1024]{1,0:T(8,128)} %concatenate.212.refs_1_.refs_3_, ...), custom_call_target="tpu_custom_call" | custom-call | flops 10499999744 | bytes 1048576 | tf_op jit(solution)/shard_map/norm_back/pallas_call | solution.py:536
  624.9 3.5 slice_bitcast_fusion.11
  629.1 4.5 collective-permute-done.87
  633.6 3.5 collective-permute-start.94
  640.5 12.1 %weight_grad.7 = (bf16[2,4,256,512]{3,2,1,0:T(8,128)(2,1)}, bf16[2,4,256,512]{3,2,1,0:T(8,128)(2,1)}) custom-call(bf16[1024,1024]{1,0:T(8,128)(2,1)} %get-tuple-element.382.refs_0_, bf16[512,1024]{1,0:T(8,128)(2,1)} %get-tuple-element.345.refs_0_.refs_1_, bf16[512,1024]{1,0:T(8,128)(2,1)} %get-tuple-element.497.refs_0_.refs_2_, ...), custom_call_target="tpu_custom_call" | custom-call | flops 14000000000 | bytes 1048576 | tf_op jit(solution)/shard_map/weight_grad/pallas_call | solution.py:536
  658.2 3.9 collective-permute-done.92
  678.1 3.6 collective-permute-start.96
  682.7 11.1 %collective-permute-done.95 = bf16[128,1024]{1,0:T(8,128)(2,1)S(1)} collective-permute-done((bf16[128,1024]{1,0:T(8,128)(2,1)S(1)}, bf16[128,1024]{1,0:T(8,128)(2,1)S(1)}, u32[]{:S(2)}, u32[]{:S(2)}) %collective-permute-start.95) | collective-permute-done | bytes 262176 | tf_op jit(solution)/shard_map/ppermute | solution.py:407
  699.5 3.7 collective-permute-start.100
  709.6 20.6 %collective-permute-done.100 = bf16[256,1024]{1,0:T(8,128)(2,1)S(1)} collective-permute-done((bf16[256,1024]{1,0:T(8,128)(2,1)S(1)}, bf16[256,1024]{1,0:T(8,128)(2,1)S(1)}, u32[]{:S(2)}, u32[]{:S(2)}) %collective-permute-start.100) | collective-permute-done | bytes 524320 | tf_op jit(solution)/shard_map/ppermute | solution.py:407
  732.3 3.3 collective-permute-start.106
  738.6 5.3 collective-permute-done.105
  752.2 4.9 collective-permute-done.111
  761.7 26.9 %collective-permute-done.109 = bf16[384,1024]{1,0:T(8,128)(2,1)} collective-permute-done((bf16[384,1024]{1,0:T(8,128)(2,1)}, bf16[384,1024]{1,0:T(8,128)(2,1)}, u32[]{:S(2)}, u32[]{:S(2)}) %collective-permute-start.109) | collective-permute-done | bytes 786464 | tf_op jit(solution)/shard_map/ppermute | solution.py:407
  792.2 3.6 collective-permute-start.114
  (718 shorter events, 262.6 us)
Async XLA Ops:
  4.0 23.8 %collective-permute-start = (bf16[384,512]{1,0:T(8,128)(2,1)}, bf16[384,512]{1,0:T(8,128)(2,1)}, u32[]{:S(2)}, u32[]{:S(2)}) collective-permute-start(bf16[384,512]{1,0:T(8,128)(2,1)} %pad_maximum_fusion.27), channel_id=1, source_target_pairs={{0,1},{1,2},{2,3},{3,0},{4,5},{5,6},{6,7},{7,4},{8,9},{9,10},{10,1... | collective-permute-start | bytes 1179656 | tf_op jit(solution)/shard_map/ppermute | solution.py:407
  7.9 20.0 %collective-permute-start.1 = (bf16[384,512]{1,0:T(8,128)(2,1)}, bf16[384,512]{1,0:T(8,128)(2,1)}, u32[]{:S(2)}, u32[]{:S(2)}) collective-permute-start(bf16[384,512]{1,0:T(8,128)(2,1)} %pad_maximum_fusion.28), channel_id=1, source_target_pairs={{0,3},{1,0},{2,1},{3,2},{4,7},{5,4},{6,5},{7,6},{8,11},{9,8},{10,9... | collective-permute-start | bytes 1179656 | tf_op jit(solution)/shard_map/ppermute | solution.py:407
  27.9 23.3 %collective-permute-start.6 = (bf16[256,512]{1,0:T(8,128)(2,1)S(1)}, bf16[256,512]{1,0:T(8,128)(2,1)S(1)}, u32[]{:S(2)}, u32[]{:S(2)}) collective-permute-start(bf16[256,512]{1,0:T(8,128)(2,1)S(1)} %get-tuple-element.230), channel_id=1, source_target_pairs={{0,1},{1,2},{2,3},{3,0},{4,5},{5,6},{6,7},{7,4},{8,9},{9,10},{10,1... | collective-permute-start | bytes 786440 | tf_op jit(solution)/shard_map/ppermute | solution.py:407
  27.9 23.2 %collective-permute-start.7 = (bf16[256,512]{1,0:T(8,128)(2,1)S(1)}, bf16[256,512]{1,0:T(8,128)(2,1)S(1)}, u32[]{:S(2)}, u32[]{:S(2)}) collective-permute-start(bf16[256,512]{1,0:T(8,128)(2,1)S(1)} %get-tuple-element.230), channel_id=1, source_target_pairs={{0,3},{1,0},{2,1},{3,2},{4,7},{5,4},{6,5},{7,6},{8,11},{9,8},{10,9... | collective-permute-start | bytes 786440 | tf_op jit(solution)/shard_map/ppermute | solution.py:407
  32.8 18.5 %collective-permute-start.8 = (bf16[256,1024]{1,0:T(8,128)(2,1)S(1)}, bf16[256,1024]{1,0:T(8,128)(2,1)S(1)}, u32[]{:S(2)}, u32[]{:S(2)}) collective-permute-start(bf16[256,1024]{1,0:T(8,128)(2,1)S(1)} %copy-done.44), channel_id=1, source_target_pairs={{0,16},{16,0},{1,17},{17,1},{2,18},{18,2},{3,19},{19,3},{4,20},{20... | collective-permute-start | bytes 1572872 | tf_op jit(solution)/shard_map/ppermute | solution.py:412
  65.1 24.8 %collective-permute-start.12 = (bf16[4,256,512]{2,1,0:T(8,128)(2,1)}, bf16[4,256,512]{2,1,0:T(8,128)(2,1)S(1)}, u32[]{:S(2)}, u32[]{:S(2)}) collective-permute-start(bf16[4,256,512]{2,1,0:T(8,128)(2,1)} %fusion.51), channel_id=1, source_target_pairs={{0,16},{16,0},{1,17},{17,1},{2,18},{18,2},{3,19},{19,3},{4,20},{20... | collective-permute-start | bytes 3145736 | tf_op jit(solution)/shard_map/ppermute | solution.py:412
  89.8 18.1 %collective-permute-start.24 = (bf16[256,1024]{1,0:T(8,128)(2,1)S(1)}, bf16[256,1024]{1,0:T(8,128)(2,1)}, u32[]{:S(2)}, u32[]{:S(2)}) collective-permute-start(bf16[256,1024]{1,0:T(8,128)(2,1)S(1)} %get-tuple-element.251), channel_id=1, source_target_pairs={{0,8},{4,12},{8,0},{12,4},{1,9},{5,13},{9,1},{13,5},{2,10},{6,14},... | collective-permute-start | bytes 1572872 | tf_op jit(solution)/shard_map/ppermute | solution.py:412
  108.0 23.2 %collective-permute-start.30 = (bf16[256,1024]{1,0:T(8,128)(2,1)S(1)}, bf16[256,1024]{1,0:T(8,128)(2,1)}, u32[]{:S(2)}, u32[]{:S(2)}) collective-permute-start(bf16[256,1024]{1,0:T(8,128)(2,1)S(1)} %collective-permute-done.27), channel_id=1, source_target_pairs={{0,8},{4,12},{8,0},{12,4},{1,9},{5,13},{9,1},{13,5},{2,10},{6,14},... | collective-permute-start | bytes 1572872 | tf_op jit(solution)/shard_map/ppermute | solution.py:412
  108.6 24.1 %collective-permute-start.28 = (bf16[128,1024]{1,0:T(8,128)(2,1)S(1)}, bf16[128,1024]{1,0:T(8,128)(2,1)}, u32[]{:S(2)}, u32[]{:S(2)}) collective-permute-start(bf16[128,1024]{1,0:T(8,128)(2,1)S(1)} %slice.800), channel_id=1, source_target_pairs={{0,3},{1,0},{2,1},{3,2},{4,7},{5,4},{6,5},{7,6},{8,11},{9,8},{10,9... | collective-permute-start | bytes 786440 | tf_op jit(solution)/shard_map/ppermute | solution.py:407
  111.4 21.3 %collective-permute-start.26 = (bf16[128,1024]{1,0:T(8,128)(2,1)}, bf16[128,1024]{1,0:T(8,128)(2,1)}, u32[]{:S(2)}, u32[]{:S(2)}) collective-permute-start(bf16[128,1024]{1,0:T(8,128)(2,1)} %slice.799), channel_id=1, source_target_pairs={{0,1},{1,2},{2,3},{3,0},{4,5},{5,6},{6,7},{7,4},{8,9},{9,10},{10,1... | collective-permute-start | bytes 786440 | tf_op jit(solution)/shard_map/ppermute | solution.py:407
  111.4 22.3 %collective-permute-start.29 = (bf16[256,1024]{1,0:T(8,128)(2,1)S(1)}, bf16[256,1024]{1,0:T(8,128)(2,1)S(1)}, u32[]{:S(2)}, u32[]{:S(2)}) collective-permute-start(bf16[256,1024]{1,0:T(8,128)(2,1)S(1)} %collective-permute-done.25), channel_id=1, source_target_pairs={{0,8},{4,12},{8,0},{12,4},{1,9},{5,13},{9,1},{13,5},{2,10},{6,14},... | collective-permute-start | bytes 1572872 | tf_op jit(solution)/shard_map/ppermute | solution.py:412
  133.6 17.2 %collective-permute-start.34 = (bf16[2,256,1024]{2,1,0:T(8,128)(2,1)S(1)}, bf16[2,256,1024]{2,1,0:T(8,128)(2,1)S(1)}, u32[]{:S(2)}, u32[]{:S(2)}) collective-permute-start(bf16[2,256,1024]{2,1,0:T(8,128)(2,1)S(1)} %pad_maximum_fusion.8.refs_13_.refs_21_.refs_12_.refs_14_), channel_id=1, source_target_pairs={{0,4},{4,0},{8,12},{12,8},{1,5},{5,1},{9,13},{13,9},{2,6},{6,2},{1... | collective-permute-start | bytes 3145736 | tf_op jit(solution)/shard_map/ppermute | solution.py:412
  156.0 22.6 %collective-permute-start.36 = (bf16[256,512]{1,0:T(8,128)(2,1)S(1)}, bf16[256,512]{1,0:T(8,128)(2,1)S(1)}, u32[]{:S(2)}, u32[]{:S(2)}) collective-permute-start(bf16[256,512]{1,0:T(8,128)(2,1)S(1)} %copy-done.28), channel_id=1, source_target_pairs={{0,1},{1,2},{2,3},{3,0},{4,5},{5,6},{6,7},{7,4},{8,9},{9,10},{10,1... | collective-permute-start | bytes 786440 | tf_op jit(solution)/shard_map/ppermute | solution.py:407
  157.1 21.5 %collective-permute-start.37 = (bf16[256,512]{1,0:T(8,128)(2,1)S(1)}, bf16[256,512]{1,0:T(8,128)(2,1)S(1)}, u32[]{:S(2)}, u32[]{:S(2)}) collective-permute-start(bf16[256,512]{1,0:T(8,128)(2,1)S(1)} %copy-done.28), channel_id=1, source_target_pairs={{0,3},{1,0},{2,1},{3,2},{4,7},{5,4},{6,5},{7,6},{8,11},{9,8},{10,9... | collective-permute-start | bytes 786440 | tf_op jit(solution)/shard_map/ppermute | solution.py:407
  160.1 19.2 %collective-permute-start.38 = (bf16[256,512]{1,0:T(8,128)(2,1)S(1)}, bf16[256,512]{1,0:T(8,128)(2,1)S(1)}, u32[]{:S(2)}, u32[]{:S(2)}) collective-permute-start(bf16[256,512]{1,0:T(8,128)(2,1)S(1)} %copy-done.28), channel_id=1, source_target_pairs={{0,8},{4,12},{8,0},{12,4},{1,9},{5,13},{9,1},{13,5},{2,10},{6,14},... | collective-permute-start | bytes 786440 | tf_op jit(solution)/shard_map/ppermute | solution.py:412
  160.5 18.7 %collective-permute-start.39 = (bf16[256,1024]{1,0:T(8,128)(2,1)S(1)}, bf16[256,1024]{1,0:T(8,128)(2,1)S(1)}, u32[]{:S(2)}, u32[]{:S(2)}) collective-permute-start(bf16[256,1024]{1,0:T(8,128)(2,1)S(1)} %get-tuple-element.275), channel_id=1, source_target_pairs={{0,8},{4,12},{8,0},{12,4},{1,9},{5,13},{9,1},{13,5},{2,10},{6,14},... | collective-permute-start | bytes 1572872 | tf_op jit(solution)/shard_map/ppermute | solution.py:412
  179.3 31.6 %collective-permute-start.43 = (bf16[256,1024]{1,0:T(8,128)(2,1)S(1)}, bf16[256,1024]{1,0:T(8,128)(2,1)S(1)}, u32[]{:S(2)}, u32[]{:S(2)}) collective-permute-start(bf16[256,1024]{1,0:T(8,128)(2,1)S(1)} %get-tuple-element.275), channel_id=1, source_target_pairs={{0,1},{1,2},{2,3},{3,0},{4,5},{5,6},{6,7},{7,4},{8,9},{9,10},{10,1... | collective-permute-start | bytes 1572872 | tf_op jit(solution)/shard_map/ppermute | solution.py:407
  179.3 31.5 %collective-permute-start.44 = (bf16[256,1024]{1,0:T(8,128)(2,1)S(1)}, bf16[256,1024]{1,0:T(8,128)(2,1)S(1)}, u32[]{:S(2)}, u32[]{:S(2)}) collective-permute-start(bf16[256,1024]{1,0:T(8,128)(2,1)S(1)} %get-tuple-element.275), channel_id=1, source_target_pairs={{0,3},{1,0},{2,1},{3,2},{4,7},{5,4},{6,5},{7,6},{8,11},{9,8},{10,9... | collective-permute-start | bytes 1572872 | tf_op jit(solution)/shard_map/ppermute | solution.py:407
  183.1 23.3 %collective-permute-start.42 = (bf16[128,512]{1,0:T(8,128)(2,1)S(1)}, bf16[128,512]{1,0:T(8,128)(2,1)S(1)}, u32[]{:S(2)}, u32[]{:S(2)}) collective-permute-start(bf16[128,512]{1,0:T(8,128)(2,1)S(1)} %slice.805), channel_id=1, source_target_pairs={{0,3},{1,0},{2,1},{3,2},{4,7},{5,4},{6,5},{7,6},{8,11},{9,8},{10,9... | collective-permute-start | bytes 393224 | tf_op jit(solution)/shard_map/ppermute | solution.py:407
  183.2 27.7 %collective-permute-start.41 = (bf16[128,512]{1,0:T(8,128)(2,1)}, bf16[128,512]{1,0:T(8,128)(2,1)S(1)}, u32[]{:S(2)}, u32[]{:S(2)}) collective-permute-start(bf16[128,512]{1,0:T(8,128)(2,1)} %slice.804), channel_id=1, source_target_pairs={{0,1},{1,2},{2,3},{3,0},{4,5},{5,6},{6,7},{7,4},{8,9},{9,10},{10,1... | collective-permute-start | bytes 393224 | tf_op jit(solution)/shard_map/ppermute | solution.py:407
  185.6 25.3 %collective-permute-start.40 = (bf16[512,1024]{1,0:T(8,128)(2,1)}, bf16[512,1024]{1,0:T(8,128)(2,1)S(1)}, u32[]{:S(2)}, u32[]{:S(2)}) collective-permute-start(bf16[512,1024]{1,0:T(8,128)(2,1)} %get-tuple-element.268), channel_id=1, source_target_pairs={{0,16},{16,0},{1,17},{17,1},{2,18},{18,2},{3,19},{19,3},{4,20},{20... | collective-permute-start | bytes 3145736 | tf_op jit(solution)/shard_map/ppermute | solution.py:412
  214.4 22.7 %collective-permute-start.45 = (bf16[512,1024]{1,0:T(8,128)(2,1)}, bf16[512,1024]{1,0:T(8,128)(2,1)}, u32[]{:S(2)}, u32[]{:S(2)}) collective-permute-start(bf16[512,1024]{1,0:T(8,128)(2,1)} %get-tuple-element.276), channel_id=1, source_target_pairs={{0,16},{16,0},{1,17},{17,1},{2,18},{18,2},{3,19},{19,3},{4,20},{20... | collective-permute-start | bytes 3145736 | tf_op jit(solution)/shard_map/ppermute | solution.py:412
  243.1 19.4 %collective-permute-start.56 = (bf16[2,256,1024]{2,1,0:T(8,128)(2,1)S(1)}, bf16[2,256,1024]{2,1,0:T(8,128)(2,1)}, u32[]{:S(2)}, u32[]{:S(2)}) collective-permute-start(bf16[2,256,1024]{2,1,0:T(8,128)(2,1)S(1)} %pad_maximum_fusion.9.refs_11_.refs_19_.refs_10_.refs_12_), channel_id=1, source_target_pairs={{0,4},{4,0},{8,12},{12,8},{1,5},{5,1},{9,13},{13,9},{2,6},{6,2},{1... | collective-permute-start | bytes 3145736 | tf_op jit(solution)/shard_map/ppermute | solution.py:412
  243.7 17.8 %collective-permute-start.55 = (bf16[256,1024]{1,0:T(8,128)(2,1)S(1)}, bf16[256,1024]{1,0:T(8,128)(2,1)S(1)}, u32[]{:S(2)}, u32[]{:S(2)}) collective-permute-start(bf16[256,1024]{1,0:T(8,128)(2,1)S(1)} %collective-permute-done.43), channel_id=1, source_target_pairs={{0,8},{4,12},{8,0},{12,4},{1,9},{5,13},{9,1},{13,5},{2,10},{6,14},... | collective-permute-start | bytes 1572872 | tf_op jit(solution)/shard_map/ppermute | solution.py:412
  262.5 29.5 %collective-permute-start.60 = (bf16[384,512]{1,0:T(8,128)(2,1)S(1)}, bf16[384,512]{1,0:T(8,128)(2,1)}, u32[]{:S(2)}, u32[]{:S(2)}) collective-permute-start(bf16[384,512]{1,0:T(8,128)(2,1)S(1)} %copy-done.55), channel_id=1, source_target_pairs={{0,1},{1,2},{2,3},{3,0},{4,5},{5,6},{6,7},{7,4},{8,9},{9,10},{10,1... | collective-permute-start | bytes 1179656 | tf_op jit(solution)/shard_map/ppermute | solution.py:407
  262.5 29.5 %collective-permute-start.61 = (bf16[384,512]{1,0:T(8,128)(2,1)}, bf16[384,512]{1,0:T(8,128)(2,1)}, u32[]{:S(2)}, u32[]{:S(2)}) collective-permute-start(bf16[384,512]{1,0:T(8,128)(2,1)} %pad_maximum_fusion.30), channel_id=1, source_target_pairs={{0,3},{1,0},{2,1},{3,2},{4,7},{5,4},{6,5},{7,6},{8,11},{9,8},{10,9... | collective-permute-start | bytes 1179656 | tf_op jit(solution)/shard_map/ppermute | solution.py:407
  266.3 25.7 %collective-permute-start.59 = (bf16[2,256,1024]{2,1,0:T(8,128)(2,1)}, bf16[2,256,1024]{2,1,0:T(8,128)(2,1)}, u32[]{:S(2)}, u32[]{:S(2)}) collective-permute-start(bf16[2,256,1024]{2,1,0:T(8,128)(2,1)} %pad_maximum_fusion.11.refs_12_.refs_20_.refs_11_.refs_13_), channel_id=1, source_target_pairs={{0,4},{4,0},{8,12},{12,8},{1,5},{5,1},{9,13},{13,9},{2,6},{6,2},{1... | collective-permute-start | bytes 3145736 | tf_op jit(solution)/shard_map/ppermute | solution.py:412
  266.3 19.3 %collective-permute-start.58 = (bf16[256,1024]{1,0:T(8,128)(2,1)S(1)}, bf16[256,1024]{1,0:T(8,128)(2,1)S(1)}, u32[]{:S(2)}, u32[]{:S(2)}) collective-permute-start(bf16[256,1024]{1,0:T(8,128)(2,1)S(1)} %constant_dynamic-update-slice_fusion.6), channel_id=1, source_target_pairs={{0,8},{4,12},{8,0},{12,4},{1,9},{5,13},{9,1},{13,5},{2,10},{6,14},... | collective-permute-start | bytes 1572872 | tf_op jit(solution)/shard_map/ppermute | solution.py:412
  267.5 24.4 %collective-permute-start.57 = (bf16[256,1024]{1,0:T(8,128)(2,1)S(1)}, bf16[256,1024]{1,0:T(8,128)(2,1)S(1)}, u32[]{:S(2)}, u32[]{:S(2)}) collective-permute-start(bf16[256,1024]{1,0:T(8,128)(2,1)S(1)} %collective-permute-done.44), channel_id=1, source_target_pairs={{0,8},{4,12},{8,0},{12,4},{1,9},{5,13},{9,1},{13,5},{2,10},{6,14},... | collective-permute-start | bytes 1572872 | tf_op jit(solution)/shard_map/ppermute | solution.py:412
  305.2 23.4 %collective-permute-start.66 = (bf16[4,256,512]{2,1,0:T(8,128)(2,1)S(1)}, bf16[4,256,512]{2,1,0:T(8,128)(2,1)S(1)}, u32[]{:S(2)}, u32[]{:S(2)}) collective-permute-start(bf16[4,256,512]{2,1,0:T(8,128)(2,1)S(1)} %fusion.52), channel_id=1, source_target_pairs={{0,16},{16,0},{1,17},{17,1},{2,18},{18,2},{3,19},{19,3},{4,20},{20... | collective-permute-start | bytes 3145736 | tf_op jit(solution)/shard_map/ppermute | solution.py:412
  328.6 22.6 %collective-permute-start.67 = (bf16[512,1024]{1,0:T(8,128)(2,1)}, bf16[512,1024]{1,0:T(8,128)(2,1)S(1)}, u32[]{:S(2)}, u32[]{:S(2)}) collective-permute-start(bf16[512,1024]{1,0:T(8,128)(2,1)} %get-tuple-element.309), channel_id=1, source_target_pairs={{0,16},{16,0},{1,17},{17,1},{2,18},{18,2},{3,19},{19,3},{4,20},{20... | collective-permute-start | bytes 3145736 | tf_op jit(solution)/shard_map/ppermute | solution.py:412
  366.7 26.6 %collective-permute-start.68 = (bf16[512,1024]{1,0:T(8,128)(2,1)}, bf16[512,1024]{1,0:T(8,128)(2,1)}, u32[]{:S(2)}, u32[]{:S(2)}) collective-permute-start(bf16[512,1024]{1,0:T(8,128)(2,1)} %get-tuple-element.324), channel_id=1, source_target_pairs={{0,16},{16,0},{1,17},{17,1},{2,18},{18,2},{3,19},{19,3},{4,20},{20... | collective-permute-start | bytes 3145736 | tf_op jit(solution)/shard_map/ppermute | solution.py:412
  411.1 30.9 %collective-permute-start.71 = (bf16[384,512]{1,0:T(8,128)(2,1)}, bf16[384,512]{1,0:T(8,128)(2,1)S(1)}, u32[]{:S(2)}, u32[]{:S(2)}) collective-permute-start(bf16[384,512]{1,0:T(8,128)(2,1)} %pad_maximum_fusion.32), channel_id=1, source_target_pairs={{0,3},{1,0},{2,1},{3,2},{4,7},{5,4},{6,5},{7,6},{8,11},{9,8},{10,9... | collective-permute-start | bytes 1179656 | tf_op jit(solution)/shard_map/ppermute | solution.py:407
  413.0 29.0 %collective-permute-start.70 = (bf16[384,512]{1,0:T(8,128)(2,1)}, bf16[384,512]{1,0:T(8,128)(2,1)S(1)}, u32[]{:S(2)}, u32[]{:S(2)}) collective-permute-start(bf16[384,512]{1,0:T(8,128)(2,1)} %pad_maximum_fusion.31), channel_id=1, source_target_pairs={{0,1},{1,2},{2,3},{3,0},{4,5},{5,6},{6,7},{7,4},{8,9},{9,10},{10,1... | collective-permute-start | bytes 1179656 | tf_op jit(solution)/shard_map/ppermute | solution.py:407
  414.7 27.3 %collective-permute-start.69 = (bf16[512,1024]{1,0:T(8,128)(2,1)}, bf16[512,1024]{1,0:T(8,128)(2,1)S(1)}, u32[]{:S(2)}, u32[]{:S(2)}) collective-permute-start(bf16[512,1024]{1,0:T(8,128)(2,1)} %get-tuple-element.344), channel_id=1, source_target_pairs={{0,16},{16,0},{1,17},{17,1},{2,18},{18,2},{3,19},{19,3},{4,20},{20... | collective-permute-start | bytes 3145736 | tf_op jit(solution)/shard_map/ppermute | solution.py:412
  442.8 43.7 %collective-permute-start.73 = (bf16[2,4,256,1024]{3,2,1,0:T(8,128)(2,1)}, bf16[2,4,256,1024]{3,2,1,0:T(8,128)(2,1)}, u32[]{:S(2)}, u32[]{:S(2)}) collective-permute-start(bf16[2,4,256,1024]{3,2,1,0:T(8,128)(2,1)} %get-tuple-element.339), channel_id=1, source_target_pairs={{0,4},{4,0},{8,12},{12,8},{1,5},{5,1},{9,13},{13,9},{2,6},{6,2},{1... | collective-permute-start | bytes 12582920 | tf_op jit(solution)/shard_map/ppermute | solution.py:412
  461.1 20.2 %collective-permute-start.74 = (bf16[384,512]{1,0:T(8,128)(2,1)}, bf16[384,512]{1,0:T(8,128)(2,1)}, u32[]{:S(2)}, u32[]{:S(2)}) collective-permute-start(bf16[384,512]{1,0:T(8,128)(2,1)} %pad_maximum_fusion.33), channel_id=1, source_target_pairs={{0,1},{1,2},{2,3},{3,0},{4,5},{5,6},{6,7},{7,4},{8,9},{9,10},{10,1... | collective-permute-start | bytes 1179656 | tf_op jit(solution)/shard_map/ppermute | solution.py:407
  461.1 25.4 %collective-permute-start.72 = (bf16[512,1024]{1,0:T(8,128)(2,1)S(1)}, bf16[512,1024]{1,0:T(8,128)(2,1)}, u32[]{:S(2)}, u32[]{:S(2)}) collective-permute-start(bf16[512,1024]{1,0:T(8,128)(2,1)S(1)} %copy-done.31), channel_id=1, source_target_pairs={{0,16},{16,0},{1,17},{17,1},{2,18},{18,2},{3,19},{19,3},{4,20},{20... | collective-permute-start | bytes 3145736 | tf_op jit(solution)/shard_map/ppermute | solution.py:412
  486.5 30.9 %collective-permute-start.81 = (bf16[128,512]{1,0:T(8,128)(2,1)}, bf16[128,512]{1,0:T(8,128)(2,1)S(1)}, u32[]{:S(2)}, u32[]{:S(2)}) collective-permute-start(bf16[128,512]{1,0:T(8,128)(2,1)} %slice.825), channel_id=1, source_target_pairs={{0,3},{1,0},{2,1},{3,2},{4,7},{5,4},{6,5},{7,6},{8,11},{9,8},{10,9... | collective-permute-start | bytes 393224 | tf_op jit(solution)/shard_map/ppermute | solution.py:407
  490.0 30.8 %collective-permute-start.80 = (bf16[128,512]{1,0:T(8,128)(2,1)S(1)}, bf16[128,512]{1,0:T(8,128)(2,1)S(1)}, u32[]{:S(2)}, u32[]{:S(2)}) collective-permute-start(bf16[128,512]{1,0:T(8,128)(2,1)S(1)} %slice.824), channel_id=1, source_target_pairs={{0,1},{1,2},{2,3},{3,0},{4,5},{5,6},{6,7},{7,4},{8,9},{9,10},{10,1... | collective-permute-start | bytes 393224 | tf_op jit(solution)/shard_map/ppermute | solution.py:407
  490.0 30.8 %collective-permute-start.79 = (bf16[128,512]{1,0:T(8,128)(2,1)}, bf16[128,512]{1,0:T(8,128)(2,1)S(1)}, u32[]{:S(2)}, u32[]{:S(2)}) collective-permute-start(bf16[128,512]{1,0:T(8,128)(2,1)} %slice.823), channel_id=1, source_target_pairs={{0,3},{1,0},{2,1},{3,2},{4,7},{5,4},{6,5},{7,6},{8,11},{9,8},{10,9... | collective-permute-start | bytes 393224 | tf_op jit(solution)/shard_map/ppermute | solution.py:407
  495.8 29.4 %collective-permute-start.77 = (bf16[2,256,1024]{2,1,0:T(8,128)(2,1)S(1)}, bf16[2,256,1024]{2,1,0:T(8,128)(2,1)}, u32[]{:S(2)}, u32[]{:S(2)}) collective-permute-start(bf16[2,256,1024]{2,1,0:T(8,128)(2,1)S(1)} %fusion.16), channel_id=1, source_target_pairs={{0,8},{4,12},{8,0},{12,4},{1,9},{5,13},{9,1},{13,5},{2,10},{6,14},... | collective-permute-start | bytes 3145736 | tf_op jit(solution)/shard_map/ppermute | solution.py:412
  497.0 28.1 %collective-permute-start.76 = (bf16[2,4,256,512]{3,2,1,0:T(8,128)(2,1)}, bf16[2,4,256,512]{3,2,1,0:T(8,128)(2,1)}, u32[]{:S(2)}, u32[]{:S(2)}) collective-permute-start(bf16[2,4,256,512]{3,2,1,0:T(8,128)(2,1)} %get-tuple-element.351), channel_id=1, source_target_pairs={{0,4},{4,0},{8,12},{12,8},{1,5},{5,1},{9,13},{13,9},{2,6},{6,2},{1... | collective-permute-start | bytes 6291464 | tf_op jit(solution)/shard_map/ppermute | solution.py:412
  526.9 25.0 %collective-permute-start.82 = (bf16[2,256,1024]{2,1,0:T(8,128)(2,1)S(1)}, bf16[2,256,1024]{2,1,0:T(8,128)(2,1)}, u32[]{:S(2)}, u32[]{:S(2)}) collective-permute-start(bf16[2,256,1024]{2,1,0:T(8,128)(2,1)S(1)} %fusion.15), channel_id=1, source_target_pairs={{0,8},{4,12},{8,0},{12,4},{1,9},{5,13},{9,1},{13,5},{2,10},{6,14},... | collective-permute-start | bytes 3145736 | tf_op jit(solution)/shard_map/ppermute | solution.py:412
  551.8 38.1 %collective-permute-start.85 = (bf16[2,4,256,1024]{3,2,1,0:T(8,128)(2,1)}, bf16[2,4,256,1024]{3,2,1,0:T(8,128)(2,1)}, u32[]{:S(2)}, u32[]{:S(2)}) collective-permute-start(bf16[2,4,256,1024]{3,2,1,0:T(8,128)(2,1)} %get-tuple-element.370), channel_id=1, source_target_pairs={{0,4},{4,0},{8,12},{12,8},{1,5},{5,1},{9,13},{13,9},{2,6},{6,2},{1... | collective-permute-start | bytes 12582920 | tf_op jit(solution)/shard_map/ppermute | solution.py:412
  557.8 32.1 %collective-permute-start.86 = (bf16[4,256,512]{2,1,0:T(8,128)(2,1)}, bf16[4,256,512]{2,1,0:T(8,128)(2,1)}, u32[]{:S(2)}, u32[]{:S(2)}) collective-permute-start(bf16[4,256,512]{2,1,0:T(8,128)(2,1)} %fusion.12), channel_id=1, source_target_pairs={{0,8},{4,12},{8,0},{12,4},{1,9},{5,13},{9,1},{13,5},{2,10},{6,14},... | collective-permute-start | bytes 3145736 | tf_op jit(solution)/shard_map/ppermute | solution.py:412
  560.9 29.0 %collective-permute-start.84 = (bf16[128,1024]{1,0:T(8,128)(2,1)S(1)}, bf16[128,1024]{1,0:T(8,128)(2,1)S(1)}, u32[]{:S(2)}, u32[]{:S(2)}) collective-permute-start(bf16[128,1024]{1,0:T(8,128)(2,1)S(1)} %get-tuple-element.368), channel_id=1, source_target_pairs={{0,3},{1,0},{2,1},{3,2},{4,7},{5,4},{6,5},{7,6},{8,11},{9,8},{10,9... | collective-permute-start | bytes 786440 | tf_op jit(solution)/shard_map/ppermute | solution.py:407
  560.9 28.0 %collective-permute-start.83 = (bf16[128,1024]{1,0:T(8,128)(2,1)S(1)}, bf16[128,1024]{1,0:T(8,128)(2,1)S(1)}, u32[]{:S(2)}, u32[]{:S(2)}) collective-permute-start(bf16[128,1024]{1,0:T(8,128)(2,1)S(1)} %get-tuple-element.367), channel_id=1, source_target_pairs={{0,1},{1,2},{2,3},{3,0},{4,5},{5,6},{6,7},{7,4},{8,9},{9,10},{10,1... | collective-permute-start | bytes 786440 | tf_op jit(solution)/shard_map/ppermute | solution.py:407
  603.7 24.7 %collective-permute-start.89 = (bf16[256,1024]{1,0:T(8,128)(2,1)}, bf16[256,1024]{1,0:T(8,128)(2,1)S(1)}, u32[]{:S(2)}, u32[]{:S(2)}) collective-permute-start(bf16[256,1024]{1,0:T(8,128)(2,1)} %pad_maximum_fusion.24), channel_id=1, source_target_pairs={{0,3},{1,0},{2,1},{3,2},{4,7},{5,4},{6,5},{7,6},{8,11},{9,8},{10,9... | collective-permute-start | bytes 1572872 | tf_op jit(solution)/shard_map/ppermute | solution.py:407
  605.5 23.6 %collective-permute-start.88 = (bf16[256,1024]{1,0:T(8,128)(2,1)}, bf16[256,1024]{1,0:T(8,128)(2,1)}, u32[]{:S(2)}, u32[]{:S(2)}) collective-permute-start(bf16[256,1024]{1,0:T(8,128)(2,1)} %pad_maximum_fusion.23), channel_id=1, source_target_pairs={{0,1},{1,2},{2,3},{3,0},{4,5},{5,6},{6,7},{7,4},{8,9},{9,10},{10,1... | collective-permute-start | bytes 1572872 | tf_op jit(solution)/shard_map/ppermute | solution.py:407
  608.7 24.9 %collective-permute-start.87 = (bf16[2,256,1024]{2,1,0:T(8,128)(2,1)}, bf16[2,256,1024]{2,1,0:T(8,128)(2,1)}, u32[]{:S(2)}, u32[]{:S(2)}) collective-permute-start(bf16[2,256,1024]{2,1,0:T(8,128)(2,1)} %fusion.17), channel_id=1, source_target_pairs={{0,8},{4,12},{8,0},{12,4},{1,9},{5,13},{9,1},{13,5},{2,10},{6,14},... | collective-permute-start | bytes 3145736 | tf_op jit(solution)/shard_map/ppermute | solution.py:412
  609.9 48.4 %collective-permute-start.90 = (bf16[512,1024]{1,0:T(8,128)(2,1)}, bf16[512,1024]{1,0:T(8,128)(2,1)}, u32[]{:S(2)}, u32[]{:S(2)}) collective-permute-start(bf16[512,1024]{1,0:T(8,128)(2,1)} %get-tuple-element.396), channel_id=1, source_target_pairs={{0,16},{16,0},{1,17},{17,1},{2,18},{18,2},{3,19},{19,3},{4,20},{20... | collective-permute-start | bytes 3145736 | tf_op jit(solution)/shard_map/ppermute | solution.py:412
  633.6 22.2 %collective-permute-start.94 = (bf16[128,512]{1,0:T(8,128)(2,1)}, bf16[128,512]{1,0:T(8,128)(2,1)}, u32[]{:S(2)}, u32[]{:S(2)}) collective-permute-start(bf16[128,512]{1,0:T(8,128)(2,1)} %get-tuple-element.390), channel_id=1, source_target_pairs={{0,3},{1,0},{2,1},{3,2},{4,7},{5,4},{6,5},{7,6},{8,11},{9,8},{10,9... | collective-permute-start | bytes 393224 | tf_op jit(solution)/shard_map/ppermute | solution.py:407
  637.1 18.6 %collective-permute-start.93 = (bf16[128,512]{1,0:T(8,128)(2,1)}, bf16[128,512]{1,0:T(8,128)(2,1)}, u32[]{:S(2)}, u32[]{:S(2)}) collective-permute-start(bf16[128,512]{1,0:T(8,128)(2,1)} %get-tuple-element.389), channel_id=1, source_target_pairs={{0,1},{1,2},{2,3},{3,0},{4,5},{5,6},{6,7},{7,4},{8,9},{9,10},{10,1... | collective-permute-start | bytes 393224 | tf_op jit(solution)/shard_map/ppermute | solution.py:407
  638.8 23.4 %collective-permute-start.92 = (bf16[2,256,1024]{2,1,0:T(8,128)(2,1)S(1)}, bf16[2,256,1024]{2,1,0:T(8,128)(2,1)}, u32[]{:S(2)}, u32[]{:S(2)}) collective-permute-start(bf16[2,256,1024]{2,1,0:T(8,128)(2,1)S(1)} %fusion.9), channel_id=1, source_target_pairs={{0,8},{4,12},{8,0},{12,4},{1,9},{5,13},{9,1},{13,5},{2,10},{6,14},... | collective-permute-start | bytes 3145736 | tf_op jit(solution)/shard_map/ppermute | solution.py:412
  640.0 23.3 %collective-permute-start.91 = (bf16[512,1024]{1,0:T(8,128)(2,1)}, bf16[512,1024]{1,0:T(8,128)(2,1)}, u32[]{:S(2)}, u32[]{:S(2)}) collective-permute-start(bf16[512,1024]{1,0:T(8,128)(2,1)} %get-tuple-element.397), channel_id=1, source_target_pairs={{0,16},{16,0},{1,17},{17,1},{2,18},{18,2},{3,19},{19,3},{4,20},{20... | collective-permute-start | bytes 3145736 | tf_op jit(solution)/shard_map/ppermute | solution.py:412
  674.9 19.0 %collective-permute-start.97 = (bf16[2,4,256,512]{3,2,1,0:T(8,128)(2,1)}, bf16[2,4,256,512]{3,2,1,0:T(8,128)(2,1)S(1)}, u32[]{:S(2)}, u32[]{:S(2)}) collective-permute-start(bf16[2,4,256,512]{3,2,1,0:T(8,128)(2,1)} %get-tuple-element.395), channel_id=1, source_target_pairs={{0,4},{4,0},{8,12},{12,8},{1,5},{5,1},{9,13},{13,9},{2,6},{6,2},{1... | collective-permute-start | bytes 6291464 | tf_op jit(solution)/shard_map/ppermute | solution.py:412
  699.5 30.6 %collective-permute-start.100 = (bf16[256,1024]{1,0:T(8,128)(2,1)S(1)}, bf16[256,1024]{1,0:T(8,128)(2,1)S(1)}, u32[]{:S(2)}, u32[]{:S(2)}) collective-permute-start(bf16[256,1024]{1,0:T(8,128)(2,1)S(1)} %pad_maximum_fusion.26), channel_id=1, source_target_pairs={{0,3},{1,0},{2,1},{3,2},{4,7},{5,4},{6,5},{7,6},{8,11},{9,8},{10,9... | collective-permute-start | bytes 1572872 | tf_op jit(solution)/shard_map/ppermute | solution.py:407
  703.2 27.0 %collective-permute-start.99 = (bf16[256,1024]{1,0:T(8,128)(2,1)S(1)}, bf16[256,1024]{1,0:T(8,128)(2,1)S(1)}, u32[]{:S(2)}, u32[]{:S(2)}) collective-permute-start(bf16[256,1024]{1,0:T(8,128)(2,1)S(1)} %pad_maximum_fusion.25), channel_id=1, source_target_pairs={{0,1},{1,2},{2,3},{3,0},{4,5},{5,6},{6,7},{7,4},{8,9},{9,10},{10,1... | collective-permute-start | bytes 1572872 | tf_op jit(solution)/shard_map/ppermute | solution.py:407
  708.3 23.2 %collective-permute-start.101 = (bf16[4,256,512]{2,1,0:T(8,128)(2,1)S(1)}, bf16[4,256,512]{2,1,0:T(8,128)(2,1)S(1)}, u32[]{:S(2)}, u32[]{:S(2)}) collective-permute-start(bf16[4,256,512]{2,1,0:T(8,128)(2,1)S(1)} %fusion.2), channel_id=1, source_target_pairs={{0,8},{4,12},{8,0},{12,4},{1,9},{5,13},{9,1},{13,5},{2,10},{6,14},... | collective-permute-start | bytes 3145736 | tf_op jit(solution)/shard_map/ppermute | solution.py:412
  750.2 38.5 %collective-permute-start.109 = (bf16[384,1024]{1,0:T(8,128)(2,1)}, bf16[384,1024]{1,0:T(8,128)(2,1)}, u32[]{:S(2)}, u32[]{:S(2)}) collective-permute-start(bf16[384,1024]{1,0:T(8,128)(2,1)} %pad_maximum_fusion.14), channel_id=1, source_target_pairs={{0,3},{1,0},{2,1},{3,2},{4,7},{5,4},{6,5},{7,6},{8,11},{9,8},{10,9... | collective-permute-start | bytes 2359304 | tf_op jit(solution)/shard_map/ppermute | solution.py:407
  752.0 36.7 %collective-permute-start.108 = (bf16[384,1024]{1,0:T(8,128)(2,1)}, bf16[384,1024]{1,0:T(8,128)(2,1)}, u32[]{:S(2)}, u32[]{:S(2)}) collective-permute-start(bf16[384,1024]{1,0:T(8,128)(2,1)} %pad_maximum_fusion.13), channel_id=1, source_target_pairs={{0,1},{1,2},{2,3},{3,0},{4,5},{5,6},{6,7},{7,4},{8,9},{9,10},{10,1... | collective-permute-start | bytes 2359304 | tf_op jit(solution)/shard_map/ppermute | solution.py:407
  789.4 17.3 %collective-permute-start.117 = (bf16[256,512]{1,0:T(8,128)(2,1)S(1)}, bf16[256,512]{1,0:T(8,128)(2,1)S(1)}, u32[]{:S(2)}, u32[]{:S(2)}) collective-permute-start(bf16[256,512]{1,0:T(8,128)(2,1)S(1)} %copy-done.56), channel_id=1, source_target_pairs={{0,16},{16,0},{1,17},{17,1},{2,18},{18,2},{3,19},{19,3},{4,20},{20... | collective-permute-start | bytes 786440 | tf_op jit(solution)/shard_map/ppermute | solution.py:412
  790.9 18.4 %collective-permute-start.113 = (bf16[128,1024]{1,0:T(8,128)(2,1)S(1)}, bf16[128,1024]{1,0:T(8,128)(2,1)S(1)}, u32[]{:S(2)}, u32[]{:S(2)}) collective-permute-start(bf16[128,1024]{1,0:T(8,128)(2,1)S(1)} %slice.867), channel_id=1, source_target_pairs={{0,1},{1,2},{2,3},{3,0},{4,5},{5,6},{6,7},{7,4},{8,9},{9,10},{10,1... | collective-permute-start | bytes 786440 | tf_op jit(solution)/shard_map/ppermute | solution.py:407
  (154 other events, 1545.8 us)

commit v8 on v7

--- a/solution.py
+++ b/solution.py
@@ -398,7 +398,7 @@
 VMEM_LIMIT = 60 * 1024 * 1024
 ROW_BLOCK = 256
 CHUNKS = 2
-COLUMN_STEP = 512
+COLUMN_STEP = 2048
 MICROSECOND = 1_000_000_000
 
 

time: 819 us -> 819 us (level)
  transfers between devices with their start and end apart: 118 -> 118, of which waited for: 37 -> 38; matrix products, arithmetic and copies ran while one was open for 18% -> 18% of each run, Pallas kernels for 33% -> 33%
where the time goes in v8:
time: 819 us; the launch traced here: 810 us
  Pallas kernels  303 us (37%)
  waiting for transfers between devices  193 us (24%)
  starting transfers between devices  121 us (15%)
  other arithmetic  94.1 us (11%)
  local copies, waits for them, and re-layouts  87 us (11%)
  between operations  11.5 us (1%)
    pallas_call x24, Pallas kernels, call(): pl.pallas_call(run, name=name, grid=grid, in_specs=[pl.BlockSpec(block, i...  303 us
    ppermute x52, waiting for transfers between devices, ring(): lax.ppermute(value, axis, [(i, (i + by) % length) for i in range(length)])  114 us
    ppermute x66, waiting for transfers between devices, swap(): return lax.ppermute(value, axis, [(i, i ^ bit) for i in range(length)])  78.9 us
    ppermute x52, starting transfers between devices, ring(): lax.ppermute(value, axis, [(i, (i + by) % length) for i in range(length)])  78.2 us
    ppermute x66, starting transfers between devices, swap(): return lax.ppermute(value, axis, [(i, i ^ bit) for i in range(length)])  42.5 us
  transfers between devices with their start and end apart: 118, of which 38 were waited for; matrix products, arithmetic and copies ran while one was open for 18% of the time, Pallas kernels for 33%

profile of v8, /device:TPU:0, one launch (start us, length us, event | category | flops | bytes accessed | tf_op | source)
XLA Modules:
  0.0 809.6 jit_solution(16432944808616848368)
XLA Ops:
  27.9 3.8 collective-permute-start.7
  41.4 4.1 collective-permute-done.4
  45.5 4.9 collective-permute-done.5
  60.3 4.8 collective-permute-done.18
  67.2 3.5 collective-permute-start.27
  78.0 4.0 collective-permute-done.27
  85.5 3.6 collective-permute-done.25
  95.3 6.4 norm_qkv.4
  101.6 6.4 norm_qkv.5
  112.8 17.2 %attend.2 = (bf16[1024,512]{1,0:T(8,128)(2,1)}, f32[4,8,1024]{2,1,0:T(8,128)}) custom-call(bf16[1024,1536]{1,0:T(8,128)(2,1)} %get-tuple-element.252.refs_0_.refs_1_.refs_2_, bf16[1024,1536]{1,0:T(8,128)(2,1)} %get-tuple-element.252.refs_0_.refs_1_.refs_2_, bf16[1024,1536]{1,0:T(8,128)(2,1)} %get-tuple-element.252.refs_0_.refs_1_.refs_2_), custom_call_target="tpu_custom_call" | custom-call | flops 19000000512 | bytes 1048576 | tf_op jit(solution)/shard_map/attend/pallas_call | solution.py:536
  136.9 13.8 %collective-permute-done.31 = bf16[256,1024]{1,0:T(8,128)(2,1)S(1)} collective-permute-done((bf16[256,1024]{1,0:T(8,128)(2,1)S(1)}, bf16[256,1024]{1,0:T(8,128)(2,1)S(1)}, u32[]{:S(2)}, u32[]{:S(2)}) %collective-permute-start.31) | collective-permute-done | bytes 524320 | tf_op jit(solution)/shard_map/ppermute | solution.py:412
  162.1 15.7 %mlp_out.4 = (bf16[1024,2048]{1,0:T(8,128)(2,1)}, bf16[1024,2048]{1,0:T(8,128)(2,1)}, bf16[512,1024]{1,0:T(8,128)(2,1)}) custom-call(bf16[1024,512]{1,0:T(8,128)(2,1)} %get-tuple-element.269.refs_0_.refs_4_, bf16[1024,1024]{1,0:T(8,128)(2,1)} %get-tuple-element.358.refs_1_.refs_0_, f32[1,2048]{1,0:T(1,128)} %bitcast.478, ...), custom_call_target="tpu_custom_call" | custom-call | flops 16000000000 | bytes 1048576 | tf_op jit(solution)/shard_map/mlp_out/pallas_call | solution.py:536
  179.1 3.8 collective-permute-start.44
  186.0 15.7 %mlp_out.5 = (bf16[1024,2048]{1,0:T(8,128)(2,1)}, bf16[1024,2048]{1,0:T(8,128)(2,1)}, bf16[512,1024]{1,0:T(8,128)(2,1)}) custom-call(bf16[1024,512]{1,0:T(8,128)(2,1)} %get-tuple-element.269.refs_0_.refs_4_, bf16[1024,1024]{1,0:T(8,128)(2,1)} %get-tuple-element.358.refs_1_.refs_0_, ...), custom_call_target="tpu_custom_call", output_to_operand_aliasing={{0}: (27, {}), {1}: (28, {})} | custom-call | flops 16000000000 | bytes 1048576 | tf_op jit(solution)/shard_map/mlp_out/pallas_call | solution.py:536
  201.7 4.4 collective-permute-done.42
  206.1 4.2 collective-permute-done.41
  228.1 3.7 collective-permute-done.48
  232.0 4.2 collective-permute-done.45
  237.4 4.8 add_convert_fusion.9
  245.8 6.4 norm_qkv.6
  252.2 6.3 norm_qkv.7
  261.6 3.8 collective-permute-start.61
  267.4 17.2 %attend.3 = (bf16[1024,512]{1,0:T(8,128)(2,1)}, f32[4,8,1024]{2,1,0:T(8,128)}) custom-call(bf16[1024,1536]{1,0:T(8,128)(2,1)} %get-tuple-element.295.refs_0_.refs_1_.refs_2_, bf16[1024,1536]{1,0:T(8,128)(2,1)} %get-tuple-element.295.refs_0_.refs_1_.refs_2_, bf16[1024,1536]{1,0:T(8,128)(2,1)} %get-tuple-element.295.refs_0_.refs_1_.refs_2_), custom_call_target="tpu_custom_call" | custom-call | flops 19000000512 | bytes 1048576 | tf_op jit(solution)/shard_map/attend/pallas_call | solution.py:536
  284.8 6.2 collective-permute-done.57
  298.9 5.3 collective-permute-done.65
  304.9 16.1 %mlp_out.6 = (bf16[1024,2048]{1,0:T(8,128)(2,1)}, bf16[1024,2048]{1,0:T(8,128)(2,1)}, bf16[512,1024]{1,0:T(8,128)(2,1)}) custom-call(bf16[1024,512]{1,0:T(8,128)(2,1)} %get-tuple-element.310.refs_0_.refs_3_, bf16[1024,1024]{1,0:T(8,128)(2,1)} %get-tuple-element.329.refs_1_.refs_0_, f32[1,2048]{1,0:T(1,128)} %bitcast.476, ...), custom_call_target="tpu_custom_call" | custom-call | flops 16000000000 | bytes 1048576 | tf_op jit(solution)/shard_map/mlp_out/pallas_call | solution.py:536
  321.0 6.7 collective-permute-done.66
  330.9 15.7 %mlp_out.7 = (bf16[1024,2048]{1,0:T(8,128)(2,1)}, bf16[1024,2048]{1,0:T(8,128)(2,1)}, bf16[512,1024]{1,0:T(8,128)(2,1)}) custom-call(bf16[1024,512]{1,0:T(8,128)(2,1)} %get-tuple-element.310.refs_0_.refs_3_, bf16[1024,1024]{1,0:T(8,128)(2,1)} %get-tuple-element.329.refs_1_.refs_0_, ...), custom_call_target="tpu_custom_call", output_to_operand_aliasing={{0}: (27, {}), {1}: (28, {})} | custom-call | flops 16000000000 | bytes 1048576 | tf_op jit(solution)/shard_map/mlp_out/pallas_call | solution.py:536
  346.6 3.7 collective-permute-done.67
  350.3 7.9 mlp_back.4
  358.2 7.6 mlp_back.5
  366.4 26.0 %attend_back.2 = (bf16[1024,1536]{1,0:T(8,128)(2,1)}, f32[1,1536]{1,0:T(1,128)}) custom-call(bf16[1024,1536]{1,0:T(8,128)(2,1)} %get-tuple-element.295.refs_0_.refs_1_.refs_2_, bf16[1024,1536]{1,0:T(8,128)(2,1)} %get-tuple-element.295.refs_0_.refs_1_.refs_2_, bf16[1024,1536]{1,0:T(8,128)(2,1)} %get-tuple-element.295.refs_0_.refs_1_.refs_2_, ...), custom_call_target="tpu_custom_call" | custom-call | flops 25999998976 | bytes 1048576 | tf_op jit(solution)/shard_map/attend_back/pallas_call | solution.py:536
  392.4 3.4 add_convert_fusion.7
  398.8 10.6 %norm_back.4 = (bf16[512,1024]{1,0:T(8,128)(2,1)}, f32[8,1024]{1,0:T(8,128)}) custom-call(bf16[512,1024]{1,0:T(8,128)(2,1)} %get-tuple-element.284.refs_0_, bf16[1024,1536]{1,0:T(8,128)(2,1)} %get-tuple-element.327.refs_1_.refs_2_, bf16[1024,2048]{1,0:T(8,128)(2,1)} %get-tuple-element.319.refs_2_, f32[8,1024]{1,0:T(8,128)} %concatenate.218.refs_1_.refs_3_, ...), custom_call_target="tpu_custom_call" | custom-call | flops 10499999744 | bytes 1048576 | tf_op jit(solution)/shard_map/norm_back/pallas_call | solution.py:536
  415.3 15.1 %weight_grad.4 = (bf16[2,4,256,1024]{3,2,1,0:T(8,128)(2,1)}, bf16[2,4,256,1024]{3,2,1,0:T(8,128)(2,1)}) custom-call(bf16[1024,1024]{1,0:T(8,128)(2,1)} %get-tuple-element.329.refs_1_.refs_0_, bf16[1024,1024]{1,0:T(8,128)(2,1)} %pad_maximum_fusion.1.refs_0_.refs_1_, bf16[1024,2048]{1,0:T(8,128)(2,1)} %get-tuple-element.319.refs_2_, ...), custom_call_target="tpu_custom_call" | custom-call | flops 14000000000 | bytes 1048576 | tf_op jit(solution)/shard_map/weight_grad/pallas_call | solution.py:536
  430.4 10.6 %norm_back.5 = (bf16[512,1024]{1,0:T(8,128)(2,1)}, f32[8,1024]{1,0:T(8,128)}) custom-call(bf16[512,1024]{1,0:T(8,128)(2,1)} %get-tuple-element.479.refs_0_, bf16[1024,1536]{1,0:T(8,128)(2,1)} %get-tuple-element.327.refs_1_.refs_2_, bf16[1024,2048]{1,0:T(8,128)(2,1)} %get-tuple-element.319.refs_2_, f32[8,1024]{1,0:T(8,128)} %concatenate.218.refs_1_.refs_3_, ...), custom_call_target="tpu_custom_call" | custom-call | flops 10499999744 | bytes 1048576 | tf_op jit(solution)/shard_map/norm_back/pallas_call | solution.py:536
  456.9 3.3 collective-permute-start.75
  460.7 12.1 %weight_grad.5 = (bf16[2,4,256,512]{3,2,1,0:T(8,128)(2,1)}, bf16[2,4,256,512]{3,2,1,0:T(8,128)(2,1)}) custom-call(bf16[1024,1024]{1,0:T(8,128)(2,1)} %get-tuple-element.335.refs_0_, bf16[1024,1024]{1,0:T(8,128)(2,1)} %pad_maximum_fusion.1.refs_0_.refs_1_, bf16[1024,1536]{1,0:T(8,128)(2,1)} %get-tuple-element.327.refs_1_.refs_2_, ...), custom_call_target="tpu_custom_call" | custom-call | flops 14000000000 | bytes 1048576 | tf_op jit(solution)/shard_map/weight_grad/pallas_call | solution.py:536
  473.6 6.8 collective-permute-done.74
  481.3 4.2 collective-permute-done.72
  485.6 3.5 collective-permute-start.81
  489.1 3.8 collective-permute-start.79
  496.1 4.7 add_convert_fusion.4
  500.9 8.0 mlp_back.6
  508.8 7.6 mlp_back.7
  519.9 4.4 collective-permute-done.78
  526.9 14.9 %weight_grad.6 = (bf16[2,4,256,1024]{3,2,1,0:T(8,128)(2,1)}, bf16[2,4,256,1024]{3,2,1,0:T(8,128)(2,1)}) custom-call(bf16[1024,1024]{1,0:T(8,128)(2,1)} %get-tuple-element.358.refs_1_.refs_0_, bf16[512,1024]{1,0:T(8,128)(2,1)} %get-tuple-element.345.refs_0_.refs_1_, bf16[512,1024]{1,0:T(8,128)(2,1)} %get-tuple-element.497.refs_0_.refs_2_, ...), custom_call_target="tpu_custom_call" | custom-call | flops 14000000000 | bytes 1048576 | tf_op jit(solution)/shard_map/weight_grad/pallas_call | solution.py:536
  541.8 9.1 %collective-permute-done.82 = bf16[2,256,1024]{2,1,0:T(8,128)(2,1)} collective-permute-done((bf16[2,256,1024]{2,1,0:T(8,128)(2,1)S(1)}, bf16[2,256,1024]{2,1,0:T(8,128)(2,1)}, u32[]{:S(2)}, u32[]{:S(2)}) %collective-permute-start.82) | collective-permute-done | bytes 1048608 | tf_op jit(solution)/shard_map/ppermute | solution.py:412
  562.1 26.0 %attend_back.3 = (bf16[1024,1536]{1,0:T(8,128)(2,1)}, f32[1,1536]{1,0:T(1,128)}) custom-call(bf16[1024,1536]{1,0:T(8,128)(2,1)} %get-tuple-element.252.refs_0_.refs_1_.refs_2_, bf16[1024,1536]{1,0:T(8,128)(2,1)} %get-tuple-element.252.refs_0_.refs_1_.refs_2_, bf16[1024,1536]{1,0:T(8,128)(2,1)} %get-tuple-element.252.refs_0_.refs_1_.refs_2_, ...), custom_call_target="tpu_custom_call" | custom-call | flops 25999998976 | bytes 1048576 | tf_op jit(solution)/shard_map/attend_back/pallas_call | solution.py:536
  589.0 10.7 %norm_back.6 = (bf16[512,1024]{1,0:T(8,128)(2,1)}, f32[8,1024]{1,0:T(8,128)}) custom-call(bf16[1024,1024]{1,0:T(8,128)(2,1)} %pad_maximum_fusion.refs_0_, bf16[1024,1536]{1,0:T(8,128)(2,1)} %get-tuple-element.376.refs_1_.refs_3_, bf16[1024,2048]{1,0:T(8,128)(2,1)} %get-tuple-element.348.refs_3_.refs_2_, f32[8,1024]{1,0:T(8,128)} %concatenate.212.refs_1_.refs_3_, ...), custom_call_target="tpu_custom_call" | custom-call | flops 10499999744 | bytes 1048576 | tf_op jit(solution)/shard_map/norm_back/pallas_call | solution.py:536
  611.5 10.8 %norm_back.7 = (bf16[512,1024]{1,0:T(8,128)(2,1)}, f32[8,1024]{1,0:T(8,128)}) custom-call(bf16[1024,1024]{1,0:T(8,128)(2,1)} %pad_maximum_fusion.refs_0_, bf16[1024,1536]{1,0:T(8,128)(2,1)} %get-tuple-element.376.refs_1_.refs_3_, bf16[1024,2048]{1,0:T(8,128)(2,1)} %get-tuple-element.348.refs_3_.refs_2_, f32[8,1024]{1,0:T(8,128)} %concatenate.212.refs_1_.refs_3_, ...), custom_call_target="tpu_custom_call" | custom-call | flops 10499999744 | bytes 1048576 | tf_op jit(solution)/shard_map/norm_back/pallas_call | solution.py:536
  623.9 3.5 slice_bitcast_fusion.11
  628.2 4.5 collective-permute-done.87
  632.7 3.5 collective-permute-start.94
  639.6 12.1 %weight_grad.7 = (bf16[2,4,256,512]{3,2,1,0:T(8,128)(2,1)}, bf16[2,4,256,512]{3,2,1,0:T(8,128)(2,1)}) custom-call(bf16[1024,1024]{1,0:T(8,128)(2,1)} %get-tuple-element.382.refs_0_, bf16[512,1024]{1,0:T(8,128)(2,1)} %get-tuple-element.345.refs_0_.refs_1_, bf16[512,1024]{1,0:T(8,128)(2,1)} %get-tuple-element.497.refs_0_.refs_2_, ...), custom_call_target="tpu_custom_call" | custom-call | flops 14000000000 | bytes 1048576 | tf_op jit(solution)/shard_map/weight_grad/pallas_call | solution.py:536
  657.3 4.0 collective-permute-done.92
  677.2 3.6 collective-permute-start.96
  681.8 11.1 %collective-permute-done.95 = bf16[128,1024]{1,0:T(8,128)(2,1)S(1)} collective-permute-done((bf16[128,1024]{1,0:T(8,128)(2,1)S(1)}, bf16[128,1024]{1,0:T(8,128)(2,1)S(1)}, u32[]{:S(2)}, u32[]{:S(2)}) %collective-permute-start.95) | collective-permute-done | bytes 262176 | tf_op jit(solution)/shard_map/ppermute | solution.py:407
  698.6 3.7 collective-permute-start.100
  708.7 20.6 %collective-permute-done.100 = bf16[256,1024]{1,0:T(8,128)(2,1)S(1)} collective-permute-done((bf16[256,1024]{1,0:T(8,128)(2,1)S(1)}, bf16[256,1024]{1,0:T(8,128)(2,1)S(1)}, u32[]{:S(2)}, u32[]{:S(2)}) %collective-permute-start.100) | collective-permute-done | bytes 524320 | tf_op jit(solution)/shard_map/ppermute | solution.py:407
  737.8 5.3 collective-permute-done.105
  751.3 4.9 collective-permute-done.111
  760.9 26.9 %collective-permute-done.109 = bf16[384,1024]{1,0:T(8,128)(2,1)} collective-permute-done((bf16[384,1024]{1,0:T(8,128)(2,1)}, bf16[384,1024]{1,0:T(8,128)(2,1)}, u32[]{:S(2)}, u32[]{:S(2)}) %collective-permute-start.109) | collective-permute-done | bytes 786464 | tf_op jit(solution)/shard_map/ppermute | solution.py:407
  791.3 3.6 collective-permute-start.114
  (718 shorter events, 263.2 us)
Async XLA Ops:
  4.0 23.8 %collective-permute-start = (bf16[384,512]{1,0:T(8,128)(2,1)}, bf16[384,512]{1,0:T(8,128)(2,1)}, u32[]{:S(2)}, u32[]{:S(2)}) collective-permute-start(bf16[384,512]{1,0:T(8,128)(2,1)} %pad_maximum_fusion.27), channel_id=1, source_target_pairs={{0,1},{1,2},{2,3},{3,0},{4,5},{5,6},{6,7},{7,4},{8,9},{9,10},{10,1... | collective-permute-start | bytes 1179656 | tf_op jit(solution)/shard_map/ppermute | solution.py:407
  7.9 20.0 %collective-permute-start.1 = (bf16[384,512]{1,0:T(8,128)(2,1)}, bf16[384,512]{1,0:T(8,128)(2,1)}, u32[]{:S(2)}, u32[]{:S(2)}) collective-permute-start(bf16[384,512]{1,0:T(8,128)(2,1)} %pad_maximum_fusion.28), channel_id=1, source_target_pairs={{0,3},{1,0},{2,1},{3,2},{4,7},{5,4},{6,5},{7,6},{8,11},{9,8},{10,9... | collective-permute-start | bytes 1179656 | tf_op jit(solution)/shard_map/ppermute | solution.py:407
  27.9 23.3 %collective-permute-start.6 = (bf16[256,512]{1,0:T(8,128)(2,1)S(1)}, bf16[256,512]{1,0:T(8,128)(2,1)S(1)}, u32[]{:S(2)}, u32[]{:S(2)}) collective-permute-start(bf16[256,512]{1,0:T(8,128)(2,1)S(1)} %get-tuple-element.230), channel_id=1, source_target_pairs={{0,1},{1,2},{2,3},{3,0},{4,5},{5,6},{6,7},{7,4},{8,9},{9,10},{10,1... | collective-permute-start | bytes 786440 | tf_op jit(solution)/shard_map/ppermute | solution.py:407
  27.9 23.2 %collective-permute-start.7 = (bf16[256,512]{1,0:T(8,128)(2,1)S(1)}, bf16[256,512]{1,0:T(8,128)(2,1)S(1)}, u32[]{:S(2)}, u32[]{:S(2)}) collective-permute-start(bf16[256,512]{1,0:T(8,128)(2,1)S(1)} %get-tuple-element.230), channel_id=1, source_target_pairs={{0,3},{1,0},{2,1},{3,2},{4,7},{5,4},{6,5},{7,6},{8,11},{9,8},{10,9... | collective-permute-start | bytes 786440 | tf_op jit(solution)/shard_map/ppermute | solution.py:407
  32.8 18.5 %collective-permute-start.8 = (bf16[256,1024]{1,0:T(8,128)(2,1)S(1)}, bf16[256,1024]{1,0:T(8,128)(2,1)S(1)}, u32[]{:S(2)}, u32[]{:S(2)}) collective-permute-start(bf16[256,1024]{1,0:T(8,128)(2,1)S(1)} %copy-done.44), channel_id=1, source_target_pairs={{0,16},{16,0},{1,17},{17,1},{2,18},{18,2},{3,19},{19,3},{4,20},{20... | collective-permute-start | bytes 1572872 | tf_op jit(solution)/shard_map/ppermute | solution.py:412
  65.1 24.8 %collective-permute-start.12 = (bf16[4,256,512]{2,1,0:T(8,128)(2,1)}, bf16[4,256,512]{2,1,0:T(8,128)(2,1)S(1)}, u32[]{:S(2)}, u32[]{:S(2)}) collective-permute-start(bf16[4,256,512]{2,1,0:T(8,128)(2,1)} %fusion.51), channel_id=1, source_target_pairs={{0,16},{16,0},{1,17},{17,1},{2,18},{18,2},{3,19},{19,3},{4,20},{20... | collective-permute-start | bytes 3145736 | tf_op jit(solution)/shard_map/ppermute | solution.py:412
  89.8 18.1 %collective-permute-start.24 = (bf16[256,1024]{1,0:T(8,128)(2,1)S(1)}, bf16[256,1024]{1,0:T(8,128)(2,1)}, u32[]{:S(2)}, u32[]{:S(2)}) collective-permute-start(bf16[256,1024]{1,0:T(8,128)(2,1)S(1)} %get-tuple-element.251), channel_id=1, source_target_pairs={{0,8},{4,12},{8,0},{12,4},{1,9},{5,13},{9,1},{13,5},{2,10},{6,14},... | collective-permute-start | bytes 1572872 | tf_op jit(solution)/shard_map/ppermute | solution.py:412
  108.0 23.2 %collective-permute-start.30 = (bf16[256,1024]{1,0:T(8,128)(2,1)S(1)}, bf16[256,1024]{1,0:T(8,128)(2,1)}, u32[]{:S(2)}, u32[]{:S(2)}) collective-permute-start(bf16[256,1024]{1,0:T(8,128)(2,1)S(1)} %collective-permute-done.27), channel_id=1, source_target_pairs={{0,8},{4,12},{8,0},{12,4},{1,9},{5,13},{9,1},{13,5},{2,10},{6,14},... | collective-permute-start | bytes 1572872 | tf_op jit(solution)/shard_map/ppermute | solution.py:412
  108.6 24.1 %collective-permute-start.28 = (bf16[128,1024]{1,0:T(8,128)(2,1)S(1)}, bf16[128,1024]{1,0:T(8,128)(2,1)}, u32[]{:S(2)}, u32[]{:S(2)}) collective-permute-start(bf16[128,1024]{1,0:T(8,128)(2,1)S(1)} %slice.800), channel_id=1, source_target_pairs={{0,3},{1,0},{2,1},{3,2},{4,7},{5,4},{6,5},{7,6},{8,11},{9,8},{10,9... | collective-permute-start | bytes 786440 | tf_op jit(solution)/shard_map/ppermute | solution.py:407
  111.4 21.3 %collective-permute-start.26 = (bf16[128,1024]{1,0:T(8,128)(2,1)}, bf16[128,1024]{1,0:T(8,128)(2,1)}, u32[]{:S(2)}, u32[]{:S(2)}) collective-permute-start(bf16[128,1024]{1,0:T(8,128)(2,1)} %slice.799), channel_id=1, source_target_pairs={{0,1},{1,2},{2,3},{3,0},{4,5},{5,6},{6,7},{7,4},{8,9},{9,10},{10,1... | collective-permute-start | bytes 786440 | tf_op jit(solution)/shard_map/ppermute | solution.py:407
  111.4 22.3 %collective-permute-start.29 = (bf16[256,1024]{1,0:T(8,128)(2,1)S(1)}, bf16[256,1024]{1,0:T(8,128)(2,1)S(1)}, u32[]{:S(2)}, u32[]{:S(2)}) collective-permute-start(bf16[256,1024]{1,0:T(8,128)(2,1)S(1)} %collective-permute-done.25), channel_id=1, source_target_pairs={{0,8},{4,12},{8,0},{12,4},{1,9},{5,13},{9,1},{13,5},{2,10},{6,14},... | collective-permute-start | bytes 1572872 | tf_op jit(solution)/shard_map/ppermute | solution.py:412
  133.6 17.2 %collective-permute-start.34 = (bf16[2,256,1024]{2,1,0:T(8,128)(2,1)S(1)}, bf16[2,256,1024]{2,1,0:T(8,128)(2,1)S(1)}, u32[]{:S(2)}, u32[]{:S(2)}) collective-permute-start(bf16[2,256,1024]{2,1,0:T(8,128)(2,1)S(1)} %pad_maximum_fusion.8.refs_13_.refs_21_.refs_12_.refs_14_), channel_id=1, source_target_pairs={{0,4},{4,0},{8,12},{12,8},{1,5},{5,1},{9,13},{13,9},{2,6},{6,2},{1... | collective-permute-start | bytes 3145736 | tf_op jit(solution)/shard_map/ppermute | solution.py:412
  156.0 21.9 %collective-permute-start.36 = (bf16[256,512]{1,0:T(8,128)(2,1)S(1)}, bf16[256,512]{1,0:T(8,128)(2,1)S(1)}, u32[]{:S(2)}, u32[]{:S(2)}) collective-permute-start(bf16[256,512]{1,0:T(8,128)(2,1)S(1)} %copy-done.28), channel_id=1, source_target_pairs={{0,1},{1,2},{2,3},{3,0},{4,5},{5,6},{6,7},{7,4},{8,9},{9,10},{10,1... | collective-permute-start | bytes 786440 | tf_op jit(solution)/shard_map/ppermute | solution.py:407
  157.1 20.8 %collective-permute-start.37 = (bf16[256,512]{1,0:T(8,128)(2,1)S(1)}, bf16[256,512]{1,0:T(8,128)(2,1)S(1)}, u32[]{:S(2)}, u32[]{:S(2)}) collective-permute-start(bf16[256,512]{1,0:T(8,128)(2,1)S(1)} %copy-done.28), channel_id=1, source_target_pairs={{0,3},{1,0},{2,1},{3,2},{4,7},{5,4},{6,5},{7,6},{8,11},{9,8},{10,9... | collective-permute-start | bytes 786440 | tf_op jit(solution)/shard_map/ppermute | solution.py:407
  160.1 18.5 %collective-permute-start.38 = (bf16[256,512]{1,0:T(8,128)(2,1)S(1)}, bf16[256,512]{1,0:T(8,128)(2,1)S(1)}, u32[]{:S(2)}, u32[]{:S(2)}) collective-permute-start(bf16[256,512]{1,0:T(8,128)(2,1)S(1)} %copy-done.28), channel_id=1, source_target_pairs={{0,8},{4,12},{8,0},{12,4},{1,9},{5,13},{9,1},{13,5},{2,10},{6,14},... | collective-permute-start | bytes 786440 | tf_op jit(solution)/shard_map/ppermute | solution.py:412
  160.5 18.6 %collective-permute-start.39 = (bf16[256,1024]{1,0:T(8,128)(2,1)S(1)}, bf16[256,1024]{1,0:T(8,128)(2,1)S(1)}, u32[]{:S(2)}, u32[]{:S(2)}) collective-permute-start(bf16[256,1024]{1,0:T(8,128)(2,1)S(1)} %get-tuple-element.275), channel_id=1, source_target_pairs={{0,8},{4,12},{8,0},{12,4},{1,9},{5,13},{9,1},{13,5},{2,10},{6,14},... | collective-permute-start | bytes 1572872 | tf_op jit(solution)/shard_map/ppermute | solution.py:412
  179.1 31.2 %collective-permute-start.43 = (bf16[256,1024]{1,0:T(8,128)(2,1)S(1)}, bf16[256,1024]{1,0:T(8,128)(2,1)S(1)}, u32[]{:S(2)}, u32[]{:S(2)}) collective-permute-start(bf16[256,1024]{1,0:T(8,128)(2,1)S(1)} %get-tuple-element.275), channel_id=1, source_target_pairs={{0,1},{1,2},{2,3},{3,0},{4,5},{5,6},{6,7},{7,4},{8,9},{9,10},{10,1... | collective-permute-start | bytes 1572872 | tf_op jit(solution)/shard_map/ppermute | solution.py:407
  179.1 31.2 %collective-permute-start.44 = (bf16[256,1024]{1,0:T(8,128)(2,1)S(1)}, bf16[256,1024]{1,0:T(8,128)(2,1)S(1)}, u32[]{:S(2)}, u32[]{:S(2)}) collective-permute-start(bf16[256,1024]{1,0:T(8,128)(2,1)S(1)} %get-tuple-element.275), channel_id=1, source_target_pairs={{0,3},{1,0},{2,1},{3,2},{4,7},{5,4},{6,5},{7,6},{8,11},{9,8},{10,9... | collective-permute-start | bytes 1572872 | tf_op jit(solution)/shard_map/ppermute | solution.py:407
  182.9 23.2 %collective-permute-start.42 = (bf16[128,512]{1,0:T(8,128)(2,1)S(1)}, bf16[128,512]{1,0:T(8,128)(2,1)S(1)}, u32[]{:S(2)}, u32[]{:S(2)}) collective-permute-start(bf16[128,512]{1,0:T(8,128)(2,1)S(1)} %slice.805), channel_id=1, source_target_pairs={{0,3},{1,0},{2,1},{3,2},{4,7},{5,4},{6,5},{7,6},{8,11},{9,8},{10,9... | collective-permute-start | bytes 393224 | tf_op jit(solution)/shard_map/ppermute | solution.py:407
  183.0 27.3 %collective-permute-start.41 = (bf16[128,512]{1,0:T(8,128)(2,1)}, bf16[128,512]{1,0:T(8,128)(2,1)S(1)}, u32[]{:S(2)}, u32[]{:S(2)}) collective-permute-start(bf16[128,512]{1,0:T(8,128)(2,1)} %slice.804), channel_id=1, source_target_pairs={{0,1},{1,2},{2,3},{3,0},{4,5},{5,6},{6,7},{7,4},{8,9},{9,10},{10,1... | collective-permute-start | bytes 393224 | tf_op jit(solution)/shard_map/ppermute | solution.py:407
  185.4 24.9 %collective-permute-start.40 = (bf16[512,1024]{1,0:T(8,128)(2,1)}, bf16[512,1024]{1,0:T(8,128)(2,1)S(1)}, u32[]{:S(2)}, u32[]{:S(2)}) collective-permute-start(bf16[512,1024]{1,0:T(8,128)(2,1)} %get-tuple-element.268), channel_id=1, source_target_pairs={{0,16},{16,0},{1,17},{17,1},{2,18},{18,2},{3,19},{19,3},{4,20},{20... | collective-permute-start | bytes 3145736 | tf_op jit(solution)/shard_map/ppermute | solution.py:412
  213.8 22.3 %collective-permute-start.45 = (bf16[512,1024]{1,0:T(8,128)(2,1)}, bf16[512,1024]{1,0:T(8,128)(2,1)}, u32[]{:S(2)}, u32[]{:S(2)}) collective-permute-start(bf16[512,1024]{1,0:T(8,128)(2,1)} %get-tuple-element.276), channel_id=1, source_target_pairs={{0,16},{16,0},{1,17},{17,1},{2,18},{18,2},{3,19},{19,3},{4,20},{20... | collective-permute-start | bytes 3145736 | tf_op jit(solution)/shard_map/ppermute | solution.py:412
  242.2 19.4 %collective-permute-start.56 = (bf16[2,256,1024]{2,1,0:T(8,128)(2,1)S(1)}, bf16[2,256,1024]{2,1,0:T(8,128)(2,1)}, u32[]{:S(2)}, u32[]{:S(2)}) collective-permute-start(bf16[2,256,1024]{2,1,0:T(8,128)(2,1)S(1)} %pad_maximum_fusion.9.refs_11_.refs_19_.refs_10_.refs_12_), channel_id=1, source_target_pairs={{0,4},{4,0},{8,12},{12,8},{1,5},{5,1},{9,13},{13,9},{2,6},{6,2},{1... | collective-permute-start | bytes 3145736 | tf_op jit(solution)/shard_map/ppermute | solution.py:412
  242.7 17.8 %collective-permute-start.55 = (bf16[256,1024]{1,0:T(8,128)(2,1)S(1)}, bf16[256,1024]{1,0:T(8,128)(2,1)S(1)}, u32[]{:S(2)}, u32[]{:S(2)}) collective-permute-start(bf16[256,1024]{1,0:T(8,128)(2,1)S(1)} %collective-permute-done.43), channel_id=1, source_target_pairs={{0,8},{4,12},{8,0},{12,4},{1,9},{5,13},{9,1},{13,5},{2,10},{6,14},... | collective-permute-start | bytes 1572872 | tf_op jit(solution)/shard_map/ppermute | solution.py:412
  261.6 29.5 %collective-permute-start.60 = (bf16[384,512]{1,0:T(8,128)(2,1)S(1)}, bf16[384,512]{1,0:T(8,128)(2,1)}, u32[]{:S(2)}, u32[]{:S(2)}) collective-permute-start(bf16[384,512]{1,0:T(8,128)(2,1)S(1)} %copy-done.55), channel_id=1, source_target_pairs={{0,1},{1,2},{2,3},{3,0},{4,5},{5,6},{6,7},{7,4},{8,9},{9,10},{10,1... | collective-permute-start | bytes 1179656 | tf_op jit(solution)/shard_map/ppermute | solution.py:407
  261.6 29.5 %collective-permute-start.61 = (bf16[384,512]{1,0:T(8,128)(2,1)}, bf16[384,512]{1,0:T(8,128)(2,1)}, u32[]{:S(2)}, u32[]{:S(2)}) collective-permute-start(bf16[384,512]{1,0:T(8,128)(2,1)} %pad_maximum_fusion.30), channel_id=1, source_target_pairs={{0,3},{1,0},{2,1},{3,2},{4,7},{5,4},{6,5},{7,6},{8,11},{9,8},{10,9... | collective-permute-start | bytes 1179656 | tf_op jit(solution)/shard_map/ppermute | solution.py:407
  265.4 25.7 %collective-permute-start.59 = (bf16[2,256,1024]{2,1,0:T(8,128)(2,1)}, bf16[2,256,1024]{2,1,0:T(8,128)(2,1)}, u32[]{:S(2)}, u32[]{:S(2)}) collective-permute-start(bf16[2,256,1024]{2,1,0:T(8,128)(2,1)} %pad_maximum_fusion.11.refs_12_.refs_20_.refs_11_.refs_13_), channel_id=1, source_target_pairs={{0,4},{4,0},{8,12},{12,8},{1,5},{5,1},{9,13},{13,9},{2,6},{6,2},{1... | collective-permute-start | bytes 3145736 | tf_op jit(solution)/shard_map/ppermute | solution.py:412
  265.4 19.3 %collective-permute-start.58 = (bf16[256,1024]{1,0:T(8,128)(2,1)S(1)}, bf16[256,1024]{1,0:T(8,128)(2,1)S(1)}, u32[]{:S(2)}, u32[]{:S(2)}) collective-permute-start(bf16[256,1024]{1,0:T(8,128)(2,1)S(1)} %constant_dynamic-update-slice_fusion.6), channel_id=1, source_target_pairs={{0,8},{4,12},{8,0},{12,4},{1,9},{5,13},{9,1},{13,5},{2,10},{6,14},... | collective-permute-start | bytes 1572872 | tf_op jit(solution)/shard_map/ppermute | solution.py:412
  266.6 24.4 %collective-permute-start.57 = (bf16[256,1024]{1,0:T(8,128)(2,1)S(1)}, bf16[256,1024]{1,0:T(8,128)(2,1)S(1)}, u32[]{:S(2)}, u32[]{:S(2)}) collective-permute-start(bf16[256,1024]{1,0:T(8,128)(2,1)S(1)} %collective-permute-done.44), channel_id=1, source_target_pairs={{0,8},{4,12},{8,0},{12,4},{1,9},{5,13},{9,1},{13,5},{2,10},{6,14},... | collective-permute-start | bytes 1572872 | tf_op jit(solution)/shard_map/ppermute | solution.py:412
  304.2 23.4 %collective-permute-start.66 = (bf16[4,256,512]{2,1,0:T(8,128)(2,1)S(1)}, bf16[4,256,512]{2,1,0:T(8,128)(2,1)S(1)}, u32[]{:S(2)}, u32[]{:S(2)}) collective-permute-start(bf16[4,256,512]{2,1,0:T(8,128)(2,1)S(1)} %fusion.52), channel_id=1, source_target_pairs={{0,16},{16,0},{1,17},{17,1},{2,18},{18,2},{3,19},{19,3},{4,20},{20... | collective-permute-start | bytes 3145736 | tf_op jit(solution)/shard_map/ppermute | solution.py:412
  327.7 22.6 %collective-permute-start.67 = (bf16[512,1024]{1,0:T(8,128)(2,1)}, bf16[512,1024]{1,0:T(8,128)(2,1)S(1)}, u32[]{:S(2)}, u32[]{:S(2)}) collective-permute-start(bf16[512,1024]{1,0:T(8,128)(2,1)} %get-tuple-element.309), channel_id=1, source_target_pairs={{0,16},{16,0},{1,17},{17,1},{2,18},{18,2},{3,19},{19,3},{4,20},{20... | collective-permute-start | bytes 3145736 | tf_op jit(solution)/shard_map/ppermute | solution.py:412
  365.8 26.6 %collective-permute-start.68 = (bf16[512,1024]{1,0:T(8,128)(2,1)}, bf16[512,1024]{1,0:T(8,128)(2,1)}, u32[]{:S(2)}, u32[]{:S(2)}) collective-permute-start(bf16[512,1024]{1,0:T(8,128)(2,1)} %get-tuple-element.324), channel_id=1, source_target_pairs={{0,16},{16,0},{1,17},{17,1},{2,18},{18,2},{3,19},{19,3},{4,20},{20... | collective-permute-start | bytes 3145736 | tf_op jit(solution)/shard_map/ppermute | solution.py:412
  410.1 30.9 %collective-permute-start.71 = (bf16[384,512]{1,0:T(8,128)(2,1)}, bf16[384,512]{1,0:T(8,128)(2,1)S(1)}, u32[]{:S(2)}, u32[]{:S(2)}) collective-permute-start(bf16[384,512]{1,0:T(8,128)(2,1)} %pad_maximum_fusion.32), channel_id=1, source_target_pairs={{0,3},{1,0},{2,1},{3,2},{4,7},{5,4},{6,5},{7,6},{8,11},{9,8},{10,9... | collective-permute-start | bytes 1179656 | tf_op jit(solution)/shard_map/ppermute | solution.py:407
  412.0 29.0 %collective-permute-start.70 = (bf16[384,512]{1,0:T(8,128)(2,1)}, bf16[384,512]{1,0:T(8,128)(2,1)S(1)}, u32[]{:S(2)}, u32[]{:S(2)}) collective-permute-start(bf16[384,512]{1,0:T(8,128)(2,1)} %pad_maximum_fusion.31), channel_id=1, source_target_pairs={{0,1},{1,2},{2,3},{3,0},{4,5},{5,6},{6,7},{7,4},{8,9},{9,10},{10,1... | collective-permute-start | bytes 1179656 | tf_op jit(solution)/shard_map/ppermute | solution.py:407
  413.8 27.3 %collective-permute-start.69 = (bf16[512,1024]{1,0:T(8,128)(2,1)}, bf16[512,1024]{1,0:T(8,128)(2,1)S(1)}, u32[]{:S(2)}, u32[]{:S(2)}) collective-permute-start(bf16[512,1024]{1,0:T(8,128)(2,1)} %get-tuple-element.344), channel_id=1, source_target_pairs={{0,16},{16,0},{1,17},{17,1},{2,18},{18,2},{3,19},{19,3},{4,20},{20... | collective-permute-start | bytes 3145736 | tf_op jit(solution)/shard_map/ppermute | solution.py:412
  441.9 43.7 %collective-permute-start.73 = (bf16[2,4,256,1024]{3,2,1,0:T(8,128)(2,1)}, bf16[2,4,256,1024]{3,2,1,0:T(8,128)(2,1)}, u32[]{:S(2)}, u32[]{:S(2)}) collective-permute-start(bf16[2,4,256,1024]{3,2,1,0:T(8,128)(2,1)} %get-tuple-element.339), channel_id=1, source_target_pairs={{0,4},{4,0},{8,12},{12,8},{1,5},{5,1},{9,13},{13,9},{2,6},{6,2},{1... | collective-permute-start | bytes 12582920 | tf_op jit(solution)/shard_map/ppermute | solution.py:412
  460.2 20.2 %collective-permute-start.74 = (bf16[384,512]{1,0:T(8,128)(2,1)}, bf16[384,512]{1,0:T(8,128)(2,1)}, u32[]{:S(2)}, u32[]{:S(2)}) collective-permute-start(bf16[384,512]{1,0:T(8,128)(2,1)} %pad_maximum_fusion.33), channel_id=1, source_target_pairs={{0,1},{1,2},{2,3},{3,0},{4,5},{5,6},{6,7},{7,4},{8,9},{9,10},{10,1... | collective-permute-start | bytes 1179656 | tf_op jit(solution)/shard_map/ppermute | solution.py:407
  460.2 25.4 %collective-permute-start.72 = (bf16[512,1024]{1,0:T(8,128)(2,1)S(1)}, bf16[512,1024]{1,0:T(8,128)(2,1)}, u32[]{:S(2)}, u32[]{:S(2)}) collective-permute-start(bf16[512,1024]{1,0:T(8,128)(2,1)S(1)} %copy-done.31), channel_id=1, source_target_pairs={{0,16},{16,0},{1,17},{17,1},{2,18},{18,2},{3,19},{19,3},{4,20},{20... | collective-permute-start | bytes 3145736 | tf_op jit(solution)/shard_map/ppermute | solution.py:412
  485.6 30.9 %collective-permute-start.81 = (bf16[128,512]{1,0:T(8,128)(2,1)}, bf16[128,512]{1,0:T(8,128)(2,1)S(1)}, u32[]{:S(2)}, u32[]{:S(2)}) collective-permute-start(bf16[128,512]{1,0:T(8,128)(2,1)} %slice.825), channel_id=1, source_target_pairs={{0,3},{1,0},{2,1},{3,2},{4,7},{5,4},{6,5},{7,6},{8,11},{9,8},{10,9... | collective-permute-start | bytes 393224 | tf_op jit(solution)/shard_map/ppermute | solution.py:407
  489.1 30.8 %collective-permute-start.80 = (bf16[128,512]{1,0:T(8,128)(2,1)S(1)}, bf16[128,512]{1,0:T(8,128)(2,1)S(1)}, u32[]{:S(2)}, u32[]{:S(2)}) collective-permute-start(bf16[128,512]{1,0:T(8,128)(2,1)S(1)} %slice.824), channel_id=1, source_target_pairs={{0,1},{1,2},{2,3},{3,0},{4,5},{5,6},{6,7},{7,4},{8,9},{9,10},{10,1... | collective-permute-start | bytes 393224 | tf_op jit(solution)/shard_map/ppermute | solution.py:407
  489.1 30.8 %collective-permute-start.79 = (bf16[128,512]{1,0:T(8,128)(2,1)}, bf16[128,512]{1,0:T(8,128)(2,1)S(1)}, u32[]{:S(2)}, u32[]{:S(2)}) collective-permute-start(bf16[128,512]{1,0:T(8,128)(2,1)} %slice.823), channel_id=1, source_target_pairs={{0,3},{1,0},{2,1},{3,2},{4,7},{5,4},{6,5},{7,6},{8,11},{9,8},{10,9... | collective-permute-start | bytes 393224 | tf_op jit(solution)/shard_map/ppermute | solution.py:407
  494.9 29.4 %collective-permute-start.77 = (bf16[2,256,1024]{2,1,0:T(8,128)(2,1)S(1)}, bf16[2,256,1024]{2,1,0:T(8,128)(2,1)}, u32[]{:S(2)}, u32[]{:S(2)}) collective-permute-start(bf16[2,256,1024]{2,1,0:T(8,128)(2,1)S(1)} %fusion.16), channel_id=1, source_target_pairs={{0,8},{4,12},{8,0},{12,4},{1,9},{5,13},{9,1},{13,5},{2,10},{6,14},... | collective-permute-start | bytes 3145736 | tf_op jit(solution)/shard_map/ppermute | solution.py:412
  496.1 28.1 %collective-permute-start.76 = (bf16[2,4,256,512]{3,2,1,0:T(8,128)(2,1)}, bf16[2,4,256,512]{3,2,1,0:T(8,128)(2,1)}, u32[]{:S(2)}, u32[]{:S(2)}) collective-permute-start(bf16[2,4,256,512]{3,2,1,0:T(8,128)(2,1)} %get-tuple-element.351), channel_id=1, source_target_pairs={{0,4},{4,0},{8,12},{12,8},{1,5},{5,1},{9,13},{13,9},{2,6},{6,2},{1... | collective-permute-start | bytes 6291464 | tf_op jit(solution)/shard_map/ppermute | solution.py:412
  526.0 25.0 %collective-permute-start.82 = (bf16[2,256,1024]{2,1,0:T(8,128)(2,1)S(1)}, bf16[2,256,1024]{2,1,0:T(8,128)(2,1)}, u32[]{:S(2)}, u32[]{:S(2)}) collective-permute-start(bf16[2,256,1024]{2,1,0:T(8,128)(2,1)S(1)} %fusion.15), channel_id=1, source_target_pairs={{0,8},{4,12},{8,0},{12,4},{1,9},{5,13},{9,1},{13,5},{2,10},{6,14},... | collective-permute-start | bytes 3145736 | tf_op jit(solution)/shard_map/ppermute | solution.py:412
  550.9 38.1 %collective-permute-start.85 = (bf16[2,4,256,1024]{3,2,1,0:T(8,128)(2,1)}, bf16[2,4,256,1024]{3,2,1,0:T(8,128)(2,1)}, u32[]{:S(2)}, u32[]{:S(2)}) collective-permute-start(bf16[2,4,256,1024]{3,2,1,0:T(8,128)(2,1)} %get-tuple-element.370), channel_id=1, source_target_pairs={{0,4},{4,0},{8,12},{12,8},{1,5},{5,1},{9,13},{13,9},{2,6},{6,2},{1... | collective-permute-start | bytes 12582920 | tf_op jit(solution)/shard_map/ppermute | solution.py:412
  556.9 32.1 %collective-permute-start.86 = (bf16[4,256,512]{2,1,0:T(8,128)(2,1)}, bf16[4,256,512]{2,1,0:T(8,128)(2,1)}, u32[]{:S(2)}, u32[]{:S(2)}) collective-permute-start(bf16[4,256,512]{2,1,0:T(8,128)(2,1)} %fusion.12), channel_id=1, source_target_pairs={{0,8},{4,12},{8,0},{12,4},{1,9},{5,13},{9,1},{13,5},{2,10},{6,14},... | collective-permute-start | bytes 3145736 | tf_op jit(solution)/shard_map/ppermute | solution.py:412
  560.0 29.0 %collective-permute-start.84 = (bf16[128,1024]{1,0:T(8,128)(2,1)S(1)}, bf16[128,1024]{1,0:T(8,128)(2,1)S(1)}, u32[]{:S(2)}, u32[]{:S(2)}) collective-permute-start(bf16[128,1024]{1,0:T(8,128)(2,1)S(1)} %get-tuple-element.368), channel_id=1, source_target_pairs={{0,3},{1,0},{2,1},{3,2},{4,7},{5,4},{6,5},{7,6},{8,11},{9,8},{10,9... | collective-permute-start | bytes 786440 | tf_op jit(solution)/shard_map/ppermute | solution.py:407
  560.0 28.0 %collective-permute-start.83 = (bf16[128,1024]{1,0:T(8,128)(2,1)S(1)}, bf16[128,1024]{1,0:T(8,128)(2,1)S(1)}, u32[]{:S(2)}, u32[]{:S(2)}) collective-permute-start(bf16[128,1024]{1,0:T(8,128)(2,1)S(1)} %get-tuple-element.367), channel_id=1, source_target_pairs={{0,1},{1,2},{2,3},{3,0},{4,5},{5,6},{6,7},{7,4},{8,9},{9,10},{10,1... | collective-permute-start | bytes 786440 | tf_op jit(solution)/shard_map/ppermute | solution.py:407
  602.8 24.7 %collective-permute-start.89 = (bf16[256,1024]{1,0:T(8,128)(2,1)}, bf16[256,1024]{1,0:T(8,128)(2,1)S(1)}, u32[]{:S(2)}, u32[]{:S(2)}) collective-permute-start(bf16[256,1024]{1,0:T(8,128)(2,1)} %pad_maximum_fusion.24), channel_id=1, source_target_pairs={{0,3},{1,0},{2,1},{3,2},{4,7},{5,4},{6,5},{7,6},{8,11},{9,8},{10,9... | collective-permute-start | bytes 1572872 | tf_op jit(solution)/shard_map/ppermute | solution.py:407
  604.6 23.6 %collective-permute-start.88 = (bf16[256,1024]{1,0:T(8,128)(2,1)}, bf16[256,1024]{1,0:T(8,128)(2,1)}, u32[]{:S(2)}, u32[]{:S(2)}) collective-permute-start(bf16[256,1024]{1,0:T(8,128)(2,1)} %pad_maximum_fusion.23), channel_id=1, source_target_pairs={{0,1},{1,2},{2,3},{3,0},{4,5},{5,6},{6,7},{7,4},{8,9},{9,10},{10,1... | collective-permute-start | bytes 1572872 | tf_op jit(solution)/shard_map/ppermute | solution.py:407
  607.8 24.9 %collective-permute-start.87 = (bf16[2,256,1024]{2,1,0:T(8,128)(2,1)}, bf16[2,256,1024]{2,1,0:T(8,128)(2,1)}, u32[]{:S(2)}, u32[]{:S(2)}) collective-permute-start(bf16[2,256,1024]{2,1,0:T(8,128)(2,1)} %fusion.17), channel_id=1, source_target_pairs={{0,8},{4,12},{8,0},{12,4},{1,9},{5,13},{9,1},{13,5},{2,10},{6,14},... | collective-permute-start | bytes 3145736 | tf_op jit(solution)/shard_map/ppermute | solution.py:412
  609.0 48.3 %collective-permute-start.90 = (bf16[512,1024]{1,0:T(8,128)(2,1)}, bf16[512,1024]{1,0:T(8,128)(2,1)}, u32[]{:S(2)}, u32[]{:S(2)}) collective-permute-start(bf16[512,1024]{1,0:T(8,128)(2,1)} %get-tuple-element.396), channel_id=1, source_target_pairs={{0,16},{16,0},{1,17},{17,1},{2,18},{18,2},{3,19},{19,3},{4,20},{20... | collective-permute-start | bytes 3145736 | tf_op jit(solution)/shard_map/ppermute | solution.py:412
  632.7 22.1 %collective-permute-start.94 = (bf16[128,512]{1,0:T(8,128)(2,1)}, bf16[128,512]{1,0:T(8,128)(2,1)}, u32[]{:S(2)}, u32[]{:S(2)}) collective-permute-start(bf16[128,512]{1,0:T(8,128)(2,1)} %get-tuple-element.390), channel_id=1, source_target_pairs={{0,3},{1,0},{2,1},{3,2},{4,7},{5,4},{6,5},{7,6},{8,11},{9,8},{10,9... | collective-permute-start | bytes 393224 | tf_op jit(solution)/shard_map/ppermute | solution.py:407
  636.2 18.6 %collective-permute-start.93 = (bf16[128,512]{1,0:T(8,128)(2,1)}, bf16[128,512]{1,0:T(8,128)(2,1)}, u32[]{:S(2)}, u32[]{:S(2)}) collective-permute-start(bf16[128,512]{1,0:T(8,128)(2,1)} %get-tuple-element.389), channel_id=1, source_target_pairs={{0,1},{1,2},{2,3},{3,0},{4,5},{5,6},{6,7},{7,4},{8,9},{9,10},{10,1... | collective-permute-start | bytes 393224 | tf_op jit(solution)/shard_map/ppermute | solution.py:407
  637.9 23.4 %collective-permute-start.92 = (bf16[2,256,1024]{2,1,0:T(8,128)(2,1)S(1)}, bf16[2,256,1024]{2,1,0:T(8,128)(2,1)}, u32[]{:S(2)}, u32[]{:S(2)}) collective-permute-start(bf16[2,256,1024]{2,1,0:T(8,128)(2,1)S(1)} %fusion.9), channel_id=1, source_target_pairs={{0,8},{4,12},{8,0},{12,4},{1,9},{5,13},{9,1},{13,5},{2,10},{6,14},... | collective-permute-start | bytes 3145736 | tf_op jit(solution)/shard_map/ppermute | solution.py:412
  639.1 23.3 %collective-permute-start.91 = (bf16[512,1024]{1,0:T(8,128)(2,1)}, bf16[512,1024]{1,0:T(8,128)(2,1)}, u32[]{:S(2)}, u32[]{:S(2)}) collective-permute-start(bf16[512,1024]{1,0:T(8,128)(2,1)} %get-tuple-element.397), channel_id=1, source_target_pairs={{0,16},{16,0},{1,17},{17,1},{2,18},{18,2},{3,19},{19,3},{4,20},{20... | collective-permute-start | bytes 3145736 | tf_op jit(solution)/shard_map/ppermute | solution.py:412
  674.1 19.0 %collective-permute-start.97 = (bf16[2,4,256,512]{3,2,1,0:T(8,128)(2,1)}, bf16[2,4,256,512]{3,2,1,0:T(8,128)(2,1)S(1)}, u32[]{:S(2)}, u32[]{:S(2)}) collective-permute-start(bf16[2,4,256,512]{3,2,1,0:T(8,128)(2,1)} %get-tuple-element.395), channel_id=1, source_target_pairs={{0,4},{4,0},{8,12},{12,8},{1,5},{5,1},{9,13},{13,9},{2,6},{6,2},{1... | collective-permute-start | bytes 6291464 | tf_op jit(solution)/shard_map/ppermute | solution.py:412
  698.6 30.6 %collective-permute-start.100 = (bf16[256,1024]{1,0:T(8,128)(2,1)S(1)}, bf16[256,1024]{1,0:T(8,128)(2,1)S(1)}, u32[]{:S(2)}, u32[]{:S(2)}) collective-permute-start(bf16[256,1024]{1,0:T(8,128)(2,1)S(1)} %pad_maximum_fusion.26), channel_id=1, source_target_pairs={{0,3},{1,0},{2,1},{3,2},{4,7},{5,4},{6,5},{7,6},{8,11},{9,8},{10,9... | collective-permute-start | bytes 1572872 | tf_op jit(solution)/shard_map/ppermute | solution.py:407
  702.3 27.0 %collective-permute-start.99 = (bf16[256,1024]{1,0:T(8,128)(2,1)S(1)}, bf16[256,1024]{1,0:T(8,128)(2,1)S(1)}, u32[]{:S(2)}, u32[]{:S(2)}) collective-permute-start(bf16[256,1024]{1,0:T(8,128)(2,1)S(1)} %pad_maximum_fusion.25), channel_id=1, source_target_pairs={{0,1},{1,2},{2,3},{3,0},{4,5},{5,6},{6,7},{7,4},{8,9},{9,10},{10,1... | collective-permute-start | bytes 1572872 | tf_op jit(solution)/shard_map/ppermute | solution.py:407
  707.4 23.2 %collective-permute-start.101 = (bf16[4,256,512]{2,1,0:T(8,128)(2,1)S(1)}, bf16[4,256,512]{2,1,0:T(8,128)(2,1)S(1)}, u32[]{:S(2)}, u32[]{:S(2)}) collective-permute-start(bf16[4,256,512]{2,1,0:T(8,128)(2,1)S(1)} %fusion.2), channel_id=1, source_target_pairs={{0,8},{4,12},{8,0},{12,4},{1,9},{5,13},{9,1},{13,5},{2,10},{6,14},... | collective-permute-start | bytes 3145736 | tf_op jit(solution)/shard_map/ppermute | solution.py:412
  749.3 38.5 %collective-permute-start.109 = (bf16[384,1024]{1,0:T(8,128)(2,1)}, bf16[384,1024]{1,0:T(8,128)(2,1)}, u32[]{:S(2)}, u32[]{:S(2)}) collective-permute-start(bf16[384,1024]{1,0:T(8,128)(2,1)} %pad_maximum_fusion.14), channel_id=1, source_target_pairs={{0,3},{1,0},{2,1},{3,2},{4,7},{5,4},{6,5},{7,6},{8,11},{9,8},{10,9... | collective-permute-start | bytes 2359304 | tf_op jit(solution)/shard_map/ppermute | solution.py:407
  751.1 36.7 %collective-permute-start.108 = (bf16[384,1024]{1,0:T(8,128)(2,1)}, bf16[384,1024]{1,0:T(8,128)(2,1)}, u32[]{:S(2)}, u32[]{:S(2)}) collective-permute-start(bf16[384,1024]{1,0:T(8,128)(2,1)} %pad_maximum_fusion.13), channel_id=1, source_target_pairs={{0,1},{1,2},{2,3},{3,0},{4,5},{5,6},{6,7},{7,4},{8,9},{9,10},{10,1... | collective-permute-start | bytes 2359304 | tf_op jit(solution)/shard_map/ppermute | solution.py:407
  788.5 17.2 %collective-permute-start.117 = (bf16[256,512]{1,0:T(8,128)(2,1)S(1)}, bf16[256,512]{1,0:T(8,128)(2,1)S(1)}, u32[]{:S(2)}, u32[]{:S(2)}) collective-permute-start(bf16[256,512]{1,0:T(8,128)(2,1)S(1)} %copy-done.56), channel_id=1, source_target_pairs={{0,16},{16,0},{1,17},{17,1},{2,18},{18,2},{3,19},{19,3},{4,20},{20... | collective-permute-start | bytes 786440 | tf_op jit(solution)/shard_map/ppermute | solution.py:412
  789.9 18.4 %collective-permute-start.113 = (bf16[128,1024]{1,0:T(8,128)(2,1)S(1)}, bf16[128,1024]{1,0:T(8,128)(2,1)S(1)}, u32[]{:S(2)}, u32[]{:S(2)}) collective-permute-start(bf16[128,1024]{1,0:T(8,128)(2,1)S(1)} %slice.867), channel_id=1, source_target_pairs={{0,1},{1,2},{2,3},{3,0},{4,5},{5,6},{6,7},{7,4},{8,9},{9,10},{10,1... | collective-permute-start | bytes 786440 | tf_op jit(solution)/shard_map/ppermute | solution.py:407
  (154 other events, 1544.8 us)
